TPU v7x, 32 devices: a whole 2x2x4 slice. The times are simulated.
32 devices in a mesh: seq: 4 (over y, x), ctx: 8 (over z, core).
Axes of the slice: x: 2, y: 2, z: 4, core: 2. Of those that a mesh axis runs over, the one named last changes fastest.
Arguments:
- block_input: bfloat16 [4, 1024, 2048], P('seq', 'ctx'), may hold values from -6 to 6
- positions: int32 [4, 1024], P('seq', 'ctx'), may hold values from 0 to 1023, as said below
- segments: int32 [4, 1024], P('seq'), may hold values from 0 to 1, as said below
- cotangent: bfloat16 [4, 1024, 2048], P('seq', 'ctx'), may hold values from -6 to 6
- attn_gain: bfloat16 [2048], P(('seq', 'ctx')), may hold values from 0.5 to 1.5
- query_weight: bfloat16 [2048, 2048], P(('seq', 'ctx')), may hold values from -0.125 to 0.125
- key_weight: bfloat16 [2048, 256], P(('seq', 'ctx')), may hold values from -0.125 to 0.125
- value_weight: bfloat16 [2048, 256], P(('seq', 'ctx')), may hold values from -0.125 to 0.125
- out_weight: bfloat16 [2048, 2048], P(('seq', 'ctx')), may hold values from -0.75 to 0.75
- mlp_gain: bfloat16 [2048], P(('seq', 'ctx')), may hold values from 0.5 to 1.5
- gate_weight: bfloat16 [2048, 5632], P(('seq', 'ctx')), may hold values from -0.125 to 0.125
- up_weight: bfloat16 [2048, 5632], P(('seq', 'ctx')), may hold values from -0.125 to 0.125
- down_weight: bfloat16 [2048, 5632], P(('seq', 'ctx')), may hold values from -0.078125 to 0.078125
Outputs:
- block_output: bfloat16 [4, 1024, 2048], P('seq', 'ctx')
- input_grad: float32 [4, 1024, 2048], P('seq', 'ctx')
- attn_gain_grad: float32 [2048], P(('seq', 'ctx'))
- query_grad: float32 [2048, 2048], P(('seq', 'ctx'))
- key_grad: float32 [2048, 256], P(('seq', 'ctx'))
- value_grad: float32 [2048, 256], P(('seq', 'ctx'))
- out_grad: float32 [2048, 2048], P(('seq', 'ctx'))
- mlp_gain_grad: float32 [2048], P(('seq', 'ctx'))
- gate_grad: float32 [2048, 5632], P(('seq', 'ctx'))
- up_grad: float32 [2048, 5632], P(('seq', 'ctx'))
- down_grad: float32 [2048, 5632], P(('seq', 'ctx'))
Inputs may be any that keep to these rules, and one draw needn't show every extreme that they name: `segments`: in each sequence the ids are 0 before one boundary and 1 from it on; the boundary lies between 640 and 896. The first document's positions rise by one and end at 1023; the second document's rise by one from 0.
All inputs are finite; a program needn't handle non-finite values.
Results may differ from a plain program's by a relative error of at most 0.017.
Values may be sent and summed in bfloat16 or wider, within the bound.
No kernel may reach another device: no remote copies, remote signals or barrier semaphores. Data moves between devices by JAX's collectives and lax.ppermute only.
A program may use at most 448 MiB of HBM per device.

v0:
```python
import jax
import jax.numpy as jnp
from jax import lax
from jax.sharding import PartitionSpec as P

HEADS = 32
KV_HEADS = 4
HEAD = 64


EPSILON = 1e-05
MASKED = -1e30


def rope_tables(position, head_size):
    half_size = head_size // 2
    inverse = 1.0 / 10000.0 ** (jnp.arange(half_size, dtype=jnp.float32) * 2.0 / head_size)
    angles = position.astype(jnp.float32)[:, None] * inverse[None, :]
    cosine = jnp.cos(angles)
    sine_table = jnp.sin(angles)
    return (jnp.concatenate([cosine, cosine], -1), jnp.concatenate([sine_table, sine_table], -1))


def rotate(values, cosine, sine_table):
    half_size = values.shape[-1] // 2
    turned = jnp.concatenate([-values[..., half_size:], values[..., :half_size]], -1)
    return values * cosine[:, None, :] + turned * sine_table[:, None, :]


def rms_scale(inputs):
    return lax.rsqrt(jnp.mean(inputs * inputs, axis=-1, keepdims=True) + EPSILON)


def norm_back(inputs, row_scale, gain, upstream):
    shaped = inputs * row_scale
    weighted = upstream * gain
    gain_term = jnp.sum(upstream * shaped, axis=0)
    return (
        row_scale * (weighted - shaped * jnp.mean(weighted * shaped, axis=-1, keepdims=True)),
        gain_term,
    )


def contract_rows(left, right):
    return lax.dot_general(
        left, right, (((0,), (0,)), ((), ())), preferred_element_type=jnp.float32
    )


def contract_cols(left, right):
    return lax.dot_general(
        left, right, (((1,), (1,)), ((), ())), preferred_element_type=jnp.float32
    )


def local(
    block_input,
    positions,
    segments,
    cotangent,
    attn_gain,
    query_weight,
    key_weight,
    value_weight,
    out_weight,
    mlp_gain,
    gate_weight,
    up_weight,
    down_weight,
):
    row_count = block_input.shape[1]
    group_size = HEADS // KV_HEADS
    score_scale = HEAD ** (-0.5)
    inputs = block_input[0].astype(jnp.float32)
    seg_all = segments[0]
    length = seg_all.shape[0]
    block_size = min(512, length)
    block_count = length // block_size
    first_row = lax.axis_index("ctx") * row_count
    query_index = first_row + jnp.arange(row_count, dtype=jnp.int32)
    seg_rows = lax.dynamic_slice_in_dim(seg_all, first_row, row_count)
    cosine, sine_table = rope_tables(positions[0], HEAD)
    starts = jnp.arange(block_count, dtype=jnp.int32) * block_size
    seg_blocks = seg_all.reshape(block_count, block_size)

    def key_mask(seg_block, block_start):
        key_index = block_start + jnp.arange(block_size, dtype=jnp.int32)
        return (seg_rows[:, None] == seg_block[None, :]) & (
            key_index[None, :] <= query_index[:, None]
        )

    def guarded(compute, running):
        result = compute(running)
        return result

    attn_params = (
        lax.all_gather(attn_gain, ("seq", "ctx"), axis=0, tiled=True),
        lax.all_gather(query_weight, ("seq", "ctx"), axis=0, tiled=True),
        lax.all_gather(key_weight, ("seq", "ctx"), axis=0, tiled=True),
        lax.all_gather(value_weight, ("seq", "ctx"), axis=0, tiled=True),
        lax.all_gather(out_weight, ("seq", "ctx"), axis=0, tiled=True),
    )
    gain_one = attn_params[0].astype(jnp.float32)
    scale_one = rms_scale(inputs)
    normed1 = (inputs * scale_one * gain_one).astype(jnp.bfloat16)
    query_raw = jnp.dot(normed1, attn_params[1], preferred_element_type=jnp.float32)
    key_raw = jnp.dot(normed1, attn_params[2], preferred_element_type=jnp.float32)
    value_raw = jnp.dot(normed1, attn_params[3], preferred_element_type=jnp.float32)
    queries = rotate(query_raw.reshape(row_count, HEADS, HEAD), cosine, sine_table).astype(
        jnp.bfloat16
    )
    keys_local = (
        rotate(key_raw.reshape(row_count, KV_HEADS, HEAD), cosine, sine_table)
        .astype(jnp.bfloat16)
        .reshape(row_count, KV_HEADS * HEAD)
    )
    values_local = value_raw.astype(jnp.bfloat16)
    keys_all, values_all = (
        lax.all_gather(keys_local, "ctx", axis=0, tiled=True),
        lax.all_gather(values_local, "ctx", axis=0, tiled=True),
    )
    key_blocks = keys_all.reshape(block_count, block_size, KV_HEADS, HEAD)
    value_blocks = values_all.reshape(block_count, block_size, KV_HEADS, HEAD)
    query_group = queries.reshape(row_count, KV_HEADS, group_size, HEAD)

    def block_scores(key_block, allowed):
        scores = (
            jnp.einsum("tkgd,jkd->kgtj", query_group, key_block, preferred_element_type=jnp.float32)
            * score_scale
        )
        return jnp.where(allowed[None, None], scores, MASKED)

    def max_step(carry, pieces):
        key_block, seg_block, block_start = pieces
        allowed = key_mask(seg_block, block_start)

        def compute(running):
            run_max, run_sum = running
            scores = block_scores(key_block, allowed)
            new_max = jnp.maximum(run_max, jnp.max(scores, axis=-1))
            exponents = jnp.where(allowed[None, None], jnp.exp(scores - new_max[..., None]), 0.0)
            return (new_max, run_sum * jnp.exp(run_max - new_max) + jnp.sum(exponents, axis=-1))

        return (guarded(compute, carry), None)

    start_max = jnp.full((KV_HEADS, group_size, row_count), MASKED, jnp.float32)
    start_sum = jnp.zeros((KV_HEADS, group_size, row_count), jnp.float32)
    (run_max, run_sum), unused = lax.scan(
        max_step, (start_max, start_sum), (key_blocks, seg_blocks, starts)
    )
    log_sum = run_max + jnp.log(run_sum)

    def block_soft(key_block, allowed):
        scores = block_scores(key_block, allowed)
        return jnp.where(allowed[None, None], jnp.exp(scores - log_sum[..., None]), 0.0)

    def value_step(carry, pieces):
        key_block, value_block, seg_block, block_start = pieces
        allowed = key_mask(seg_block, block_start)

        def compute(running):
            acc_out, acc_fix = running
            soft_weights = block_soft(key_block, allowed)
            rounded = soft_weights.astype(jnp.bfloat16)
            leftover = (soft_weights - rounded.astype(jnp.float32)).astype(jnp.bfloat16)
            acc_out = acc_out + jnp.einsum(
                "kgtj,jkd->tkgd", rounded, value_block, preferred_element_type=jnp.float32
            )
            acc_fix = acc_fix + jnp.einsum(
                "kgtj,jkd->tkgd", leftover, value_block, preferred_element_type=jnp.float32
            )
            return (acc_out, acc_fix)

        return (guarded(compute, carry), None)

    zero_mix = jnp.zeros((row_count, KV_HEADS, group_size, HEAD), jnp.float32)
    (acc_out, acc_fix), unused = lax.scan(
        value_step, (zero_mix, zero_mix), (key_blocks, value_blocks, seg_blocks, starts)
    )
    attn_low = acc_out.reshape(row_count, HEADS * HEAD).astype(jnp.bfloat16)
    full_mix = acc_out + acc_fix
    residual = inputs + jnp.dot(attn_low, attn_params[4], preferred_element_type=jnp.float32)
    mlp_params = (
        lax.all_gather(mlp_gain, ("seq", "ctx"), axis=0, tiled=True),
        lax.all_gather(gate_weight, ("seq", "ctx"), axis=0, tiled=True),
        lax.all_gather(up_weight, ("seq", "ctx"), axis=0, tiled=True),
        lax.all_gather(down_weight, ("seq", "ctx"), axis=0, tiled=True),
    )
    gain_two = mlp_params[0].astype(jnp.float32)
    scale_two = rms_scale(residual)
    normed2 = (residual * scale_two * gain_two).astype(jnp.bfloat16)
    gate_proj = jnp.dot(normed2, mlp_params[1], preferred_element_type=jnp.float32)
    up_proj = jnp.dot(normed2, mlp_params[2], preferred_element_type=jnp.float32)
    sigmoid_gate = jax.nn.sigmoid(gate_proj)
    silu_gate = gate_proj * sigmoid_gate
    hidden = (silu_gate * up_proj).astype(jnp.bfloat16)
    block_output = (residual + contract_cols(hidden, mlp_params[3])).astype(jnp.bfloat16)
    out_back = cotangent[0]
    out_float = out_back.astype(jnp.float32)
    mlp_again = (
        lax.all_gather(mlp_gain, ("seq", "ctx"), axis=0, tiled=True),
        lax.all_gather(gate_weight, ("seq", "ctx"), axis=0, tiled=True),
        lax.all_gather(up_weight, ("seq", "ctx"), axis=0, tiled=True),
        lax.all_gather(down_weight, ("seq", "ctx"), axis=0, tiled=True),
    )
    down_grad = lax.psum_scatter(
        contract_rows(out_back, hidden), ("seq", "ctx"), scatter_dimension=0, tiled=True
    )
    hidden_back = jnp.dot(out_back, mlp_again[3], preferred_element_type=jnp.float32)
    gate_back = (
        hidden_back * up_proj * sigmoid_gate * (1.0 + gate_proj * (1.0 - sigmoid_gate))
    ).astype(jnp.bfloat16)
    upper_back = (hidden_back * silu_gate).astype(jnp.bfloat16)
    gate_full_grad = contract_rows(normed2, gate_back)
    up_full_grad = contract_rows(normed2, upper_back)
    normed2_back = contract_cols(gate_back, mlp_again[1]) + contract_cols(upper_back, mlp_again[2])
    residual_norm, mlp_gain_term = norm_back(
        residual, scale_two, mlp_again[0].astype(jnp.float32), normed2_back
    )
    mlp_sums = (
        lax.psum_scatter(mlp_gain_term, ("seq", "ctx"), scatter_dimension=0, tiled=True),
        lax.psum_scatter(gate_full_grad, ("seq", "ctx"), scatter_dimension=0, tiled=True),
        lax.psum_scatter(up_full_grad, ("seq", "ctx"), scatter_dimension=0, tiled=True),
    )
    residual_back = out_float + residual_norm
    attn_again = (
        lax.all_gather(attn_gain, ("seq", "ctx"), axis=0, tiled=True),
        lax.all_gather(query_weight, ("seq", "ctx"), axis=0, tiled=True),
        lax.all_gather(key_weight, ("seq", "ctx"), axis=0, tiled=True),
        lax.all_gather(value_weight, ("seq", "ctx"), axis=0, tiled=True),
        lax.all_gather(out_weight, ("seq", "ctx"), axis=0, tiled=True),
    )
    residual_low = residual_back.astype(jnp.bfloat16)
    out_full_grad = contract_rows(attn_low, residual_low)
    attn_back = contract_cols(residual_low, attn_again[4]).astype(jnp.bfloat16)
    grad_mix = attn_back.reshape(row_count, KV_HEADS, group_size, HEAD)
    delta_rows = jnp.transpose(jnp.sum(grad_mix.astype(jnp.float32) * full_mix, axis=-1), (1, 2, 0))

    def grad_step(carry, pieces):
        key_block, value_block, seg_block, block_start = pieces
        allowed = key_mask(seg_block, block_start)

        def compute(acc_query):
            soft_weights = block_soft(key_block, allowed)
            rounded = soft_weights.astype(jnp.bfloat16)
            value_part = jnp.einsum(
                "kgtj,tkgd->jkd", rounded, grad_mix, preferred_element_type=jnp.float32
            )
            soft_back = jnp.einsum(
                "tkgd,jkd->kgtj", grad_mix, value_block, preferred_element_type=jnp.float32
            )
            score_back = (soft_weights * (soft_back - delta_rows[..., None])).astype(jnp.bfloat16)
            acc_query = acc_query + jnp.einsum(
                "kgtj,jkd->tkgd", score_back, key_block, preferred_element_type=jnp.float32
            )
            key_part = jnp.einsum(
                "kgtj,tkgd->jkd", score_back, query_group, preferred_element_type=jnp.float32
            )
            return (acc_query, (key_part, value_part))

        return guarded(compute, carry)

    acc_query, (key_parts, value_parts) = lax.scan(
        grad_step, zero_mix, (key_blocks, value_blocks, seg_blocks, starts)
    )
    key_sums, value_sums = (
        lax.psum_scatter(
            key_parts.reshape(length, KV_HEADS * HEAD).astype(jnp.bfloat16),
            "ctx",
            scatter_dimension=0,
            tiled=True,
        ).astype(jnp.float32),
        lax.psum_scatter(
            value_parts.reshape(length, KV_HEADS * HEAD).astype(jnp.bfloat16),
            "ctx",
            scatter_dimension=0,
            tiled=True,
        ).astype(jnp.float32),
    )
    query_low = (
        rotate((acc_query * score_scale).reshape(row_count, HEADS, HEAD), cosine, -sine_table)
        .astype(jnp.bfloat16)
        .reshape(row_count, HEADS * HEAD)
    )
    key_low = (
        rotate((key_sums * score_scale).reshape(row_count, KV_HEADS, HEAD), cosine, -sine_table)
        .astype(jnp.bfloat16)
        .reshape(row_count, KV_HEADS * HEAD)
    )
    value_low = value_sums.astype(jnp.bfloat16)
    query_full_grad = contract_rows(normed1, query_low)
    key_full_grad = contract_rows(normed1, key_low)
    value_full_grad = contract_rows(normed1, value_low)
    normed1_back = (
        contract_cols(query_low, attn_again[1])
        + contract_cols(key_low, attn_again[2])
        + contract_cols(value_low, attn_again[3])
    )
    input_norm, attn_gain_term = norm_back(
        inputs, scale_one, attn_again[0].astype(jnp.float32), normed1_back
    )
    attn_sums = (
        lax.psum_scatter(attn_gain_term, ("seq", "ctx"), scatter_dimension=0, tiled=True),
        lax.psum_scatter(query_full_grad, ("seq", "ctx"), scatter_dimension=0, tiled=True),
        lax.psum_scatter(key_full_grad, ("seq", "ctx"), scatter_dimension=0, tiled=True),
        lax.psum_scatter(value_full_grad, ("seq", "ctx"), scatter_dimension=0, tiled=True),
        lax.psum_scatter(out_full_grad, ("seq", "ctx"), scatter_dimension=0, tiled=True),
    )
    input_grad = residual_back + input_norm
    return (
        block_output[None],
        input_grad[None],
        attn_sums[0],
        attn_sums[1],
        attn_sums[2],
        attn_sums[3],
        attn_sums[4],
        mlp_sums[0],
        mlp_sums[1],
        mlp_sums[2],
        down_grad,
    )


def solution(mesh):
    placed = (
        P("seq", "ctx", None),
        P("seq", "ctx"),
        P("seq", None),
        P("seq", "ctx", None),
        P(("seq", "ctx")),
        P(("seq", "ctx"), None),
        P(("seq", "ctx"), None),
        P(("seq", "ctx"), None),
        P(("seq", "ctx"), None),
        P(("seq", "ctx")),
        P(("seq", "ctx"), None),
        P(("seq", "ctx"), None),
        P(("seq", "ctx"), None),
    )
    return jax.shard_map(
        local,
        mesh=mesh,
        in_specs=placed,
        out_specs=(
            P("seq", "ctx", None),
            P("seq", "ctx", None),
            P(("seq", "ctx")),
            P(("seq", "ctx"), None),
            P(("seq", "ctx"), None),
            P(("seq", "ctx"), None),
            P(("seq", "ctx"), None),
            P(("seq", "ctx")),
            P(("seq", "ctx"), None),
            P(("seq", "ctx"), None),
            P(("seq", "ctx"), None),
        ),
        check_vma=False,
    )
```

profile of v0, /device:TPU:0, one launch (start us, length us, event | category | flops | bytes accessed | tf_op | source)
XLA Modules:
  0.0 3001.4 jit_solution(6440990506185782220)
XLA Ops:
  13.7 42.1 %all-reduce.5 = (bf16[2048]{0:T(1024)(128)(2,1)S(1)}, bf16[2048]{0:T(1024)(128)(2,1)S(1)}) all-reduce(bf16[2048]{0:T(1024)(128)(2,1)S(1)} %dynamic-update-slice, bf16[2048]{0:T(1024)(128)(2,1)S(1)} %dynamic-update-slice.1), channel_id=1, replica_groups=mesh['seq'=4,'ctx'=8] {'seq','ctx'}, use_global_device_ids=true, to_apply=%add | all-reduce | flops 4096 | bytes 16384
  61.1 6.6 all-gather.8.cloned.1.call-done
  67.7 1.7 convolution_convert_fusion.1
  69.4 14.8 all_gather.44
  85.9 37.6 %all-gather.10.cloned.1.call-done = bf16[2048,256]{1,0:T(8,128)(2,1)} async-done(((bf16[64,256]{1,0:T(8,128)(2,1)}), bf16[2048,256]{1,0:T(8,128)(2,1)}) %all-gather.10.cloned.1.call-update) | async-done | bytes 1048592 | tf_op jit(solution)/shard_map/all_gather | solution.py:99
  125.6 14.4 all_gather.46
  140.4 62.5 %all-gather.12.cloned.1.call-done = bf16[2048,2048]{1,0:T(8,128)(2,1)} async-done(((bf16[64,2048]{1,0:T(8,128)(2,1)}), bf16[2048,2048]{1,0:T(8,128)(2,1)}) %all-gather.12.cloned.1.call-update) | async-done | bytes 8388624 | tf_op jit(solution)/shard_map/all_gather | solution.py:98
  202.9 12.3 copy.60
  215.2 5.9 fusion.100
  221.4 21.4 while.41
  222.9 4.6 fusion.194
  227.6 4.5 select_reduce_fusion.2
  233.6 4.6 fusion.194
  238.3 4.5 select_reduce_fusion.2
  242.9 35.3 %while.42 = (s32[]{:T(128)}, f32[128,4,8,64]{0,3,2,1:T(8,128)S(1)}, f32[128,4,8,64]{0,3,2,1:T(8,128)}, bf16[2,512,4,64]{1,3,2,0:T(8,128)(2,1)}, s32[128]{0:T(128...) while((s32[]{:T(128)}, f32[128,4,8,64]{0,3,2,1:T(8,128)S(1)}, ...), condition=%wide.region_6.7_spmd.clone, body=%wide.region_5.6_spmd.clone.sunk | while | flops 833815168 | bytes 64466716 | solution.py:177
  242.9 4.6 fusion.201
  249.0 6.4 fusion.202
  256.4 3.5 fusion.203
  260.9 4.6 fusion.201
  267.0 5.9 fusion.202
  273.5 3.5 fusion.203
  278.3 3.3 all-gather.14.cloned.1.call-done
  281.5 4.7 multiply_reduce_fusion.3
  286.5 140.3 %all-gather.16.cloned.1.call-done = bf16[2048,5632]{1,0:T(8,128)(2,1)} async-done(((bf16[64,5632]{1,0:T(8,128)(2,1)}), bf16[2048,5632]{1,0:T(8,128)(2,1)}) %all-gather.16.cloned.1.call-update) | async-done | bytes 23068688 | tf_op jit(solution)/shard_map/all_gather | solution.py:185
  426.8 12.3 fusion.121
  439.1 132.5 %all-gather.18.cloned.1.call-done = bf16[2048,5632]{1,0:T(8,128)(2,1)} async-done(((bf16[64,5632]{1,0:T(8,128)(2,1)}), bf16[2048,5632]{1,0:T(8,128)(2,1)}) %all-gather.18.cloned.1.call-update) | async-done | bytes 23068688 | tf_op jit(solution)/shard_map/all_gather | solution.py:186
  571.6 12.4 fusion.122
  584.0 132.6 %all-gather.20.cloned.1.call-done = bf16[2048,5632]{1,0:T(8,128)(2,1)} async-done(((bf16[64,5632]{1,0:T(8,128)(2,1)}), bf16[2048,5632]{1,0:T(8,128)(2,1)}) %all-gather.20.cloned.1.call-update) | async-done | bytes 23068688 | tf_op jit(solution)/shard_map/all_gather | solution.py:187
  716.6 14.5 multiply_convert_fusion
  731.1 12.8 fusion.123
  743.9 13.8 multiply_reduce_fusion
  757.7 1.8 multiply_add_fusion
  760.4 7.2 convolution_convert_fusion
  767.6 2.1 copy.64
  771.4 33.1 %while.43 = (s32[]{:T(128)}, f32[128,4,8,64]{0,3,2,1:T(8,128)S(1)}, bf16[2,512,4,64]{1,3,2,0:T(8,128)(2,1)}, bf16[2,512,4,64]{1,3,2,0:T(8,128)(2,1)}, bf16[2,512...) while((s32[]{:T(128)}, f32[128,4,8,64]{0,3,2,1:T(8,128)S(1)}, ...), condition=%wide.region_11.12_spmd.clone, body=%wide.region_10.11_spmd.clone.sunk | while | flops 1368064640 | bytes 140505040 | solution.py:263
  774.3 4.4 fusion.215
  778.8 3.3 fusion.216
  785.1 2.0 fusion.218
  790.9 4.4 fusion.215
  795.3 3.3 fusion.216
  801.6 2.0 fusion.218
  810.8 26.4 reduce-scatter.28.cloned.1.call-done
  838.3 1.9 fusion.118
  840.3 29.2 reduce-scatter.30.cloned.1.call-done
  869.5 2.7 fusion.116
  874.9 8.3 fusion.104
  884.6 8.1 fusion.106
  893.7 19.3 fusion.125
  913.0 19.2 fusion.126
  933.3 19.3 convolution_bitcast_fusion.2
  952.6 42.4 %copy.86 = f32[2048,5632]{1,0:T(8,128)} copy(f32[2048,5632]{0,1:T(8,128)} %convolution_bitcast_fusion.2) | data formatting | bytes 92274688
  995.0 1.8 fusion.96
  996.8 6.3 fusion.124
  1003.2 12.8 fusion.77
  1016.0 1.7 convolution_add_fusion.1
  1017.7 2.7 fusion.90
  1020.5 38.1 %all-reduce.4 = (f32[2048]{0:T(1024)S(1)}, f32[2048]{0:T(1024)S(1)}) all-reduce(f32[2048]{0:T(1024)S(1)} %get-tuple-element.446, f32[2048]{0:T(1024)S(1)} %copy-done.39), channel_id=4, replica_groups=mesh['seq'=4,'ctx'=8] {'seq','ctx'}, use_global_device_ids=true, to_apply=%region_16.17.clone | all-reduce | flops 4096 | bytes 32768
  1059.8 2.6 fusion.89
  1062.3 84.6 %reduce-scatter.20.cloned.1.call-done = f32[64,256]{1,0:T(8,128)} async-done(((f32[2048,256]{1,0:T(8,128)}), f32[64,256]{1,0:T(8,128)}) %reduce-scatter.20.cloned.1.call-update) | async-done | bytes 65552 | tf_op jit(solution)/shard_map/reduce_scatter | solution.py:306
  1146.9 185.7 %reduce-scatter.16.cloned.1.call-done = f32[64,2048]{1,0:T(8,128)} async-done(((f32[2048,2048]{1,0:T(8,128)}), f32[64,2048]{1,0:T(8,128)}) %reduce-scatter.16.cloned.1.call-update) | async-done | bytes 524304 | tf_op jit(solution)/shard_map/reduce_scatter | solution.py:304
  1332.6 187.2 %reduce-scatter.22.cloned.1.call-done = f32[64,2048]{1,0:T(8,128)} async-done(((f32[2048,2048]{1,0:T(8,128)}), f32[64,2048]{1,0:T(8,128)}) %reduce-scatter.22.cloned.1.call-update) | async-done | bytes 524304 | tf_op jit(solution)/shard_map/reduce_scatter | solution.py:307
  1519.9 492.3 %reduce-scatter.24.cloned.1.call-done = f32[64,5632]{1,0:T(8,128)} async-done(((f32[2048,5632]{1,0:T(8,128)}), f32[64,5632]{1,0:T(8,128)}) %reduce-scatter.24.cloned.1.call-update) | async-done | bytes 1441808 | tf_op jit(solution)/shard_map/reduce_scatter | solution.py:222
  2012.2 491.2 %reduce-scatter.26.cloned.1.call-done = f32[64,5632]{1,0:T(8,128)} async-done(((f32[2048,5632]{1,0:T(8,128)}), f32[64,5632]{1,0:T(8,128)}) %reduce-scatter.26.cloned.1.call-update) | async-done | bytes 1441808 | tf_op jit(solution)/shard_map/reduce_scatter | solution.py:223
  2503.4 491.3 %reduce-scatter.32.cloned.1.call-done = f32[64,5632]{1,0:T(8,128)} async-done(((f32[2048,5632]{1,0:T(8,128)}), f32[64,5632]{1,0:T(8,128)}) %reduce-scatter.32.cloned.1.call-update) | async-done | bytes 1441808
  (245 shorter events, 56.3 us)
Async XLA Ops:
  7.2 117.8 %copy-start.4 = (bf16[1,128,2048]{2,1,0:T(8,128)(2,1)S(1)}, bf16[1,128,2048]{2,1,0:T(8,128)(2,1)}, u32[]{:S(2)}) copy-start(bf16[1,128,2048]{2,1,0:T(8,128)(2,1)} %param.19) | copy-start | bytes 1572868
  7.2 60.5 %all-gather.8.cloned.1.call-start = ((), (), s32[]{:S(2)}) async-start(), calls=%async_computation.9 | async-start | bytes 1081344 | tf_op jit(solution)/shard_map/all_gather | solution.py:100
  7.9 115.6 %all-gather.10.cloned.1.call-start = ((), (), s32[]{:S(2)}) async-start(), calls=%async_computation.10 | async-start | bytes 1081344 | tf_op jit(solution)/shard_map/all_gather | solution.py:99
  8.7 194.2 %all-gather.12.cloned.1.call-start = ((), (), s32[]{:S(2)}) async-start(), calls=%async_computation.11 | async-start | bytes 8650752 | tf_op jit(solution)/shard_map/all_gather | solution.py:98
  9.4 272.1 %all-gather.14.cloned.1.call-start = ((), (), s32[]{:S(2)}) async-start(), calls=%async_computation.12 | async-start | bytes 8650752 | tf_op jit(solution)/shard_map/all_gather | solution.py:101
  10.0 416.8 %all-gather.16.cloned.1.call-start = ((), (), s32[]{:S(2)}) async-start(), calls=%async_computation.13 | async-start | bytes 23789568 | tf_op jit(solution)/shard_map/all_gather | solution.py:185
  10.6 561.0 %all-gather.18.cloned.1.call-start = ((), (), s32[]{:S(2)}) async-start(), calls=%async_computation.14 | async-start | bytes 23789568 | tf_op jit(solution)/shard_map/all_gather | solution.py:186
  11.1 705.4 %all-gather.20.cloned.1.call-start = ((), (), s32[]{:S(2)}) async-start(), calls=%async_computation.15 | async-start | bytes 23789568 | tf_op jit(solution)/shard_map/all_gather | solution.py:187
  11.9 825.3 %reduce-scatter.28.cloned.1.call-start = ((), (), s32[]{:S(2)}) async-start(), calls=%async_computation.22 | async-start | bytes 589824
  55.9 159.4 %copy-start.35 = (f32[2048]{0:T(1024)}, f32[2048]{0:T(1024)S(1)}, u32[]{:S(2)}) copy-start(f32[2048]{0:T(1024)S(1)} %convert_element_type.128) | copy-start | bytes 24580
  59.9 161.3 %copy-start.25 = (f32[128,64]{0,1:T(8,128)}, f32[128,64]{0,1:T(8,128)S(1)}, u32[]{:S(2)}) copy-start(f32[128,64]{0,1:T(8,128)S(1)} %get-tuple-element.536) | copy-start | bytes 98308
  61.1 154.1 %copy-start.40 = (f32[128]{0:T(128)}, f32[128]{0:T(128)S(1)}, u32[]{:S(2)}) copy-start(f32[128]{0:T(128)S(1)} %add_rsqrt_fusion.1) | copy-start | bytes 1540
  249.0 6.4 slice-start
  249.0 6.4 copy-start.23
  249.0 7.4 slice-start.1
  267.0 6.0 slice-start
  267.0 6.0 copy-start.23
  267.0 6.5 slice-start.1
  278.2 3.4 copy-start.18
  278.3 8.0 copy-start.16
  286.3 471.4 %copy-start.6 = (f32[128,2048]{1,0:T(8,128)}, f32[128,2048]{1,0:T(8,128)S(1)}, u32[]{:S(2)}) copy-start(f32[128,2048]{1,0:T(8,128)S(1)} %get-tuple-element.542) | copy-start | bytes 3145732
  286.5 285.1 %copy-start.10 = (bf16[128,2048]{1,0:T(8,128)(2,1)}, bf16[128,2048]{1,0:T(8,128)(2,1)S(1)}, u32[]{:S(2)}) copy-start(bf16[128,2048]{1,0:T(8,128)(2,1)S(1)} %multiply_convert_fusion.3) | copy-start | bytes 1572868
  439.1 277.4 %copy-start.20 = (bf16[1,128,2048]{2,1,0:T(8,128)(2,1)S(1)}, bf16[1,128,2048]{2,1,0:T(8,128)(2,1)}, u32[]{:S(2)}) copy-start(bf16[1,128,2048]{2,1,0:T(8,128)(2,1)} %param.22) | copy-start | bytes 1572868
  731.1 12.8 copy-start.14
  731.1 12.8 copy-start.13
  757.7 13.6 copy-start.3
  760.4 9.2 copy-start.19
  771.3 66.9 %copy-start.29 = (f32[128,64]{0,1:T(8,128)S(1)}, f32[128,64]{0,1:T(8,128)}, u32[]{:S(2)}) copy-start(f32[128,64]{0,1:T(8,128)} %get-tuple-element.546) | copy-start | bytes 98308
  771.4 66.9 %copy-start.26 = (f32[128,64]{0,1:T(8,128)S(1)}, f32[128,64]{0,1:T(8,128)}, u32[]{:S(2)}) copy-start(f32[128,64]{0,1:T(8,128)} %copy-done.25) | copy-start | bytes 98308
  771.4 2.9 copy-start.22
  771.4 2.9 copy-start.34
  772.7 6.1 copy-start.1
  778.8 3.4 copy-start.30
  778.8 3.6 copy-start
  778.8 6.2 copy-start.2
  778.8 6.3 copy-start.32
  783.8 3.3 copy-start.31
  787.9 2.9 copy-start.22
  787.9 2.9 copy-start.34
  789.2 6.1 copy-start.1
  795.3 3.4 copy-start.30
  795.3 3.6 copy-start
  795.3 6.2 copy-start.2
  795.3 6.3 copy-start.32
  800.3 3.3 copy-start.31
  804.4 33.8 %copy-start.5 = (bf16[1,128,2048]{2,1,0:T(8,128)(2,1)S(1)}, bf16[1,128,2048]{2,1,0:T(8,128)(2,1)}, u32[]{:S(2)}) copy-start(bf16[1,128,2048]{2,1,0:T(8,128)(2,1)} %param.19) | copy-start | bytes 1572868
  804.4 33.8 %copy-start.36 = (f32[2048]{0:T(1024)S(1)}, f32[2048]{0:T(1024)}, u32[]{:S(2)}) copy-start(f32[2048]{0:T(1024)} %copy-done.35) | copy-start | bytes 24580
  804.4 33.9 %copy-start.41 = (f32[128]{0:T(128)S(1)}, f32[128]{0:T(128)}, u32[]{:S(2)}) copy-start(f32[128]{0:T(128)} %copy-done.40) | copy-start | bytes 1540
  807.6 61.9 %reduce-scatter.30.cloned.1.call-start = ((), (), s32[]{:S(2)}) async-start(), calls=%async_computation.23 | async-start | bytes 589824
  810.7 251.6 %reduce-scatter.18.cloned.1.call-start = ((), (), s32[]{:S(2)}) async-start(), calls=%async_computation.17 | async-start | bytes 2162688 | tf_op jit(solution)/shard_map/reduce_scatter | solution.py:305
  838.3 36.4 %copy-start.27 = (bf16[128,256]{0,1:T(8,128)(2,1)}, bf16[128,256]{0,1:T(8,128)(2,1)S(1)}, u32[]{:S(2)}) copy-start(bf16[128,256]{0,1:T(8,128)(2,1)S(1)} %fusion.111) | copy-start | bytes 196612
  838.3 36.4 %copy-start.38 = (f32[128,64]{0,1:T(8,128)S(1)}, f32[128,64]{0,1:T(8,128)}, u32[]{:S(2)}) copy-start(f32[128,64]{0,1:T(8,128)} %get-tuple-element.535) | copy-start | bytes 98308
  840.2 306.7 %reduce-scatter.20.cloned.1.call-start = ((), (), s32[]{:S(2)}) async-start(), calls=%async_computation.18 | async-start | bytes 2162688 | tf_op jit(solution)/shard_map/reduce_scatter | solution.py:306
  872.2 460.4 %reduce-scatter.16.cloned.1.call-start = ((), (), s32[]{:S(2)}) async-start(), calls=%async_computation.16 | async-start | bytes 17301504 | tf_op jit(solution)/shard_map/reduce_scatter | solution.py:304
  883.2 1.4 copy-start.17
  883.2 636.6 %reduce-scatter.22.cloned.1.call-start = ((), (), s32[]{:S(2)}) async-start(), calls=%async_computation.19 | async-start | bytes 17301504 | tf_op jit(solution)/shard_map/reduce_scatter | solution.py:307
  892.7 1119.5 %reduce-scatter.24.cloned.1.call-start = ((), (), s32[]{:S(2)}) async-start(), calls=%async_computation.20 | async-start | bytes 47579136 | tf_op jit(solution)/shard_map/reduce_scatter | solution.py:222
  913.0 1590.4 %reduce-scatter.26.cloned.1.call-start = ((), (), s32[]{:S(2)}) async-start(), calls=%async_computation.21 | async-start | bytes 47579136 | tf_op jit(solution)/shard_map/reduce_scatter | solution.py:223
  932.3 2062.4 %reduce-scatter.32.cloned.1.call-start = ((), (), s32[]{:S(2)}) async-start(), calls=%async_computation.24 | async-start | bytes 47579136
  995.0 8.2 copy-start.7
  995.0 8.2 copy-start.12
  1003.2 12.8 copy-start.28
  1003.2 14.5 copy-start.37
  1003.2 17.3 copy-start.39
  (9 other events, 8.9 us)
Sparse Core Ops, SparseCore 0:
  11.0 56.6 all-gather.7
  70.7 52.7 all-gather.9
  126.5 76.3 all-gather.11
  205.8 75.7 all-gather.13
  284.2 142.5 all-gather.15
  429.5 142.0 all-gather.17
  574.5 142.0 all-gather.19
  807.7 29.4 reduce-scatter.27
  840.0 29.4 reduce-scatter.29
  872.2 136.6 reduce-scatter.17
  1011.8 135.0 reduce-scatter.19
  1149.6 182.9 reduce-scatter.15
  1335.5 184.3 reduce-scatter.21
  1522.6 489.5 reduce-scatter.23
  2014.9 488.4 reduce-scatter.25
  2506.1 488.4 reduce-scatter.31
where the time goes:
time: 3010 us; the launch traced here: 3000 us
  waiting for transfers between devices  2510 us (83%)
  matrix products  251 us (8%)
  blocking collectives  109 us (4%)
  local copies, waits for them, and re-layouts  88.5 us (3%)
    unnamed x19, waiting for transfers between devices  551 us
    reduce_scatter x1, waiting for transfers between devices, local(): lax.psum_scatter(gate_full_grad, ('seq', 'ctx'), scatter_dimension=0, til...  492 us
    reduce_scatter x1, waiting for transfers between devices, local(): lax.psum_scatter(up_full_grad, ('seq', 'ctx'), scatter_dimension=0, tiled...  491 us
    reduce_scatter x1, waiting for transfers between devices, local(): lax.psum_scatter(out_full_grad, ('seq', 'ctx'), scatter_dimension=0, tile...  187 us
    reduce_scatter x1, waiting for transfers between devices, local(): lax.psum_scatter(query_full_grad, ('seq', 'ctx'), scatter_dimension=0, ti...  186 us
    all_gather x1, waiting for transfers between devices, local(): lax.all_gather(gate_weight, ('seq', 'ctx'), axis=0, tiled=True)  140 us
    all_gather x1, waiting for transfers between devices, local(): lax.all_gather(down_weight, ('seq', 'ctx'), axis=0, tiled=True)  133 us
    all_gather x1, waiting for transfers between devices, local(): lax.all_gather(up_weight, ('seq', 'ctx'), axis=0, tiled=True)  132 us
  transfers between devices with their start and end apart: 16, of which 15 were waited for; matrix products, arithmetic and copies ran while one was open for 9% of the time, Pallas kernels for 0%

commit v1 on v0

--- a/solution.py
+++ b/solution.py
@@ -1,6 +1,8 @@
 import jax
 import jax.numpy as jnp
 from jax import lax
+from jax.experimental import pallas as pl
+from jax.experimental.pallas import tpu as pltpu
 from jax.sharding import PartitionSpec as P
 
 HEADS = 32
@@ -53,7 +55,7 @@
     )
 
 
-def local(
+def local_rows(
     block_input,
     positions,
     segments,
@@ -322,6 +324,374 @@
     )
 
 
+SEQ_X = [(0, 1), (1, 0), (2, 3), (3, 2)]
+SEQ_Y = [(0, 2), (2, 0), (1, 3), (3, 1)]
+
+
+def gather_ctx(block):
+    return lax.all_gather(block, "ctx", axis=0, tiled=True)
+
+
+def reduce_ctx(partial):
+    return lax.psum_scatter(partial, "ctx", scatter_dimension=0, tiled=True)
+
+
+def exchange_ctx(pieces):
+    return lax.all_to_all(pieces, "ctx", 0, 0, tiled=True)
+
+
+def gather_seq(block):
+    rows, width = block.shape
+    half = rows // 2
+    mine = lax.axis_index("seq")
+    from_x = lax.ppermute(block, "seq", SEQ_X)
+    from_y = lax.ppermute(block, "seq", SEQ_Y)
+    far_top = lax.ppermute(from_x[:half], "seq", SEQ_Y)
+    far_low = lax.ppermute(from_y[half:], "seq", SEQ_X)
+    whole = jnp.zeros((4 * rows, width), block.dtype)
+    for piece, start in (
+        (block, mine * rows),
+        (from_x, (mine ^ 1) * rows),
+        (from_y, (mine ^ 2) * rows),
+        (far_top, (mine ^ 3) * rows),
+        (far_low, (mine ^ 3) * rows + half),
+    ):
+        whole = lax.dynamic_update_slice_in_dim(whole, piece, start, 0)
+    return whole
+
+
+def reduce_seq(partial):
+    rows = partial.shape[0] // 4
+    half = rows // 2
+    mine = lax.axis_index("seq")
+
+    def part(other, low):
+        start = (mine ^ other) * rows + (half if low else 0)
+        return lax.dynamic_slice_in_dim(partial, start, half, 0)
+
+    def add(left, right):
+        return left.astype(jnp.float32) + right.astype(jnp.float32)
+
+    top_near = lax.ppermute(part(1, False), "seq", SEQ_X)
+    top_far = lax.ppermute(part(3, False), "seq", SEQ_X)
+    low_near = lax.ppermute(part(2, True), "seq", SEQ_Y)
+    low_far = lax.ppermute(part(3, True), "seq", SEQ_Y)
+    top_send = add(part(2, False), top_far).astype(jnp.bfloat16)
+    low_send = add(part(1, True), low_far).astype(jnp.bfloat16)
+    top_last = lax.ppermute(top_send, "seq", SEQ_Y)
+    low_last = lax.ppermute(low_send, "seq", SEQ_X)
+    return jnp.concatenate(
+        [
+            add(part(0, False), top_near) + top_last.astype(jnp.float32),
+            add(part(0, True), low_near) + low_last.astype(jnp.float32),
+        ],
+        axis=0,
+    ).astype(jnp.bfloat16)
+
+
+def to_slices(weight):
+    rows, width = weight.shape
+    return jnp.transpose(weight.reshape(rows, 8, width // 8), (1, 0, 2))
+
+
+def from_slices(pieces):
+    count, rows, width = pieces.shape
+    return jnp.transpose(pieces, (1, 0, 2)).reshape(rows, count * width)
+
+
+def head_slices(weight):
+    rows = weight.shape[0]
+    split = weight.reshape(rows, KV_HEADS, 8, HEAD)
+    return jnp.transpose(split, (2, 0, 1, 3)).reshape(8, rows, KV_HEADS * HEAD)
+
+
+def from_head_slices(pieces):
+    rows = pieces.shape[1]
+    split = pieces.reshape(8, rows, KV_HEADS, HEAD)
+    return jnp.transpose(split, (1, 2, 0, 3)).reshape(rows, HEADS * HEAD)
+
+
+def attend_mask(edge, first_row, block, span):
+    row = first_row + lax.broadcasted_iota(jnp.int32, (block, span), 0)
+    column = lax.broadcasted_iota(jnp.int32, (block, span), 1)
+    return (column <= row) & (column >= jnp.where(row >= edge, edge, 0))
+
+
+def soft_rows(query, key, allowed):
+    scores = lax.dot_general(
+        query, key, (((1,), (1,)), ((), ())), preferred_element_type=jnp.float32
+    )
+    scores = jnp.where(allowed, scores, MASKED)
+    exponents = jnp.exp(scores - jnp.max(scores, axis=-1, keepdims=True))
+    return exponents * (1.0 / jnp.sum(exponents, axis=-1, keepdims=True))
+
+
+def attend_kernel(edge_ref, query_ref, key_ref, value_ref, mix_ref, *, block, blocks):
+    step = pl.program_id(1)
+    for index in range(blocks):
+
+        @pl.when(step == index)
+        def _(index=index):
+            span = (index + 1) * block
+            allowed = attend_mask(edge_ref[0], index * block, block, span)
+            mixed = []
+            for head in range(2):
+                cut = slice(head * HEAD, (head + 1) * HEAD)
+                soft = soft_rows(query_ref[:, cut], key_ref[:span, cut], allowed)
+                mixed.append(
+                    jnp.dot(
+                        soft.astype(jnp.bfloat16),
+                        value_ref[:span, cut],
+                        preferred_element_type=jnp.float32,
+                    )
+                )
+            mix_ref[...] = jnp.concatenate(mixed, axis=-1).astype(mix_ref.dtype)
+
+
+def attend_back_kernel(
+    edge_ref,
+    query_ref,
+    key_ref,
+    value_ref,
+    back_ref,
+    query_back_ref,
+    key_back_ref,
+    value_back_ref,
+    *,
+    block,
+    blocks,
+    score_scale,
+):
+    step = pl.program_id(1)
+
+    @pl.when(step == 0)
+    def _():
+        key_back_ref[...] = jnp.zeros_like(key_back_ref)
+        value_back_ref[...] = jnp.zeros_like(value_back_ref)
+
+    for index in range(blocks):
+
+        @pl.when(step == index)
+        def _(index=index):
+            span = (index + 1) * block
+            allowed = attend_mask(edge_ref[0], index * block, block, span)
+            query_parts, key_parts, value_parts = [], [], []
+            for head in range(2):
+                cut = slice(head * HEAD, (head + 1) * HEAD)
+                query, key = query_ref[:, cut], key_ref[:span, cut]
+                back = back_ref[:, cut]
+                soft = soft_rows(query, key, allowed)
+                soft_back = contract_cols(back, value_ref[:span, cut])
+                delta = jnp.sum(soft * soft_back, axis=-1, keepdims=True)
+                score_back = (soft * (soft_back - delta)).astype(jnp.bfloat16)
+                query_parts.append(
+                    jnp.dot(score_back, key, preferred_element_type=jnp.float32) * score_scale
+                )
+                key_parts.append(contract_rows(score_back, query))
+                value_parts.append(contract_rows(soft.astype(jnp.bfloat16), back))
+            query_back_ref[...] = jnp.concatenate(query_parts, axis=-1)
+            key_back_ref[:span, :] += jnp.concatenate(key_parts, axis=-1)
+            value_back_ref[:span, :] += jnp.concatenate(value_parts, axis=-1)
+
+
+def attend_specs(length, block):
+    rows = pl.BlockSpec((block, 2 * HEAD), lambda pair, step: (step, pair))
+    whole = pl.BlockSpec((length, 2 * HEAD), lambda pair, step: (0, pair))
+    edge = pl.BlockSpec(memory_space=pltpu.SMEM)
+    return edge, rows, whole
+
+
+def attend(edge, queries, keys, values):
+    length, width = queries.shape
+    block = 256
+    blocks = length // block
+    scalar, rows, whole = attend_specs(length, block)
+
+    def body(*refs):
+        attend_kernel(*refs, block=block, blocks=blocks)
+
+    return pl.pallas_call(
+        body,
+        name="attend",
+        grid=(width // (2 * HEAD), blocks),
+        in_specs=[scalar, rows, whole, whole],
+        out_specs=rows,
+        out_shape=jax.ShapeDtypeStruct((length, width), jnp.bfloat16),
+    )(edge, queries, keys, values)
+
+
+def attend_back(edge, queries, keys, values, back, score_scale):
+    length, width = queries.shape
+    block = 256
+    blocks = length // block
+    scalar, rows, whole = attend_specs(length, block)
+
+    def body(*refs):
+        attend_back_kernel(*refs, block=block, blocks=blocks, score_scale=score_scale)
+
+    shape = jax.ShapeDtypeStruct((length, width), jnp.float32)
+    return pl.pallas_call(
+        body,
+        name="attend_back",
+        grid=(width // (2 * HEAD), blocks),
+        in_specs=[scalar, rows, whole, whole, rows],
+        out_specs=(rows, whole, whole),
+        out_shape=(shape, shape, shape),
+    )(edge, queries, keys, values, back)
+
+
+def turn(values, cosine, sine_table):
+    half = HEAD // 2
+    lane = lax.broadcasted_iota(jnp.int32, values.shape, 1) % HEAD
+    turned = jnp.where(
+        lane < half, -jnp.roll(values, -half, axis=1), jnp.roll(values, half, axis=1)
+    )
+    return values * cosine + turned * sine_table
+
+
+def local_columns(
+    block_input,
+    positions,
+    segments,
+    cotangent,
+    attn_gain,
+    query_weight,
+    key_weight,
+    value_weight,
+    out_weight,
+    mlp_gain,
+    gate_weight,
+    up_weight,
+    down_weight,
+):
+    f32, bf16 = jnp.float32, jnp.bfloat16
+    score_scale = HEAD ** (-0.5)
+    length = segments.shape[1]
+    rows = query_weight.shape[0]
+    head_width = KV_HEADS * HEAD
+    inputs = block_input[0].astype(f32)
+    out_back = cotangent[0]
+    gain_one = attn_gain.astype(f32)[:, None]
+    gain_two = mlp_gain.astype(f32)[:, None]
+
+    def fold(weight, gain):
+        return (weight.astype(f32) * gain).astype(bf16)
+
+    inputs_all = gather_ctx(block_input[0])
+    key_value = jnp.concatenate([fold(key_weight, gain_one), fold(value_weight, gain_one)], axis=1)
+    attn_pieces = jnp.concatenate(
+        [
+            head_slices(fold(query_weight, gain_one)),
+            jnp.broadcast_to(key_value[None], (8,) + key_value.shape),
+        ],
+        axis=2,
+    )
+    attn_cols = gather_seq(exchange_ctx(attn_pieces).reshape(8 * rows, 3 * head_width))
+    out_rows = gather_seq(out_weight)
+    gate_cols = gather_seq(
+        exchange_ctx(to_slices(fold(gate_weight, gain_two))).reshape(8 * rows, -1)
+    )
+    up_cols = gather_seq(exchange_ctx(to_slices(fold(up_weight, gain_two))).reshape(8 * rows, -1))
+    down_cols = gather_seq(exchange_ctx(to_slices(down_weight)).reshape(8 * rows, -1))
+    back_all = gather_ctx(out_back)
+
+    edge = jnp.sum((segments[0] == 0).astype(jnp.int32))
+    token = jnp.arange(length, dtype=jnp.int32)
+    position = jnp.where(token < edge, token + (length - edge), token - edge)
+    cosine, sine_table = rope_tables(position, HEAD)
+    cosine = jnp.tile(cosine, (1, KV_HEADS))
+    sine_table = jnp.tile(sine_table, (1, KV_HEADS))
+    edge = edge[None]
+
+    wide = inputs_all.astype(f32)
+    shaped_all = (wide * rms_scale(wide)).astype(bf16)
+    raw = jnp.dot(shaped_all, attn_cols, preferred_element_type=f32)
+    queries = turn(raw[:, :head_width], cosine, sine_table).astype(bf16)
+    keys = turn(raw[:, head_width : 2 * head_width], cosine, sine_table).astype(bf16)
+    values = raw[:, 2 * head_width :].astype(bf16)
+    queries = queries * jnp.asarray(score_scale, bf16)
+    attn_low = attend(edge, queries, keys, values)
+    mixed = jnp.dot(attn_low, out_rows, preferred_element_type=f32).astype(bf16)
+    residual = inputs + reduce_ctx(mixed).astype(f32)
+    scale_two = rms_scale(residual)
+    shaped_two = residual * scale_two
+    normed_all = gather_ctx(shaped_two.astype(bf16))
+    gate_proj = jnp.dot(normed_all, gate_cols, preferred_element_type=f32)
+    up_proj = jnp.dot(normed_all, up_cols, preferred_element_type=f32)
+    sigmoid_gate = jax.nn.sigmoid(gate_proj)
+    silu_gate = gate_proj * sigmoid_gate
+    hidden = (silu_gate * up_proj).astype(bf16)
+    hidden_back = jnp.dot(back_all, down_cols, preferred_element_type=f32)
+    gate_back = (
+        hidden_back * up_proj * sigmoid_gate * (1.0 + gate_proj * (1.0 - sigmoid_gate))
+    ).astype(bf16)
+    upper_back = (hidden_back * silu_gate).astype(bf16)
+    weighted = reduce_ctx(
+        (contract_cols(gate_back, gate_cols) + contract_cols(upper_back, up_cols)).astype(bf16)
+    ).astype(f32)
+    residual_back = out_back.astype(f32) + scale_two * (
+        weighted - shaped_two * jnp.mean(weighted * shaped_two, axis=-1, keepdims=True)
+    )
+    low_all = gather_ctx(residual_back.astype(bf16))
+    attn_back = contract_cols(low_all, out_rows).astype(bf16)
+    query_back, key_back, value_back = attend_back(
+        edge, queries, keys, values, attn_back, score_scale
+    )
+    heads_back = jnp.concatenate(
+        [
+            turn(query_back, cosine, -sine_table).astype(bf16),
+            turn(key_back, cosine, -sine_table).astype(bf16),
+            value_back.astype(bf16),
+        ],
+        axis=1,
+    )
+    weighted_one = reduce_ctx(contract_cols(heads_back, attn_cols).astype(bf16)).astype(f32)
+    scale_one = rms_scale(inputs)
+    shaped_one = inputs * scale_one
+    input_grad = residual_back + scale_one * (
+        weighted_one - shaped_one * jnp.mean(weighted_one * shaped_one, axis=-1, keepdims=True)
+    )
+    block_output = (
+        residual + reduce_ctx(contract_cols(hidden, down_cols).astype(bf16)).astype(f32)
+    ).astype(bf16)
+
+    def column_grad(left, right):
+        slices = reduce_seq(contract_rows(left, right).astype(bf16))
+        return exchange_ctx(slices.reshape(8, rows, -1)).astype(f32)
+
+    down_grad = from_slices(column_grad(back_all, hidden))
+    gate_rows = from_slices(column_grad(normed_all, gate_back))
+    up_rows = from_slices(column_grad(normed_all, upper_back))
+    out_grad = reduce_seq(contract_rows(attn_low, low_all).astype(bf16)).astype(f32)
+    attn_grad = column_grad(shaped_all, heads_back)
+    query_rows = from_head_slices(attn_grad[:, :, :head_width])
+    pair_rows = jnp.sum(attn_grad[:, :, head_width:], axis=0)
+    key_rows, value_rows = pair_rows[:, :head_width], pair_rows[:, head_width:]
+
+    def row_sum(weight, grad):
+        return jnp.sum(weight.astype(f32) * grad, axis=1)
+
+    attn_gain_grad = (
+        row_sum(query_weight, query_rows)
+        + row_sum(key_weight, key_rows)
+        + row_sum(value_weight, value_rows)
+    )
+    mlp_gain_grad = row_sum(gate_weight, gate_rows) + row_sum(up_weight, up_rows)
+    return (
+        block_output[None],
+        input_grad[None],
+        attn_gain_grad,
+        query_rows * gain_one,
+        key_rows * gain_one,
+        value_rows * gain_one,
+        out_grad,
+        mlp_gain_grad,
+        gate_rows * gain_two,
+        up_rows * gain_two,
+        down_grad,
+    )
+
+
 def solution(mesh):
     placed = (
         P("seq", "ctx", None),
@@ -338,22 +708,33 @@
         P(("seq", "ctx"), None),
         P(("seq", "ctx"), None),
     )
-    return jax.shard_map(
-        local,
-        mesh=mesh,
-        in_specs=placed,
-        out_specs=(
-            P("seq", "ctx", None),
-            P("seq", "ctx", None),
-            P(("seq", "ctx")),
-            P(("seq", "ctx"), None),
-            P(("seq", "ctx"), None),
-            P(("seq", "ctx"), None),
-            P(("seq", "ctx"), None),
-            P(("seq", "ctx")),
-            P(("seq", "ctx"), None),
-            P(("seq", "ctx"), None),
-            P(("seq", "ctx"), None),
-        ),
-        check_vma=False,
-    )
+    seq_count, ctx_count = mesh.shape["seq"], mesh.shape["ctx"]
+
+    def run(*args):
+        width = args[0].shape[2]
+        fits = (
+            seq_count == KV_HEADS == 4
+            and ctx_count == HEADS // KV_HEADS == 8
+            and width == seq_count * ctx_count * HEAD
+        )
+        return jax.shard_map(
+            local_columns if fits else local_rows,
+            mesh=mesh,
+            in_specs=placed,
+            out_specs=(
+                P("seq", "ctx", None),
+                P("seq", "ctx", None),
+                P(("seq", "ctx")),
+                P(("seq", "ctx"), None),
+                P(("seq", "ctx"), None),
+                P(("seq", "ctx"), None),
+                P(("seq", "ctx"), None),
+                P(("seq", "ctx")),
+                P(("seq", "ctx"), None),
+                P(("seq", "ctx"), None),
+                P(("seq", "ctx"), None),
+            ),
+            check_vma=False,
+        )(*args)
+
+    return run

time: 3010 us -> 794 us (0.26)
  waiting for transfers between devices: 2510 us -> 378 us
  matrix products: 251 us -> 88.4 us
  blocking collectives: 109 us -> 0 us
  starting transfers between devices: 1.02 us -> 92.5 us
  local copies, waits for them, and re-layouts: 88.5 us -> 124 us
  Pallas kernels: 0 us -> 33.1 us
    reduce_scatter x6 -> x4, waiting for transfers between devices: 1440 us -> 102 us  [reduce_ctx(): return lax.psum_scatter(partial, 'ctx', scatter_dimension=0, tiled=True)]
    unnamed x19 -> x8, waiting for transfers between devices: 551 us -> 1.46 us
    all_gather x7 -> x4, waiting for transfers between devices: 515 us -> 45.5 us  [gather_ctx(): return lax.all_gather(block, 'ctx', axis=0, tiled=True)]
    all_to_all x0 -> x8, waiting for transfers between devices: none -> 154 us  [exchange_ctx(): return lax.all_to_all(pieces, 'ctx', 0, 0, tiled=True)]
    dot_general x25 -> x5, matrix products: 115 us -> 32.2 us  [the longest x1 8.38 us: local_columns(): hidden_back = jnp.dot(back_all, down_cols, preferred_element_type=f32)]
    unnamed x2 -> x0, blocking collectives: 80.2 us -> none
    ppermute x0 -> x50, waiting for transfers between devices: none -> 75 us  [the longest x5 17.4 us: reduce_seq(): low_near = lax.ppermute(part(2, True), 'seq', SEQ_Y)]
    ppermute x0 -> x50, starting transfers between devices: none -> 56.4 us  [the longest x5 7.9 us: reduce_seq(): top_far = lax.ppermute(part(3, False), 'seq', SEQ_X)]
  transfers between devices with their start and end apart: 16 -> 66, of which waited for: 15 -> 26; matrix products, arithmetic and copies ran while one was open for 9% -> 25% of each run, Pallas kernels for 0% -> 0%
where the time goes in v1:
time: 794 us; the launch traced here: 784 us
  waiting for transfers between devices  378 us (48%)
  local copies, waits for them, and re-layouts  124 us (16%)
  starting transfers between devices  92.5 us (12%)
  matrix products  88.4 us (11%)
  other arithmetic  51.2 us (6%)
  Pallas kernels  33.1 us (4%)
  between operations  16.3 us (2%)
    all_to_all x8, waiting for transfers between devices, exchange_ctx(): return lax.all_to_all(pieces, 'ctx', 0, 0, tiled=True)  154 us
    reduce_scatter x4, waiting for transfers between devices, reduce_ctx(): return lax.psum_scatter(partial, 'ctx', scatter_dimension=0, tiled=True)  102 us
    all_gather x4, waiting for transfers between devices, gather_ctx(): return lax.all_gather(block, 'ctx', axis=0, tiled=True)  45.5 us
    all_to_all x8, starting transfers between devices, exchange_ctx(): return lax.all_to_all(pieces, 'ctx', 0, 0, tiled=True)  35.4 us
    dot_general x5, matrix products, contract_cols(): lax.dot_general(left, right, (((1,), (1,)), ((), ())), preferred_element_...  31.1 us
    dynamic_update_slice x25, local copies, waits for them, and re-layouts, gather_seq(): whole = lax.dynamic_update_slice_in_dim(whole, piece, start, 0)  29.6 us
    dot_general x5, matrix products, contract_rows(): lax.dot_general(left, right, (((0,), (0,)), ((), ())), preferred_element_...  25 us
    pallas_call x1, Pallas kernels, attend_back(): pl.pallas_call(body, name='attend_back', grid=(width // (2 * HEAD), block...  19.9 us
  transfers between devices with their start and end apart: 66, of which 26 were waited for; matrix products, arithmetic and copies ran while one was open for 25% of the time, Pallas kernels for 0%

profile of v1, /device:TPU:0, one launch (start us, length us, event | category | flops | bytes accessed | tf_op | source)
XLA Modules:
  0.0 783.7 jit_solution(2253300943133811713)
XLA Ops:
  11.9 6.4 all-to-all-start
  32.9 25.7 %all-to-all-done = bf16[8,64,768]{2,1,0:T(8,128)(2,1)S(1)} async-done(((bf16[8,64,768]{2,1,0:T(8,128)(2,1)}), bf16[8,64,768]{2,1,0:T(8,128)(2,1)S(1)}, u32[]{:S(2)}, u32[]{:S(2)}) %all-to-all-start) | async-done | bytes 786464 | tf_op jit(solution)/shard_map/all_to_all | solution.py:340
  66.3 8.7 %collective-permute-done.1 = bf16[512,768]{1,0:T(8,128)(2,1)S(1)} collective-permute-done((bf16[512,768]{1,0:T(8,128)(2,1)S(1)}, bf16[512,768]{1,0:T(8,128)(2,1)S(1)}, u32[]{:S(2)}, u32[]{:S(2)}) %collective-permute-start.1) | collective-permute-done | bytes 786464 | tf_op jit(solution)/shard_map/ppermute | solution.py:348
  83.7 2.7 collective-permute-done.2
  88.0 3.2 fusion
  91.5 5.3 fusion.15
  100.8 13.2 %attend.1 = bf16[1024,256]{1,0:T(8,128)(2,1)} custom-call(s32[1]{0:T(128)} %bitcast.1.refs_0_, bf16[1024,256]{1,0:T(8,128)(2,1)} %get-tuple-element.31.refs_1_, bf16[1024,256]{1,0:T(8,128)(2,1)} %fusion.31.refs_2_, bf16[1024,256]{1,0:T(8,128)(2,1)} %get-tuple-element.30.refs_3_), custom_call_target="tpu_custom_call" | custom-call | tf_op jit(solution)/shard_map/attend/pallas_call | solution.py:513
  114.0 4.8 convolution_convert_fusion.1
  119.6 52.2 %reduce-scatter.5.cloned.1.call-done = bf16[128,2048]{1,0:T(8,128)(2,1)} async-done(((bf16[1024,2048]{1,0:T(8,128)(2,1)}), bf16[128,2048]{1,0:T(8,128)(2,1)}) %reduce-scatter.5.cloned.1.call-update) | async-done | bytes 524304 | tf_op jit(solution)/shard_map/reduce_scatter | solution.py:336
  178.0 3.6 all-to-all-start.3
  181.6 2.7 fusion.17
  184.4 2.5 reshape.150
  189.0 35.0 %all-to-all-done.3 = bf16[8,64,704]{2,1,0:T(8,128)(2,1)S(1)} async-done(((bf16[8,64,704]{2,1,0:T(8,128)(2,1)}), bf16[8,64,704]{2,1,0:T(8,128)(2,1)S(1)}, u32[]{:S(2)}, u32[]{:S(2)}) %all-to-all-start.3) | async-done | bytes 720928 | tf_op jit(solution)/shard_map/all_to_all | solution.py:340
  224.0 4.2 all-to-all-start.1
  228.2 2.5 reshape.152
  232.9 18.1 %all-to-all-done.1 = bf16[8,64,704]{2,1,0:T(8,128)(2,1)} async-done(((bf16[8,64,704]{2,1,0:T(8,128)(2,1)}), bf16[8,64,704]{2,1,0:T(8,128)(2,1)}, u32[]{:S(2)}, u32[]{:S(2)}) %all-to-all-start.1) | async-done | bytes 720928 | tf_op jit(solution)/shard_map/all_to_all | solution.py:340
  251.0 4.2 all-to-all-start.2
  259.8 2.3 copy.110
  263.2 34.5 %all-to-all-done.2 = bf16[8,64,704]{2,1,0:T(8,128)(2,1)} async-done(((bf16[8,64,704]{2,1,0:T(8,128)(2,1)}), bf16[8,64,704]{2,1,0:T(8,128)(2,1)}, u32[]{:S(2)}, u32[]{:S(2)}) %all-to-all-start.2) | async-done | bytes 720928 | tf_op jit(solution)/shard_map/all_to_all | solution.py:340
  297.7 2.3 copy.117
  304.6 2.2 broadcast.115.clone.2
  307.0 2.6 constant_dynamic-update-slice_fusion.9
  315.1 2.3 copy.125
  319.7 2.3 copy.113
  325.2 2.3 copy.111
  330.7 2.3 copy.120
  335.2 2.3 copy.118
  363.1 8.4 %fusion.4 = f32[704,1024]{1,0:T(8,128)} fusion(bf16[2048,704]{1,0:T(8,128)(2,1)} %constant_dynamic-update-slice_fusion, bf16[1,1024,2048]{2,1,0:T(8,128)(2,1)} %all-gather.13.cloned.1.call-done), kind=kOutput, calls=%fused_computation.7 | convolution fusion | flops 2952790016 | bytes 9961472 | tf_op jit(solution)/shard_map/dot_general | solution.py:624
  371.5 6.3 fusion.74
  377.8 7.5 fusion.11
  385.3 6.5 fusion.75
  391.8 5.1 add_convert_fusion
  397.0 49.3 %reduce-scatter.9.cloned.1.call-done = bf16[128,2048]{1,0:T(8,128)(2,1)} async-done(((bf16[1024,2048]{1,0:T(8,128)(2,1)}), bf16[128,2048]{1,0:T(8,128)(2,1)}) %reduce-scatter.9.cloned.1.call-update) | async-done | bytes 524304 | tf_op jit(solution)/shard_map/reduce_scatter | solution.py:336
  447.8 2.4 fusion.66
  450.3 45.4 %all-gather.9.cloned.1.call-done = bf16[1024,2048]{1,0:T(8,128)(2,1)} async-done(((bf16[128,2048]{1,0:T(8,128)(2,1)}), bf16[1024,2048]{1,0:T(8,128)(2,1)}) %all-gather.9.cloned.1.call-update) | async-done | bytes 4194320 | tf_op jit(solution)/shard_map/all_gather | solution.py:332
  495.7 4.6 convolution_convert_fusion.7.refs_4_
  500.3 19.9 %attend_back.1 = (f32[1024,256]{1,0:T(8,128)}, f32[1024,256]{1,0:T(8,128)}, f32[1024,256]{1,0:T(8,128)}) custom-call(s32[1]{0:T(128)} %bitcast.1.refs_0_, bf16[1024,256]{1,0:T(8,128)(2,1)} %get-tuple-element.31.refs_1_, bf16[1024,256]{1,0:T(8,128)(2,1)} %fusion.31.refs_2_, bf16[1024,256]{1,0:T(8,128)(2,1)} %get-tuple-element.30.refs_3_, ...), custom_call_target="tpu_custom_call" | custom-call | tf_op jit(solution)/shard_map/attend_back/pallas_call | solution.py:533
  525.6 7.0 convolution_convert_fusion.2
  534.0 5.7 fusion.6
  545.6 7.2 collective-permute-done.45
  555.4 5.8 convolution_convert_fusion.4
  565.4 3.6 collective-permute-done.46
  577.9 3.7 collective-permute-done.49
  584.1 3.5 all-to-all-start.7
  587.7 5.8 convolution_convert_fusion.5
  601.9 4.1 collective-permute-done.33
  608.3 5.4 collective-permute-done.43
  616.2 5.0 all-to-all-start.6
  621.2 7.9 %convolution_convert_fusion = bf16[1024,2048]{1,0:T(8,128)(2,1)} fusion(bf16[1024,704]{0,1:T(8,128)(2,1)} %get-tuple-element.23, bf16[2048,704]{1,0:T(8,128)(2,1)} %constant_dynamic-update-slice_fusion), kind=kOutput, calls=%fused_computation.9 | convolution fusion | flops 2954887168 | bytes 8519680 | tf_op jit(solution)/shard_map/dot_general | solution.py:53
  633.9 6.2 collective-permute-done.35
  640.1 2.9 collective-permute-done.37
  645.1 2.3 copy.134
  647.4 4.9 all-to-all-start.5
  658.9 27.8 %all-to-all-done.5 = bf16[8,64,704]{2,1,0:T(8,128)(2,1)} async-done(((bf16[8,64,704]{2,1,0:T(8,128)(2,1)}), bf16[8,64,704]{2,1,0:T(8,128)(2,1)}, u32[]{:S(2)}, u32[]{:S(2)}) %all-to-all-start.5) | async-done | bytes 720928 | tf_op jit(solution)/shard_map/all_to_all | solution.py:340
  690.6 6.4 convolution_convert_fusion.3
  703.8 5.4 collective-permute-done.21
  715.4 2.3 collective-permute-done.20
  720.0 3.8 collective-permute-done.22
  725.2 11.2 %collective-permute-done.23 = bf16[256,768]{1,0:T(8,128)(2,1)S(1)} collective-permute-done((bf16[256,768]{1,0:T(8,128)(2,1)S(1)}, bf16[256,768]{1,0:T(8,128)(2,1)S(1)}, u32[]{:S(2)}, u32[]{:S(2)}) %collective-permute-start.23) | collective-permute-done | bytes 393248 | tf_op jit(solution)/shard_map/ppermute | solution.py:377
  738.4 3.5 all-to-all-start.4
  743.7 5.2 collective-permute-done.31
  749.8 13.1 %all-to-all-done.4 = bf16[8,64,768]{2,1,0:T(8,128)(2,1)S(1)} async-done(((bf16[8,64,768]{2,1,0:T(8,128)(2,1)}), bf16[8,64,768]{2,1,0:T(8,128)(2,1)S(1)}, u32[]{:S(2)}, u32[]{:S(2)}) %all-to-all-start.4) | async-done | bytes 786464 | tf_op jit(solution)/shard_map/all_to_all | solution.py:340
  766.8 2.4 reshape.157
  773.3 3.1 fusion.28
  (338 shorter events, 196.1 us)
Async XLA Ops:
  7.2 80.8 %all-gather.11.cloned.1.call-start = ((), (), s32[]{:S(2)}) async-start(), calls=%async_computation.18 | async-start | bytes 4718592 | tf_op jit(solution)/shard_map/all_gather | solution.py:332
  11.9 46.7 %all-to-all-start = ((bf16[8,64,768]{2,1,0:T(8,128)(2,1)}), bf16[8,64,768]{2,1,0:T(8,128)(2,1)S(1)}, u32[]{:S(2)}, u32[]{:S(2)}) async-start(bf16[8,64,768]{2,1,0:T(8,128)(2,1)} %pad_maximum_fusion.1), calls=%async_computation | async-start | bytes 1572864 | tf_op jit(solution)/shard_map/all_to_all | solution.py:340
  18.2 153.6 %reduce-scatter.5.cloned.1.call-start = ((), (), s32[]{:S(2)}) async-start(), calls=%async_computation.12 | async-start | bytes 4718592 | tf_op jit(solution)/shard_map/reduce_scatter | solution.py:336
  18.3 11.6 %collective-permute-start.5 = (bf16[64,2048]{1,0:T(8,128)(2,1)}, bf16[64,2048]{1,0:T(8,128)(2,1)}, u32[]{:S(2)}, u32[]{:S(2)}) collective-permute-start(bf16[64,2048]{1,0:T(8,128)(2,1)} %param.20), channel_id=1, source_target_pairs={{0,16},{16,0},{8,24},{24,8},{1,17},{17,1},{9,25},{25,9},{2,18},{18... | collective-permute-start | bytes 786440 | tf_op jit(solution)/shard_map/ppermute | solution.py:348
  19.8 11.6 %collective-permute-start.4 = (bf16[64,2048]{1,0:T(8,128)(2,1)}, bf16[64,2048]{1,0:T(8,128)(2,1)}, u32[]{:S(2)}, u32[]{:S(2)}) collective-permute-start(bf16[64,2048]{1,0:T(8,128)(2,1)} %param.20), channel_id=1, source_target_pairs={{0,8},{8,0},{16,24},{24,16},{1,9},{9,1},{17,25},{25,17},{2,10},{10... | collective-permute-start | bytes 786440 | tf_op jit(solution)/shard_map/ppermute | solution.py:347
  30.8 34.8 %collective-permute-start.7 = (bf16[32,2048]{1,0:T(8,128)(2,1)S(1)}, bf16[32,2048]{1,0:T(8,128)(2,1)S(1)}, u32[]{:S(2)}, u32[]{:S(2)}) collective-permute-start(bf16[32,2048]{1,0:T(8,128)(2,1)S(1)} %slice.159), channel_id=1, source_target_pairs={{0,8},{8,0},{16,24},{24,16},{1,9},{9,1},{17,25},{25,17},{2,10},{10... | collective-permute-start | bytes 393224 | tf_op jit(solution)/shard_map/ppermute | solution.py:350
  32.3 32.6 %collective-permute-start.6 = (bf16[32,2048]{1,0:T(8,128)(2,1)S(1)}, bf16[32,2048]{1,0:T(8,128)(2,1)S(1)}, u32[]{:S(2)}, u32[]{:S(2)}) collective-permute-start(bf16[32,2048]{1,0:T(8,128)(2,1)S(1)} %slice.158), channel_id=1, source_target_pairs={{0,16},{16,0},{8,24},{24,8},{1,17},{17,1},{9,25},{25,9},{2,18},{18... | collective-permute-start | bytes 393224 | tf_op jit(solution)/shard_map/ppermute | solution.py:349
  58.6 16.4 %collective-permute-start.1 = (bf16[512,768]{1,0:T(8,128)(2,1)S(1)}, bf16[512,768]{1,0:T(8,128)(2,1)S(1)}, u32[]{:S(2)}, u32[]{:S(2)}) collective-permute-start(bf16[512,768]{1,0:T(8,128)(2,1)S(1)} %bitcast.140), channel_id=1, source_target_pairs={{0,16},{16,0},{8,24},{24,8},{1,17},{17,1},{9,25},{25,9},{2,18},{18... | collective-permute-start | bytes 2359304 | tf_op jit(solution)/shard_map/ppermute | solution.py:348
  60.1 18.5 %collective-permute-start = (bf16[512,768]{1,0:T(8,128)(2,1)S(1)}, bf16[512,768]{1,0:T(8,128)(2,1)S(1)}, u32[]{:S(2)}, u32[]{:S(2)}) collective-permute-start(bf16[512,768]{1,0:T(8,128)(2,1)S(1)} %bitcast.141), channel_id=1, source_target_pairs={{0,8},{8,0},{16,24},{24,16},{1,9},{9,1},{17,25},{25,17},{2,10},{10... | collective-permute-start | bytes 2359304 | tf_op jit(solution)/shard_map/ppermute | solution.py:347
  75.0 12.2 %collective-permute-start.3 = (bf16[256,768]{1,0:T(8,128)(2,1)S(1)}, bf16[256,768]{1,0:T(8,128)(2,1)S(1)}, u32[]{:S(2)}, u32[]{:S(2)}) collective-permute-start(bf16[256,768]{1,0:T(8,128)(2,1)S(1)} %slice.146), channel_id=1, source_target_pairs={{0,8},{8,0},{16,24},{24,16},{1,9},{9,1},{17,25},{25,17},{2,10},{10... | collective-permute-start | bytes 1179656 | tf_op jit(solution)/shard_map/ppermute | solution.py:350
  78.6 7.8 %collective-permute-start.2 = (bf16[256,768]{1,0:T(8,128)(2,1)S(1)}, bf16[256,768]{1,0:T(8,128)(2,1)S(1)}, u32[]{:S(2)}, u32[]{:S(2)}) collective-permute-start(bf16[256,768]{1,0:T(8,128)(2,1)S(1)} %slice.145), channel_id=1, source_target_pairs={{0,16},{16,0},{8,24},{24,8},{1,17},{17,1},{9,25},{25,9},{2,18},{18... | collective-permute-start | bytes 1179656 | tf_op jit(solution)/shard_map/ppermute | solution.py:349
  118.8 244.3 %all-gather.13.cloned.1.call-start = ((), (), s32[]{:S(2)}) async-start(), calls=%async_computation.19 | async-start | bytes 4718592 | tf_op jit(solution)/shard_map/all_gather | solution.py:332
  119.6 251.9 %all-gather.7.cloned.1.call-start = ((), (), s32[]{:S(2)}) async-start(), calls=%async_computation.13 | async-start | bytes 4718592 | tf_op jit(solution)/shard_map/all_gather | solution.py:332
  178.0 46.0 %all-to-all-start.3 = ((bf16[8,64,704]{2,1,0:T(8,128)(2,1)}), bf16[8,64,704]{2,1,0:T(8,128)(2,1)S(1)}, u32[]{:S(2)}, u32[]{:S(2)}) async-start(bf16[8,64,704]{2,1,0:T(8,128)(2,1)} %bitcast.145), calls=%async_computation.4 | async-start | bytes 1572864 | tf_op jit(solution)/shard_map/all_to_all | solution.py:340
  224.0 27.0 %all-to-all-start.1 = ((bf16[8,64,704]{2,1,0:T(8,128)(2,1)}), bf16[8,64,704]{2,1,0:T(8,128)(2,1)}, u32[]{:S(2)}, u32[]{:S(2)}) async-start(bf16[8,64,704]{2,1,0:T(8,128)(2,1)} %bitcast.144), calls=%async_computation.2 | async-start | bytes 1572864 | tf_op jit(solution)/shard_map/all_to_all | solution.py:340
  251.0 46.7 %all-to-all-start.2 = ((bf16[8,64,704]{2,1,0:T(8,128)(2,1)}), bf16[8,64,704]{2,1,0:T(8,128)(2,1)}, u32[]{:S(2)}, u32[]{:S(2)}) async-start(bf16[8,64,704]{2,1,0:T(8,128)(2,1)} %bitcast.143), calls=%async_computation.3 | async-start | bytes 1572864 | tf_op jit(solution)/shard_map/all_to_all | solution.py:340
  255.3 191.0 %reduce-scatter.9.cloned.1.call-start = ((), (), s32[]{:S(2)}) async-start(), calls=%async_computation.15 | async-start | bytes 4718592 | tf_op jit(solution)/shard_map/reduce_scatter | solution.py:336
  256.9 44.6 %collective-permute-start.17 = (bf16[512,704]{0,1:T(8,128)(2,1)}, bf16[512,704]{0,1:T(8,128)(2,1)}, u32[]{:S(2)}, u32[]{:S(2)}) collective-permute-start(bf16[512,704]{0,1:T(8,128)(2,1)} %copy.124), channel_id=1, source_target_pairs={{0,16},{16,0},{8,24},{24,8},{1,17},{17,1},{9,25},{25,9},{2,18},{18... | collective-permute-start | bytes 2162696 | tf_op jit(solution)/shard_map/ppermute | solution.py:348
  258.3 54.4 %collective-permute-start.16 = (bf16[512,704]{0,1:T(8,128)(2,1)}, bf16[512,704]{0,1:T(8,128)(2,1)}, u32[]{:S(2)}, u32[]{:S(2)}) collective-permute-start(bf16[512,704]{0,1:T(8,128)(2,1)} %copy.124), channel_id=1, source_target_pairs={{0,8},{8,0},{16,24},{24,16},{1,9},{9,1},{17,25},{25,17},{2,10},{10... | collective-permute-start | bytes 2162696 | tf_op jit(solution)/shard_map/ppermute | solution.py:347
  262.1 55.3 %collective-permute-start.9 = (bf16[512,704]{0,1:T(8,128)(2,1)}, bf16[512,704]{0,1:T(8,128)(2,1)}, u32[]{:S(2)}, u32[]{:S(2)}) collective-permute-start(bf16[512,704]{0,1:T(8,128)(2,1)} %copy.110), channel_id=1, source_target_pairs={{0,16},{16,0},{8,24},{24,8},{1,17},{17,1},{9,25},{25,9},{2,18},{18... | collective-permute-start | bytes 2162696 | tf_op jit(solution)/shard_map/ppermute | solution.py:348
  262.6 59.3 %collective-permute-start.8 = (bf16[512,704]{0,1:T(8,128)(2,1)}, bf16[512,704]{0,1:T(8,128)(2,1)}, u32[]{:S(2)}, u32[]{:S(2)}) collective-permute-start(bf16[512,704]{0,1:T(8,128)(2,1)} %copy.110), channel_id=1, source_target_pairs={{0,8},{8,0},{16,24},{24,16},{1,9},{9,1},{17,25},{25,17},{2,10},{10... | collective-permute-start | bytes 2162696 | tf_op jit(solution)/shard_map/ppermute | solution.py:347
  300.0 27.4 %collective-permute-start.13 = (bf16[512,704]{0,1:T(8,128)(2,1)}, bf16[512,704]{0,1:T(8,128)(2,1)}, u32[]{:S(2)}, u32[]{:S(2)}) collective-permute-start(bf16[512,704]{0,1:T(8,128)(2,1)} %copy.117), channel_id=1, source_target_pairs={{0,16},{16,0},{8,24},{24,8},{1,17},{17,1},{9,25},{25,9},{2,18},{18... | collective-permute-start | bytes 2162696 | tf_op jit(solution)/shard_map/ppermute | solution.py:348
  301.5 31.5 %collective-permute-start.12 = (bf16[512,704]{0,1:T(8,128)(2,1)}, bf16[512,704]{0,1:T(8,128)(2,1)}, u32[]{:S(2)}, u32[]{:S(2)}) collective-permute-start(bf16[512,704]{0,1:T(8,128)(2,1)} %copy.117), channel_id=1, source_target_pairs={{0,8},{8,0},{16,24},{24,16},{1,9},{9,1},{17,25},{25,17},{2,10},{10... | collective-permute-start | bytes 2162696 | tf_op jit(solution)/shard_map/ppermute | solution.py:347
  312.7 30.1 %collective-permute-start.19 = (bf16[256,704]{0,1:T(8,128)(2,1)}, bf16[256,704]{0,1:T(8,128)(2,1)}, u32[]{:S(2)}, u32[]{:S(2)}) collective-permute-start(bf16[256,704]{0,1:T(8,128)(2,1)} %slice.165), channel_id=1, source_target_pairs={{0,8},{8,0},{16,24},{24,16},{1,9},{9,1},{17,25},{25,17},{2,10},{10... | collective-permute-start | bytes 1081352 | tf_op jit(solution)/shard_map/ppermute | solution.py:350
  317.3 30.2 %collective-permute-start.18 = (bf16[256,704]{0,1:T(8,128)(2,1)}, bf16[256,704]{0,1:T(8,128)(2,1)}, u32[]{:S(2)}, u32[]{:S(2)}) collective-permute-start(bf16[256,704]{0,1:T(8,128)(2,1)} %slice.164), channel_id=1, source_target_pairs={{0,16},{16,0},{8,24},{24,8},{1,17},{17,1},{9,25},{25,9},{2,18},{18... | collective-permute-start | bytes 1081352 | tf_op jit(solution)/shard_map/ppermute | solution.py:349
  322.0 26.7 %collective-permute-start.11 = (bf16[256,704]{0,1:T(8,128)(2,1)}, bf16[256,704]{0,1:T(8,128)(2,1)}, u32[]{:S(2)}, u32[]{:S(2)}) collective-permute-start(bf16[256,704]{0,1:T(8,128)(2,1)} %slice.161), channel_id=1, source_target_pairs={{0,8},{8,0},{16,24},{24,16},{1,9},{9,1},{17,25},{25,17},{2,10},{10... | collective-permute-start | bytes 1081352 | tf_op jit(solution)/shard_map/ppermute | solution.py:350
  327.4 23.1 %collective-permute-start.10 = (bf16[256,704]{0,1:T(8,128)(2,1)}, bf16[256,704]{0,1:T(8,128)(2,1)}, u32[]{:S(2)}, u32[]{:S(2)}) collective-permute-start(bf16[256,704]{0,1:T(8,128)(2,1)} %slice.160), channel_id=1, source_target_pairs={{0,16},{16,0},{8,24},{24,8},{1,17},{17,1},{9,25},{25,9},{2,18},{18... | collective-permute-start | bytes 1081352 | tf_op jit(solution)/shard_map/ppermute | solution.py:349
  332.9 19.5 %collective-permute-start.15 = (bf16[256,704]{0,1:T(8,128)(2,1)}, bf16[256,704]{0,1:T(8,128)(2,1)}, u32[]{:S(2)}, u32[]{:S(2)}) collective-permute-start(bf16[256,704]{0,1:T(8,128)(2,1)} %slice.163), channel_id=1, source_target_pairs={{0,8},{8,0},{16,24},{24,16},{1,9},{9,1},{17,25},{25,17},{2,10},{10... | collective-permute-start | bytes 1081352 | tf_op jit(solution)/shard_map/ppermute | solution.py:350
  342.8 11.6 %collective-permute-start.14 = (bf16[256,704]{0,1:T(8,128)(2,1)}, bf16[256,704]{0,1:T(8,128)(2,1)}, u32[]{:S(2)}, u32[]{:S(2)}) collective-permute-start(bf16[256,704]{0,1:T(8,128)(2,1)} %slice.162), channel_id=1, source_target_pairs={{0,16},{16,0},{8,24},{24,8},{1,17},{17,1},{9,25},{25,9},{2,18},{18... | collective-permute-start | bytes 1081352 | tf_op jit(solution)/shard_map/ppermute | solution.py:349
  397.0 98.7 %all-gather.9.cloned.1.call-start = ((), (), s32[]{:S(2)}) async-start(), calls=%async_computation.16 | async-start | bytes 4718592 | tf_op jit(solution)/shard_map/all_gather | solution.py:332
  450.2 321.6 %reduce-scatter.11.cloned.1.call-start = ((), (), s32[]{:S(2)}) async-start(), calls=%async_computation.17 | async-start | bytes 4718592 | tf_op jit(solution)/shard_map/reduce_scatter | solution.py:336
  541.4 11.3 %collective-permute-start.45 = (bf16[256,704]{0,1:T(8,128)(2,1)S(1)}, bf16[256,704]{0,1:T(8,128)(2,1)S(1)}, u32[]{:S(2)}, u32[]{:S(2)}) collective-permute-start(bf16[256,704]{0,1:T(8,128)(2,1)S(1)} %get-tuple-element.45), channel_id=1, source_target_pairs={{0,8},{8,0},{16,24},{24,16},{1,9},{9,1},{17,25},{25,17},{2,10},{10... | collective-permute-start | bytes 1081352 | tf_op jit(solution)/shard_map/ppermute | solution.py:376
  543.0 22.4 %collective-permute-start.44 = (bf16[256,704]{0,1:T(8,128)(2,1)S(1)}, bf16[256,704]{0,1:T(8,128)(2,1)S(1)}, u32[]{:S(2)}, u32[]{:S(2)}) collective-permute-start(bf16[256,704]{0,1:T(8,128)(2,1)S(1)} %get-tuple-element.42), channel_id=1, source_target_pairs={{0,8},{8,0},{16,24},{24,16},{1,9},{9,1},{17,25},{25,17},{2,10},{10... | collective-permute-start | bytes 1081352 | tf_op jit(solution)/shard_map/ppermute | solution.py:375
  543.5 21.9 %collective-permute-start.48 = (bf16[256,704]{0,1:T(8,128)(2,1)S(1)}, bf16[256,704]{0,1:T(8,128)(2,1)S(1)}, u32[]{:S(2)}, u32[]{:S(2)}) collective-permute-start(bf16[256,704]{0,1:T(8,128)(2,1)S(1)} %get-tuple-element.43), channel_id=1, source_target_pairs={{0,16},{16,0},{8,24},{24,8},{1,17},{17,1},{9,25},{25,9},{2,18},{18... | collective-permute-start | bytes 1081352 | tf_op jit(solution)/shard_map/ppermute | solution.py:378
  545.0 31.4 %collective-permute-start.47 = (bf16[256,704]{0,1:T(8,128)(2,1)S(1)}, bf16[256,704]{0,1:T(8,128)(2,1)}, u32[]{:S(2)}, u32[]{:S(2)}) collective-permute-start(bf16[256,704]{0,1:T(8,128)(2,1)S(1)} %get-tuple-element.44), channel_id=1, source_target_pairs={{0,16},{16,0},{8,24},{24,8},{1,17},{17,1},{9,25},{25,9},{2,18},{18... | collective-permute-start | bytes 1081352 | tf_op jit(solution)/shard_map/ppermute | solution.py:377
  553.9 15.1 %collective-permute-start.46 = (bf16[256,704]{0,1:T(8,128)(2,1)S(1)}, bf16[256,704]{0,1:T(8,128)(2,1)S(1)}, u32[]{:S(2)}, u32[]{:S(2)}) collective-permute-start(bf16[256,704]{0,1:T(8,128)(2,1)S(1)} %fusion.51), channel_id=1, source_target_pairs={{0,16},{16,0},{8,24},{24,8},{1,17},{17,1},{9,25},{25,9},{2,18},{18... | collective-permute-start | bytes 1081352 | tf_op jit(solution)/shard_map/ppermute | solution.py:381
  563.9 10.0 %collective-permute-start.39 = (bf16[256,704]{0,1:T(8,128)(2,1)}, bf16[256,704]{0,1:T(8,128)(2,1)}, u32[]{:S(2)}, u32[]{:S(2)}) collective-permute-start(bf16[256,704]{0,1:T(8,128)(2,1)} %get-tuple-element.51), channel_id=1, source_target_pairs={{0,8},{8,0},{16,24},{24,16},{1,9},{9,1},{17,25},{25,17},{2,10},{10... | collective-permute-start | bytes 1081352 | tf_op jit(solution)/shard_map/ppermute | solution.py:376
  570.3 11.4 %collective-permute-start.49 = (bf16[256,704]{0,1:T(8,128)(2,1)S(1)}, bf16[256,704]{0,1:T(8,128)(2,1)S(1)}, u32[]{:S(2)}, u32[]{:S(2)}) collective-permute-start(bf16[256,704]{0,1:T(8,128)(2,1)S(1)} %get-tuple-element.41), channel_id=1, source_target_pairs={{0,8},{8,0},{16,24},{24,16},{1,9},{9,1},{17,25},{25,17},{2,10},{10... | collective-permute-start | bytes 1081352 | tf_op jit(solution)/shard_map/ppermute | solution.py:382
  571.9 24.3 %collective-permute-start.38 = (bf16[256,704]{0,1:T(8,128)(2,1)}, bf16[256,704]{0,1:T(8,128)(2,1)}, u32[]{:S(2)}, u32[]{:S(2)}) collective-permute-start(bf16[256,704]{0,1:T(8,128)(2,1)} %get-tuple-element.48), channel_id=1, source_target_pairs={{0,8},{8,0},{16,24},{24,16},{1,9},{9,1},{17,25},{25,17},{2,10},{10... | collective-permute-start | bytes 1081352 | tf_op jit(solution)/shard_map/ppermute | solution.py:375
  572.4 23.8 %collective-permute-start.42 = (bf16[256,704]{0,1:T(8,128)(2,1)S(1)}, bf16[256,704]{0,1:T(8,128)(2,1)}, u32[]{:S(2)}, u32[]{:S(2)}) collective-permute-start(bf16[256,704]{0,1:T(8,128)(2,1)S(1)} %get-tuple-element.49), channel_id=1, source_target_pairs={{0,16},{16,0},{8,24},{24,8},{1,17},{17,1},{9,25},{25,9},{2,18},{18... | collective-permute-start | bytes 1081352 | tf_op jit(solution)/shard_map/ppermute | solution.py:378
  574.0 34.4 %collective-permute-start.41 = (bf16[256,704]{0,1:T(8,128)(2,1)S(1)}, bf16[256,704]{0,1:T(8,128)(2,1)}, u32[]{:S(2)}, u32[]{:S(2)}) collective-permute-start(bf16[256,704]{0,1:T(8,128)(2,1)S(1)} %get-tuple-element.50), channel_id=1, source_target_pairs={{0,16},{16,0},{8,24},{24,8},{1,17},{17,1},{9,25},{25,9},{2,18},{18... | collective-permute-start | bytes 1081352 | tf_op jit(solution)/shard_map/ppermute | solution.py:377
  576.4 20.3 %collective-permute-start.40 = (bf16[256,704]{0,1:T(8,128)(2,1)}, bf16[256,704]{0,1:T(8,128)(2,1)}, u32[]{:S(2)}, u32[]{:S(2)}) collective-permute-start(bf16[256,704]{0,1:T(8,128)(2,1)} %add_convert_fusion.9), channel_id=1, source_target_pairs={{0,16},{16,0},{8,24},{24,8},{1,17},{17,1},{9,25},{25,9},{2,18},{18... | collective-permute-start | bytes 1081352 | tf_op jit(solution)/shard_map/ppermute | solution.py:381
  584.1 32.0 %all-to-all-start.7 = ((bf16[8,64,704]{2,1,0:T(8,128)(2,1)}), bf16[8,64,704]{2,1,0:T(8,128)(2,1)S(1)}, u32[]{:S(2)}, u32[]{:S(2)}) async-start(bf16[8,64,704]{2,1,0:T(8,128)(2,1)} %bitcast.34), calls=%async_computation.11 | async-start | bytes 1572864 | tf_op jit(solution)/shard_map/all_to_all | solution.py:340
  594.7 11.3 %collective-permute-start.33 = (bf16[256,704]{0,1:T(8,128)(2,1)S(1)}, bf16[256,704]{0,1:T(8,128)(2,1)S(1)}, u32[]{:S(2)}, u32[]{:S(2)}) collective-permute-start(bf16[256,704]{0,1:T(8,128)(2,1)S(1)} %get-tuple-element.57), channel_id=1, source_target_pairs={{0,8},{8,0},{16,24},{24,16},{1,9},{9,1},{17,25},{25,17},{2,10},{10... | collective-permute-start | bytes 1081352 | tf_op jit(solution)/shard_map/ppermute | solution.py:376
  598.3 15.4 %collective-permute-start.43 = (bf16[256,704]{0,1:T(8,128)(2,1)S(1)}, bf16[256,704]{0,1:T(8,128)(2,1)S(1)}, u32[]{:S(2)}, u32[]{:S(2)}) collective-permute-start(bf16[256,704]{0,1:T(8,128)(2,1)S(1)} %get-tuple-element.47), channel_id=1, source_target_pairs={{0,8},{8,0},{16,24},{24,16},{1,9},{9,1},{17,25},{25,17},{2,10},{10... | collective-permute-start | bytes 1081352 | tf_op jit(solution)/shard_map/ppermute | solution.py:382
  599.9 30.8 %collective-permute-start.32 = (bf16[256,704]{0,1:T(8,128)(2,1)}, bf16[256,704]{0,1:T(8,128)(2,1)}, u32[]{:S(2)}, u32[]{:S(2)}) collective-permute-start(bf16[256,704]{0,1:T(8,128)(2,1)} %get-tuple-element.54), channel_id=1, source_target_pairs={{0,8},{8,0},{16,24},{24,16},{1,9},{9,1},{17,25},{25,17},{2,10},{10... | collective-permute-start | bytes 1081352 | tf_op jit(solution)/shard_map/ppermute | solution.py:375
  600.4 30.3 %collective-permute-start.36 = (bf16[256,704]{0,1:T(8,128)(2,1)}, bf16[256,704]{0,1:T(8,128)(2,1)}, u32[]{:S(2)}, u32[]{:S(2)}) collective-permute-start(bf16[256,704]{0,1:T(8,128)(2,1)} %get-tuple-element.55), channel_id=1, source_target_pairs={{0,16},{16,0},{8,24},{24,8},{1,17},{17,1},{9,25},{25,9},{2,18},{18... | collective-permute-start | bytes 1081352 | tf_op jit(solution)/shard_map/ppermute | solution.py:378
  606.9 23.8 %collective-permute-start.34 = (bf16[256,704]{0,1:T(8,128)(2,1)}, bf16[256,704]{0,1:T(8,128)(2,1)}, u32[]{:S(2)}, u32[]{:S(2)}) collective-permute-start(bf16[256,704]{0,1:T(8,128)(2,1)} %add_convert_fusion.13), channel_id=1, source_target_pairs={{0,16},{16,0},{8,24},{24,8},{1,17},{17,1},{9,25},{25,9},{2,18},{18... | collective-permute-start | bytes 1081352 | tf_op jit(solution)/shard_map/ppermute | solution.py:381
  616.2 31.2 %all-to-all-start.6 = ((bf16[8,64,704]{2,1,0:T(8,128)(2,1)}), bf16[8,64,704]{2,1,0:T(8,128)(2,1)S(1)}, u32[]{:S(2)}, u32[]{:S(2)}) async-start(bf16[8,64,704]{2,1,0:T(8,128)(2,1)} %bitcast.24), calls=%async_computation.10 | async-start | bytes 1572864 | tf_op jit(solution)/shard_map/all_to_all | solution.py:340
  621.2 152.0 %reduce-scatter.7.cloned.1.call-start = ((), (), s32[]{:S(2)}) async-start(), calls=%async_computation.14 | async-start | bytes 4718592 | tf_op jit(solution)/shard_map/reduce_scatter | solution.py:336
  629.2 10.9 %collective-permute-start.35 = (bf16[256,704]{0,1:T(8,128)(2,1)S(1)}, bf16[256,704]{0,1:T(8,128)(2,1)}, u32[]{:S(2)}, u32[]{:S(2)}) collective-permute-start(bf16[256,704]{0,1:T(8,128)(2,1)S(1)} %copy-done.31), channel_id=1, source_target_pairs={{0,16},{16,0},{8,24},{24,8},{1,17},{17,1},{9,25},{25,9},{2,18},{18... | collective-permute-start | bytes 1081352 | tf_op jit(solution)/shard_map/ppermute | solution.py:377
  632.4 10.6 %collective-permute-start.37 = (bf16[256,704]{0,1:T(8,128)(2,1)S(1)}, bf16[256,704]{0,1:T(8,128)(2,1)S(1)}, u32[]{:S(2)}, u32[]{:S(2)}) collective-permute-start(bf16[256,704]{0,1:T(8,128)(2,1)S(1)} %get-tuple-element.53), channel_id=1, source_target_pairs={{0,8},{8,0},{16,24},{24,16},{1,9},{9,1},{17,25},{25,17},{2,10},{10... | collective-permute-start | bytes 1081352 | tf_op jit(solution)/shard_map/ppermute | solution.py:382
  647.4 39.3 %all-to-all-start.5 = ((bf16[8,64,704]{2,1,0:T(8,128)(2,1)}), bf16[8,64,704]{2,1,0:T(8,128)(2,1)}, u32[]{:S(2)}, u32[]{:S(2)}) async-start(bf16[8,64,704]{2,1,0:T(8,128)(2,1)} %bitcast.22), calls=%async_computation.9 | async-start | bytes 1572864 | tf_op jit(solution)/shard_map/all_to_all | solution.py:340
  697.2 12.1 %collective-permute-start.21 = (bf16[256,768]{1,0:T(8,128)(2,1)S(1)}, bf16[256,768]{1,0:T(8,128)(2,1)S(1)}, u32[]{:S(2)}, u32[]{:S(2)}) collective-permute-start(bf16[256,768]{1,0:T(8,128)(2,1)S(1)} %get-tuple-element.29), channel_id=1, source_target_pairs={{0,8},{8,0},{16,24},{24,16},{1,9},{9,1},{17,25},{25,17},{2,10},{10... | collective-permute-start | bytes 1179656 | tf_op jit(solution)/shard_map/ppermute | solution.py:376
  701.8 15.8 %collective-permute-start.20 = (bf16[256,768]{1,0:T(8,128)(2,1)S(1)}, bf16[256,768]{1,0:T(8,128)(2,1)S(1)}, u32[]{:S(2)}, u32[]{:S(2)}) collective-permute-start(bf16[256,768]{1,0:T(8,128)(2,1)S(1)} %get-tuple-element.26), channel_id=1, source_target_pairs={{0,8},{8,0},{16,24},{24,16},{1,9},{9,1},{17,25},{25,17},{2,10},{10... | collective-permute-start | bytes 1179656 | tf_op jit(solution)/shard_map/ppermute | solution.py:375
  703.4 15.1 %collective-permute-start.24 = (bf16[256,768]{1,0:T(8,128)(2,1)S(1)}, bf16[256,768]{1,0:T(8,128)(2,1)S(1)}, u32[]{:S(2)}, u32[]{:S(2)}) collective-permute-start(bf16[256,768]{1,0:T(8,128)(2,1)S(1)} %get-tuple-element.27), channel_id=1, source_target_pairs={{0,16},{16,0},{8,24},{24,8},{1,17},{17,1},{9,25},{25,9},{2,18},{18... | collective-permute-start | bytes 1179656 | tf_op jit(solution)/shard_map/ppermute | solution.py:378
  709.4 14.4 %collective-permute-start.22 = (bf16[256,768]{1,0:T(8,128)(2,1)S(1)}, bf16[256,768]{1,0:T(8,128)(2,1)S(1)}, u32[]{:S(2)}, u32[]{:S(2)}) collective-permute-start(bf16[256,768]{1,0:T(8,128)(2,1)S(1)} %add_convert_fusion.5), channel_id=1, source_target_pairs={{0,16},{16,0},{8,24},{24,8},{1,17},{17,1},{9,25},{25,9},{2,18},{18... | collective-permute-start | bytes 1179656 | tf_op jit(solution)/shard_map/ppermute | solution.py:381
  712.3 29.7 %collective-permute-start.26 = (bf16[32,2048]{1,0:T(8,128)(2,1)}, bf16[32,2048]{1,0:T(8,128)(2,1)S(1)}, u32[]{:S(2)}, u32[]{:S(2)}) collective-permute-start(bf16[32,2048]{1,0:T(8,128)(2,1)} %get-tuple-element.66), channel_id=1, source_target_pairs={{0,8},{8,0},{16,24},{24,16},{1,9},{9,1},{17,25},{25,17},{2,10},{10... | collective-permute-start | bytes 393224 | tf_op jit(solution)/shard_map/ppermute | solution.py:375
  713.8 28.2 %collective-permute-start.30 = (bf16[32,2048]{1,0:T(8,128)(2,1)}, bf16[32,2048]{1,0:T(8,128)(2,1)S(1)}, u32[]{:S(2)}, u32[]{:S(2)}) collective-permute-start(bf16[32,2048]{1,0:T(8,128)(2,1)} %get-tuple-element.67), channel_id=1, source_target_pairs={{0,16},{16,0},{8,24},{24,8},{1,17},{17,1},{9,25},{25,9},{2,18},{18... | collective-permute-start | bytes 393224 | tf_op jit(solution)/shard_map/ppermute | solution.py:378
  717.7 26.0 %collective-permute-start.29 = (bf16[32,2048]{1,0:T(8,128)(2,1)}, bf16[32,2048]{1,0:T(8,128)(2,1)S(1)}, u32[]{:S(2)}, u32[]{:S(2)}) collective-permute-start(bf16[32,2048]{1,0:T(8,128)(2,1)} %get-tuple-element.68), channel_id=1, source_target_pairs={{0,16},{16,0},{8,24},{24,8},{1,17},{17,1},{9,25},{25,9},{2,18},{18... | collective-permute-start | bytes 393224 | tf_op jit(solution)/shard_map/ppermute | solution.py:377
  718.5 6.0 collective-permute-start.27
  723.8 12.6 %collective-permute-start.23 = (bf16[256,768]{1,0:T(8,128)(2,1)S(1)}, bf16[256,768]{1,0:T(8,128)(2,1)S(1)}, u32[]{:S(2)}, u32[]{:S(2)}) collective-permute-start(bf16[256,768]{1,0:T(8,128)(2,1)S(1)} %get-tuple-element.28), channel_id=1, source_target_pairs={{0,16},{16,0},{8,24},{24,8},{1,17},{17,1},{9,25},{25,9},{2,18},{18... | collective-permute-start | bytes 1179656 | tf_op jit(solution)/shard_map/ppermute | solution.py:377
  724.5 12.6 %collective-permute-start.25 = (bf16[256,768]{1,0:T(8,128)(2,1)S(1)}, bf16[256,768]{1,0:T(8,128)(2,1)S(1)}, u32[]{:S(2)}, u32[]{:S(2)}) collective-permute-start(bf16[256,768]{1,0:T(8,128)(2,1)S(1)} %get-tuple-element.25), channel_id=1, source_target_pairs={{0,8},{8,0},{16,24},{24,16},{1,9},{9,1},{17,25},{25,17},{2,10},{10... | collective-permute-start | bytes 1179656 | tf_op jit(solution)/shard_map/ppermute | solution.py:382
  738.4 24.4 %all-to-all-start.4 = ((bf16[8,64,768]{2,1,0:T(8,128)(2,1)}), bf16[8,64,768]{2,1,0:T(8,128)(2,1)S(1)}, u32[]{:S(2)}, u32[]{:S(2)}) async-start(bf16[8,64,768]{2,1,0:T(8,128)(2,1)} %bitcast.20), calls=%async_computation.8 | async-start | bytes 1572864 | tf_op jit(solution)/shard_map/all_to_all | solution.py:340
  (48 other events, 330.0 us)
Sparse Core Ops, SparseCore 0:
  9.6 64.9 all-gather.10
  118.9 52.8 reduce-scatter.4
  173.4 67.2 all-gather.12
  242.2 63.9 all-gather.6
  397.1 49.1 reduce-scatter.8
  450.3 45.3 all-gather.8
  532.8 48.7 reduce-scatter.10
  630.8 64.7 reduce-scatter.6

commit v2 on v1

--- a/solution.py
+++ b/solution.py
@@ -340,12 +340,14 @@
     return lax.all_to_all(pieces, "ctx", 0, 0, tiled=True)
 
 
-def gather_seq(block):
+def gather_seq_near(block):
+    return lax.ppermute(block, "seq", SEQ_X), lax.ppermute(block, "seq", SEQ_Y)
+
+
+def gather_seq_far(block, from_x, from_y):
     rows, width = block.shape
     half = rows // 2
     mine = lax.axis_index("seq")
-    from_x = lax.ppermute(block, "seq", SEQ_X)
-    from_y = lax.ppermute(block, "seq", SEQ_Y)
     far_top = lax.ppermute(from_x[:half], "seq", SEQ_Y)
     far_low = lax.ppermute(from_y[half:], "seq", SEQ_X)
     whole = jnp.zeros((4 * rows, width), block.dtype)
@@ -360,43 +362,80 @@
     return whole
 
 
-def reduce_seq(partial):
-    rows = partial.shape[0] // 4
+def gather_seq(block):
+    return gather_seq_far(block, *gather_seq_near(block))
+
+
+def seq_part(partials, other, low):
+    rows = partials[0].shape[0] // 4
     half = rows // 2
-    mine = lax.axis_index("seq")
-
-    def part(other, low):
-        start = (mine ^ other) * rows + (half if low else 0)
-        return lax.dynamic_slice_in_dim(partial, start, half, 0)
-
-    def add(left, right):
-        return left.astype(jnp.float32) + right.astype(jnp.float32)
-
-    top_near = lax.ppermute(part(1, False), "seq", SEQ_X)
-    top_far = lax.ppermute(part(3, False), "seq", SEQ_X)
-    low_near = lax.ppermute(part(2, True), "seq", SEQ_Y)
-    low_far = lax.ppermute(part(3, True), "seq", SEQ_Y)
-    top_send = add(part(2, False), top_far).astype(jnp.bfloat16)
-    low_send = add(part(1, True), low_far).astype(jnp.bfloat16)
+    start = (lax.axis_index("seq") ^ other) * rows + (half if low else 0)
+    return jnp.concatenate(
+        [lax.dynamic_slice_in_dim(partial, start, half, 0) for partial in partials], axis=1
+    )
+
+
+def reduce_seq_near(partials):
+    return (
+        lax.ppermute(seq_part(partials, 3, False), "seq", SEQ_X),
+        lax.ppermute(seq_part(partials, 3, True), "seq", SEQ_Y),
+        lax.ppermute(seq_part(partials, 1, False), "seq", SEQ_X),
+        lax.ppermute(seq_part(partials, 2, True), "seq", SEQ_Y),
+    )
+
+
+def add_wide(*terms):
+    total = terms[0].astype(jnp.float32)
+    for term in terms[1:]:
+        total = total + term.astype(jnp.float32)
+    return total
+
+
+def reduce_seq_far(partials, top_far, low_far, top_near, low_near):
+    top_send = add_wide(seq_part(partials, 2, False), top_far).astype(jnp.bfloat16)
+    low_send = add_wide(seq_part(partials, 1, True), low_far).astype(jnp.bfloat16)
     top_last = lax.ppermute(top_send, "seq", SEQ_Y)
     low_last = lax.ppermute(low_send, "seq", SEQ_X)
     return jnp.concatenate(
         [
-            add(part(0, False), top_near) + top_last.astype(jnp.float32),
-            add(part(0, True), low_near) + low_last.astype(jnp.float32),
+            add_wide(seq_part(partials, 0, False), top_near, top_last),
+            add_wide(seq_part(partials, 0, True), low_near, low_last),
         ],
         axis=0,
     ).astype(jnp.bfloat16)
 
 
-def to_slices(weight):
+def reduce_seq(partials):
+    return reduce_seq_far(partials, *reduce_seq_near(partials))
+
+
+def tie(*values):
+    return lax.optimization_barrier(values)
+
+
+def ff_split(width):
+    main = width // 8 // 128 * 128
+    return main, width // 8 - main
+
+
+def ff_slices(weight):
     rows, width = weight.shape
-    return jnp.transpose(weight.reshape(rows, 8, width // 8), (1, 0, 2))
-
-
-def from_slices(pieces):
-    count, rows, width = pieces.shape
-    return jnp.transpose(pieces, (1, 0, 2)).reshape(rows, count * width)
+    main, tail = ff_split(width)
+    return (
+        jnp.transpose(weight[:, : 8 * main].reshape(rows, 8, main), (1, 0, 2)),
+        jnp.transpose(weight[:, 8 * main :].reshape(rows, 8, tail), (1, 0, 2)),
+    )
+
+
+def ff_rows(main, tail):
+    count, rows, width = main.shape
+    return jnp.concatenate(
+        [
+            jnp.transpose(main, (1, 0, 2)).reshape(rows, count * width),
+            jnp.transpose(tail, (1, 0, 2)).reshape(rows, count * tail.shape[2]),
+        ],
+        axis=1,
+    )
 
 
 def head_slices(weight):
@@ -578,6 +617,7 @@
         return (weight.astype(f32) * gain).astype(bf16)
 
     inputs_all = gather_ctx(block_input[0])
+    back_all = gather_ctx(out_back)
     key_value = jnp.concatenate([fold(key_weight, gain_one), fold(value_weight, gain_one)], axis=1)
     attn_pieces = jnp.concatenate(
         [
@@ -586,14 +626,18 @@
         ],
         axis=2,
     )
-    attn_cols = gather_seq(exchange_ctx(attn_pieces).reshape(8 * rows, 3 * head_width))
+    main, tail = ff_split(gate_weight.shape[1])
+    both = 2 * (main + tail)
+    gate_main, gate_tail = ff_slices(fold(gate_weight, gain_two))
+    up_main, up_tail = ff_slices(fold(up_weight, gain_two))
+    mlp_pieces = jnp.concatenate(
+        [gate_main, up_main, gate_tail, up_tail, *ff_slices(down_weight)], axis=2
+    )
+    attn_own = exchange_ctx(attn_pieces).reshape(8 * rows, 3 * head_width)
+    attn_own, mlp_pieces = tie(attn_own, mlp_pieces)
+    attn_cols = gather_seq(attn_own)
     out_rows = gather_seq(out_weight)
-    gate_cols = gather_seq(
-        exchange_ctx(to_slices(fold(gate_weight, gain_two))).reshape(8 * rows, -1)
-    )
-    up_cols = gather_seq(exchange_ctx(to_slices(fold(up_weight, gain_two))).reshape(8 * rows, -1))
-    down_cols = gather_seq(exchange_ctx(to_slices(down_weight)).reshape(8 * rows, -1))
-    back_all = gather_ctx(out_back)
+    mlp_own = exchange_ctx(mlp_pieces).reshape(8 * rows, -1)
 
     edge = jnp.sum((segments[0] == 0).astype(jnp.int32))
     token = jnp.arange(length, dtype=jnp.int32)
@@ -611,32 +655,62 @@
     values = raw[:, 2 * head_width :].astype(bf16)
     queries = queries * jnp.asarray(score_scale, bf16)
     attn_low = attend(edge, queries, keys, values)
+    attn_low, out_rows, mlp_own, back_all = tie(attn_low, out_rows, mlp_own, back_all)
     mixed = jnp.dot(attn_low, out_rows, preferred_element_type=f32).astype(bf16)
-    residual = inputs + reduce_ctx(mixed).astype(f32)
+    mixed_own = reduce_ctx(mixed)
+    mlp_near = gather_seq_near(mlp_own)
+    mixed_own, *mlp_near = tie(mixed_own, *mlp_near)
+    residual = inputs + mixed_own.astype(f32)
     scale_two = rms_scale(residual)
     shaped_two = residual * scale_two
     normed_all = gather_ctx(shaped_two.astype(bf16))
-    gate_proj = jnp.dot(normed_all, gate_cols, preferred_element_type=f32)
-    up_proj = jnp.dot(normed_all, up_cols, preferred_element_type=f32)
+    mlp_cols = gather_seq_far(mlp_own, *mlp_near)
+    gate_up, down_cols = mlp_cols[:, :both], mlp_cols[:, both:]
+    hidden_back = jnp.dot(back_all, down_cols, preferred_element_type=f32)
+    normed_all, hidden_back = tie(normed_all, hidden_back)
+    proj = jnp.dot(normed_all, gate_up, preferred_element_type=f32)
+
+    def halves(left_tail, right_tail, left, right):
+        return jnp.concatenate([left, left_tail], axis=1), jnp.concatenate([right, right_tail], axis=1)
+
+    gate_proj, up_proj = halves(
+        proj[:, 2 * main : 2 * main + tail],
+        proj[:, 2 * main + tail :],
+        proj[:, :main],
+        proj[:, main : 2 * main],
+    )
     sigmoid_gate = jax.nn.sigmoid(gate_proj)
     silu_gate = gate_proj * sigmoid_gate
     hidden = (silu_gate * up_proj).astype(bf16)
-    hidden_back = jnp.dot(back_all, down_cols, preferred_element_type=f32)
     gate_back = (
         hidden_back * up_proj * sigmoid_gate * (1.0 + gate_proj * (1.0 - sigmoid_gate))
     ).astype(bf16)
     upper_back = (hidden_back * silu_gate).astype(bf16)
-    weighted = reduce_ctx(
-        (contract_cols(gate_back, gate_cols) + contract_cols(upper_back, up_cols)).astype(bf16)
-    ).astype(f32)
+    gate_up_back = jnp.concatenate(
+        [gate_back[:, :main], upper_back[:, :main], gate_back[:, main:], upper_back[:, main:]],
+        axis=1,
+    )
+    weighted = reduce_ctx(contract_cols(gate_up_back, gate_up).astype(bf16))
+    gate_up_grad = contract_rows(normed_all, gate_up_back).astype(bf16)
+    down_grad = contract_rows(back_all, hidden).astype(bf16)
+    mixed_out = contract_cols(hidden, down_cols).astype(bf16)
+    weighted, gate_up_grad, down_grad, mixed_out = tie(weighted, gate_up_grad, down_grad, mixed_out)
+    mlp_grads = [gate_up_grad, down_grad]
+    weighted = weighted.astype(f32)
     residual_back = out_back.astype(f32) + scale_two * (
         weighted - shaped_two * jnp.mean(weighted * shaped_two, axis=-1, keepdims=True)
     )
     low_all = gather_ctx(residual_back.astype(bf16))
+    mlp_grads_near = reduce_seq_near(mlp_grads)
+    low_all, mixed_out, *mlp_grads_near = tie(low_all, mixed_out, *mlp_grads_near)
+    out_own = reduce_ctx(mixed_out)
+    mlp_grads_own = reduce_seq_far(mlp_grads, *mlp_grads_near)
     attn_back = contract_cols(low_all, out_rows).astype(bf16)
     query_back, key_back, value_back = attend_back(
         edge, queries, keys, values, attn_back, score_scale
     )
+    out_grad = reduce_seq([contract_rows(attn_low, low_all).astype(bf16)]).astype(f32)
+    query_back, mlp_grads_own, out_own = tie(query_back, mlp_grads_own, out_own)
     heads_back = jnp.concatenate(
         [
             turn(query_back, cosine, -sine_table).astype(bf16),
@@ -651,19 +725,14 @@
     input_grad = residual_back + scale_one * (
         weighted_one - shaped_one * jnp.mean(weighted_one * shaped_one, axis=-1, keepdims=True)
     )
-    block_output = (
-        residual + reduce_ctx(contract_cols(hidden, down_cols).astype(bf16)).astype(f32)
-    ).astype(bf16)
-
-    def column_grad(left, right):
-        slices = reduce_seq(contract_rows(left, right).astype(bf16))
-        return exchange_ctx(slices.reshape(8, rows, -1)).astype(f32)
-
-    down_grad = from_slices(column_grad(back_all, hidden))
-    gate_rows = from_slices(column_grad(normed_all, gate_back))
-    up_rows = from_slices(column_grad(normed_all, upper_back))
-    out_grad = reduce_seq(contract_rows(attn_low, low_all).astype(bf16)).astype(f32)
-    attn_grad = column_grad(shaped_all, heads_back)
+    block_output = (residual + out_own.astype(f32)).astype(bf16)
+
+    mlp_grad = exchange_ctx(mlp_grads_own.reshape(8, rows, -1)).astype(f32)
+    attn_grad_own = reduce_seq([contract_rows(shaped_all, heads_back).astype(bf16)])
+    attn_grad = exchange_ctx(attn_grad_own.reshape(8, rows, -1)).astype(f32)
+    gate_rows = ff_rows(mlp_grad[:, :, :main], mlp_grad[:, :, 2 * main : 2 * main + tail])
+    up_rows = ff_rows(mlp_grad[:, :, main : 2 * main], mlp_grad[:, :, 2 * main + tail : both])
+    down_grad = ff_rows(mlp_grad[:, :, both : both + main], mlp_grad[:, :, both + main :])
     query_rows = from_head_slices(attn_grad[:, :, :head_width])
     pair_rows = jnp.sum(attn_grad[:, :, head_width:], axis=0)
     key_rows, value_rows = pair_rows[:, :head_width], pair_rows[:, head_width:]

time: 794 us -> 634 us (0.80)
  waiting for transfers between devices: 378 us -> 286 us
  starting transfers between devices: 92.5 us -> 50.2 us
  local copies, waits for them, and re-layouts: 124 us -> 106 us
  matrix products: 88.4 us -> 79.4 us
    reduce_scatter x4, waiting for transfers between devices: 102 us -> 31.1 us  [reduce_ctx(): return lax.psum_scatter(partial, 'ctx', scatter_dimension=0, tiled=True)]
    ppermute x50 -> x30, waiting for transfers between devices: 75 us -> 137 us  [the longest x3 57 us: gather_seq_near(): lax.ppermute(block, 'seq', SEQ_X)]
    all_to_all x8 -> x4, waiting for transfers between devices: 154 us -> 111 us  [exchange_ctx(): return lax.all_to_all(pieces, 'ctx', 0, 0, tiled=True)]
    all_gather x4, waiting for transfers between devices: 45.5 us -> 5.05 us  [gather_ctx(): return lax.all_gather(block, 'ctx', axis=0, tiled=True)]
    ppermute x50 -> x30, starting transfers between devices: 56.4 us -> 33 us  [the longest x3 5.47 us: gather_seq_near(): lax.ppermute(block, 'seq', SEQ_X)]
    ppermute x12 -> x2, local copies, waits for them, and re-layouts: 22.7 us -> 3.33 us  [the longest x1 1.68 us: gather_seq_far(): far_top = lax.ppermute(from_x[:half], 'seq', SEQ_Y)]
    all_to_all x8 -> x4, starting transfers between devices: 35.4 us -> 16.3 us  [exchange_ctx(): return lax.all_to_all(pieces, 'ctx', 0, 0, tiled=True)]
    reshape x15 -> x11, local copies, waits for them, and re-layouts: 25.6 us -> 7.75 us  [the longest x3 5.01 us: ff_rows(): jnp.transpose(main, (1, 0, 2)).reshape(rows, count * width)]
  transfers between devices with their start and end apart: 66 -> 42, of which waited for: 26 -> 25; matrix products, arithmetic and copies ran while one was open for 25% -> 29% of each run, Pallas kernels for 0% -> 5%
where the time goes in v2:
time: 634 us; the launch traced here: 627 us
  waiting for transfers between devices  286 us (45%)
  local copies, waits for them, and re-layouts  106 us (17%)
  matrix products  79.4 us (13%)
  other arithmetic  56.8 us (9%)
  starting transfers between devices  50.2 us (8%)
  Pallas kernels  32.6 us (5%)
  between operations  16.1 us (3%)
    all_to_all x4, waiting for transfers between devices, exchange_ctx(): return lax.all_to_all(pieces, 'ctx', 0, 0, tiled=True)  111 us
    ppermute x3, waiting for transfers between devices, gather_seq_near(): lax.ppermute(block, 'seq', SEQ_X)  57 us
    reduce_scatter x4, waiting for transfers between devices, reduce_ctx(): return lax.psum_scatter(partial, 'ctx', scatter_dimension=0, tiled=True)  31.1 us
    dot_general x4, matrix products, contract_cols(): lax.dot_general(left, right, (((1,), (1,)), ((), ())), preferred_element_...  27.3 us
    dot_general x4, matrix products, contract_rows(): lax.dot_general(left, right, (((0,), (0,)), ((), ())), preferred_element_...  26.6 us
    ppermute x3, waiting for transfers between devices, reduce_seq_near(): lax.ppermute(seq_part(partials, 2, True), 'seq', SEQ_Y)  22.3 us
    pallas_call x1, Pallas kernels, attend_back(): pl.pallas_call(body, name='attend_back', grid=(width // (2 * HEAD), block...  19.5 us
    ppermute x3, waiting for transfers between devices, reduce_seq_near(): lax.ppermute(seq_part(partials, 3, True), 'seq', SEQ_Y)  18.7 us
  transfers between devices with their start and end apart: 42, of which 25 were waited for; matrix products, arithmetic and copies ran while one was open for 29% of the time, Pallas kernels for 5%

profile of v2, /device:TPU:0, one launch (start us, length us, event | category | flops | bytes accessed | tf_op | source)
XLA Modules:
  0.0 627.2 jit_solution(12671957554171155168)
XLA Ops:
  7.9 3.0 collective-permute-start.4
  16.4 4.9 all-to-all-start
  29.3 2.3 bitcast_bitcast_fusion
  37.5 4.5 concatenate.100
  45.3 17.7 %all-to-all-done = bf16[8,64,768]{2,1,0:T(8,128)(2,1)S(1)} async-done(((bf16[8,64,768]{2,1,0:T(8,128)(2,1)}), bf16[8,64,768]{2,1,0:T(8,128)(2,1)S(1)}, u32[]{:S(2)}, u32[]{:S(2)}) %all-to-all-start) | async-done | bytes 786464 | tf_op jit(solution)/shard_map/all_to_all | solution.py:340
  67.5 3.6 all-to-all-start.1
  72.7 10.0 %collective-permute-done = bf16[512,768]{1,0:T(8,128)(2,1)} collective-permute-done((bf16[512,768]{1,0:T(8,128)(2,1)S(1)}, bf16[512,768]{1,0:T(8,128)(2,1)}, u32[]{:S(2)}, u32[]{:S(2)}) %collective-permute-start) | collective-permute-done | bytes 786464 | tf_op jit(solution)/shard_map/ppermute | solution.py:344
  88.7 2.1 constant_dynamic-update-slice_fusion.13
  90.8 2.1 constant_dynamic-update-slice_fusion.12
  96.2 3.2 fusion
  99.6 5.4 fusion.14
  109.8 13.0 %attend.1 = bf16[1024,256]{1,0:T(8,128)(2,1)} custom-call(s32[1]{0:T(128)} %bitcast.1.refs_0_, bf16[1024,256]{1,0:T(8,128)(2,1)} %get-tuple-element.97.refs_1_, bf16[1024,256]{1,0:T(8,128)(2,1)} %fusion.30.refs_2_, bf16[1024,256]{1,0:T(8,128)(2,1)} %get-tuple-element.96.refs_3_), custom_call_target="tpu_custom_call" | custom-call | tf_op jit(solution)/shard_map/attend/pallas_call | solution.py:552
  122.9 33.7 %all-to-all-done.1 = bf16[8,64,2112]{2,1,0:T(8,128)(2,1)S(1)} async-done(((bf16[8,64,2112]{2,1,0:T(8,128)(2,1)}), bf16[8,64,2112]{2,1,0:T(8,128)(2,1)S(1)}, u32[]{:S(2)}, u32[]{:S(2)}) %all-to-all-start.1) | async-done | bytes 2162720 | tf_op jit(solution)/shard_map/all_to_all | solution.py:340
  157.8 4.6 convolution_convert_fusion.2
  162.8 2.4 copy.241
  167.7 47.0 %collective-permute-done.8 = bf16[512,2112]{0,1:T(8,128)(2,1)} collective-permute-done((bf16[512,2112]{0,1:T(8,128)(2,1)}, bf16[512,2112]{0,1:T(8,128)(2,1)}, u32[]{:S(2)}, u32[]{:S(2)}) %collective-permute-start.8) | collective-permute-done | bytes 2162720 | tf_op jit(solution)/shard_map/ppermute | solution.py:344
  217.2 2.0 fusion.46
  219.3 2.3 slice.187
  222.6 2.3 slice.188
  225.9 4.1 broadcast_in_dim.18
  231.5 2.9 copy.243
  234.4 4.1 copy.244
  242.5 4.2 collective-permute-done.10
  254.5 5.2 fusion.11
  259.7 3.8 all-gather.7.cloned.1.call-done
  263.5 10.2 %fusion.4 = f32[1024,1408]{0,1:T(8,128)S(1)} fusion(bf16[1024,2048]{1,0:T(8,128)(2,1)} %all-gather.7.cloned.1.call-done, bf16[2048,2112]{1,0:T(8,128)(2,1)} %constant_dynamic-update-slice_fusion), kind=kOutput, calls=%fused_computation.7 | convolution fusion | flops 5905580032 | bytes 15728640 | tf_op jit(solution)/shard_map/dot_general | solution.py:671
  274.1 2.8 multiply_convert_fusion
  278.3 11.4 %fusion.6 = bf16[1024,2048]{1,0:T(8,128)(2,1)} fusion(bf16[2048,2112]{1,0:T(8,128)(2,1)} %constant_dynamic-update-slice_fusion, bf16[1024,64]{0,1:T(8,128)(2,1)S(1)} %slice.245, bf16[1024,64]{0,1:T(8,128)(2,1)S(1)} %slice.244, bf16[1024,640]{0,1:T(8,128)(2,1)S(1)} %slice.243, bf16[1024,640]{0,1:T(8,128)(2,1)S(1)} %slice.242), kind=kOutput, calls=%fused_computation.9 | convolution fusion | flops 5919211520 | bytes 12845056 | tf_op jit(solution)/shard_map/dot_general | solution.py:53
  291.0 7.0 %convolution_convert_fusion.1 = bf16[1024,2048]{1,0:T(8,128)(2,1)} fusion(bf16[1024,704]{0,1:T(8,128)(2,1)S(1)} %copy-done.28, bf16[2048,2112]{1,0:T(8,128)(2,1)} %constant_dynamic-update-slice_fusion), kind=kOutput, calls=%fused_computation.10 | convolution fusion | flops 2954887168 | bytes 8781824 | tf_op jit(solution)/shard_map/dot_general | solution.py:53
  298.0 6.8 %convolution_convert_fusion.5 = bf16[2048,704]{0,1:T(8,128)(2,1)} fusion(bf16[1024,704]{0,1:T(8,128)(2,1)S(1)} %copy-done.28, bf16[1024,2048]{1,0:T(8,128)(2,1)} %bitcast.121), kind=kOutput, calls=%fused_computation.14 | convolution fusion | flops 2954231808 | bytes 8519680 | tf_op jit(solution)/shard_map/dot_general | solution.py:47
  304.8 11.7 %convolution_convert_fusion = bf16[2048,1408]{0,1:T(8,128)(2,1)} fusion(bf16[1024,2048]{1,0:T(8,128)(2,1)S(1)} %copy-done.58, bf16[1024,64]{0,1:T(8,128)(2,1)S(1)} %slice.245, bf16[1024,64]{0,1:T(8,128)(2,1)S(1)} %slice.244, bf16[1024,640]{0,1:T(8,128)(2,1)S(1)} %copy-done.33, bf16[1024,640]{0,1:T(8,128)(2,1)S(1)} %slice.242), kind=kOutput, calls=%fused_computation.4 | convolution fusion | flops 5919997952 | bytes 12845056 | tf_op jit(solution)/shard_map/dot_general | solution.py:47
  316.5 22.0 %reduce-scatter.7.cloned.1.call-done = bf16[128,2048]{1,0:T(8,128)(2,1)} async-done(((bf16[1024,2048]{1,0:T(8,128)(2,1)}), bf16[128,2048]{1,0:T(8,128)(2,1)}) %reduce-scatter.7.cloned.1.call-update) | async-done | bytes 524304 | tf_op jit(solution)/shard_map/reduce_scatter | solution.py:336
  340.5 2.3 fusion.61
  343.0 3.2 constant_dynamic-slice_fusion.14
  353.3 22.3 %collective-permute-done.15 = bf16[256,2112]{0,1:T(8,128)(2,1)S(1)} collective-permute-done((bf16[256,2112]{0,1:T(8,128)(2,1)S(1)}, bf16[256,2112]{0,1:T(8,128)(2,1)S(1)}, u32[]{:S(2)}, u32[]{:S(2)}) %collective-permute-start.15) | collective-permute-done | bytes 1081376 | tf_op jit(solution)/shard_map/ppermute | solution.py:383
  377.2 18.7 %collective-permute-done.13 = bf16[256,2112]{0,1:T(8,128)(2,1)} collective-permute-done((bf16[256,2112]{0,1:T(8,128)(2,1)S(1)}, bf16[256,2112]{0,1:T(8,128)(2,1)}, u32[]{:S(2)}, u32[]{:S(2)}) %collective-permute-start.13) | collective-permute-done | bytes 1081376 | tf_op jit(solution)/shard_map/ppermute | solution.py:381
  397.3 2.9 add_convert_fusion.3
  400.8 2.5 add_convert_fusion.1
  404.8 2.1 convolution_convert_fusion.7.refs_4_
  406.9 19.5 %attend_back.1 = (f32[1024,256]{1,0:T(8,128)}, f32[1024,256]{1,0:T(8,128)}, f32[1024,256]{1,0:T(8,128)}) custom-call(s32[1]{0:T(128)} %bitcast.1.refs_0_, bf16[1024,256]{1,0:T(8,128)(2,1)} %get-tuple-element.97.refs_1_, bf16[1024,256]{1,0:T(8,128)(2,1)} %fusion.30.refs_2_, bf16[1024,256]{1,0:T(8,128)(2,1)} %get-tuple-element.96.refs_3_, ...), custom_call_target="tpu_custom_call" | custom-call | tf_op jit(solution)/shard_map/attend_back/pallas_call | solution.py:572
  426.4 2.2 convert_element_type.310
  428.6 2.3 fusion.69
  437.7 9.0 %reduce-scatter.9.cloned.1.call-done = bf16[128,2048]{1,0:T(8,128)(2,1)} async-done(((bf16[1024,2048]{1,0:T(8,128)(2,1)}), bf16[128,2048]{1,0:T(8,128)(2,1)}) %reduce-scatter.9.cloned.1.call-update) | async-done | bytes 524304 | tf_op jit(solution)/shard_map/reduce_scatter | solution.py:336
  451.5 4.4 convolution_convert_fusion.4
  460.4 8.5 %collective-permute-done.19 = bf16[256,768]{1,0:T(8,128)(2,1)S(1)} collective-permute-done((bf16[256,768]{1,0:T(8,128)(2,1)S(1)}, bf16[256,768]{1,0:T(8,128)(2,1)S(1)}, u32[]{:S(2)}, u32[]{:S(2)}) %collective-permute-start.19) | collective-permute-done | bytes 393248 | tf_op jit(solution)/shard_map/ppermute | solution.py:380
  471.1 3.2 collective-permute-done.18
  474.3 5.7 collective-permute-done.20
  482.6 6.9 %convolution_convert_fusion.3 = bf16[1024,2048]{1,0:T(8,128)(2,1)} fusion(bf16[2048,768]{1,0:T(8,128)(2,1)} %constant_dynamic-update-slice_fusion.10, bf16[1024,256]{1,0:T(8,128)(2,1)S(1)} %copy-done.40, bf16[1024,256]{1,0:T(8,128)(2,1)S(1)} %get-tuple-element.115, bf16[1024,256]{1,0:T(8,128)(2,1)S(1)} %get-tuple-element.114), kind=kOutput, calls=%fused_computation.12 | convolution fusion | flops 3228041216 | bytes 8912896 | tf_op jit(solution)/shard_map/dot_general | solution.py:53
  493.0 4.2 all-to-all-start.2
  497.2 2.6 copy.256
  499.8 31.3 %all-to-all-done.2 = bf16[8,64,768]{2,1,0:T(8,128)(2,1)} async-done(((bf16[8,64,768]{2,1,0:T(8,128)(2,1)}), bf16[8,64,768]{2,1,0:T(8,128)(2,1)}, u32[]{:S(2)}, u32[]{:S(2)}) %all-to-all-start.2) | async-done | bytes 786464 | tf_op jit(solution)/shard_map/all_to_all | solution.py:340
  531.1 3.6 all-to-all-start.3
  534.8 3.7 convolution_convert_fusion.6
  542.8 2.8 collective-permute-done.25
  547.9 3.8 collective-permute-done.26
  554.0 3.9 collective-permute-done.29
  561.5 2.4 reshape.154
  563.9 2.8 copy.280
  566.7 2.4 reshape.155
  572.9 28.5 %all-to-all-done.3 = bf16[8,64,2112]{2,1,0:T(8,128)(2,1)S(1)} async-done(((bf16[8,64,2112]{2,1,0:T(8,128)(2,1)}), bf16[8,64,2112]{2,1,0:T(8,128)(2,1)S(1)}, u32[]{:S(2)}, u32[]{:S(2)}) %all-to-all-start.3) | async-done | bytes 2162720 | tf_op jit(solution)/shard_map/all_to_all | solution.py:340
  604.2 2.5 copy.269
  606.9 2.5 copy.270
  611.7 2.1 broadcast_multiply_fusion
  617.0 3.1 fusion.27
  (307 shorter events, 130.6 us)
Async XLA Ops:
  7.2 8.1 %copy-start.42 = (bf16[64,256]{1,0:T(8,128)(2,1)S(1)}, bf16[64,256]{1,0:T(8,128)(2,1)}, u32[]{:S(2)}) copy-start(bf16[64,256]{1,0:T(8,128)(2,1)} %param.18) | copy-start | bytes 98308
  7.2 8.1 %copy-start.44 = (bf16[64,256]{1,0:T(8,128)(2,1)S(1)}, bf16[64,256]{1,0:T(8,128)(2,1)}, u32[]{:S(2)}) copy-start(bf16[64,256]{1,0:T(8,128)(2,1)} %param.19) | copy-start | bytes 98308
  7.2 89.0 %all-gather.11.cloned.1.call-start = ((), (), s32[]{:S(2)}) async-start(), calls=%async_computation.14 | async-start | bytes 4718592 | tf_op jit(solution)/shard_map/all_gather | solution.py:332
  7.9 34.3 %collective-permute-start.4 = (bf16[64,2048]{1,0:T(8,128)(2,1)}, bf16[64,2048]{1,0:T(8,128)(2,1)}, u32[]{:S(2)}, u32[]{:S(2)}) collective-permute-start(bf16[64,2048]{1,0:T(8,128)(2,1)} %param.20), channel_id=1, source_target_pairs={{0,8},{8,0},{16,24},{24,16},{1,9},{9,1},{17,25},{25,17},{2,10},{10... | collective-permute-start | bytes 786440 | tf_op jit(solution)/shard_map/ppermute | solution.py:344
  11.0 32.7 %collective-permute-start.5 = (bf16[64,2048]{1,0:T(8,128)(2,1)}, bf16[64,2048]{1,0:T(8,128)(2,1)}, u32[]{:S(2)}, u32[]{:S(2)}) collective-permute-start(bf16[64,2048]{1,0:T(8,128)(2,1)} %param.20), channel_id=1, source_target_pairs={{0,16},{16,0},{8,24},{24,8},{1,17},{17,1},{9,25},{25,9},{2,18},{18... | collective-permute-start | bytes 786440 | tf_op jit(solution)/shard_map/ppermute | solution.py:344
  14.9 7.1 %copy-start.59 = (bf16[64]{0:T(256)(128)(2,1)S(1)}, bf16[64]{0:T(256)(128)(2,1)}, u32[]{:S(2)}) copy-start(bf16[64]{0:T(256)(128)(2,1)} %param.21) | copy-start | bytes 388
  15.0 7.1 %copy-start.48 = (s32[1,1024]{1,0:T(1,128)S(1)}, s32[1,1024]{1,0:T(1,128)}, u32[]{:S(2)}) copy-start(s32[1,1024]{1,0:T(1,128)} %param.14) | copy-start | bytes 12292
  15.0 7.8 %copy-start.22 = (bf16[64,5632]{1,0:T(8,128)(2,1)S(1)}, bf16[64,5632]{1,0:T(8,128)(2,1)}, u32[]{:S(2)}) copy-start(bf16[64,5632]{1,0:T(8,128)(2,1)} %param.23) | copy-start | bytes 2162692
  16.4 46.6 %all-to-all-start = ((bf16[8,64,768]{2,1,0:T(8,128)(2,1)}), bf16[8,64,768]{2,1,0:T(8,128)(2,1)S(1)}, u32[]{:S(2)}, u32[]{:S(2)}) async-start(bf16[8,64,768]{2,1,0:T(8,128)(2,1)} %pad_maximum_fusion.10), calls=%async_computation | async-start | bytes 1572864 | tf_op jit(solution)/shard_map/all_to_all | solution.py:340
  21.3 136.5 %all-gather.13.cloned.1.call-start = ((), (), s32[]{:S(2)}) async-start(), calls=%async_computation.15 | async-start | bytes 4718592 | tf_op jit(solution)/shard_map/all_gather | solution.py:332
  37.5 4.6 copy-start.41
  43.1 28.2 %collective-permute-start.6 = (bf16[32,2048]{1,0:T(8,128)(2,1)S(1)}, bf16[32,2048]{1,0:T(8,128)(2,1)S(1)}, u32[]{:S(2)}, u32[]{:S(2)}) collective-permute-start(bf16[32,2048]{1,0:T(8,128)(2,1)S(1)} %slice.234), channel_id=1, source_target_pairs={{0,16},{16,0},{8,24},{24,8},{1,17},{17,1},{9,25},{25,9},{2,18},{18... | collective-permute-start | bytes 393224 | tf_op jit(solution)/shard_map/ppermute | solution.py:351
  44.6 27.4 %collective-permute-start.7 = (bf16[32,2048]{1,0:T(8,128)(2,1)S(1)}, bf16[32,2048]{1,0:T(8,128)(2,1)S(1)}, u32[]{:S(2)}, u32[]{:S(2)}) collective-permute-start(bf16[32,2048]{1,0:T(8,128)(2,1)S(1)} %slice.235), channel_id=1, source_target_pairs={{0,8},{8,0},{16,24},{24,16},{1,9},{9,1},{17,25},{25,17},{2,10},{10... | collective-permute-start | bytes 393224 | tf_op jit(solution)/shard_map/ppermute | solution.py:352
  63.0 19.7 %collective-permute-start = (bf16[512,768]{1,0:T(8,128)(2,1)S(1)}, bf16[512,768]{1,0:T(8,128)(2,1)}, u32[]{:S(2)}, u32[]{:S(2)}) collective-permute-start(bf16[512,768]{1,0:T(8,128)(2,1)S(1)} %bitcast.111), channel_id=1, source_target_pairs={{0,8},{8,0},{16,24},{24,16},{1,9},{9,1},{17,25},{25,17},{2,10},{10... | collective-permute-start | bytes 2359304 | tf_op jit(solution)/shard_map/ppermute | solution.py:344
  64.0 20.5 %collective-permute-start.1 = (bf16[512,768]{1,0:T(8,128)(2,1)S(1)}, bf16[512,768]{1,0:T(8,128)(2,1)}, u32[]{:S(2)}, u32[]{:S(2)}) collective-permute-start(bf16[512,768]{1,0:T(8,128)(2,1)S(1)} %bitcast.112), channel_id=1, source_target_pairs={{0,16},{16,0},{8,24},{24,8},{1,17},{17,1},{9,25},{25,9},{2,18},{18... | collective-permute-start | bytes 2359304 | tf_op jit(solution)/shard_map/ppermute | solution.py:344
  67.5 89.1 %all-to-all-start.1 = ((bf16[8,64,2112]{2,1,0:T(8,128)(2,1)}), bf16[8,64,2112]{2,1,0:T(8,128)(2,1)S(1)}, u32[]{:S(2)}, u32[]{:S(2)}) async-start(bf16[8,64,2112]{2,1,0:T(8,128)(2,1)} %concatenate.100), calls=%async_computation.1 | async-start | bytes 4456448 | tf_op jit(solution)/shard_map/all_to_all | solution.py:340
  71.1 144.8 %reduce-scatter.5.cloned.1.call-start = ((), (), s32[]{:S(2)}) async-start(), calls=%async_computation.8 | async-start | bytes 4718592 | tf_op jit(solution)/shard_map/reduce_scatter | solution.py:336
  83.7 10.4 %collective-permute-start.2 = (bf16[256,768]{1,0:T(8,128)(2,1)S(1)}, bf16[256,768]{1,0:T(8,128)(2,1)S(1)}, u32[]{:S(2)}, u32[]{:S(2)}) collective-permute-start(bf16[256,768]{1,0:T(8,128)(2,1)S(1)} %slice.221), channel_id=1, source_target_pairs={{0,16},{16,0},{8,24},{24,8},{1,17},{17,1},{9,25},{25,9},{2,18},{18... | collective-permute-start | bytes 1179656 | tf_op jit(solution)/shard_map/ppermute | solution.py:351
  85.6 9.8 %collective-permute-start.3 = (bf16[256,768]{1,0:T(8,128)(2,1)S(1)}, bf16[256,768]{1,0:T(8,128)(2,1)S(1)}, u32[]{:S(2)}, u32[]{:S(2)}) collective-permute-start(bf16[256,768]{1,0:T(8,128)(2,1)S(1)} %slice.222), channel_id=1, source_target_pairs={{0,8},{8,0},{16,24},{24,16},{1,9},{9,1},{17,25},{25,17},{2,10},{10... | collective-permute-start | bytes 1179656 | tf_op jit(solution)/shard_map/ppermute | solution.py:352
  99.6 5.4 copy-start.49
  162.5 53.4 %copy-start = (bf16[1,128,2048]{2,1,0:T(8,128)(2,1)S(1)}, bf16[1,128,2048]{2,1,0:T(8,128)(2,1)}, u32[]{:S(2)}) copy-start(bf16[1,128,2048]{2,1,0:T(8,128)(2,1)} %param.13) | copy-start | bytes 1572868
  162.5 101.0 %all-gather.7.cloned.1.call-start = ((), (), s32[]{:S(2)}) async-start(), calls=%async_computation.9 | async-start | bytes 4718592 | tf_op jit(solution)/shard_map/all_gather | solution.py:332
  165.2 49.5 %collective-permute-start.8 = (bf16[512,2112]{0,1:T(8,128)(2,1)}, bf16[512,2112]{0,1:T(8,128)(2,1)}, u32[]{:S(2)}, u32[]{:S(2)}) collective-permute-start(bf16[512,2112]{0,1:T(8,128)(2,1)} %copy.241), channel_id=1, source_target_pairs={{0,8},{8,0},{16,24},{24,16},{1,9},{9,1},{17,25},{25,17},{2,10},{10... | collective-permute-start | bytes 6488072 | tf_op jit(solution)/shard_map/ppermute | solution.py:344
  166.7 49.2 %collective-permute-start.9 = (bf16[512,2112]{0,1:T(8,128)(2,1)}, bf16[512,2112]{0,1:T(8,128)(2,1)}, u32[]{:S(2)}, u32[]{:S(2)}) collective-permute-start(bf16[512,2112]{0,1:T(8,128)(2,1)} %copy.241), channel_id=1, source_target_pairs={{0,16},{16,0},{8,24},{24,8},{1,17},{17,1},{9,25},{25,9},{2,18},{18... | collective-permute-start | bytes 6488072 | tf_op jit(solution)/shard_map/ppermute | solution.py:344
  219.2 119.3 %reduce-scatter.7.cloned.1.call-start = ((), (), s32[]{:S(2)}) async-start(), calls=%async_computation.10 | async-start | bytes 4718592 | tf_op jit(solution)/shard_map/reduce_scatter | solution.py:336
  221.6 25.2 %collective-permute-start.10 = (bf16[256,2112]{0,1:T(8,128)(2,1)}, bf16[256,2112]{0,1:T(8,128)(2,1)}, u32[]{:S(2)}, u32[]{:S(2)}) collective-permute-start(bf16[256,2112]{0,1:T(8,128)(2,1)} %slice.187), channel_id=1, source_target_pairs={{0,16},{16,0},{8,24},{24,8},{1,17},{17,1},{9,25},{25,9},{2,18},{18... | collective-permute-start | bytes 3244040 | tf_op jit(solution)/shard_map/ppermute | solution.py:351
  224.9 24.8 %collective-permute-start.11 = (bf16[256,2112]{0,1:T(8,128)(2,1)}, bf16[256,2112]{0,1:T(8,128)(2,1)}, u32[]{:S(2)}, u32[]{:S(2)}) collective-permute-start(bf16[256,2112]{0,1:T(8,128)(2,1)} %slice.188), channel_id=1, source_target_pairs={{0,8},{8,0},{16,24},{24,16},{1,9},{9,1},{17,25},{25,17},{2,10},{10... | collective-permute-start | bytes 3244040 | tf_op jit(solution)/shard_map/ppermute | solution.py:352
  289.7 107.5 %all-gather.9.cloned.1.call-start = ((), (), s32[]{:S(2)}) async-start(), calls=%async_computation.11 | async-start | bytes 4718592 | tf_op jit(solution)/shard_map/all_gather | solution.py:332
  298.0 6.8 %copy-start.33 = (bf16[1024,640]{0,1:T(8,128)(2,1)S(1)}, bf16[1024,640]{0,1:T(8,128)(2,1)}, u32[]{:S(2)}) copy-start(bf16[1024,640]{0,1:T(8,128)(2,1)} %copy-done.32) | copy-start | bytes 3932164
  298.0 6.8 %copy-start.58 = (bf16[1024,2048]{1,0:T(8,128)(2,1)S(1)}, bf16[1024,2048]{1,0:T(8,128)(2,1)}, u32[]{:S(2)}) copy-start(bf16[1024,2048]{1,0:T(8,128)(2,1)} %all-gather.7.cloned.1.call-done) | copy-start | bytes 12582916
  304.8 33.8 %copy-start.7 = (bf16[128,2048]{1,0:T(8,128)(2,1)S(1)}, bf16[128,2048]{1,0:T(8,128)(2,1)}, u32[]{:S(2)}) copy-start(bf16[128,2048]{1,0:T(8,128)(2,1)} %reduce-scatter.5.cloned.1.call-done) | copy-start | bytes 1572868
  304.8 35.7 %copy-start.13 = (bf16[1,128,2048]{2,1,0:T(8,128)(2,1)S(1)}, bf16[1,128,2048]{2,1,0:T(8,128)(2,1)}, u32[]{:S(2)}) copy-start(bf16[1,128,2048]{2,1,0:T(8,128)(2,1)} %param.15) | copy-start | bytes 1572868
  342.8 103.9 %reduce-scatter.9.cloned.1.call-start = ((), (), s32[]{:S(2)}) async-start(), calls=%async_computation.12 | async-start | bytes 4718592 | tf_op jit(solution)/shard_map/reduce_scatter | solution.py:336
  348.8 26.8 %collective-permute-start.15 = (bf16[256,2112]{0,1:T(8,128)(2,1)S(1)}, bf16[256,2112]{0,1:T(8,128)(2,1)S(1)}, u32[]{:S(2)}, u32[]{:S(2)}) collective-permute-start(bf16[256,2112]{0,1:T(8,128)(2,1)S(1)} %pad_maximum_fusion.9), channel_id=1, source_target_pairs={{0,16},{16,0},{8,24},{24,8},{1,17},{17,1},{9,25},{25,9},{2,18},{18... | collective-permute-start | bytes 3244040 | tf_op jit(solution)/shard_map/ppermute | solution.py:383
  350.4 26.8 %collective-permute-start.14 = (bf16[256,2112]{0,1:T(8,128)(2,1)S(1)}, bf16[256,2112]{0,1:T(8,128)(2,1)S(1)}, u32[]{:S(2)}, u32[]{:S(2)}) collective-permute-start(bf16[256,2112]{0,1:T(8,128)(2,1)S(1)} %pad_maximum_fusion.8), channel_id=1, source_target_pairs={{0,8},{8,0},{16,24},{24,16},{1,9},{9,1},{17,25},{25,17},{2,10},{10... | collective-permute-start | bytes 3244040 | tf_op jit(solution)/shard_map/ppermute | solution.py:382
  352.0 43.8 %collective-permute-start.13 = (bf16[256,2112]{0,1:T(8,128)(2,1)S(1)}, bf16[256,2112]{0,1:T(8,128)(2,1)}, u32[]{:S(2)}, u32[]{:S(2)}) collective-permute-start(bf16[256,2112]{0,1:T(8,128)(2,1)S(1)} %pad_maximum_fusion.7), channel_id=1, source_target_pairs={{0,16},{16,0},{8,24},{24,8},{1,17},{17,1},{9,25},{25,9},{2,18},{18... | collective-permute-start | bytes 3244040 | tf_op jit(solution)/shard_map/ppermute | solution.py:381
  352.7 44.5 %collective-permute-start.12 = (bf16[256,2112]{0,1:T(8,128)(2,1)S(1)}, bf16[256,2112]{0,1:T(8,128)(2,1)}, u32[]{:S(2)}, u32[]{:S(2)}) collective-permute-start(bf16[256,2112]{0,1:T(8,128)(2,1)S(1)} %pad_maximum_fusion.6), channel_id=1, source_target_pairs={{0,8},{8,0},{16,24},{24,16},{1,9},{9,1},{17,25},{25,17},{2,10},{10... | collective-permute-start | bytes 3244040 | tf_op jit(solution)/shard_map/ppermute | solution.py:380
  375.6 20.3 %copy-start.34 = (bf16[256,2112]{0,1:T(8,128)(2,1)}, bf16[256,2112]{0,1:T(8,128)(2,1)S(1)}, u32[]{:S(2)}) copy-start(bf16[256,2112]{0,1:T(8,128)(2,1)S(1)} %collective-permute-done.15) | copy-start | bytes 3244036
  377.2 18.7 %copy-start.36 = (bf16[256,2112]{0,1:T(8,128)(2,1)}, bf16[256,2112]{0,1:T(8,128)(2,1)S(1)}, u32[]{:S(2)}) copy-start(bf16[256,2112]{0,1:T(8,128)(2,1)S(1)} %collective-permute-done.14) | copy-start | bytes 3244036
  397.2 218.4 %reduce-scatter.11.cloned.1.call-start = ((), (), s32[]{:S(2)}) async-start(), calls=%async_computation.13 | async-start | bytes 4718592 | tf_op jit(solution)/shard_map/reduce_scatter | solution.py:336
  397.3 7.5 %copy-start.20 = (bf16[256,2048]{1,0:T(8,128)(2,1)S(1)}, bf16[256,2048]{1,0:T(8,128)(2,1)}, u32[]{:S(2)}) copy-start(bf16[256,2048]{1,0:T(8,128)(2,1)} %constant_dynamic-update-slice_fusion.5) | copy-start | bytes 3145732
  397.3 7.5 %copy-start.57 = (bf16[1024,2048]{1,0:T(8,128)(2,1)S(1)}, bf16[1024,2048]{1,0:T(8,128)(2,1)}, u32[]{:S(2)}) copy-start(bf16[1024,2048]{1,0:T(8,128)(2,1)} %all-gather.9.cloned.1.call-done) | copy-start | bytes 12582916
  400.2 32.4 %collective-permute-start.16 = (bf16[256,2112]{0,1:T(8,128)(2,1)}, bf16[256,2112]{0,1:T(8,128)(2,1)}, u32[]{:S(2)}, u32[]{:S(2)}) collective-permute-start(bf16[256,2112]{0,1:T(8,128)(2,1)} %add_convert_fusion.3), channel_id=1, source_target_pairs={{0,16},{16,0},{8,24},{24,8},{1,17},{17,1},{9,25},{25,9},{2,18},{18... | collective-permute-start | bytes 3244040 | tf_op jit(solution)/shard_map/ppermute | solution.py:397
  403.3 31.1 %collective-permute-start.17 = (bf16[256,2112]{0,1:T(8,128)(2,1)}, bf16[256,2112]{0,1:T(8,128)(2,1)}, u32[]{:S(2)}, u32[]{:S(2)}) collective-permute-start(bf16[256,2112]{0,1:T(8,128)(2,1)} %add_convert_fusion.1), channel_id=1, source_target_pairs={{0,8},{8,0},{16,24},{24,16},{1,9},{9,1},{17,25},{25,17},{2,10},{10... | collective-permute-start | bytes 3244040 | tf_op jit(solution)/shard_map/ppermute | solution.py:398
  436.1 10.6 %copy-start.5 = (f32[1024,256]{1,0:T(8,128)S(1)}, f32[1024,256]{1,0:T(8,128)}, u32[]{:S(2)}) copy-start(f32[1024,256]{1,0:T(8,128)} %get-tuple-element.61) | copy-start | bytes 3145732
  455.9 25.2 %copy-start.21 = (bf16[2048,768]{1,0:T(8,128)(2,1)}, bf16[2048,768]{1,0:T(8,128)(2,1)S(1)}, u32[]{:S(2)}) copy-start(bf16[2048,768]{1,0:T(8,128)(2,1)S(1)} %convolution_convert_fusion.4) | copy-start | bytes 9437188
  456.9 12.0 %collective-permute-start.19 = (bf16[256,768]{1,0:T(8,128)(2,1)S(1)}, bf16[256,768]{1,0:T(8,128)(2,1)S(1)}, u32[]{:S(2)}, u32[]{:S(2)}) collective-permute-start(bf16[256,768]{1,0:T(8,128)(2,1)S(1)} %get-tuple-element.95), channel_id=1, source_target_pairs={{0,8},{8,0},{16,24},{24,16},{1,9},{9,1},{17,25},{25,17},{2,10},{10... | collective-permute-start | bytes 1179656 | tf_op jit(solution)/shard_map/ppermute | solution.py:380
  458.4 16.0 %collective-permute-start.18 = (bf16[256,768]{1,0:T(8,128)(2,1)S(1)}, bf16[256,768]{1,0:T(8,128)(2,1)S(1)}, u32[]{:S(2)}, u32[]{:S(2)}) collective-permute-start(bf16[256,768]{1,0:T(8,128)(2,1)S(1)} %get-tuple-element.92), channel_id=1, source_target_pairs={{0,8},{8,0},{16,24},{24,16},{1,9},{9,1},{17,25},{25,17},{2,10},{10... | collective-permute-start | bytes 1179656 | tf_op jit(solution)/shard_map/ppermute | solution.py:382
  458.9 15.4 %collective-permute-start.22 = (bf16[256,768]{1,0:T(8,128)(2,1)S(1)}, bf16[256,768]{1,0:T(8,128)(2,1)S(1)}, u32[]{:S(2)}, u32[]{:S(2)}) collective-permute-start(bf16[256,768]{1,0:T(8,128)(2,1)S(1)} %get-tuple-element.93), channel_id=1, source_target_pairs={{0,16},{16,0},{8,24},{24,8},{1,17},{17,1},{9,25},{25,9},{2,18},{18... | collective-permute-start | bytes 1179656 | tf_op jit(solution)/shard_map/ppermute | solution.py:381
  469.0 11.0 %collective-permute-start.20 = (bf16[256,768]{1,0:T(8,128)(2,1)S(1)}, bf16[256,768]{1,0:T(8,128)(2,1)S(1)}, u32[]{:S(2)}, u32[]{:S(2)}) collective-permute-start(bf16[256,768]{1,0:T(8,128)(2,1)S(1)} %add_convert_fusion.8), channel_id=1, source_target_pairs={{0,16},{16,0},{8,24},{24,8},{1,17},{17,1},{9,25},{25,9},{2,18},{18... | collective-permute-start | bytes 1179656 | tf_op jit(solution)/shard_map/ppermute | solution.py:397
  470.5 18.9 %collective-permute-start.21 = (bf16[256,768]{1,0:T(8,128)(2,1)}, bf16[256,768]{1,0:T(8,128)(2,1)}, u32[]{:S(2)}, u32[]{:S(2)}) collective-permute-start(bf16[256,768]{1,0:T(8,128)(2,1)} %get-tuple-element.94), channel_id=1, source_target_pairs={{0,16},{16,0},{8,24},{24,8},{1,17},{17,1},{9,25},{25,9},{2,18},{18... | collective-permute-start | bytes 1179656 | tf_op jit(solution)/shard_map/ppermute | solution.py:383
  481.1 8.4 %collective-permute-start.23 = (bf16[256,768]{1,0:T(8,128)(2,1)}, bf16[256,768]{1,0:T(8,128)(2,1)}, u32[]{:S(2)}, u32[]{:S(2)}) collective-permute-start(bf16[256,768]{1,0:T(8,128)(2,1)} %get-tuple-element.91), channel_id=1, source_target_pairs={{0,8},{8,0},{16,24},{24,16},{1,9},{9,1},{17,25},{25,17},{2,10},{10... | collective-permute-start | bytes 1179656 | tf_op jit(solution)/shard_map/ppermute | solution.py:398
  489.5 7.7 %copy-start.9 = (bf16[512,2112]{0,1:T(8,128)(2,1)S(1)}, bf16[512,2112]{0,1:T(8,128)(2,1)}, u32[]{:S(2)}) copy-start(bf16[512,2112]{0,1:T(8,128)(2,1)} %pad_maximum_fusion.3) | copy-start | bytes 6488068
  493.0 38.2 %all-to-all-start.2 = ((bf16[8,64,768]{2,1,0:T(8,128)(2,1)}), bf16[8,64,768]{2,1,0:T(8,128)(2,1)}, u32[]{:S(2)}, u32[]{:S(2)}) async-start(bf16[8,64,768]{2,1,0:T(8,128)(2,1)} %bitcast.114), calls=%async_computation.6 | async-start | bytes 1572864 | tf_op jit(solution)/shard_map/all_to_all | solution.py:340
  531.1 70.4 %all-to-all-start.3 = ((bf16[8,64,2112]{2,1,0:T(8,128)(2,1)}), bf16[8,64,2112]{2,1,0:T(8,128)(2,1)S(1)}, u32[]{:S(2)}, u32[]{:S(2)}) async-start(bf16[8,64,2112]{2,1,0:T(8,128)(2,1)} %bitcast.22), calls=%async_computation.7 | async-start | bytes 4456448 | tf_op jit(solution)/shard_map/all_to_all | solution.py:340
  534.7 19.2 %copy-start.55 = (f32[128]{0:T(128)S(1)}, f32[128]{0:T(128)}, u32[]{:S(2)}) copy-start(f32[128]{0:T(128)} %get-tuple-element.65) | copy-start | bytes 1540
  538.4 7.2 %copy-start.38 = (bf16[256,2048]{1,0:T(8,128)(2,1)}, bf16[256,2048]{1,0:T(8,128)(2,1)S(1)}, u32[]{:S(2)}) copy-start(bf16[256,2048]{1,0:T(8,128)(2,1)S(1)} %convolution_convert_fusion.6) | copy-start | bytes 3145732
  539.3 6.4 %collective-permute-start.25 = (bf16[32,2048]{1,0:T(8,128)(2,1)S(1)}, bf16[32,2048]{1,0:T(8,128)(2,1)S(1)}, u32[]{:S(2)}, u32[]{:S(2)}) collective-permute-start(bf16[32,2048]{1,0:T(8,128)(2,1)S(1)} %get-tuple-element.125), channel_id=1, source_target_pairs={{0,8},{8,0},{16,24},{24,16},{1,9},{9,1},{17,25},{25,17},{2,10},{10... | collective-permute-start | bytes 393224 | tf_op jit(solution)/shard_map/ppermute | solution.py:380
  540.3 7.5 %collective-permute-start.24 = (bf16[32,2048]{1,0:T(8,128)(2,1)}, bf16[32,2048]{1,0:T(8,128)(2,1)S(1)}, u32[]{:S(2)}, u32[]{:S(2)}) collective-permute-start(bf16[32,2048]{1,0:T(8,128)(2,1)} %get-tuple-element.122), channel_id=1, source_target_pairs={{0,8},{8,0},{16,24},{24,16},{1,9},{9,1},{17,25},{25,17},{2,10},{10... | collective-permute-start | bytes 393224 | tf_op jit(solution)/shard_map/ppermute | solution.py:382
  541.3 6.5 %collective-permute-start.28 = (bf16[32,2048]{1,0:T(8,128)(2,1)}, bf16[32,2048]{1,0:T(8,128)(2,1)}, u32[]{:S(2)}, u32[]{:S(2)}) collective-permute-start(bf16[32,2048]{1,0:T(8,128)(2,1)} %get-tuple-element.123), channel_id=1, source_target_pairs={{0,16},{16,0},{8,24},{24,8},{1,17},{17,1},{9,25},{25,9},{2,18},{18... | collective-permute-start | bytes 393224 | tf_op jit(solution)/shard_map/ppermute | solution.py:381
  545.7 6.0 collective-permute-start.26
  547.3 6.7 %collective-permute-start.27 = (bf16[32,2048]{1,0:T(8,128)(2,1)}, bf16[32,2048]{1,0:T(8,128)(2,1)S(1)}, u32[]{:S(2)}, u32[]{:S(2)}) collective-permute-start(bf16[32,2048]{1,0:T(8,128)(2,1)} %get-tuple-element.124), channel_id=1, source_target_pairs={{0,16},{16,0},{8,24},{24,8},{1,17},{17,1},{9,25},{25,9},{2,18},{18... | collective-permute-start | bytes 393224 | tf_op jit(solution)/shard_map/ppermute | solution.py:383
  552.9 5.0 collective-permute-start.29
  566.7 4.7 copy-start.39
  (39 other events, 91.0 us)
Sparse Core Ops, SparseCore 0:
  9.6 66.4 all-gather.10
  77.7 80.0 all-gather.12
  162.6 47.5 reduce-scatter.4
  219.3 44.0 all-gather.6
  289.8 48.7 reduce-scatter.6
  342.9 45.3 all-gather.8
  397.3 49.3 reduce-scatter.8
  489.6 75.7 reduce-scatter.10

commit v3 on v2

--- a/solution.py
+++ b/solution.py
@@ -375,13 +375,23 @@
     )
 
 
+def seq_parts(partials):
+    return (
+        seq_part(partials, 3, False),
+        seq_part(partials, 3, True),
+        seq_part(partials, 1, False),
+        seq_part(partials, 2, True),
+    )
+
+
+def send_parts(parts):
+    return tuple(
+        lax.ppermute(part, "seq", axis) for part, axis in zip(parts, (SEQ_X, SEQ_Y) * 2)
+    )
+
+
 def reduce_seq_near(partials):
-    return (
-        lax.ppermute(seq_part(partials, 3, False), "seq", SEQ_X),
-        lax.ppermute(seq_part(partials, 3, True), "seq", SEQ_Y),
-        lax.ppermute(seq_part(partials, 1, False), "seq", SEQ_X),
-        lax.ppermute(seq_part(partials, 2, True), "seq", SEQ_Y),
-    )
+    return send_parts(seq_parts(partials))
 
 
 def add_wide(*terms):
@@ -391,9 +401,15 @@
     return total
 
 
-def reduce_seq_far(partials, top_far, low_far, top_near, low_near):
-    top_send = add_wide(seq_part(partials, 2, False), top_far).astype(jnp.bfloat16)
-    low_send = add_wide(seq_part(partials, 1, True), low_far).astype(jnp.bfloat16)
+def far_sums(partials, top_far, low_far):
+    return (
+        add_wide(seq_part(partials, 2, False), top_far).astype(jnp.bfloat16),
+        add_wide(seq_part(partials, 1, True), low_far).astype(jnp.bfloat16),
+    )
+
+
+def reduce_seq_far(partials, sums, top_near, low_near):
+    top_send, low_send = sums
     top_last = lax.ppermute(top_send, "seq", SEQ_Y)
     low_last = lax.ppermute(low_send, "seq", SEQ_X)
     return jnp.concatenate(
@@ -406,11 +422,16 @@
 
 
 def reduce_seq(partials):
-    return reduce_seq_far(partials, *reduce_seq_near(partials))
+    top_far, low_far, *nears = reduce_seq_near(partials)
+    return reduce_seq_far(partials, far_sums(partials, top_far, low_far), *nears)
 
 
 def tie(*values):
     return lax.optimization_barrier(values)
+
+
+def swap_cores(block):
+    return lax.ppermute(block, "ctx", [(device, device ^ 1) for device in range(8)])
 
 
 def ff_split(width):
@@ -540,6 +561,14 @@
     return edge, rows, whole
 
 
+def attend_cost(length, width, products):
+    return pl.CostEstimate(
+        flops=8 * products * length * length * width,
+        transcendentals=length * length * width // HEAD,
+        bytes_accessed=(2 * products + 4) * length * width,
+    )
+
+
 def attend(edge, queries, keys, values):
     length, width = queries.shape
     block = 256
@@ -556,6 +585,7 @@
         in_specs=[scalar, rows, whole, whole],
         out_specs=rows,
         out_shape=jax.ShapeDtypeStruct((length, width), jnp.bfloat16),
+        cost_estimate=attend_cost(length, width, 2),
     )(edge, queries, keys, values)
 
 
@@ -576,6 +606,7 @@
         in_specs=[scalar, rows, whole, whole, rows],
         out_specs=(rows, whole, whole),
         out_shape=(shape, shape, shape),
+        cost_estimate=attend_cost(length, width, 5),
     )(edge, queries, keys, values, back)
 
 
@@ -617,12 +648,11 @@
         return (weight.astype(f32) * gain).astype(bf16)
 
     inputs_all = gather_ctx(block_input[0])
-    back_all = gather_ctx(out_back)
-    key_value = jnp.concatenate([fold(key_weight, gain_one), fold(value_weight, gain_one)], axis=1)
+    key_value = jnp.stack([fold(key_weight, gain_one), fold(value_weight, gain_one)])
     attn_pieces = jnp.concatenate(
         [
             head_slices(fold(query_weight, gain_one)),
-            jnp.broadcast_to(key_value[None], (8,) + key_value.shape),
+            jnp.tile(key_value, (4, 1, 1)),
         ],
         axis=2,
     )
@@ -633,9 +663,20 @@
     mlp_pieces = jnp.concatenate(
         [gate_main, up_main, gate_tail, up_tail, *ff_slices(down_weight)], axis=2
     )
-    attn_own = exchange_ctx(attn_pieces).reshape(8 * rows, 3 * head_width)
+    attn_own = exchange_ctx(attn_pieces).reshape(8 * rows, 2 * head_width)
     attn_own, mlp_pieces = tie(attn_own, mlp_pieces)
     attn_cols = gather_seq(attn_own)
+    core = lax.axis_index("ctx") % 2
+    own_cols = attn_cols[:, head_width:]
+    other_cols = swap_cores(own_cols)
+    attn_cols = jnp.concatenate(
+        [
+            attn_cols[:, :head_width],
+            jnp.where(core == 0, own_cols, other_cols),
+            jnp.where(core == 0, other_cols, own_cols),
+        ],
+        axis=1,
+    )
     out_rows = gather_seq(out_weight)
     mlp_own = exchange_ctx(mlp_pieces).reshape(8 * rows, -1)
 
@@ -650,24 +691,26 @@
     wide = inputs_all.astype(f32)
     shaped_all = (wide * rms_scale(wide)).astype(bf16)
     raw = jnp.dot(shaped_all, attn_cols, preferred_element_type=f32)
+    raw, mlp_own = tie(raw, mlp_own)
+    mlp_near = gather_seq_near(mlp_own)
     queries = turn(raw[:, :head_width], cosine, sine_table).astype(bf16)
     keys = turn(raw[:, head_width : 2 * head_width], cosine, sine_table).astype(bf16)
     values = raw[:, 2 * head_width :].astype(bf16)
     queries = queries * jnp.asarray(score_scale, bf16)
     attn_low = attend(edge, queries, keys, values)
-    attn_low, out_rows, mlp_own, back_all = tie(attn_low, out_rows, mlp_own, back_all)
+    attn_low, out_rows, back_late = tie(attn_low, out_rows, out_back)
     mixed = jnp.dot(attn_low, out_rows, preferred_element_type=f32).astype(bf16)
     mixed_own = reduce_ctx(mixed)
-    mlp_near = gather_seq_near(mlp_own)
     mixed_own, *mlp_near = tie(mixed_own, *mlp_near)
     residual = inputs + mixed_own.astype(f32)
     scale_two = rms_scale(residual)
     shaped_two = residual * scale_two
-    normed_all = gather_ctx(shaped_two.astype(bf16))
+    shaped_low = shaped_two.astype(bf16)
+    normed_all = gather_ctx(shaped_low)
+    shaped_two, back_late = tie(shaped_two, back_late)
     mlp_cols = gather_seq_far(mlp_own, *mlp_near)
+    back_all = gather_ctx(back_late)
     gate_up, down_cols = mlp_cols[:, :both], mlp_cols[:, both:]
-    hidden_back = jnp.dot(back_all, down_cols, preferred_element_type=f32)
-    normed_all, hidden_back = tie(normed_all, hidden_back)
     proj = jnp.dot(normed_all, gate_up, preferred_element_type=f32)
 
     def halves(left_tail, right_tail, left, right):
@@ -682,6 +725,10 @@
     sigmoid_gate = jax.nn.sigmoid(gate_proj)
     silu_gate = gate_proj * sigmoid_gate
     hidden = (silu_gate * up_proj).astype(bf16)
+    mixed_out = contract_cols(hidden, down_cols).astype(bf16)
+    mixed_out, back_all = tie(mixed_out, back_all)
+    out_own = reduce_ctx(mixed_out)
+    hidden_back = jnp.dot(back_all, down_cols, preferred_element_type=f32)
     gate_back = (
         hidden_back * up_proj * sigmoid_gate * (1.0 + gate_proj * (1.0 - sigmoid_gate))
     ).astype(bf16)
@@ -691,26 +738,29 @@
         axis=1,
     )
     weighted = reduce_ctx(contract_cols(gate_up_back, gate_up).astype(bf16))
+    gate_up_back, hidden, out_own = tie(gate_up_back, hidden, out_own)
     gate_up_grad = contract_rows(normed_all, gate_up_back).astype(bf16)
     down_grad = contract_rows(back_all, hidden).astype(bf16)
-    mixed_out = contract_cols(hidden, down_cols).astype(bf16)
-    weighted, gate_up_grad, down_grad, mixed_out = tie(weighted, gate_up_grad, down_grad, mixed_out)
     mlp_grads = [gate_up_grad, down_grad]
+    mlp_parts = seq_parts(mlp_grads)
+    mlp_first = send_parts(mlp_parts[:2])
+    weighted, *mlp_first = tie(weighted, *mlp_first)
     weighted = weighted.astype(f32)
     residual_back = out_back.astype(f32) + scale_two * (
         weighted - shaped_two * jnp.mean(weighted * shaped_two, axis=-1, keepdims=True)
     )
-    low_all = gather_ctx(residual_back.astype(bf16))
-    mlp_grads_near = reduce_seq_near(mlp_grads)
-    low_all, mixed_out, *mlp_grads_near = tie(low_all, mixed_out, *mlp_grads_near)
-    out_own = reduce_ctx(mixed_out)
-    mlp_grads_own = reduce_seq_far(mlp_grads, *mlp_grads_near)
+    residual_low = residual_back.astype(bf16)
+    low_all = gather_ctx(residual_low)
+    residual_back, *mlp_first = tie(residual_back, *mlp_first)
+    mlp_near = send_parts(mlp_parts[2:])
+    mlp_sums = far_sums(mlp_grads, *mlp_first)
+    mlp_grads_own = reduce_seq_far(mlp_grads, mlp_sums, *mlp_near)
+    low_all, mlp_grads_own = tie(low_all, mlp_grads_own)
+    mlp_grad = exchange_ctx(mlp_grads_own.reshape(8, rows, -1))
     attn_back = contract_cols(low_all, out_rows).astype(bf16)
     query_back, key_back, value_back = attend_back(
         edge, queries, keys, values, attn_back, score_scale
     )
-    out_grad = reduce_seq([contract_rows(attn_low, low_all).astype(bf16)]).astype(f32)
-    query_back, mlp_grads_own, out_own = tie(query_back, mlp_grads_own, out_own)
     heads_back = jnp.concatenate(
         [
             turn(query_back, cosine, -sine_table).astype(bf16),
@@ -719,23 +769,33 @@
         ],
         axis=1,
     )
-    weighted_one = reduce_ctx(contract_cols(heads_back, attn_cols).astype(bf16)).astype(f32)
+    weighted_part = contract_cols(heads_back, attn_cols).astype(bf16)
+    weighted_part, mlp_grad, heads_back, low_all = tie(weighted_part, mlp_grad, heads_back, low_all)
+    weighted_one = reduce_ctx(weighted_part).astype(f32)
+    attn_full_grad = contract_rows(shaped_all, heads_back)
+    key_part = attn_full_grad[:, head_width : 2 * head_width]
+    value_part = attn_full_grad[:, 2 * head_width :]
+    other_part = swap_cores(jnp.where(core == 0, value_part, key_part).astype(bf16))
+    own_part = jnp.where(core == 0, key_part, value_part) + other_part.astype(f32)
+    attn_grad_own = reduce_seq(
+        [jnp.concatenate([attn_full_grad[:, :head_width].astype(bf16), own_part.astype(bf16)], axis=1)]
+    )
+    out_grad = reduce_seq([contract_rows(attn_low, low_all).astype(bf16)]).astype(f32)
+    mlp_grad = mlp_grad.astype(f32)
+    attn_grad = exchange_ctx(attn_grad_own.reshape(8, rows, -1)).astype(f32)
+
     scale_one = rms_scale(inputs)
     shaped_one = inputs * scale_one
     input_grad = residual_back + scale_one * (
         weighted_one - shaped_one * jnp.mean(weighted_one * shaped_one, axis=-1, keepdims=True)
     )
     block_output = (residual + out_own.astype(f32)).astype(bf16)
-
-    mlp_grad = exchange_ctx(mlp_grads_own.reshape(8, rows, -1)).astype(f32)
-    attn_grad_own = reduce_seq([contract_rows(shaped_all, heads_back).astype(bf16)])
-    attn_grad = exchange_ctx(attn_grad_own.reshape(8, rows, -1)).astype(f32)
     gate_rows = ff_rows(mlp_grad[:, :, :main], mlp_grad[:, :, 2 * main : 2 * main + tail])
     up_rows = ff_rows(mlp_grad[:, :, main : 2 * main], mlp_grad[:, :, 2 * main + tail : both])
     down_grad = ff_rows(mlp_grad[:, :, both : both + main], mlp_grad[:, :, both + main :])
     query_rows = from_head_slices(attn_grad[:, :, :head_width])
-    pair_rows = jnp.sum(attn_grad[:, :, head_width:], axis=0)
-    key_rows, value_rows = pair_rows[:, :head_width], pair_rows[:, head_width:]
+    pair_rows = jnp.sum(attn_grad[:, :, head_width:].reshape(4, 2, rows, head_width), axis=0)
+    key_rows, value_rows = pair_rows[0], pair_rows[1]
 
     def row_sum(weight, grad):
         return jnp.sum(weight.astype(f32) * grad, axis=1)

time: 634 us -> 609 us (0.961)
  waiting for transfers between devices: 286 us -> 268 us
  local copies, waits for them, and re-layouts: 106 us -> 90.7 us
  other arithmetic: 56.8 us -> 65.9 us
    all_to_all x4, waiting for transfers between devices: 111 us -> 58.9 us  [exchange_ctx(): return lax.all_to_all(pieces, 'ctx', 0, 0, tiled=True)]
    all_gather x4, waiting for transfers between devices: 5.05 us -> 37.8 us  [gather_ctx(): return lax.all_gather(block, 'ctx', axis=0, tiled=True)]
    reduce_scatter x4, waiting for transfers between devices: 31.1 us -> 55.5 us  [reduce_ctx(): return lax.psum_scatter(partial, 'ctx', scatter_dimension=0, tiled=True)]
    ppermute x12 -> x14, waiting for transfers between devices: 58.5 us -> 42 us  [the longest x12 42 us: send_parts(): lax.ppermute(part, 'seq', axis)]
    dot_general x4, matrix products: 26.6 us -> 19.6 us  [contract_rows(): lax.dot_general(left, right, (((0,), (0,)), ((), ())), preferred_element_...]
    convert_element_type x8 -> x9, other arithmetic: 11.5 us -> 16.2 us  [the longest x3 3.69 us: far_sums(): add_wide(seq_part(partials, 2, False), top_far).astype(jnp.bfloat16)]
    optimization_barrier x4 -> x5, local copies, waits for them, and re-layouts: 12 us -> 15.2 us  [tie(): return lax.optimization_barrier(values)]
    unnamed x123 -> x107, local copies, waits for them, and re-layouts: 13.9 us -> 15.4 us
  transfers between devices with their start and end apart: 42 -> 44, of which waited for: 25 -> 26; matrix products, arithmetic and copies ran while one was open for 29% -> 33% of each run, Pallas kernels for 5% -> 3%
where the time goes in v3:
time: 609 us; the launch traced here: 599 us
  waiting for transfers between devices  268 us (44%)
  local copies, waits for them, and re-layouts  90.7 us (15%)
  matrix products  76 us (12%)
  other arithmetic  65.9 us (11%)
  starting transfers between devices  49.4 us (8%)
  Pallas kernels  32.9 us (5%)
  between operations  16.1 us (3%)
    all_to_all x4, waiting for transfers between devices, exchange_ctx(): return lax.all_to_all(pieces, 'ctx', 0, 0, tiled=True)  58.9 us
    reduce_scatter x4, waiting for transfers between devices, reduce_ctx(): return lax.psum_scatter(partial, 'ctx', scatter_dimension=0, tiled=True)  55.5 us
    ppermute x3, waiting for transfers between devices, gather_seq_near(): lax.ppermute(block, 'seq', SEQ_X)  52.5 us
    ppermute x12, waiting for transfers between devices, send_parts(): lax.ppermute(part, 'seq', axis)  42 us
    all_gather x4, waiting for transfers between devices, gather_ctx(): return lax.all_gather(block, 'ctx', axis=0, tiled=True)  37.8 us
    dot_general x4, matrix products, contract_cols(): lax.dot_general(left, right, (((1,), (1,)), ((), ())), preferred_element_...  27.5 us
    pallas_call x1, Pallas kernels, attend_back(): pl.pallas_call(body, name='attend_back', grid=(width // (2 * HEAD), block...  19.7 us
    dot_general x4, matrix products, contract_rows(): lax.dot_general(left, right, (((0,), (0,)), ((), ())), preferred_element_...  19.6 us
  transfers between devices with their start and end apart: 44, of which 26 were waited for; matrix products, arithmetic and copies ran while one was open for 33% of the time, Pallas kernels for 3%

profile of v3, /device:TPU:0, one launch (start us, length us, event | category | flops | bytes accessed | tf_op | source)
XLA Modules:
  0.0 598.8 jit_solution(12283889299568566936)
XLA Ops:
  7.9 3.0 collective-permute-start.5
  16.3 4.9 all-to-all-start
  25.1 4.1 concatenate.102
  31.1 19.3 %all-to-all-done = bf16[8,64,512]{2,1,0:T(8,128)(2,1)} async-done(((bf16[8,64,512]{2,1,0:T(8,128)(2,1)}), bf16[8,64,512]{2,1,0:T(8,128)(2,1)}, u32[]{:S(2)}, u32[]{:S(2)}) %all-to-all-start) | async-done | bytes 524320 | tf_op jit(solution)/shard_map/all_to_all | solution.py:340
  54.4 4.4 all-to-all-start.1
  59.6 6.0 collective-permute-done
  70.5 2.6 collective-permute-done.2
  80.5 1.7 collective-permute-start.7
  83.6 1.7 constant_dynamic-update-slice_fusion.8
  85.3 1.7 constant_dynamic-update-slice_fusion.7
  89.5 3.1 broadcast_select_fusion.1
  92.5 3.2 fusion
  96.0 5.3 fusion.15
  101.3 15.4 %all-to-all-done.1 = bf16[8,64,2112]{2,1,0:T(8,128)(2,1)} async-done(((bf16[8,64,2112]{2,1,0:T(8,128)(2,1)}), bf16[8,64,2112]{2,1,0:T(8,128)(2,1)}, u32[]{:S(2)}, u32[]{:S(2)}) %all-to-all-start.1) | async-done | bytes 2162720 | tf_op jit(solution)/shard_map/all_to_all | solution.py:340
  121.9 13.2 %attend.1 = bf16[1024,256]{1,0:T(8,128)(2,1)} custom-call(s32[1]{0:T(128)} %bitcast.1.refs_0_, bf16[1024,256]{1,0:T(8,128)(2,1)} %get-tuple-element.106.refs_1_, bf16[1024,256]{1,0:T(8,128)(2,1)} %fusion.37.refs_2_, bf16[1024,256]{1,0:T(8,128)(2,1)} %get-tuple-element.105.refs_3_), custom_call_target="tpu_custom_call" | custom-call | flops 4294967296 | bytes 2097152 | tf_op jit(solution)/shard_map/attend/pallas_call | solution.py:581
  135.1 4.7 convolution_convert_fusion.1
  139.9 4.1 copy.98
  146.6 46.5 %collective-permute-done.9 = bf16[512,2112]{0,1:T(8,128)(2,1)S(1)} collective-permute-done((bf16[512,2112]{0,1:T(8,128)(2,1)}, bf16[512,2112]{0,1:T(8,128)(2,1)S(1)}, u32[]{:S(2)}, u32[]{:S(2)}) %collective-permute-start.9) | collective-permute-done | bytes 2162720 | tf_op jit(solution)/shard_map/ppermute | solution.py:344
  195.8 2.4 fusion.73
  201.1 2.3 slice.206
  204.3 4.1 broadcast_in_dim.30
  208.4 3.1 constant_dynamic-update-slice_fusion.4
  211.5 3.1 copy.100
  214.7 4.1 copy.101
  222.8 2.0 collective-permute-done.11
  231.1 12.2 %all-gather.6.cloned.1.call-done = bf16[1024,2048]{1,0:T(8,128)(2,1)} async-done(((bf16[128,2048]{1,0:T(8,128)(2,1)}), bf16[1024,2048]{1,0:T(8,128)(2,1)}) %all-gather.6.cloned.1.call-update) | async-done | bytes 4194320 | tf_op jit(solution)/shard_map/all_gather | solution.py:332
  243.3 10.5 %fusion.4 = f32[1024,1408]{1,0:T(8,128)S(1)} fusion(bf16[1024,2048]{1,0:T(8,128)(2,1)} %all-gather.6.cloned.1.call-done, bf16[2048,2112]{1,0:T(8,128)(2,1)} %constant_dynamic-update-slice_fusion), kind=kOutput, calls=%fused_computation.7 | convolution fusion | flops 5905580032 | bytes 15728640 | tf_op jit(solution)/shard_map/dot_general | solution.py:714
  258.0 6.9 %convolution_convert_fusion.3 = bf16[1024,2048]{1,0:T(8,128)(2,1)} fusion(bf16[1024,704]{1,0:T(8,128)(2,1)S(1)} %multiply_convert_fusion.2, bf16[2048,2112]{1,0:T(8,128)(2,1)} %constant_dynamic-update-slice_fusion), kind=kOutput, calls=%fused_computation.28 | convolution fusion | flops 2954887168 | bytes 8781824 | tf_op jit(solution)/shard_map/dot_general | solution.py:53
  264.9 25.5 %all-gather.8.cloned.1.call-done = bf16[1024,2048]{1,0:T(8,128)(2,1)} async-done(((bf16[128,2048]{1,0:T(8,128)(2,1)}), bf16[1024,2048]{1,0:T(8,128)(2,1)}) %all-gather.8.cloned.1.call-update) | async-done | bytes 4194320 | tf_op jit(solution)/shard_map/all_gather | solution.py:332
  290.5 8.3 %multiply_convert_fusion = (bf16[1024,704]{1,0:T(8,128)(2,1)S(1)}, bf16[1024,704]{1,0:T(8,128)(2,1)S(1)}) fusion(f32[1024,64]{1,0:T(8,128)S(1)} %get-tuple-element.97, f32[1024,640]{1,0:T(8,128)S(1)} %get-tuple-element.95, f32[1024,64]{1,0:T(8,128)} %copy-done.23, f32[1024,640]{1,0:T(8,128)} %copy-done.8, ...), kind=kOutput, calls=%fused_computation.33 | convolution fusion | flops 2963603456 | bytes 16252928 | tf_op jit(solution)/shard_map/dot_general | solution.py:731
  299.2 4.3 concatenate.112
  303.5 11.0 %fusion.6 = bf16[1024,2048]{1,0:T(8,128)(2,1)} fusion(bf16[1024,1408]{1,0:T(8,128)(2,1)} %concatenate.112, bf16[2048,2112]{1,0:T(8,128)(2,1)} %constant_dynamic-update-slice_fusion), kind=kOutput, calls=%fused_computation.25 | convolution fusion | flops 5907677184 | bytes 12845056 | tf_op jit(solution)/shard_map/dot_general | solution.py:53
  314.6 26.7 %reduce-scatter.7.cloned.1.call-done = bf16[128,2048]{1,0:T(8,128)(2,1)} async-done(((bf16[1024,2048]{1,0:T(8,128)(2,1)}), bf16[128,2048]{1,0:T(8,128)(2,1)}) %reduce-scatter.7.cloned.1.call-update) | async-done | bytes 524304 | tf_op jit(solution)/shard_map/reduce_scatter | solution.py:336
  341.4 5.5 convolution_convert_fusion.4
  349.6 6.6 %convolution_convert_fusion = bf16[2048,1408]{0,1:T(8,128)(2,1)S(1)} fusion(bf16[1024,2048]{1,0:T(8,128)(2,1)S(1)} %copy-done.50, bf16[1024,1408]{1,0:T(8,128)(2,1)S(1)} %copy-done.16), kind=kOutput, calls=%fused_computation.4 | convolution fusion | flops 5908463616 | bytes 12845056 | tf_op jit(solution)/shard_map/dot_general | solution.py:47
  356.2 1.9 constant_dynamic-slice_fusion.15
  363.1 28.8 %reduce-scatter.9.cloned.1.call-done = bf16[128,2048]{1,0:T(8,128)(2,1)} async-done(((bf16[1024,2048]{1,0:T(8,128)(2,1)}), bf16[128,2048]{1,0:T(8,128)(2,1)}) %reduce-scatter.9.cloned.1.call-update) | async-done | bytes 524304 | tf_op jit(solution)/shard_map/reduce_scatter | solution.py:336
  393.1 2.8 fusion.71
  395.9 2.1 pad_maximum_fusion.11
  399.5 2.7 add_convert_fusion.1
  405.3 2.5 add_convert_fusion.3
  408.3 16.8 %collective-permute-done.17 = bf16[256,2112]{0,1:T(8,128)(2,1)} collective-permute-done((bf16[256,2112]{0,1:T(8,128)(2,1)}, bf16[256,2112]{0,1:T(8,128)(2,1)}, u32[]{:S(2)}, u32[]{:S(2)}) %collective-permute-start.17) | collective-permute-done | bytes 1081376 | tf_op jit(solution)/shard_map/ppermute | solution.py:389
  425.1 4.2 collective-permute-done.18
  429.3 2.0 add_convert_fusion
  431.3 17.8 %collective-permute-done.15 = bf16[256,2112]{0,1:T(8,128)(2,1)} collective-permute-done((bf16[256,2112]{0,1:T(8,128)(2,1)}, bf16[256,2112]{0,1:T(8,128)(2,1)}, u32[]{:S(2)}, u32[]{:S(2)}) %collective-permute-start.15) | collective-permute-done | bytes 1081376 | tf_op jit(solution)/shard_map/ppermute | solution.py:389
  449.1 1.9 add_convert_fusion.2
  451.3 2.5 copy.109
  453.8 4.0 all-to-all-start.2
  457.9 4.6 convolution_convert_fusion.6.refs_4_
  462.5 19.7 %attend_back.1 = (f32[1024,256]{1,0:T(8,128)}, f32[1024,256]{1,0:T(8,128)}, f32[1024,256]{1,0:T(8,128)}) custom-call(s32[1]{0:T(128)} %bitcast.1.refs_0_, bf16[1024,256]{1,0:T(8,128)(2,1)} %get-tuple-element.106.refs_1_, bf16[1024,256]{1,0:T(8,128)(2,1)} %fusion.37.refs_2_, bf16[1024,256]{1,0:T(8,128)(2,1)} %get-tuple-element.105.refs_3_, ...), custom_call_target="tpu_custom_call" | custom-call | flops 10737418240 | bytes 3670016 | tf_op jit(solution)/shard_map/attend_back/pallas_call | solution.py:602
  489.7 5.0 convolution_convert_fusion.2
  494.7 14.9 %all-to-all-done.2 = bf16[8,64,2112]{2,1,0:T(8,128)(2,1)S(1)} async-done(((bf16[8,64,2112]{2,1,0:T(8,128)(2,1)}), bf16[8,64,2112]{2,1,0:T(8,128)(2,1)S(1)}, u32[]{:S(2)}, u32[]{:S(2)}) %all-to-all-start.2) | async-done | bytes 2162720 | tf_op jit(solution)/shard_map/all_to_all | solution.py:340
  509.7 6.2 %fusion.13 = f32[2048,768]{0,1:T(8,128)S(1)} fusion(bf16[1024,768]{1,0:T(8,128)(2,1)} %pad_maximum_fusion.4, bf16[1,1024,2048]{2,1,0:T(8,128)(2,1)} %all-gather.12.cloned.1.call-done, f32[1024]{0:T(1024)S(1)} %copy-done.46), kind=kOutput, calls=%fused_computation.54 | convolution fusion | flops 3227516928 | bytes 12062720 | tf_op jit(solution)/shard_map/dot_general | solution.py:47
  517.3 3.6 copy-done.49
  534.6 3.1 add_convert_fusion.4
  540.9 3.6 collective-permute-done.21
  548.9 2.0 collective-permute-done.28
  552.4 1.8 add_convert_fusion.12
  556.5 3.2 collective-permute-done.22
  561.1 3.5 all-to-all-start.3
  564.6 3.7 broadcast_multiply_fusion
  570.7 9.2 %all-to-all-done.3 = bf16[8,64,512]{2,1,0:T(8,128)(2,1)S(1)} async-done(((bf16[8,64,512]{2,1,0:T(8,128)(2,1)}), bf16[8,64,512]{2,1,0:T(8,128)(2,1)S(1)}, u32[]{:S(2)}, u32[]{:S(2)}) %all-to-all-start.3) | async-done | bytes 524320 | tf_op jit(solution)/shard_map/all_to_all | solution.py:340
  585.1 2.0 broadcast_multiply_fusion.2
  589.0 2.7 fusion.28
  (302 shorter events, 120.1 us)
Async XLA Ops:
  7.2 8.1 %copy-start.38 = (bf16[64,256]{1,0:T(8,128)(2,1)S(1)}, bf16[64,256]{1,0:T(8,128)(2,1)}, u32[]{:S(2)}) copy-start(bf16[64,256]{1,0:T(8,128)(2,1)} %param.18) | copy-start | bytes 98308
  7.2 8.1 %copy-start.40 = (bf16[64,256]{1,0:T(8,128)(2,1)S(1)}, bf16[64,256]{1,0:T(8,128)(2,1)}, u32[]{:S(2)}) copy-start(bf16[64,256]{1,0:T(8,128)(2,1)} %param.19) | copy-start | bytes 98308
  7.2 85.3 %all-gather.12.cloned.1.call-start = ((), (), s32[]{:S(2)}) async-start(), calls=%async_computation.15 | async-start | bytes 4718592 | tf_op jit(solution)/shard_map/all_gather | solution.py:332
  7.9 71.7 %collective-permute-start.5 = (bf16[64,2048]{1,0:T(8,128)(2,1)}, bf16[64,2048]{1,0:T(8,128)(2,1)}, u32[]{:S(2)}, u32[]{:S(2)}) collective-permute-start(bf16[64,2048]{1,0:T(8,128)(2,1)} %param.20), channel_id=1, source_target_pairs={{0,8},{8,0},{16,24},{24,16},{1,9},{9,1},{17,25},{25,17},{2,10},{10... | collective-permute-start | bytes 786440 | tf_op jit(solution)/shard_map/ppermute | solution.py:344
  11.0 71.2 %collective-permute-start.6 = (bf16[64,2048]{1,0:T(8,128)(2,1)}, bf16[64,2048]{1,0:T(8,128)(2,1)}, u32[]{:S(2)}, u32[]{:S(2)}) collective-permute-start(bf16[64,2048]{1,0:T(8,128)(2,1)} %param.20), channel_id=1, source_target_pairs={{0,16},{16,0},{8,24},{24,8},{1,17},{17,1},{9,25},{25,9},{2,18},{18... | collective-permute-start | bytes 786440 | tf_op jit(solution)/shard_map/ppermute | solution.py:344
  14.7 6.5 %copy-start.51 = (bf16[64]{0:T(256)(128)(2,1)S(1)}, bf16[64]{0:T(256)(128)(2,1)}, u32[]{:S(2)}) copy-start(bf16[64]{0:T(256)(128)(2,1)} %param.21) | copy-start | bytes 388
  14.7 6.5 %copy-start.17 = (bf16[64,5632]{1,0:T(8,128)(2,1)S(1)}, bf16[64,5632]{1,0:T(8,128)(2,1)}, u32[]{:S(2)}) copy-start(bf16[64,5632]{1,0:T(8,128)(2,1)} %param.23) | copy-start | bytes 2162692
  14.8 6.5 %copy-start.19 = (bf16[64,5632]{1,0:T(8,128)(2,1)S(1)}, bf16[64,5632]{1,0:T(8,128)(2,1)}, u32[]{:S(2)}) copy-start(bf16[64,5632]{1,0:T(8,128)(2,1)} %param.22) | copy-start | bytes 2162692
  16.3 34.1 %all-to-all-start = ((bf16[8,64,512]{2,1,0:T(8,128)(2,1)}), bf16[8,64,512]{2,1,0:T(8,128)(2,1)}, u32[]{:S(2)}, u32[]{:S(2)}) async-start(bf16[8,64,512]{2,1,0:T(8,128)(2,1)} %pad_maximum_fusion.12), calls=%async_computation | async-start | bytes 1048576 | tf_op jit(solution)/shard_map/all_to_all | solution.py:340
  51.7 13.9 %collective-permute-start = (bf16[512,512]{0,1:T(8,128)(2,1)S(1)}, bf16[512,512]{0,1:T(8,128)(2,1)S(1)}, u32[]{:S(2)}, u32[]{:S(2)}) collective-permute-start(bf16[512,512]{0,1:T(8,128)(2,1)S(1)} %copy.91), channel_id=1, source_target_pairs={{0,8},{8,0},{16,24},{24,16},{1,9},{9,1},{17,25},{25,17},{2,10},{10... | collective-permute-start | bytes 1572872 | tf_op jit(solution)/shard_map/ppermute | solution.py:344
  53.4 13.5 %collective-permute-start.1 = (bf16[512,512]{0,1:T(8,128)(2,1)S(1)}, bf16[512,512]{0,1:T(8,128)(2,1)}, u32[]{:S(2)}, u32[]{:S(2)}) collective-permute-start(bf16[512,512]{0,1:T(8,128)(2,1)S(1)} %copy.91), channel_id=1, source_target_pairs={{0,16},{16,0},{8,24},{24,8},{1,17},{17,1},{9,25},{25,9},{2,18},{18... | collective-permute-start | bytes 1572872 | tf_op jit(solution)/shard_map/ppermute | solution.py:344
  54.4 62.4 %all-to-all-start.1 = ((bf16[8,64,2112]{2,1,0:T(8,128)(2,1)}), bf16[8,64,2112]{2,1,0:T(8,128)(2,1)}, u32[]{:S(2)}, u32[]{:S(2)}) async-start(bf16[8,64,2112]{2,1,0:T(8,128)(2,1)} %concatenate.102), calls=%async_computation.1 | async-start | bytes 4456448 | tf_op jit(solution)/shard_map/all_to_all | solution.py:340
  58.8 135.6 %reduce-scatter.5.cloned.1.call-start = ((), (), s32[]{:S(2)}) async-start(), calls=%async_computation.8 | async-start | bytes 4718592 | tf_op jit(solution)/shard_map/reduce_scatter | solution.py:336
  65.6 7.5 %collective-permute-start.2 = (bf16[256,512]{0,1:T(8,128)(2,1)S(1)}, bf16[256,512]{0,1:T(8,128)(2,1)S(1)}, u32[]{:S(2)}, u32[]{:S(2)}) collective-permute-start(bf16[256,512]{0,1:T(8,128)(2,1)S(1)} %slice.242), channel_id=1, source_target_pairs={{0,16},{16,0},{8,24},{24,8},{1,17},{17,1},{9,25},{25,9},{2,18},{18... | collective-permute-start | bytes 786440 | tf_op jit(solution)/shard_map/ppermute | solution.py:351
  67.8 6.9 %collective-permute-start.3 = (bf16[256,512]{0,1:T(8,128)(2,1)S(1)}, bf16[256,512]{0,1:T(8,128)(2,1)S(1)}, u32[]{:S(2)}, u32[]{:S(2)}) collective-permute-start(bf16[256,512]{0,1:T(8,128)(2,1)S(1)} %slice.243), channel_id=1, source_target_pairs={{0,8},{8,0},{16,24},{24,16},{1,9},{9,1},{17,25},{25,17},{2,10},{10... | collective-permute-start | bytes 786440 | tf_op jit(solution)/shard_map/ppermute | solution.py:352
  75.8 13.7 %collective-permute-start.4 = (bf16[2048,256]{0,1:T(8,128)(2,1)}, bf16[2048,256]{0,1:T(8,128)(2,1)}, u32[]{:S(2)}, u32[]{:S(2)}) collective-permute-start(bf16[2048,256]{0,1:T(8,128)(2,1)} %slice.245), channel_id=1, source_target_pairs={{0,1},{1,0},{2,3},{3,2},{4,5},{5,4},{6,7},{7,6},{8,9},{9,8},{10,11... | collective-permute-start | bytes 3145736 | tf_op jit(solution)/shard_map/ppermute | solution.py:434
  80.5 6.4 %collective-permute-start.7 = (bf16[32,2048]{1,0:T(8,128)(2,1)S(1)}, bf16[32,2048]{1,0:T(8,128)(2,1)S(1)}, u32[]{:S(2)}, u32[]{:S(2)}) collective-permute-start(bf16[32,2048]{1,0:T(8,128)(2,1)S(1)} %slice.247), channel_id=1, source_target_pairs={{0,16},{16,0},{8,24},{24,8},{1,17},{17,1},{9,25},{25,9},{2,18},{18... | collective-permute-start | bytes 393224 | tf_op jit(solution)/shard_map/ppermute | solution.py:351
  83.1 5.7 collective-permute-start.8
  139.8 54.6 %copy-start.6 = (bf16[1,128,2048]{2,1,0:T(8,128)(2,1)S(1)}, bf16[1,128,2048]{2,1,0:T(8,128)(2,1)}, u32[]{:S(2)}) copy-start(bf16[1,128,2048]{2,1,0:T(8,128)(2,1)} %param.13) | copy-start | bytes 1572868
  139.8 103.5 %all-gather.6.cloned.1.call-start = ((), (), s32[]{:S(2)}) async-start(), calls=%async_computation.9 | async-start | bytes 4718592 | tf_op jit(solution)/shard_map/all_gather | solution.py:332
  144.0 49.1 %collective-permute-start.9 = (bf16[512,2112]{0,1:T(8,128)(2,1)}, bf16[512,2112]{0,1:T(8,128)(2,1)S(1)}, u32[]{:S(2)}, u32[]{:S(2)}) collective-permute-start(bf16[512,2112]{0,1:T(8,128)(2,1)} %copy.98), channel_id=1, source_target_pairs={{0,8},{8,0},{16,24},{24,16},{1,9},{9,1},{17,25},{25,17},{2,10},{10... | collective-permute-start | bytes 6488072 | tf_op jit(solution)/shard_map/ppermute | solution.py:344
  145.5 48.9 %collective-permute-start.10 = (bf16[512,2112]{0,1:T(8,128)(2,1)}, bf16[512,2112]{0,1:T(8,128)(2,1)}, u32[]{:S(2)}, u32[]{:S(2)}) collective-permute-start(bf16[512,2112]{0,1:T(8,128)(2,1)} %copy.98), channel_id=1, source_target_pairs={{0,16},{16,0},{8,24},{24,8},{1,17},{17,1},{9,25},{25,9},{2,18},{18... | collective-permute-start | bytes 6488072 | tf_op jit(solution)/shard_map/ppermute | solution.py:344
  198.2 92.2 %all-gather.8.cloned.1.call-start = ((), (), s32[]{:S(2)}) async-start(), calls=%async_computation.10 | async-start | bytes 4718592 | tf_op jit(solution)/shard_map/all_gather | solution.py:332
  198.8 142.6 %reduce-scatter.7.cloned.1.call-start = ((), (), s32[]{:S(2)}) async-start(), calls=%async_computation.11 | async-start | bytes 4718592 | tf_op jit(solution)/shard_map/reduce_scatter | solution.py:336
  199.9 24.9 %collective-permute-start.11 = (bf16[256,2112]{0,1:T(8,128)(2,1)}, bf16[256,2112]{0,1:T(8,128)(2,1)}, u32[]{:S(2)}, u32[]{:S(2)}) collective-permute-start(bf16[256,2112]{0,1:T(8,128)(2,1)} %slice.205), channel_id=1, source_target_pairs={{0,16},{16,0},{8,24},{24,8},{1,17},{17,1},{9,25},{25,9},{2,18},{18... | collective-permute-start | bytes 3244040 | tf_op jit(solution)/shard_map/ppermute | solution.py:351
  203.4 24.7 %collective-permute-start.12 = (bf16[256,2112]{0,1:T(8,128)(2,1)}, bf16[256,2112]{0,1:T(8,128)(2,1)S(1)}, u32[]{:S(2)}, u32[]{:S(2)}) collective-permute-start(bf16[256,2112]{0,1:T(8,128)(2,1)} %slice.206), channel_id=1, source_target_pairs={{0,8},{8,0},{16,24},{24,16},{1,9},{9,1},{17,25},{25,17},{2,10},{10... | collective-permute-start | bytes 3244040 | tf_op jit(solution)/shard_map/ppermute | solution.py:352
  290.5 101.4 %reduce-scatter.9.cloned.1.call-start = ((), (), s32[]{:S(2)}) async-start(), calls=%async_computation.12 | async-start | bytes 4718592 | tf_op jit(solution)/shard_map/reduce_scatter | solution.py:336
  314.5 26.8 %copy-start.25 = (bf16[1024,704]{1,0:T(8,128)(2,1)S(1)}, bf16[1024,704]{1,0:T(8,128)(2,1)}, u32[]{:S(2)}) copy-start(bf16[1024,704]{1,0:T(8,128)(2,1)} %copy-done.24) | copy-start | bytes 4325380
  314.5 136.7 %all-gather.10.cloned.1.call-start = ((), (), s32[]{:S(2)}) async-start(), calls=%async_computation.13 | async-start | bytes 4718592 | tf_op jit(solution)/shard_map/all_gather | solution.py:332
  341.4 7.1 %copy-start.50 = (bf16[1024,2048]{1,0:T(8,128)(2,1)S(1)}, bf16[1024,2048]{1,0:T(8,128)(2,1)}, u32[]{:S(2)}) copy-start(bf16[1024,2048]{1,0:T(8,128)(2,1)} %all-gather.6.cloned.1.call-done) | copy-start | bytes 12582916
  358.1 33.9 %copy-start.9 = (f32[128,2048]{1,0:T(8,128)S(1)}, f32[128,2048]{1,0:T(8,128)}, u32[]{:S(2)}) copy-start(f32[128,2048]{1,0:T(8,128)} %get-tuple-element.60) | copy-start | bytes 3145732
  359.1 32.8 %collective-permute-start.13 = (bf16[256,2112]{0,1:T(8,128)(2,1)}, bf16[256,2112]{0,1:T(8,128)(2,1)}, u32[]{:S(2)}, u32[]{:S(2)}) collective-permute-start(bf16[256,2112]{0,1:T(8,128)(2,1)} %pad_maximum_fusion.8), channel_id=1, source_target_pairs={{0,8},{8,0},{16,24},{24,16},{1,9},{9,1},{17,25},{25,17},{2,10},{10... | collective-permute-start | bytes 3244040 | tf_op jit(solution)/shard_map/ppermute | solution.py:389
  361.6 30.3 %collective-permute-start.14 = (bf16[256,2112]{0,1:T(8,128)(2,1)}, bf16[256,2112]{0,1:T(8,128)(2,1)}, u32[]{:S(2)}, u32[]{:S(2)}) collective-permute-start(bf16[256,2112]{0,1:T(8,128)(2,1)} %pad_maximum_fusion.9), channel_id=1, source_target_pairs={{0,16},{16,0},{8,24},{24,8},{1,17},{17,1},{9,25},{25,9},{2,18},{18... | collective-permute-start | bytes 3244040 | tf_op jit(solution)/shard_map/ppermute | solution.py:389
  398.0 27.1 %collective-permute-start.17 = (bf16[256,2112]{0,1:T(8,128)(2,1)}, bf16[256,2112]{0,1:T(8,128)(2,1)}, u32[]{:S(2)}, u32[]{:S(2)}) collective-permute-start(bf16[256,2112]{0,1:T(8,128)(2,1)} %pad_maximum_fusion.11), channel_id=1, source_target_pairs={{0,16},{16,0},{8,24},{24,8},{1,17},{17,1},{9,25},{25,9},{2,18},{18... | collective-permute-start | bytes 3244040 | tf_op jit(solution)/shard_map/ppermute | solution.py:389
  399.5 5.8 copy-start.21
  399.5 5.8 copy-start.26
  402.2 27.0 %collective-permute-start.18 = (bf16[256,2112]{0,1:T(8,128)(2,1)}, bf16[256,2112]{0,1:T(8,128)(2,1)}, u32[]{:S(2)}, u32[]{:S(2)}) collective-permute-start(bf16[256,2112]{0,1:T(8,128)(2,1)} %add_convert_fusion.1), channel_id=1, source_target_pairs={{0,8},{8,0},{16,24},{24,16},{1,9},{9,1},{17,25},{25,17},{2,10},{10... | collective-permute-start | bytes 3244040 | tf_op jit(solution)/shard_map/ppermute | solution.py:414
  404.7 24.5 %copy-start.20 = (bf16[256,1408]{0,1:T(8,128)(2,1)S(1)}, bf16[256,1408]{0,1:T(8,128)(2,1)}, u32[]{:S(2)}) copy-start(bf16[256,1408]{0,1:T(8,128)(2,1)} %get-tuple-element.90) | copy-start | bytes 2162692
  404.7 24.5 %copy-start.28 = (bf16[256,704]{0,1:T(8,128)(2,1)S(1)}, bf16[256,704]{0,1:T(8,128)(2,1)}, u32[]{:S(2)}) copy-start(bf16[256,704]{0,1:T(8,128)(2,1)} %get-tuple-element.120) | copy-start | bytes 1081348
  404.7 44.4 %collective-permute-start.15 = (bf16[256,2112]{0,1:T(8,128)(2,1)}, bf16[256,2112]{0,1:T(8,128)(2,1)}, u32[]{:S(2)}, u32[]{:S(2)}) collective-permute-start(bf16[256,2112]{0,1:T(8,128)(2,1)} %pad_maximum_fusion.10), channel_id=1, source_target_pairs={{0,8},{8,0},{16,24},{24,16},{1,9},{9,1},{17,25},{25,17},{2,10},{10... | collective-permute-start | bytes 3244040 | tf_op jit(solution)/shard_map/ppermute | solution.py:389
  407.8 41.3 %collective-permute-start.16 = (bf16[256,2112]{0,1:T(8,128)(2,1)}, bf16[256,2112]{0,1:T(8,128)(2,1)}, u32[]{:S(2)}, u32[]{:S(2)}) collective-permute-start(bf16[256,2112]{0,1:T(8,128)(2,1)} %add_convert_fusion.3), channel_id=1, source_target_pairs={{0,16},{16,0},{8,24},{24,8},{1,17},{17,1},{9,25},{25,9},{2,18},{18... | collective-permute-start | bytes 3244040 | tf_op jit(solution)/shard_map/ppermute | solution.py:413
  429.3 19.8 %copy-start.27 = (bf16[256,704]{0,1:T(8,128)(2,1)S(1)}, bf16[256,704]{0,1:T(8,128)(2,1)}, u32[]{:S(2)}) copy-start(bf16[256,704]{0,1:T(8,128)(2,1)} %get-tuple-element.117) | copy-start | bytes 1081348
  453.8 55.9 %all-to-all-start.2 = ((bf16[8,64,2112]{2,1,0:T(8,128)(2,1)}), bf16[8,64,2112]{2,1,0:T(8,128)(2,1)S(1)}, u32[]{:S(2)}, u32[]{:S(2)}) async-start(bf16[8,64,2112]{2,1,0:T(8,128)(2,1)} %bitcast.110), calls=%async_computation.5 | async-start | bytes 4456448 | tf_op jit(solution)/shard_map/all_to_all | solution.py:340
  457.8 129.8 %reduce-scatter.11.cloned.1.call-start = ((), (), s32[]{:S(2)}) async-start(), calls=%async_computation.14 | async-start | bytes 4718592 | tf_op jit(solution)/shard_map/reduce_scatter | solution.py:336
  494.7 15.0 %copy-start.46 = (f32[1024]{0:T(1024)S(1)}, f32[1024]{0:T(1024)}, u32[]{:S(2)}) copy-start(f32[1024]{0:T(1024)} %copy-done.45) | copy-start | bytes 12292
  515.9 7.2 %copy-start.11 = (f32[2048,768]{0,1:T(8,128)}, f32[2048,768]{0,1:T(8,128)S(1)}, u32[]{:S(2)}) copy-start(f32[2048,768]{0,1:T(8,128)S(1)} %fusion.13) | copy-start | bytes 18874372
  517.2 17.3 %collective-permute-start.19 = (bf16[2048,256]{0,1:T(8,128)(2,1)}, bf16[2048,256]{0,1:T(8,128)(2,1)}, u32[]{:S(2)}, u32[]{:S(2)}) collective-permute-start(bf16[2048,256]{0,1:T(8,128)(2,1)} %get-tuple-element.83), channel_id=1, source_target_pairs={{0,1},{1,0},{2,3},{3,2},{4,5},{5,4},{6,7},{7,6},{8,9},{9,8},{10,11... | collective-permute-start | bytes 3145736 | tf_op jit(solution)/shard_map/ppermute | solution.py:434
  523.1 16.3 %collective-permute-start.27 = (bf16[32,2048]{1,0:T(8,128)(2,1)}, bf16[32,2048]{1,0:T(8,128)(2,1)}, u32[]{:S(2)}, u32[]{:S(2)}) collective-permute-start(bf16[32,2048]{1,0:T(8,128)(2,1)} %get-tuple-element.145), channel_id=1, source_target_pairs={{0,8},{8,0},{16,24},{24,16},{1,9},{9,1},{17,25},{25,17},{2,10},{10... | collective-permute-start | bytes 393224 | tf_op jit(solution)/shard_map/ppermute | solution.py:389
  524.5 22.3 %collective-permute-start.26 = (bf16[32,2048]{1,0:T(8,128)(2,1)}, bf16[32,2048]{1,0:T(8,128)(2,1)}, u32[]{:S(2)}, u32[]{:S(2)}) collective-permute-start(bf16[32,2048]{1,0:T(8,128)(2,1)} %get-tuple-element.142), channel_id=1, source_target_pairs={{0,8},{8,0},{16,24},{24,16},{1,9},{9,1},{17,25},{25,17},{2,10},{10... | collective-permute-start | bytes 393224 | tf_op jit(solution)/shard_map/ppermute | solution.py:389
  525.1 23.2 %collective-permute-start.30 = (bf16[32,2048]{1,0:T(8,128)(2,1)}, bf16[32,2048]{1,0:T(8,128)(2,1)}, u32[]{:S(2)}, u32[]{:S(2)}) collective-permute-start(bf16[32,2048]{1,0:T(8,128)(2,1)} %get-tuple-element.143), channel_id=1, source_target_pairs={{0,16},{16,0},{8,24},{24,8},{1,17},{17,1},{9,25},{25,9},{2,18},{18... | collective-permute-start | bytes 393224 | tf_op jit(solution)/shard_map/ppermute | solution.py:389
  525.6 43.2 %collective-permute-start.29 = (bf16[32,2048]{1,0:T(8,128)(2,1)}, bf16[32,2048]{1,0:T(8,128)(2,1)S(1)}, u32[]{:S(2)}, u32[]{:S(2)}) collective-permute-start(bf16[32,2048]{1,0:T(8,128)(2,1)} %get-tuple-element.144), channel_id=1, source_target_pairs={{0,16},{16,0},{8,24},{24,8},{1,17},{17,1},{9,25},{25,9},{2,18},{18... | collective-permute-start | bytes 393224 | tf_op jit(solution)/shard_map/ppermute | solution.py:389
  537.8 6.7 %collective-permute-start.21 = (bf16[256,512]{0,1:T(8,128)(2,1)S(1)}, bf16[256,512]{0,1:T(8,128)(2,1)S(1)}, u32[]{:S(2)}, u32[]{:S(2)}) collective-permute-start(bf16[256,512]{0,1:T(8,128)(2,1)S(1)} %get-tuple-element.130), channel_id=1, source_target_pairs={{0,8},{8,0},{16,24},{24,16},{1,9},{9,1},{17,25},{25,17},{2,10},{10... | collective-permute-start | bytes 786440 | tf_op jit(solution)/shard_map/ppermute | solution.py:389
  539.3 7.3 %collective-permute-start.24 = (bf16[256,512]{0,1:T(8,128)(2,1)S(1)}, bf16[256,512]{0,1:T(8,128)(2,1)S(1)}, u32[]{:S(2)}, u32[]{:S(2)}) collective-permute-start(bf16[256,512]{0,1:T(8,128)(2,1)S(1)} %get-tuple-element.132), channel_id=1, source_target_pairs={{0,16},{16,0},{8,24},{24,8},{1,17},{17,1},{9,25},{25,9},{2,18},{18... | collective-permute-start | bytes 786440 | tf_op jit(solution)/shard_map/ppermute | solution.py:389
  544.5 6.4 %collective-permute-start.28 = (bf16[32,2048]{1,0:T(8,128)(2,1)S(1)}, bf16[32,2048]{1,0:T(8,128)(2,1)S(1)}, u32[]{:S(2)}, u32[]{:S(2)}) collective-permute-start(bf16[32,2048]{1,0:T(8,128)(2,1)S(1)} %add_convert_fusion.13), channel_id=1, source_target_pairs={{0,16},{16,0},{8,24},{24,8},{1,17},{17,1},{9,25},{25,9},{2,18},{18... | collective-permute-start | bytes 393224 | tf_op jit(solution)/shard_map/ppermute | solution.py:413
  546.6 9.2 %collective-permute-start.20 = (bf16[256,512]{0,1:T(8,128)(2,1)S(1)}, bf16[256,512]{0,1:T(8,128)(2,1)S(1)}, u32[]{:S(2)}, u32[]{:S(2)}) collective-permute-start(bf16[256,512]{0,1:T(8,128)(2,1)S(1)} %get-tuple-element.129), channel_id=1, source_target_pairs={{0,8},{8,0},{16,24},{24,16},{1,9},{9,1},{17,25},{25,17},{2,10},{10... | collective-permute-start | bytes 786440 | tf_op jit(solution)/shard_map/ppermute | solution.py:389
  546.8 9.7 %collective-permute-start.23 = (bf16[256,512]{0,1:T(8,128)(2,1)S(1)}, bf16[256,512]{0,1:T(8,128)(2,1)S(1)}, u32[]{:S(2)}, u32[]{:S(2)}) collective-permute-start(bf16[256,512]{0,1:T(8,128)(2,1)S(1)} %get-tuple-element.131), channel_id=1, source_target_pairs={{0,16},{16,0},{8,24},{24,8},{1,17},{17,1},{9,25},{25,9},{2,18},{18... | collective-permute-start | bytes 786440 | tf_op jit(solution)/shard_map/ppermute | solution.py:389
  548.3 11.5 %collective-permute-start.22 = (bf16[256,512]{0,1:T(8,128)(2,1)S(1)}, bf16[256,512]{0,1:T(8,128)(2,1)S(1)}, u32[]{:S(2)}, u32[]{:S(2)}) collective-permute-start(bf16[256,512]{0,1:T(8,128)(2,1)S(1)} %get-tuple-element.133), channel_id=1, source_target_pairs={{0,16},{16,0},{8,24},{24,8},{1,17},{17,1},{9,25},{25,9},{2,18},{18... | collective-permute-start | bytes 786440 | tf_op jit(solution)/shard_map/ppermute | solution.py:413
  550.9 8.9 %collective-permute-start.25 = (bf16[256,512]{0,1:T(8,128)(2,1)S(1)}, bf16[256,512]{0,1:T(8,128)(2,1)S(1)}, u32[]{:S(2)}, u32[]{:S(2)}) collective-permute-start(bf16[256,512]{0,1:T(8,128)(2,1)S(1)} %get-tuple-element.134), channel_id=1, source_target_pairs={{0,8},{8,0},{16,24},{24,16},{1,9},{9,1},{17,25},{25,17},{2,10},{10... | collective-permute-start | bytes 786440 | tf_op jit(solution)/shard_map/ppermute | solution.py:414
  555.8 13.0 %collective-permute-start.31 = (bf16[32,2048]{1,0:T(8,128)(2,1)}, bf16[32,2048]{1,0:T(8,128)(2,1)}, u32[]{:S(2)}, u32[]{:S(2)}) collective-permute-start(bf16[32,2048]{1,0:T(8,128)(2,1)} %get-tuple-element.141), channel_id=1, source_target_pairs={{0,8},{8,0},{16,24},{24,16},{1,9},{9,1},{17,25},{25,17},{2,10},{10... | collective-permute-start | bytes 393224 | tf_op jit(solution)/shard_map/ppermute | solution.py:414
  561.1 18.8 %all-to-all-start.3 = ((bf16[8,64,512]{2,1,0:T(8,128)(2,1)}), bf16[8,64,512]{2,1,0:T(8,128)(2,1)S(1)}, u32[]{:S(2)}, u32[]{:S(2)}) async-start(bf16[8,64,512]{2,1,0:T(8,128)(2,1)} %bitcast.23), calls=%async_computation.7 | async-start | bytes 1048576 | tf_op jit(solution)/shard_map/all_to_all | solution.py:340
  581.9 5.8 copy-start.7
  581.9 7.1 %copy-start.13 = (bf16[128,2048]{1,0:T(8,128)(2,1)S(1)}, bf16[128,2048]{1,0:T(8,128)(2,1)}, u32[]{:S(2)}) copy-start(bf16[128,2048]{1,0:T(8,128)(2,1)} %reduce-scatter.5.cloned.1.call-done) | copy-start | bytes 1572868
  581.9 7.1 %copy-start.15 = (f32[128,2048]{1,0:T(8,128)S(1)}, f32[128,2048]{1,0:T(8,128)}, u32[]{:S(2)}) copy-start(f32[128,2048]{1,0:T(8,128)} %get-tuple-element.63) | copy-start | bytes 3145732
  583.0 6.0 copy-start.36
  (34 other events, 93.5 us)
Sparse Core Ops, SparseCore 0:
  9.6 72.5 all-gather.11
  139.9 48.3 reduce-scatter.4
  198.3 44.9 all-gather.5
  244.7 45.6 all-gather.7
  292.6 48.7 reduce-scatter.6
  343.5 48.3 reduce-scatter.8
  396.0 45.3 all-gather.9
  509.8 47.8 reduce-scatter.10

commit v4 on v3

--- a/solution.py
+++ b/solution.py
@@ -660,11 +660,10 @@
     both = 2 * (main + tail)
     gate_main, gate_tail = ff_slices(fold(gate_weight, gain_two))
     up_main, up_tail = ff_slices(fold(up_weight, gain_two))
-    mlp_pieces = jnp.concatenate(
-        [gate_main, up_main, gate_tail, up_tail, *ff_slices(down_weight)], axis=2
-    )
+    down_pieces = jnp.concatenate(ff_slices(down_weight), axis=2)
+    gate_up_pieces = jnp.concatenate([gate_main, up_main, gate_tail, up_tail], axis=2)
     attn_own = exchange_ctx(attn_pieces).reshape(8 * rows, 2 * head_width)
-    attn_own, mlp_pieces = tie(attn_own, mlp_pieces)
+    attn_own, down_pieces, gate_up_pieces = tie(attn_own, down_pieces, gate_up_pieces)
     attn_cols = gather_seq(attn_own)
     core = lax.axis_index("ctx") % 2
     own_cols = attn_cols[:, head_width:]
@@ -678,7 +677,9 @@
         axis=1,
     )
     out_rows = gather_seq(out_weight)
-    mlp_own = exchange_ctx(mlp_pieces).reshape(8 * rows, -1)
+    down_own = exchange_ctx(down_pieces).reshape(8 * rows, -1)
+    down_own, gate_up_pieces = tie(down_own, gate_up_pieces)
+    gate_up_own = exchange_ctx(gate_up_pieces).reshape(8 * rows, -1)
 
     edge = jnp.sum((segments[0] == 0).astype(jnp.int32))
     token = jnp.arange(length, dtype=jnp.int32)
@@ -691,26 +692,29 @@
     wide = inputs_all.astype(f32)
     shaped_all = (wide * rms_scale(wide)).astype(bf16)
     raw = jnp.dot(shaped_all, attn_cols, preferred_element_type=f32)
-    raw, mlp_own = tie(raw, mlp_own)
-    mlp_near = gather_seq_near(mlp_own)
+    raw, down_own = tie(raw, down_own)
+    down_near = gather_seq_near(down_own)
     queries = turn(raw[:, :head_width], cosine, sine_table).astype(bf16)
     keys = turn(raw[:, head_width : 2 * head_width], cosine, sine_table).astype(bf16)
     values = raw[:, 2 * head_width :].astype(bf16)
     queries = queries * jnp.asarray(score_scale, bf16)
     attn_low = attend(edge, queries, keys, values)
-    attn_low, out_rows, back_late = tie(attn_low, out_rows, out_back)
+    attn_low, out_rows, back_late, gate_up_own, *down_near = tie(
+        attn_low, out_rows, out_back, gate_up_own, *down_near
+    )
+    gate_up_near = gather_seq_near(gate_up_own)
+    down_cols = gather_seq_far(down_own, *down_near)
     mixed = jnp.dot(attn_low, out_rows, preferred_element_type=f32).astype(bf16)
     mixed_own = reduce_ctx(mixed)
-    mixed_own, *mlp_near = tie(mixed_own, *mlp_near)
+    mixed_own, down_cols, *gate_up_near = tie(mixed_own, down_cols, *gate_up_near)
     residual = inputs + mixed_own.astype(f32)
     scale_two = rms_scale(residual)
     shaped_two = residual * scale_two
     shaped_low = shaped_two.astype(bf16)
     normed_all = gather_ctx(shaped_low)
     shaped_two, back_late = tie(shaped_two, back_late)
-    mlp_cols = gather_seq_far(mlp_own, *mlp_near)
+    gate_up = gather_seq_far(gate_up_own, *gate_up_near)
     back_all = gather_ctx(back_late)
-    gate_up, down_cols = mlp_cols[:, :both], mlp_cols[:, both:]
     proj = jnp.dot(normed_all, gate_up, preferred_element_type=f32)
 
     def halves(left_tail, right_tail, left, right):
@@ -738,24 +742,21 @@
         axis=1,
     )
     weighted = reduce_ctx(contract_cols(gate_up_back, gate_up).astype(bf16))
-    gate_up_back, hidden, out_own = tie(gate_up_back, hidden, out_own)
     gate_up_grad = contract_rows(normed_all, gate_up_back).astype(bf16)
     down_grad = contract_rows(back_all, hidden).astype(bf16)
     mlp_grads = [gate_up_grad, down_grad]
-    mlp_parts = seq_parts(mlp_grads)
-    mlp_first = send_parts(mlp_parts[:2])
-    weighted, *mlp_first = tie(weighted, *mlp_first)
+    out_own, *mlp_parts = tie(out_own, *seq_parts(mlp_grads))
+    mlp_near = send_parts(mlp_parts)
+    weighted, *mlp_near = tie(weighted, *mlp_near)
     weighted = weighted.astype(f32)
     residual_back = out_back.astype(f32) + scale_two * (
         weighted - shaped_two * jnp.mean(weighted * shaped_two, axis=-1, keepdims=True)
     )
     residual_low = residual_back.astype(bf16)
     low_all = gather_ctx(residual_low)
-    residual_back, *mlp_first = tie(residual_back, *mlp_first)
-    mlp_near = send_parts(mlp_parts[2:])
-    mlp_sums = far_sums(mlp_grads, *mlp_first)
-    mlp_grads_own = reduce_seq_far(mlp_grads, mlp_sums, *mlp_near)
-    low_all, mlp_grads_own = tie(low_all, mlp_grads_own)
+    residual_back, *mlp_near = tie(residual_back, *mlp_near)
+    mlp_sums = far_sums(mlp_grads, *mlp_near[:2])
+    mlp_grads_own = reduce_seq_far(mlp_grads, mlp_sums, *mlp_near[2:])
     mlp_grad = exchange_ctx(mlp_grads_own.reshape(8, rows, -1))
     attn_back = contract_cols(low_all, out_rows).astype(bf16)
     query_back, key_back, value_back = attend_back(
@@ -769,20 +770,24 @@
         ],
         axis=1,
     )
-    weighted_part = contract_cols(heads_back, attn_cols).astype(bf16)
-    weighted_part, mlp_grad, heads_back, low_all = tie(weighted_part, mlp_grad, heads_back, low_all)
-    weighted_one = reduce_ctx(weighted_part).astype(f32)
+    heads_back, mlp_grad = tie(heads_back, mlp_grad)
     attn_full_grad = contract_rows(shaped_all, heads_back)
     key_part = attn_full_grad[:, head_width : 2 * head_width]
     value_part = attn_full_grad[:, 2 * head_width :]
-    other_part = swap_cores(jnp.where(core == 0, value_part, key_part).astype(bf16))
+    other_part = jnp.where(core == 0, value_part, key_part).astype(bf16)
+    heads_back, other_part = tie(heads_back, other_part)
+    other_part = swap_cores(other_part)
+    weighted_part = contract_cols(heads_back, attn_cols).astype(bf16)
+    weighted_part, low_all = tie(weighted_part, low_all)
+    weighted_one = reduce_ctx(weighted_part).astype(f32)
     own_part = jnp.where(core == 0, key_part, value_part) + other_part.astype(f32)
     attn_grad_own = reduce_seq(
         [jnp.concatenate([attn_full_grad[:, :head_width].astype(bf16), own_part.astype(bf16)], axis=1)]
     )
     out_grad = reduce_seq([contract_rows(attn_low, low_all).astype(bf16)]).astype(f32)
+    attn_grad_own, mlp_grad = tie(attn_grad_own, mlp_grad)
     mlp_grad = mlp_grad.astype(f32)
-    attn_grad = exchange_ctx(attn_grad_own.reshape(8, rows, -1)).astype(f32)
+    attn_grad = exchange_ctx(attn_grad_own.reshape(8, rows, -1))
 
     scale_one = rms_scale(inputs)
     shaped_one = inputs * scale_one
@@ -793,6 +798,10 @@
     gate_rows = ff_rows(mlp_grad[:, :, :main], mlp_grad[:, :, 2 * main : 2 * main + tail])
     up_rows = ff_rows(mlp_grad[:, :, main : 2 * main], mlp_grad[:, :, 2 * main + tail : both])
     down_grad = ff_rows(mlp_grad[:, :, both : both + main], mlp_grad[:, :, both + main :])
+    attn_grad, out_grad, gate_rows, up_rows, down_grad = tie(
+        attn_grad, out_grad, gate_rows, up_rows, down_grad
+    )
+    attn_grad = attn_grad.astype(f32)
     query_rows = from_head_slices(attn_grad[:, :, :head_width])
     pair_rows = jnp.sum(attn_grad[:, :, head_width:].reshape(4, 2, rows, head_width), axis=0)
     key_rows, value_rows = pair_rows[0], pair_rows[1]

time: 609 us -> 594 us (0.975)
  waiting for transfers between devices: 268 us -> 244 us
  starting transfers between devices: 49.4 us -> 61 us
  other arithmetic: 65.9 us -> 57.5 us
  local copies, waits for them, and re-layouts: 90.7 us -> 97.8 us
    ppermute x3 -> x4, waiting for transfers between devices: 52.5 us -> 6.1 us  [gather_seq_near(): lax.ppermute(block, 'seq', SEQ_X)]
    ppermute x3 -> x4, waiting for transfers between devices: 4.26 us -> 36.1 us  [gather_seq_far(): far_low = lax.ppermute(from_y[half:], 'seq', SEQ_X)]
    ppermute x12, waiting for transfers between devices: 42 us -> 11 us  [send_parts(): lax.ppermute(part, 'seq', axis)]
    all_gather x4, waiting for transfers between devices: 37.8 us -> 55.9 us  [gather_ctx(): return lax.all_gather(block, 'ctx', axis=0, tiled=True)]
    ppermute x3, waiting for transfers between devices: 5.22 us -> 21.2 us  [reduce_seq_far(): top_last = lax.ppermute(top_send, 'seq', SEQ_Y)]
    all_to_all x4 -> x5, waiting for transfers between devices: 58.9 us -> 46 us  [exchange_ctx(): return lax.all_to_all(pieces, 'ctx', 0, 0, tiled=True)]
    optimization_barrier x5 -> x6, local copies, waits for them, and re-layouts: 15.2 us -> 10.2 us  [tie(): return lax.optimization_barrier(values)]
    dynamic_update_slice x15 -> x20, local copies, waits for them, and re-layouts: 15.1 us -> 19.6 us  [gather_seq_far(): whole = lax.dynamic_update_slice_in_dim(whole, piece, start, 0)]
  transfers between devices with their start and end apart: 44 -> 49, of which waited for: 26 -> 24; matrix products, arithmetic and copies ran while one was open for 33% -> 33% of each run, Pallas kernels for 3% -> 6%
where the time goes in v4:
time: 594 us; the launch traced here: 587 us
  waiting for transfers between devices  244 us (41%)
  local copies, waits for them, and re-layouts  97.8 us (16%)
  matrix products  78.2 us (13%)
  starting transfers between devices  61 us (10%)
  other arithmetic  57.5 us (10%)
  Pallas kernels  32.7 us (6%)
  between operations  16.3 us (3%)
    all_gather x4, waiting for transfers between devices, gather_ctx(): return lax.all_gather(block, 'ctx', axis=0, tiled=True)  55.9 us
    reduce_scatter x4, waiting for transfers between devices, reduce_ctx(): return lax.psum_scatter(partial, 'ctx', scatter_dimension=0, tiled=True)  55.4 us
    all_to_all x5, waiting for transfers between devices, exchange_ctx(): return lax.all_to_all(pieces, 'ctx', 0, 0, tiled=True)  46 us
    ppermute x4, waiting for transfers between devices, gather_seq_far(): far_low = lax.ppermute(from_y[half:], 'seq', SEQ_X)  36.1 us
    dot_general x4, matrix products, contract_cols(): lax.dot_general(left, right, (((1,), (1,)), ((), ())), preferred_element_...  27.8 us
    dot_general x4, matrix products, contract_rows(): lax.dot_general(left, right, (((0,), (0,)), ((), ())), preferred_element_...  21.8 us
    ppermute x3, waiting for transfers between devices, reduce_seq_far(): top_last = lax.ppermute(top_send, 'seq', SEQ_Y)  21.2 us
    all_to_all x5, starting transfers between devices, exchange_ctx(): return lax.all_to_all(pieces, 'ctx', 0, 0, tiled=True)  21.2 us
  transfers between devices with their start and end apart: 49, of which 24 were waited for; matrix products, arithmetic and copies ran while one was open for 33% of the time, Pallas kernels for 6%

profile of v4, /device:TPU:0, one launch (start us, length us, event | category | flops | bytes accessed | tf_op | source)
XLA Modules:
  0.0 587.1 jit_solution(9096530841841823187)
XLA Ops:
  7.9 3.1 collective-permute-start.6
  16.3 4.9 all-to-all-start
  25.4 2.2 concatenate.106
  29.2 21.1 %all-to-all-done = bf16[8,64,512]{2,1,0:T(8,128)(2,1)S(1)} async-done(((bf16[8,64,512]{2,1,0:T(8,128)(2,1)}), bf16[8,64,512]{2,1,0:T(8,128)(2,1)S(1)}, u32[]{:S(2)}, u32[]{:S(2)}) %all-to-all-start) | async-done | bytes 524320 | tf_op jit(solution)/shard_map/all_to_all | solution.py:340
  57.1 3.5 all-to-all-start.1
  60.7 6.1 %collective-permute-done = bf16[512,512]{0,1:T(8,128)(2,1)S(1)} collective-permute-done((bf16[512,512]{0,1:T(8,128)(2,1)S(1)}, bf16[512,512]{0,1:T(8,128)(2,1)S(1)}, u32[]{:S(2)}, u32[]{:S(2)}) %collective-permute-start) | collective-permute-done | bytes 524320 | tf_op jit(solution)/shard_map/ppermute | solution.py:344
  72.2 2.3 collective-permute-done.2
  74.6 2.7 collective-permute-done.3
  79.5 2.5 copy.83
  83.2 2.6 copy.84
  91.8 2.0 collective-permute-done.7
  95.1 2.9 copy.87
  98.0 4.3 all-to-all-start.2
  102.6 3.0 broadcast_select_fusion.1
  105.6 3.2 fusion
  109.1 5.3 fusion.5
  114.4 2.3 copy.88
  123.4 13.0 %attend.1 = bf16[1024,256]{1,0:T(8,128)(2,1)} custom-call(s32[1]{0:T(128)} %bitcast.1.refs_0_, bf16[1024,256]{1,0:T(8,128)(2,1)} %get-tuple-element.146.refs_1_, bf16[1024,256]{1,0:T(8,128)(2,1)} %fusion.27.refs_2_, bf16[1024,256]{1,0:T(8,128)(2,1)} %get-tuple-element.145.refs_3_), custom_call_target="tpu_custom_call" | custom-call | flops 4294967296 | bytes 2097152 | tf_op jit(solution)/shard_map/attend/pallas_call | solution.py:581
  137.3 4.7 convolution_convert_fusion.2
  149.4 1.9 broadcast_in_dim.33
  156.9 27.5 %collective-permute-done.12 = bf16[256,704]{0,1:T(8,128)(2,1)} collective-permute-done((bf16[256,704]{0,1:T(8,128)(2,1)}, bf16[256,704]{0,1:T(8,128)(2,1)}, u32[]{:S(2)}, u32[]{:S(2)}) %collective-permute-start.12) | collective-permute-done | bytes 360480 | tf_op jit(solution)/shard_map/ppermute | solution.py:352
  188.3 3.4 reduce-scatter.5.cloned.1.call-done
  193.1 2.4 fusion.63
  198.9 2.9 broadcast_in_dim.34
  201.8 2.8 constant_dynamic-update-slice_fusion.4
  206.0 2.6 constant_dynamic-update-slice_fusion.3
  209.8 3.6 collective-permute-done.15
  214.3 5.9 %collective-permute-done.16 = bf16[256,1408]{1,0:T(8,128)(2,1)S(1)} collective-permute-done((bf16[256,1408]{1,0:T(8,128)(2,1)S(1)}, bf16[256,1408]{1,0:T(8,128)(2,1)S(1)}, u32[]{:S(2)}, u32[]{:S(2)}) %collective-permute-start.16) | collective-permute-done | bytes 720928 | tf_op jit(solution)/shard_map/ppermute | solution.py:352
  221.1 19.9 %all-gather.6.cloned.1.call-done = bf16[1024,2048]{1,0:T(8,128)(2,1)} async-done(((bf16[128,2048]{1,0:T(8,128)(2,1)}), bf16[1024,2048]{1,0:T(8,128)(2,1)}) %all-gather.6.cloned.1.call-update) | async-done | bytes 4194320 | tf_op jit(solution)/shard_map/all_gather | solution.py:332
  241.0 10.5 %fusion.76 = f32[1024,1408]{1,0:T(8,128)S(1)} fusion(bf16[1024,2048]{1,0:T(8,128)(2,1)} %all-gather.6.cloned.1.call-done, bf16[2048,1408]{1,0:T(8,128)(2,1)} %constant_dynamic-update-slice_fusion), kind=kOutput, calls=%fused_computation.231 | convolution fusion | flops 5905580032 | bytes 15728640 | tf_op jit(solution)/shard_map/dot_general | solution.py:718
  255.8 6.9 %convolution_convert_fusion.4 = bf16[1024,2048]{1,0:T(8,128)(2,1)} fusion(bf16[1024,704]{1,0:T(8,128)(2,1)S(1)} %multiply_convert_fusion.2, bf16[2048,704]{1,0:T(8,128)(2,1)} %constant_dynamic-update-slice_fusion.5), kind=kOutput, calls=%fused_computation.24 | convolution fusion | flops 2954887168 | bytes 8519680 | tf_op jit(solution)/shard_map/dot_general | solution.py:53
  262.7 25.5 %all-gather.8.cloned.1.call-done = bf16[1024,2048]{1,0:T(8,128)(2,1)} async-done(((bf16[128,2048]{1,0:T(8,128)(2,1)}), bf16[1024,2048]{1,0:T(8,128)(2,1)}) %all-gather.8.cloned.1.call-update) | async-done | bytes 4194320 | tf_op jit(solution)/shard_map/all_gather | solution.py:332
  288.2 8.3 %multiply_convert_fusion = (bf16[1024,704]{1,0:T(8,128)(2,1)S(1)}, bf16[1024,704]{1,0:T(8,128)(2,1)S(1)}) fusion(f32[1024,64]{1,0:T(8,128)S(1)} %get-tuple-element.137, f32[1024,640]{1,0:T(8,128)S(1)} %get-tuple-element.135, f32[1024,64]{1,0:T(8,128)} %copy-done.22, f32[1024,640]{1,0:T(8,128)} %copy-done.8, ...), kind=kOutput, calls=%fused_computation.29 | convolution fusion | flops 2963603456 | bytes 15728640 | tf_op jit(solution)/shard_map/dot_general | solution.py:735
  296.8 3.9 concatenate.116
  300.7 11.1 %convolution_convert_fusion.1 = bf16[1024,2048]{1,0:T(8,128)(2,1)} fusion(bf16[1024,1408]{1,0:T(8,128)(2,1)} %concatenate.116, bf16[2048,1408]{1,0:T(8,128)(2,1)} %constant_dynamic-update-slice_fusion), kind=kOutput, calls=%fused_computation.21 | convolution fusion | flops 5907677184 | bytes 12845056 | tf_op jit(solution)/shard_map/dot_general | solution.py:53
  313.2 5.6 convolution_convert_fusion.5
  321.1 6.6 %convolution_convert_fusion = bf16[2048,1408]{0,1:T(8,128)(2,1)S(1)} fusion(bf16[1024,2048]{1,0:T(8,128)(2,1)S(1)} %copy-done.49, bf16[1024,1408]{1,0:T(8,128)(2,1)S(1)} %copy-done.16), kind=kOutput, calls=%fused_computation.4 | convolution fusion | flops 5908463616 | bytes 12845056 | tf_op jit(solution)/shard_map/dot_general | solution.py:47
  333.6 5.5 reduce-scatter.7.cloned.1.call-done
  343.1 46.5 %reduce-scatter.9.cloned.1.call-done = bf16[128,2048]{1,0:T(8,128)(2,1)} async-done(((bf16[1024,2048]{1,0:T(8,128)(2,1)}), bf16[128,2048]{1,0:T(8,128)(2,1)}) %reduce-scatter.9.cloned.1.call-update) | async-done | bytes 524304 | tf_op jit(solution)/shard_map/reduce_scatter | solution.py:336
  390.9 2.7 fusion.61
  393.6 1.9 add_convert_fusion.3
  400.1 19.2 %collective-permute-done.21 = bf16[256,2112]{0,1:T(8,128)(2,1)S(1)} collective-permute-done((bf16[256,2112]{0,1:T(8,128)(2,1)S(1)}, bf16[256,2112]{0,1:T(8,128)(2,1)S(1)}, u32[]{:S(2)}, u32[]{:S(2)}) %collective-permute-start.21) | collective-permute-done | bytes 1081376 | tf_op jit(solution)/shard_map/ppermute | solution.py:413
  424.0 2.6 copy.99
  426.5 4.3 all-to-all-start.3
  430.9 10.6 %all-gather.10.cloned.1.call-done = bf16[1024,2048]{1,0:T(8,128)(2,1)} async-done(((bf16[128,2048]{1,0:T(8,128)(2,1)}), bf16[1024,2048]{1,0:T(8,128)(2,1)}) %all-gather.10.cloned.1.call-update) | async-done | bytes 4194320 | tf_op jit(solution)/shard_map/all_gather | solution.py:332
  441.5 4.6 convolution_convert_fusion.7.refs_4_
  446.0 19.7 %attend_back.1 = (f32[1024,256]{1,0:T(8,128)}, f32[1024,256]{1,0:T(8,128)}, f32[1024,256]{1,0:T(8,128)}) custom-call(s32[1]{0:T(128)} %bitcast.1.refs_0_, bf16[1024,256]{1,0:T(8,128)(2,1)} %get-tuple-element.146.refs_1_, bf16[1024,256]{1,0:T(8,128)(2,1)} %fusion.27.refs_2_, bf16[1024,256]{1,0:T(8,128)(2,1)} %get-tuple-element.145.refs_3_, ...), custom_call_target="tpu_custom_call" | custom-call | flops 10737418240 | bytes 3670016 | tf_op jit(solution)/shard_map/attend_back/pallas_call | solution.py:602
  472.2 13.1 %all-to-all-done.3 = bf16[8,64,2112]{2,1,0:T(8,128)(2,1)S(1)} async-done(((bf16[8,64,2112]{2,1,0:T(8,128)(2,1)}), bf16[8,64,2112]{2,1,0:T(8,128)(2,1)S(1)}, u32[]{:S(2)}, u32[]{:S(2)}) %all-to-all-start.3) | async-done | bytes 2162720 | tf_op jit(solution)/shard_map/all_to_all | solution.py:340
  485.3 6.0 %fusion.3 = f32[2048,768]{0,1:T(8,128)S(1)} fusion(bf16[1024,768]{1,0:T(8,128)(2,1)} %pad_maximum_fusion.4, bf16[1,1024,2048]{2,1,0:T(8,128)(2,1)} %all-gather.12.cloned.1.call-done, f32[1024]{0:T(1024)S(1)} %add_rsqrt_fusion), kind=kOutput, calls=%fused_computation.47 | convolution fusion | flops 3227516928 | bytes 12062720 | tf_op jit(solution)/shard_map/dot_general | solution.py:47
  491.3 2.6 copy-done.10
  496.6 5.2 convolution_convert_fusion.3
  501.9 3.6 convolution_convert_fusion.6
  509.8 2.3 collective-permute-done.31
  513.6 2.8 add_convert_fusion.4
  520.9 5.0 collective-permute-done.25
  530.5 3.7 collective-permute-done.24
  534.3 2.0 collective-permute-done.26
  539.2 4.1 all-to-all-start.4
  549.8 10.8 %all-to-all-done.4 = bf16[8,64,512]{2,1,0:T(8,128)(2,1)} async-done(((bf16[8,64,512]{2,1,0:T(8,128)(2,1)}), bf16[8,64,512]{2,1,0:T(8,128)(2,1)}, u32[]{:S(2)}, u32[]{:S(2)}) %all-to-all-start.4) | async-done | bytes 524320 | tf_op jit(solution)/shard_map/all_to_all | solution.py:340
  560.6 1.9 fusion.75
  564.0 2.9 copy.107
  566.8 2.4 reshape.172
  569.3 3.5 broadcast_multiply_fusion
  577.2 2.7 fusion.18
  (318 shorter events, 135.9 us)
Async XLA Ops:
  7.2 8.1 %copy-start.42 = (bf16[64,256]{1,0:T(8,128)(2,1)S(1)}, bf16[64,256]{1,0:T(8,128)(2,1)}, u32[]{:S(2)}) copy-start(bf16[64,256]{1,0:T(8,128)(2,1)} %param.19) | copy-start | bytes 98308
  7.2 8.1 %copy-start.40 = (bf16[64,256]{1,0:T(8,128)(2,1)S(1)}, bf16[64,256]{1,0:T(8,128)(2,1)}, u32[]{:S(2)}) copy-start(bf16[64,256]{1,0:T(8,128)(2,1)} %param.18) | copy-start | bytes 98308
  7.2 98.4 %all-gather.12.cloned.1.call-start = ((), (), s32[]{:S(2)}) async-start(), calls=%async_computation.16 | async-start | bytes 4718592 | tf_op jit(solution)/shard_map/all_gather | solution.py:332
  7.9 77.8 %collective-permute-start.6 = (bf16[64,2048]{1,0:T(8,128)(2,1)}, bf16[64,2048]{1,0:T(8,128)(2,1)}, u32[]{:S(2)}, u32[]{:S(2)}) collective-permute-start(bf16[64,2048]{1,0:T(8,128)(2,1)} %param.20), channel_id=1, source_target_pairs={{0,16},{16,0},{8,24},{24,8},{1,17},{17,1},{9,25},{25,9},{2,18},{18... | collective-permute-start | bytes 786440 | tf_op jit(solution)/shard_map/ppermute | solution.py:344
  11.0 76.2 %collective-permute-start.5 = (bf16[64,2048]{1,0:T(8,128)(2,1)}, bf16[64,2048]{1,0:T(8,128)(2,1)}, u32[]{:S(2)}, u32[]{:S(2)}) collective-permute-start(bf16[64,2048]{1,0:T(8,128)(2,1)} %param.20), channel_id=1, source_target_pairs={{0,8},{8,0},{16,24},{24,16},{1,9},{9,1},{17,25},{25,17},{2,10},{10... | collective-permute-start | bytes 786440 | tf_op jit(solution)/shard_map/ppermute | solution.py:344
  14.7 6.5 %copy-start.50 = (bf16[64]{0:T(256)(128)(2,1)S(1)}, bf16[64]{0:T(256)(128)(2,1)}, u32[]{:S(2)}) copy-start(bf16[64]{0:T(256)(128)(2,1)} %param.21) | copy-start | bytes 388
  14.7 6.5 %copy-start.17 = (bf16[64,5632]{1,0:T(8,128)(2,1)S(1)}, bf16[64,5632]{1,0:T(8,128)(2,1)}, u32[]{:S(2)}) copy-start(bf16[64,5632]{1,0:T(8,128)(2,1)} %param.23) | copy-start | bytes 2162692
  14.8 6.5 %copy-start.18 = (bf16[64,5632]{1,0:T(8,128)(2,1)S(1)}, bf16[64,5632]{1,0:T(8,128)(2,1)}, u32[]{:S(2)}) copy-start(bf16[64,5632]{1,0:T(8,128)(2,1)} %param.22) | copy-start | bytes 2162692
  16.3 34.0 %all-to-all-start = ((bf16[8,64,512]{2,1,0:T(8,128)(2,1)}), bf16[8,64,512]{2,1,0:T(8,128)(2,1)S(1)}, u32[]{:S(2)}, u32[]{:S(2)}) async-start(bf16[8,64,512]{2,1,0:T(8,128)(2,1)} %pad_maximum_fusion.15), calls=%async_computation | async-start | bytes 1048576 | tf_op jit(solution)/shard_map/all_to_all | solution.py:340
  28.2 28.2 %copy-start.39 = (bf16[64,2048]{1,0:T(8,128)(2,1)S(1)}, bf16[64,2048]{1,0:T(8,128)(2,1)}, u32[]{:S(2)}) copy-start(bf16[64,2048]{1,0:T(8,128)(2,1)} %param.20) | copy-start | bytes 786436
  52.4 16.9 %collective-permute-start.1 = (bf16[512,512]{0,1:T(8,128)(2,1)S(1)}, bf16[512,512]{0,1:T(8,128)(2,1)}, u32[]{:S(2)}, u32[]{:S(2)}) collective-permute-start(bf16[512,512]{0,1:T(8,128)(2,1)S(1)} %copy.80), channel_id=1, source_target_pairs={{0,16},{16,0},{8,24},{24,8},{1,17},{17,1},{9,25},{25,9},{2,18},{18... | collective-permute-start | bytes 1572872 | tf_op jit(solution)/shard_map/ppermute | solution.py:344
  53.3 13.4 %collective-permute-start = (bf16[512,512]{0,1:T(8,128)(2,1)S(1)}, bf16[512,512]{0,1:T(8,128)(2,1)S(1)}, u32[]{:S(2)}, u32[]{:S(2)}) collective-permute-start(bf16[512,512]{0,1:T(8,128)(2,1)S(1)} %copy.80), channel_id=1, source_target_pairs={{0,8},{8,0},{16,24},{24,16},{1,9},{9,1},{17,25},{25,17},{2,10},{10... | collective-permute-start | bytes 1572872 | tf_op jit(solution)/shard_map/ppermute | solution.py:344
  57.1 38.0 %all-to-all-start.1 = ((bf16[8,64,704]{2,1,0:T(8,128)(2,1)}), bf16[8,64,704]{2,1,0:T(8,128)(2,1)S(1)}, u32[]{:S(2)}, u32[]{:S(2)}) async-start(bf16[8,64,704]{2,1,0:T(8,128)(2,1)} %pad_maximum_fusion.14), calls=%async_computation.1 | async-start | bytes 1572864 | tf_op jit(solution)/shard_map/all_to_all | solution.py:340
  67.5 7.0 %collective-permute-start.2 = (bf16[256,512]{0,1:T(8,128)(2,1)S(1)}, bf16[256,512]{0,1:T(8,128)(2,1)S(1)}, u32[]{:S(2)}, u32[]{:S(2)}) collective-permute-start(bf16[256,512]{0,1:T(8,128)(2,1)S(1)} %slice.242), channel_id=1, source_target_pairs={{0,16},{16,0},{8,24},{24,8},{1,17},{17,1},{9,25},{25,9},{2,18},{18... | collective-permute-start | bytes 786440 | tf_op jit(solution)/shard_map/ppermute | solution.py:351
  70.2 7.1 %collective-permute-start.3 = (bf16[256,512]{0,1:T(8,128)(2,1)S(1)}, bf16[256,512]{0,1:T(8,128)(2,1)S(1)}, u32[]{:S(2)}, u32[]{:S(2)}) collective-permute-start(bf16[256,512]{0,1:T(8,128)(2,1)S(1)} %slice.243), channel_id=1, source_target_pairs={{0,8},{8,0},{16,24},{24,16},{1,9},{9,1},{17,25},{25,17},{2,10},{10... | collective-permute-start | bytes 786440 | tf_op jit(solution)/shard_map/ppermute | solution.py:352
  71.1 7.4 %copy-start.35 = (f32[1024,64]{0,1:T(8,128)S(1)}, f32[1024,64]{0,1:T(8,128)}, u32[]{:S(2)}) copy-start(f32[1024,64]{0,1:T(8,128)} %get-tuple-element.212) | copy-start | bytes 786436
  78.4 24.2 %collective-permute-start.4 = (bf16[2048,256]{0,1:T(8,128)(2,1)}, bf16[2048,256]{0,1:T(8,128)(2,1)}, u32[]{:S(2)}, u32[]{:S(2)}) collective-permute-start(bf16[2048,256]{0,1:T(8,128)(2,1)} %slice.245), channel_id=1, source_target_pairs={{0,1},{1,0},{2,3},{3,2},{4,5},{5,4},{6,7},{7,6},{8,9},{9,8},{10,11... | collective-permute-start | bytes 3145736 | tf_op jit(solution)/shard_map/ppermute | solution.py:434
  86.6 7.8 %collective-permute-start.8 = (bf16[32,2048]{1,0:T(8,128)(2,1)S(1)}, bf16[32,2048]{1,0:T(8,128)(2,1)S(1)}, u32[]{:S(2)}, u32[]{:S(2)}) collective-permute-start(bf16[32,2048]{1,0:T(8,128)(2,1)S(1)} %slice.248), channel_id=1, source_target_pairs={{0,8},{8,0},{16,24},{24,16},{1,9},{9,1},{17,25},{25,17},{2,10},{10... | collective-permute-start | bytes 393224 | tf_op jit(solution)/shard_map/ppermute | solution.py:352
  88.1 5.7 collective-permute-start.7
  98.0 39.3 %all-to-all-start.2 = ((bf16[8,64,1408]{2,1,0:T(8,128)(2,1)}), bf16[8,64,1408]{2,1,0:T(8,128)(2,1)}, u32[]{:S(2)}, u32[]{:S(2)}) async-start(bf16[8,64,1408]{2,1,0:T(8,128)(2,1)} %copy.87), calls=%async_computation.2 | async-start | bytes 2883584 | tf_op jit(solution)/shard_map/all_to_all | solution.py:340
  102.3 89.5 %reduce-scatter.5.cloned.1.call-start = ((), (), s32[]{:S(2)}) async-start(), calls=%async_computation.9 | async-start | bytes 4718592 | tf_op jit(solution)/shard_map/reduce_scatter | solution.py:336
  116.7 20.6 %collective-permute-start.10 = (bf16[512,704]{0,1:T(8,128)(2,1)}, bf16[512,704]{0,1:T(8,128)(2,1)}, u32[]{:S(2)}, u32[]{:S(2)}) collective-permute-start(bf16[512,704]{0,1:T(8,128)(2,1)} %copy.88), channel_id=1, source_target_pairs={{0,16},{16,0},{8,24},{24,8},{1,17},{17,1},{9,25},{25,9},{2,18},{18... | collective-permute-start | bytes 2162696 | tf_op jit(solution)/shard_map/ppermute | solution.py:344
  117.0 20.3 %collective-permute-start.9 = (bf16[512,704]{0,1:T(8,128)(2,1)}, bf16[512,704]{0,1:T(8,128)(2,1)}, u32[]{:S(2)}, u32[]{:S(2)}) collective-permute-start(bf16[512,704]{0,1:T(8,128)(2,1)} %copy.88), channel_id=1, source_target_pairs={{0,8},{8,0},{16,24},{24,16},{1,9},{9,1},{17,25},{25,17},{2,10},{10... | collective-permute-start | bytes 2162696 | tf_op jit(solution)/shard_map/ppermute | solution.py:344
  142.0 9.3 %copy-start.12 = (bf16[8,64,704]{2,1,0:T(8,128)(2,1)S(1)}, bf16[8,64,704]{2,1,0:T(8,128)(2,1)}, u32[]{:S(2)}) copy-start(bf16[8,64,704]{2,1,0:T(8,128)(2,1)} %copy-done.11) | copy-start | bytes 2162692
  142.0 99.0 %all-gather.6.cloned.1.call-start = ((), (), s32[]{:S(2)}) async-start(), calls=%async_computation.10 | async-start | bytes 4718592 | tf_op jit(solution)/shard_map/all_gather | solution.py:332
  142.5 45.8 %collective-permute-start.14 = (bf16[512,1408]{1,0:T(8,128)(2,1)}, bf16[512,1408]{1,0:T(8,128)(2,1)S(1)}, u32[]{:S(2)}, u32[]{:S(2)}) collective-permute-start(bf16[512,1408]{1,0:T(8,128)(2,1)} %bitcast.19), channel_id=1, source_target_pairs={{0,16},{16,0},{8,24},{24,8},{1,17},{17,1},{9,25},{25,9},{2,18},{18... | collective-permute-start | bytes 4325384 | tf_op jit(solution)/shard_map/ppermute | solution.py:344
  143.4 44.9 %collective-permute-start.13 = (bf16[512,1408]{1,0:T(8,128)(2,1)}, bf16[512,1408]{1,0:T(8,128)(2,1)}, u32[]{:S(2)}, u32[]{:S(2)}) collective-permute-start(bf16[512,1408]{1,0:T(8,128)(2,1)} %bitcast.19), channel_id=1, source_target_pairs={{0,8},{8,0},{16,24},{24,16},{1,9},{9,1},{17,25},{25,17},{2,10},{10... | collective-permute-start | bytes 4325384 | tf_op jit(solution)/shard_map/ppermute | solution.py:344
  147.3 37.1 %collective-permute-start.12 = (bf16[256,704]{0,1:T(8,128)(2,1)}, bf16[256,704]{0,1:T(8,128)(2,1)}, u32[]{:S(2)}, u32[]{:S(2)}) collective-permute-start(bf16[256,704]{0,1:T(8,128)(2,1)} %slice.206), channel_id=1, source_target_pairs={{0,8},{8,0},{16,24},{24,16},{1,9},{9,1},{17,25},{25,17},{2,10},{10... | collective-permute-start | bytes 1081352 | tf_op jit(solution)/shard_map/ppermute | solution.py:352
  148.2 37.4 %collective-permute-start.11 = (bf16[256,704]{0,1:T(8,128)(2,1)S(1)}, bf16[256,704]{0,1:T(8,128)(2,1)}, u32[]{:S(2)}, u32[]{:S(2)}) collective-permute-start(bf16[256,704]{0,1:T(8,128)(2,1)S(1)} %slice.205), channel_id=1, source_target_pairs={{0,16},{16,0},{8,24},{24,8},{1,17},{17,1},{9,25},{25,9},{2,18},{18... | collective-permute-start | bytes 1081352 | tf_op jit(solution)/shard_map/ppermute | solution.py:351
  156.0 35.8 %copy-start.6 = (bf16[1,128,2048]{2,1,0:T(8,128)(2,1)S(1)}, bf16[1,128,2048]{2,1,0:T(8,128)(2,1)}, u32[]{:S(2)}) copy-start(bf16[1,128,2048]{2,1,0:T(8,128)(2,1)} %param.13) | copy-start | bytes 1572868
  195.5 92.6 %all-gather.8.cloned.1.call-start = ((), (), s32[]{:S(2)}) async-start(), calls=%async_computation.11 | async-start | bytes 4718592 | tf_op jit(solution)/shard_map/all_gather | solution.py:332
  196.1 143.0 %reduce-scatter.7.cloned.1.call-start = ((), (), s32[]{:S(2)}) async-start(), calls=%async_computation.12 | async-start | bytes 4718592 | tf_op jit(solution)/shard_map/reduce_scatter | solution.py:336
  197.3 16.1 %collective-permute-start.15 = (bf16[256,1408]{1,0:T(8,128)(2,1)S(1)}, bf16[256,1408]{1,0:T(8,128)(2,1)S(1)}, u32[]{:S(2)}, u32[]{:S(2)}) collective-permute-start(bf16[256,1408]{1,0:T(8,128)(2,1)S(1)} %slice.207), channel_id=1, source_target_pairs={{0,16},{16,0},{8,24},{24,8},{1,17},{17,1},{9,25},{25,9},{2,18},{18... | collective-permute-start | bytes 2162696 | tf_op jit(solution)/shard_map/ppermute | solution.py:351
  204.6 15.6 %collective-permute-start.16 = (bf16[256,1408]{1,0:T(8,128)(2,1)S(1)}, bf16[256,1408]{1,0:T(8,128)(2,1)S(1)}, u32[]{:S(2)}, u32[]{:S(2)}) collective-permute-start(bf16[256,1408]{1,0:T(8,128)(2,1)S(1)} %slice.208), channel_id=1, source_target_pairs={{0,8},{8,0},{16,24},{24,16},{1,9},{9,1},{17,25},{25,17},{2,10},{10... | collective-permute-start | bytes 2162696 | tf_op jit(solution)/shard_map/ppermute | solution.py:352
  288.2 101.4 %reduce-scatter.9.cloned.1.call-start = ((), (), s32[]{:S(2)}) async-start(), calls=%async_computation.13 | async-start | bytes 4718592 | tf_op jit(solution)/shard_map/reduce_scatter | solution.py:336
  311.8 129.7 %all-gather.10.cloned.1.call-start = ((), (), s32[]{:S(2)}) async-start(), calls=%async_computation.14 | async-start | bytes 4718592 | tf_op jit(solution)/shard_map/all_gather | solution.py:332
  313.2 7.0 %copy-start.49 = (bf16[1024,2048]{1,0:T(8,128)(2,1)S(1)}, bf16[1024,2048]{1,0:T(8,128)(2,1)}, u32[]{:S(2)}) copy-start(bf16[1024,2048]{1,0:T(8,128)(2,1)} %all-gather.6.cloned.1.call-done) | copy-start | bytes 12582916
  331.5 58.1 %copy-start.9 = (f32[128,2048]{1,0:T(8,128)S(1)}, f32[128,2048]{1,0:T(8,128)}, u32[]{:S(2)}) copy-start(f32[128,2048]{1,0:T(8,128)} %get-tuple-element.89) | copy-start | bytes 3145732
  339.1 50.6 %collective-permute-start.17 = (bf16[256,2112]{0,1:T(8,128)(2,1)}, bf16[256,2112]{0,1:T(8,128)(2,1)}, u32[]{:S(2)}, u32[]{:S(2)}) collective-permute-start(bf16[256,2112]{0,1:T(8,128)(2,1)} %pad_maximum_fusion.10), channel_id=1, source_target_pairs={{0,8},{8,0},{16,24},{24,16},{1,9},{9,1},{17,25},{25,17},{2,10},{10... | collective-permute-start | bytes 3244040 | tf_op jit(solution)/shard_map/ppermute | solution.py:389
  340.5 49.1 %collective-permute-start.18 = (bf16[256,2112]{0,1:T(8,128)(2,1)}, bf16[256,2112]{0,1:T(8,128)(2,1)}, u32[]{:S(2)}, u32[]{:S(2)}) collective-permute-start(bf16[256,2112]{0,1:T(8,128)(2,1)} %pad_maximum_fusion.11), channel_id=1, source_target_pairs={{0,16},{16,0},{8,24},{24,8},{1,17},{17,1},{9,25},{25,9},{2,18},{18... | collective-permute-start | bytes 3244040 | tf_op jit(solution)/shard_map/ppermute | solution.py:389
  342.0 47.6 %collective-permute-start.19 = (bf16[256,2112]{0,1:T(8,128)(2,1)}, bf16[256,2112]{0,1:T(8,128)(2,1)}, u32[]{:S(2)}, u32[]{:S(2)}) collective-permute-start(bf16[256,2112]{0,1:T(8,128)(2,1)} %pad_maximum_fusion.12), channel_id=1, source_target_pairs={{0,8},{8,0},{16,24},{24,16},{1,9},{9,1},{17,25},{25,17},{2,10},{10... | collective-permute-start | bytes 3244040 | tf_op jit(solution)/shard_map/ppermute | solution.py:389
  342.6 47.1 %collective-permute-start.20 = (bf16[256,2112]{0,1:T(8,128)(2,1)}, bf16[256,2112]{0,1:T(8,128)(2,1)}, u32[]{:S(2)}, u32[]{:S(2)}) collective-permute-start(bf16[256,2112]{0,1:T(8,128)(2,1)} %pad_maximum_fusion.13), channel_id=1, source_target_pairs={{0,16},{16,0},{8,24},{24,8},{1,17},{17,1},{9,25},{25,9},{2,18},{18... | collective-permute-start | bytes 3244040 | tf_op jit(solution)/shard_map/ppermute | solution.py:389
  395.5 23.8 %copy-start.28 = (bf16[256,704]{0,1:T(8,128)(2,1)S(1)}, bf16[256,704]{0,1:T(8,128)(2,1)}, u32[]{:S(2)}) copy-start(bf16[256,704]{0,1:T(8,128)(2,1)} %get-tuple-element.157) | copy-start | bytes 1081348
  395.5 23.8 %collective-permute-start.21 = (bf16[256,2112]{0,1:T(8,128)(2,1)S(1)}, bf16[256,2112]{0,1:T(8,128)(2,1)S(1)}, u32[]{:S(2)}, u32[]{:S(2)}) collective-permute-start(bf16[256,2112]{0,1:T(8,128)(2,1)S(1)} %add_convert_fusion.3), channel_id=1, source_target_pairs={{0,16},{16,0},{8,24},{24,8},{1,17},{17,1},{9,25},{25,9},{2,18},{18... | collective-permute-start | bytes 3244040 | tf_op jit(solution)/shard_map/ppermute | solution.py:413
  398.5 23.5 %collective-permute-start.22 = (bf16[256,2112]{0,1:T(8,128)(2,1)S(1)}, bf16[256,2112]{0,1:T(8,128)(2,1)S(1)}, u32[]{:S(2)}, u32[]{:S(2)}) collective-permute-start(bf16[256,2112]{0,1:T(8,128)(2,1)S(1)} %add_convert_fusion.1), channel_id=1, source_target_pairs={{0,8},{8,0},{16,24},{24,16},{1,9},{9,1},{17,25},{25,17},{2,10},{10... | collective-permute-start | bytes 3244040 | tf_op jit(solution)/shard_map/ppermute | solution.py:414
  426.5 58.8 %all-to-all-start.3 = ((bf16[8,64,2112]{2,1,0:T(8,128)(2,1)}), bf16[8,64,2112]{2,1,0:T(8,128)(2,1)S(1)}, u32[]{:S(2)}, u32[]{:S(2)}) async-start(bf16[8,64,2112]{2,1,0:T(8,128)(2,1)} %bitcast.112), calls=%async_computation.6 | async-start | bytes 4456448 | tf_op jit(solution)/shard_map/all_to_all | solution.py:340
  430.9 144.9 %reduce-scatter.11.cloned.1.call-start = ((), (), s32[]{:S(2)}) async-start(), calls=%async_computation.15 | async-start | bytes 4718592 | tf_op jit(solution)/shard_map/reduce_scatter | solution.py:336
  501.8 11.8 %collective-permute-start.23 = (bf16[2048,256]{0,1:T(8,128)(2,1)}, bf16[2048,256]{0,1:T(8,128)(2,1)S(1)}, u32[]{:S(2)}, u32[]{:S(2)}) collective-permute-start(bf16[2048,256]{0,1:T(8,128)(2,1)} %get-tuple-element.105), channel_id=1, source_target_pairs={{0,1},{1,0},{2,3},{3,2},{4,5},{5,4},{6,7},{7,6},{8,9},{9,8},{10,11... | collective-permute-start | bytes 3145736 | tf_op jit(solution)/shard_map/ppermute | solution.py:434
  505.6 6.4 %collective-permute-start.31 = (bf16[32,2048]{1,0:T(8,128)(2,1)S(1)}, bf16[32,2048]{1,0:T(8,128)(2,1)S(1)}, u32[]{:S(2)}, u32[]{:S(2)}) collective-permute-start(bf16[32,2048]{1,0:T(8,128)(2,1)S(1)} %get-tuple-element.185), channel_id=1, source_target_pairs={{0,8},{8,0},{16,24},{24,16},{1,9},{9,1},{17,25},{25,17},{2,10},{10... | collective-permute-start | bytes 393224 | tf_op jit(solution)/shard_map/ppermute | solution.py:389
  507.1 11.0 %collective-permute-start.30 = (bf16[32,2048]{1,0:T(8,128)(2,1)S(1)}, bf16[32,2048]{1,0:T(8,128)(2,1)S(1)}, u32[]{:S(2)}, u32[]{:S(2)}) collective-permute-start(bf16[32,2048]{1,0:T(8,128)(2,1)S(1)} %get-tuple-element.182), channel_id=1, source_target_pairs={{0,8},{8,0},{16,24},{24,16},{1,9},{9,1},{17,25},{25,17},{2,10},{10... | collective-permute-start | bytes 393224 | tf_op jit(solution)/shard_map/ppermute | solution.py:389
  507.7 11.0 %collective-permute-start.34 = (bf16[32,2048]{1,0:T(8,128)(2,1)S(1)}, bf16[32,2048]{1,0:T(8,128)(2,1)S(1)}, u32[]{:S(2)}, u32[]{:S(2)}) collective-permute-start(bf16[32,2048]{1,0:T(8,128)(2,1)S(1)} %get-tuple-element.183), channel_id=1, source_target_pairs={{0,16},{16,0},{8,24},{24,8},{1,17},{17,1},{9,25},{25,9},{2,18},{18... | collective-permute-start | bytes 393224 | tf_op jit(solution)/shard_map/ppermute | solution.py:389
  509.2 19.0 %collective-permute-start.33 = (bf16[32,2048]{1,0:T(8,128)(2,1)S(1)}, bf16[32,2048]{1,0:T(8,128)(2,1)S(1)}, u32[]{:S(2)}, u32[]{:S(2)}) collective-permute-start(bf16[32,2048]{1,0:T(8,128)(2,1)S(1)} %get-tuple-element.184), channel_id=1, source_target_pairs={{0,16},{16,0},{8,24},{24,8},{1,17},{17,1},{9,25},{25,9},{2,18},{18... | collective-permute-start | bytes 393224 | tf_op jit(solution)/shard_map/ppermute | solution.py:389
  512.1 6.6 %collective-permute-start.32 = (bf16[32,2048]{1,0:T(8,128)(2,1)S(1)}, bf16[32,2048]{1,0:T(8,128)(2,1)S(1)}, u32[]{:S(2)}, u32[]{:S(2)}) collective-permute-start(bf16[32,2048]{1,0:T(8,128)(2,1)S(1)} %add_convert_fusion.13), channel_id=1, source_target_pairs={{0,16},{16,0},{8,24},{24,8},{1,17},{17,1},{9,25},{25,9},{2,18},{18... | collective-permute-start | bytes 393224 | tf_op jit(solution)/shard_map/ppermute | solution.py:413
  516.6 9.2 %collective-permute-start.25 = (bf16[256,512]{0,1:T(8,128)(2,1)S(1)}, bf16[256,512]{0,1:T(8,128)(2,1)S(1)}, u32[]{:S(2)}, u32[]{:S(2)}) collective-permute-start(bf16[256,512]{0,1:T(8,128)(2,1)S(1)} %get-tuple-element.170), channel_id=1, source_target_pairs={{0,8},{8,0},{16,24},{24,16},{1,9},{9,1},{17,25},{25,17},{2,10},{10... | collective-permute-start | bytes 786440 | tf_op jit(solution)/shard_map/ppermute | solution.py:389
  518.2 8.3 %collective-permute-start.28 = (bf16[256,512]{0,1:T(8,128)(2,1)S(1)}, bf16[256,512]{0,1:T(8,128)(2,1)S(1)}, u32[]{:S(2)}, u32[]{:S(2)}) collective-permute-start(bf16[256,512]{0,1:T(8,128)(2,1)S(1)} %get-tuple-element.172), channel_id=1, source_target_pairs={{0,16},{16,0},{8,24},{24,8},{1,17},{17,1},{9,25},{25,9},{2,18},{18... | collective-permute-start | bytes 786440 | tf_op jit(solution)/shard_map/ppermute | solution.py:389
  518.8 10.9 %collective-permute-start.35 = (bf16[32,2048]{1,0:T(8,128)(2,1)S(1)}, bf16[32,2048]{1,0:T(8,128)(2,1)S(1)}, u32[]{:S(2)}, u32[]{:S(2)}) collective-permute-start(bf16[32,2048]{1,0:T(8,128)(2,1)S(1)} %get-tuple-element.181), channel_id=1, source_target_pairs={{0,8},{8,0},{16,24},{24,16},{1,9},{9,1},{17,25},{25,17},{2,10},{10... | collective-permute-start | bytes 393224 | tf_op jit(solution)/shard_map/ppermute | solution.py:414
  520.4 13.9 %collective-permute-start.24 = (bf16[256,512]{0,1:T(8,128)(2,1)S(1)}, bf16[256,512]{0,1:T(8,128)(2,1)S(1)}, u32[]{:S(2)}, u32[]{:S(2)}) collective-permute-start(bf16[256,512]{0,1:T(8,128)(2,1)S(1)} %get-tuple-element.169), channel_id=1, source_target_pairs={{0,8},{8,0},{16,24},{24,16},{1,9},{9,1},{17,25},{25,17},{2,10},{10... | collective-permute-start | bytes 786440 | tf_op jit(solution)/shard_map/ppermute | solution.py:389
  525.8 8.4 %collective-permute-start.27 = (bf16[256,512]{0,1:T(8,128)(2,1)S(1)}, bf16[256,512]{0,1:T(8,128)(2,1)S(1)}, u32[]{:S(2)}, u32[]{:S(2)}) collective-permute-start(bf16[256,512]{0,1:T(8,128)(2,1)S(1)} %get-tuple-element.171), channel_id=1, source_target_pairs={{0,16},{16,0},{8,24},{24,8},{1,17},{17,1},{9,25},{25,9},{2,18},{18... | collective-permute-start | bytes 786440 | tf_op jit(solution)/shard_map/ppermute | solution.py:389
  526.6 9.6 %collective-permute-start.26 = (bf16[256,512]{0,1:T(8,128)(2,1)S(1)}, bf16[256,512]{0,1:T(8,128)(2,1)S(1)}, u32[]{:S(2)}, u32[]{:S(2)}) collective-permute-start(bf16[256,512]{0,1:T(8,128)(2,1)S(1)} %get-tuple-element.173), channel_id=1, source_target_pairs={{0,16},{16,0},{8,24},{24,8},{1,17},{17,1},{9,25},{25,9},{2,18},{18... | collective-permute-start | bytes 786440 | tf_op jit(solution)/shard_map/ppermute | solution.py:413
  528.1 9.8 %collective-permute-start.29 = (bf16[256,512]{0,1:T(8,128)(2,1)S(1)}, bf16[256,512]{0,1:T(8,128)(2,1)S(1)}, u32[]{:S(2)}, u32[]{:S(2)}) collective-permute-start(bf16[256,512]{0,1:T(8,128)(2,1)S(1)} %get-tuple-element.174), channel_id=1, source_target_pairs={{0,8},{8,0},{16,24},{24,16},{1,9},{9,1},{17,25},{25,17},{2,10},{10... | collective-permute-start | bytes 786440 | tf_op jit(solution)/shard_map/ppermute | solution.py:414
  539.2 21.4 %all-to-all-start.4 = ((bf16[8,64,512]{2,1,0:T(8,128)(2,1)}), bf16[8,64,512]{2,1,0:T(8,128)(2,1)}, u32[]{:S(2)}, u32[]{:S(2)}) async-start(bf16[8,64,512]{2,1,0:T(8,128)(2,1)} %bitcast.24), calls=%async_computation.8 | async-start | bytes 1048576 | tf_op jit(solution)/shard_map/all_to_all | solution.py:340
  564.0 5.2 copy-start.21
  564.0 5.3 copy-start.48
  569.3 6.5 %copy-start.7 = (bf16[1,128,2048]{2,1,0:T(8,128)(2,1)S(1)}, bf16[1,128,2048]{2,1,0:T(8,128)(2,1)}, u32[]{:S(2)}) copy-start(bf16[1,128,2048]{2,1,0:T(8,128)(2,1)} %param.13) | copy-start | bytes 1572868
  (38 other events, 92.8 us)
Sparse Core Ops, SparseCore 0:
  9.6 72.8 all-gather.11
  142.1 49.5 reduce-scatter.4
  195.6 45.3 all-gather.5
  242.5 45.6 all-gather.7
  290.3 48.7 reduce-scatter.6
  341.2 48.3 reduce-scatter.8
  393.7 47.7 all-gather.9
  501.9 49.4 reduce-scatter.10

commit v5 on v4

--- a/solution.py
+++ b/solution.py
@@ -663,24 +663,6 @@
     down_pieces = jnp.concatenate(ff_slices(down_weight), axis=2)
     gate_up_pieces = jnp.concatenate([gate_main, up_main, gate_tail, up_tail], axis=2)
     attn_own = exchange_ctx(attn_pieces).reshape(8 * rows, 2 * head_width)
-    attn_own, down_pieces, gate_up_pieces = tie(attn_own, down_pieces, gate_up_pieces)
-    attn_cols = gather_seq(attn_own)
-    core = lax.axis_index("ctx") % 2
-    own_cols = attn_cols[:, head_width:]
-    other_cols = swap_cores(own_cols)
-    attn_cols = jnp.concatenate(
-        [
-            attn_cols[:, :head_width],
-            jnp.where(core == 0, own_cols, other_cols),
-            jnp.where(core == 0, other_cols, own_cols),
-        ],
-        axis=1,
-    )
-    out_rows = gather_seq(out_weight)
-    down_own = exchange_ctx(down_pieces).reshape(8 * rows, -1)
-    down_own, gate_up_pieces = tie(down_own, gate_up_pieces)
-    gate_up_own = exchange_ctx(gate_up_pieces).reshape(8 * rows, -1)
-
     edge = jnp.sum((segments[0] == 0).astype(jnp.int32))
     token = jnp.arange(length, dtype=jnp.int32)
     position = jnp.where(token < edge, token + (length - edge), token - edge)
@@ -688,15 +670,27 @@
     cosine = jnp.tile(cosine, (1, KV_HEADS))
     sine_table = jnp.tile(sine_table, (1, KV_HEADS))
     edge = edge[None]
+    attn_own, down_pieces, gate_up_pieces, cosine, sine_table = tie(
+        attn_own, down_pieces, gate_up_pieces, cosine, sine_table
+    )
+    attn_cols = gather_seq(attn_own)
+    core = lax.axis_index("ctx") % 2
+    other_cols = swap_cores(attn_cols[:, head_width:])
+    out_rows = gather_seq(out_weight)
+    down_own = exchange_ctx(down_pieces).reshape(8 * rows, -1)
+    down_own, gate_up_pieces = tie(down_own, gate_up_pieces)
+    gate_up_own = exchange_ctx(gate_up_pieces).reshape(8 * rows, -1)
 
     wide = inputs_all.astype(f32)
     shaped_all = (wide * rms_scale(wide)).astype(bf16)
     raw = jnp.dot(shaped_all, attn_cols, preferred_element_type=f32)
-    raw, down_own = tie(raw, down_own)
+    raw_other = jnp.dot(shaped_all, other_cols, preferred_element_type=f32)
+    raw, raw_other, down_own = tie(raw, raw_other, down_own)
+    raw_own = raw[:, head_width:]
     down_near = gather_seq_near(down_own)
     queries = turn(raw[:, :head_width], cosine, sine_table).astype(bf16)
-    keys = turn(raw[:, head_width : 2 * head_width], cosine, sine_table).astype(bf16)
-    values = raw[:, 2 * head_width :].astype(bf16)
+    keys = turn(jnp.where(core == 0, raw_own, raw_other), cosine, sine_table).astype(bf16)
+    values = jnp.where(core == 0, raw_other, raw_own).astype(bf16)
     queries = queries * jnp.asarray(score_scale, bf16)
     attn_low = attend(edge, queries, keys, values)
     attn_low, out_rows, back_late, gate_up_own, *down_near = tie(
@@ -762,27 +756,30 @@
     query_back, key_back, value_back = attend_back(
         edge, queries, keys, values, attn_back, score_scale
     )
+    key_low = turn(key_back, cosine, -sine_table).astype(bf16)
+    value_low = value_back.astype(bf16)
+    other_back = jnp.where(core == 0, value_low, key_low)
+    other_back, mlp_grad = tie(other_back, mlp_grad)
+    other_part = contract_rows(shaped_all, other_back).astype(bf16)
     heads_back = jnp.concatenate(
         [
             turn(query_back, cosine, -sine_table).astype(bf16),
-            turn(key_back, cosine, -sine_table).astype(bf16),
-            value_back.astype(bf16),
+            jnp.where(core == 0, key_low, value_low),
         ],
         axis=1,
     )
-    heads_back, mlp_grad = tie(heads_back, mlp_grad)
-    attn_full_grad = contract_rows(shaped_all, heads_back)
-    key_part = attn_full_grad[:, head_width : 2 * head_width]
-    value_part = attn_full_grad[:, 2 * head_width :]
-    other_part = jnp.where(core == 0, value_part, key_part).astype(bf16)
     heads_back, other_part = tie(heads_back, other_part)
     other_part = swap_cores(other_part)
-    weighted_part = contract_cols(heads_back, attn_cols).astype(bf16)
+    weighted_part = contract_cols(
+        jnp.concatenate([heads_back, other_back], axis=1),
+        jnp.concatenate([attn_cols, other_cols], axis=1),
+    ).astype(bf16)
     weighted_part, low_all = tie(weighted_part, low_all)
     weighted_one = reduce_ctx(weighted_part).astype(f32)
-    own_part = jnp.where(core == 0, key_part, value_part) + other_part.astype(f32)
+    attn_part = contract_rows(shaped_all, heads_back)
+    own_part = attn_part[:, head_width:] + other_part.astype(f32)
     attn_grad_own = reduce_seq(
-        [jnp.concatenate([attn_full_grad[:, :head_width].astype(bf16), own_part.astype(bf16)], axis=1)]
+        [jnp.concatenate([attn_part[:, :head_width].astype(bf16), own_part.astype(bf16)], axis=1)]
     )
     out_grad = reduce_seq([contract_rows(attn_low, low_all).astype(bf16)]).astype(f32)
     attn_grad_own, mlp_grad = tie(attn_grad_own, mlp_grad)

time: 594 us -> 586 us (0.987)
  waiting for transfers between devices: 244 us -> 224 us
  local copies, waits for them, and re-layouts: 97.8 us -> 106 us
    all_gather x4, waiting for transfers between devices: 55.9 us -> 48.4 us  [gather_ctx(): return lax.all_gather(block, 'ctx', axis=0, tiled=True)]
    ppermute x4, waiting for transfers between devices: 7.91 us -> 1.05 us  [gather_seq_far(): far_top = lax.ppermute(from_x[:half], 'seq', SEQ_Y)]
    all_to_all x5, waiting for transfers between devices: 46 us -> 39.2 us  [exchange_ctx(): return lax.all_to_all(pieces, 'ctx', 0, 0, tiled=True)]
    unnamed x105 -> x95, local copies, waits for them, and re-layouts: 14.8 us -> 10.4 us
    dot_general x4 -> x5, matrix products: 21.8 us -> 20.7 us  [contract_rows(): lax.dot_general(left, right, (((0,), (0,)), ((), ())), preferred_element_...]
  transfers between devices with their start and end apart: 49 -> 49, of which waited for: 24 -> 23; matrix products, arithmetic and copies ran while one was open for 33% -> 36% of each run, Pallas kernels for 6% -> 6%
where the time goes in v5:
time: 586 us; the launch traced here: 578 us
  waiting for transfers between devices  224 us (38%)
  local copies, waits for them, and re-layouts  106 us (18%)
  matrix products  83 us (14%)
  starting transfers between devices  58.6 us (10%)
  other arithmetic  56.5 us (10%)
  Pallas kernels  33.5 us (6%)
  between operations  16.1 us (3%)
    reduce_scatter x4, waiting for transfers between devices, reduce_ctx(): return lax.psum_scatter(partial, 'ctx', scatter_dimension=0, tiled=True)  53 us
    all_gather x4, waiting for transfers between devices, gather_ctx(): return lax.all_gather(block, 'ctx', axis=0, tiled=True)  48.4 us
    all_to_all x5, waiting for transfers between devices, exchange_ctx(): return lax.all_to_all(pieces, 'ctx', 0, 0, tiled=True)  39.2 us
    ppermute x4, waiting for transfers between devices, gather_seq_far(): far_low = lax.ppermute(from_y[half:], 'seq', SEQ_X)  35 us
    dot_general x4, matrix products, contract_cols(): lax.dot_general(left, right, (((1,), (1,)), ((), ())), preferred_element_...  29.3 us
    dynamic_update_slice x20, local copies, waits for them, and re-layouts, gather_seq_far(): whole = lax.dynamic_update_slice_in_dim(whole, piece, start, 0)  25.5 us
    ppermute x3, waiting for transfers between devices, reduce_seq_far(): top_last = lax.ppermute(top_send, 'seq', SEQ_Y)  24.4 us
    all_to_all x5, starting transfers between devices, exchange_ctx(): return lax.all_to_all(pieces, 'ctx', 0, 0, tiled=True)  22.1 us
  transfers between devices with their start and end apart: 49, of which 23 were waited for; matrix products, arithmetic and copies ran while one was open for 36% of the time, Pallas kernels for 6%

profile of v5, /device:TPU:0, one launch (start us, length us, event | category | flops | bytes accessed | tf_op | source)
XLA Modules:
  0.0 578.4 jit_solution(11635463959003251421)
XLA Ops:
  7.9 3.1 collective-permute-start.6
  16.3 5.0 all-to-all-start
  27.7 2.2 concatenate.109
  35.2 16.1 %all-to-all-done = bf16[8,64,512]{2,1,0:T(8,128)(2,1)} async-done(((bf16[8,64,512]{2,1,0:T(8,128)(2,1)}), bf16[8,64,512]{2,1,0:T(8,128)(2,1)}, u32[]{:S(2)}, u32[]{:S(2)}) %all-to-all-start) | async-done | bytes 524320 | tf_op jit(solution)/shard_map/all_to_all | solution.py:340
  52.5 3.5 all-to-all-start.1
  58.8 11.7 %collective-permute-done = bf16[512,512]{1,0:T(8,128)(2,1)S(1)} collective-permute-done((bf16[512,512]{1,0:T(8,128)(2,1)}, bf16[512,512]{1,0:T(8,128)(2,1)S(1)}, u32[]{:S(2)}, u32[]{:S(2)}) %collective-permute-start) | collective-permute-done | bytes 524320 | tf_op jit(solution)/shard_map/ppermute | solution.py:344
  72.8 1.9 constant_dynamic-update-slice_fusion.19
  82.6 2.7 collective-permute-done.3
  86.1 2.3 slice.227
  88.4 2.6 copy.80
  91.0 4.6 all-to-all-start.2
  96.0 3.2 fusion
  99.5 5.3 fusion.68
  104.8 3.5 fusion.66
  118.2 13.6 %attend.1 = bf16[1024,256]{1,0:T(8,128)(2,1)} custom-call(s32[1]{0:T(128)} %bitcast.1.refs_0_, bf16[1024,256]{1,0:T(8,128)(2,1)} %get-tuple-element.168.refs_1_, bf16[1024,256]{1,0:T(8,128)(2,1)} %fusion.30.refs_2_, bf16[1024,256]{1,0:T(8,128)(2,1)} %get-tuple-element.167.refs_3_), custom_call_target="tpu_custom_call" | custom-call | flops 4294967296 | bytes 2097152 | tf_op jit(solution)/shard_map/attend/pallas_call | solution.py:581
  131.9 4.6 convolution_convert_fusion.2
  143.5 1.9 broadcast_in_dim.33
  147.7 2.3 copy.84
  151.0 2.2 constant_dynamic-update-slice_fusion.7
  153.1 25.3 %collective-permute-done.12 = bf16[256,704]{0,1:T(8,128)(2,1)} collective-permute-done((bf16[256,704]{0,1:T(8,128)(2,1)}, bf16[256,704]{0,1:T(8,128)(2,1)}, u32[]{:S(2)}, u32[]{:S(2)}) %collective-permute-start.12) | collective-permute-done | bytes 360480 | tf_op jit(solution)/shard_map/ppermute | solution.py:352
  182.3 4.8 reduce-scatter.5.cloned.1.call-done
  188.6 2.4 fusion.73
  194.3 2.9 broadcast_in_dim.34
  197.2 2.8 constant_dynamic-update-slice_fusion.4
  202.5 2.6 constant_dynamic-update-slice_fusion.3
  205.1 2.6 constant_dynamic-update-slice_fusion.2
  209.7 7.0 %collective-permute-done.16 = bf16[256,1408]{1,0:T(8,128)(2,1)S(1)} collective-permute-done((bf16[256,1408]{1,0:T(8,128)(2,1)S(1)}, bf16[256,1408]{1,0:T(8,128)(2,1)S(1)}, u32[]{:S(2)}, u32[]{:S(2)}) %collective-permute-start.16) | collective-permute-done | bytes 720928 | tf_op jit(solution)/shard_map/ppermute | solution.py:352
  217.7 18.8 %all-gather.6.cloned.1.call-done = bf16[1024,2048]{1,0:T(8,128)(2,1)} async-done(((bf16[128,2048]{1,0:T(8,128)(2,1)}), bf16[1024,2048]{1,0:T(8,128)(2,1)}) %all-gather.6.cloned.1.call-update) | async-done | bytes 4194320 | tf_op jit(solution)/shard_map/all_gather | solution.py:332
  236.4 10.6 %fusion.86 = f32[1024,1408]{1,0:T(8,128)S(1)} fusion(bf16[1024,2048]{1,0:T(8,128)(2,1)} %all-gather.6.cloned.1.call-done, bf16[2048,1408]{1,0:T(8,128)(2,1)} %constant_dynamic-update-slice_fusion), kind=kOutput, calls=%fused_computation.239 | convolution fusion | flops 5905580032 | bytes 15728640 | tf_op jit(solution)/shard_map/dot_general | solution.py:712
  252.1 7.0 %convolution_convert_fusion.4 = bf16[1024,2048]{1,0:T(8,128)(2,1)} fusion(bf16[1024,704]{1,0:T(8,128)(2,1)S(1)} %multiply_convert_fusion.2, bf16[2048,704]{1,0:T(8,128)(2,1)} %constant_dynamic-update-slice_fusion.5), kind=kOutput, calls=%fused_computation.24 | convolution fusion | flops 2954887168 | bytes 8519680 | tf_op jit(solution)/shard_map/dot_general | solution.py:53
  259.1 24.5 %all-gather.8.cloned.1.call-done = bf16[1024,2048]{1,0:T(8,128)(2,1)} async-done(((bf16[128,2048]{1,0:T(8,128)(2,1)}), bf16[1024,2048]{1,0:T(8,128)(2,1)}) %all-gather.8.cloned.1.call-update) | async-done | bytes 4194320 | tf_op jit(solution)/shard_map/all_gather | solution.py:332
  283.7 8.8 %multiply_convert_fusion = (bf16[1024,704]{1,0:T(8,128)(2,1)S(1)}, bf16[1024,704]{1,0:T(8,128)(2,1)S(1)}) fusion(f32[1024,64]{1,0:T(8,128)S(1)} %get-tuple-element.143, f32[1024,640]{1,0:T(8,128)} %copy-done.5, f32[1024,64]{1,0:T(8,128)S(1)} %get-tuple-element.144, f32[1024,640]{1,0:T(8,128)} %copy-done.6, ...), kind=kOutput, calls=%fused_computation.31 | convolution fusion | flops 2963603456 | bytes 15728640 | tf_op jit(solution)/shard_map/dot_general | solution.py:729
  295.2 5.1 concatenate.118
  300.3 11.0 %convolution_convert_fusion.1 = bf16[1024,2048]{1,0:T(8,128)(2,1)} fusion(bf16[1024,1408]{1,0:T(8,128)(2,1)} %concatenate.118, bf16[2048,1408]{1,0:T(8,128)(2,1)} %constant_dynamic-update-slice_fusion), kind=kOutput, calls=%fused_computation.21 | convolution fusion | flops 5907677184 | bytes 12845056 | tf_op jit(solution)/shard_map/dot_general | solution.py:53
  311.6 6.1 %convolution_convert_fusion.5 = bf16[2048,704]{0,1:T(8,128)(2,1)S(1)} fusion(bf16[1024,2048]{1,0:T(8,128)(2,1)} %all-gather.8.cloned.1.call-done, bf16[1024,704]{1,0:T(8,128)(2,1)} %copy-done.26), kind=kOutput, calls=%fused_computation.25 | convolution fusion | flops 2954231808 | bytes 8519680 | tf_op jit(solution)/shard_map/dot_general | solution.py:47
  320.0 6.6 %convolution_convert_fusion = bf16[2048,1408]{0,1:T(8,128)(2,1)S(1)} fusion(bf16[1024,2048]{1,0:T(8,128)(2,1)S(1)} %copy-done.44, bf16[1024,1408]{1,0:T(8,128)(2,1)S(1)} %copy-done.17), kind=kOutput, calls=%fused_computation.4 | convolution fusion | flops 5908463616 | bytes 12845056 | tf_op jit(solution)/shard_map/dot_general | solution.py:47
  326.6 2.1 constant_dynamic-slice_fusion.11
  338.6 46.5 %reduce-scatter.9.cloned.1.call-done = bf16[128,2048]{1,0:T(8,128)(2,1)} async-done(((bf16[1024,2048]{1,0:T(8,128)(2,1)}), bf16[128,2048]{1,0:T(8,128)(2,1)}) %reduce-scatter.9.cloned.1.call-update) | async-done | bytes 524304 | tf_op jit(solution)/shard_map/reduce_scatter | solution.py:336
  386.3 2.7 fusion.71
  395.5 19.2 %collective-permute-done.21 = bf16[256,2112]{0,1:T(8,128)(2,1)S(1)} collective-permute-done((bf16[256,2112]{0,1:T(8,128)(2,1)S(1)}, bf16[256,2112]{0,1:T(8,128)(2,1)S(1)}, u32[]{:S(2)}, u32[]{:S(2)}) %collective-permute-start.21) | collective-permute-done | bytes 1081376 | tf_op jit(solution)/shard_map/ppermute | solution.py:413
  414.8 1.9 add_convert_fusion.2
  420.8 4.1 copy.92
  424.9 4.5 all-to-all-start.3
  429.5 5.1 all-gather.10.cloned.1.call-done
  434.6 4.3 convolution_convert_fusion.8.refs_4_
  438.9 19.9 %attend_back.1 = (f32[1024,256]{1,0:T(8,128)}, f32[1024,256]{1,0:T(8,128)}, f32[1024,256]{1,0:T(8,128)}) custom-call(s32[1]{0:T(128)} %bitcast.1.refs_0_, bf16[1024,256]{1,0:T(8,128)(2,1)} %get-tuple-element.168.refs_1_, bf16[1024,256]{1,0:T(8,128)(2,1)} %fusion.30.refs_2_, bf16[1024,256]{1,0:T(8,128)(2,1)} %get-tuple-element.167.refs_3_, ...), custom_call_target="tpu_custom_call" | custom-call | flops 10737418240 | bytes 3670016 | tf_op jit(solution)/shard_map/attend_back/pallas_call | solution.py:602
  458.8 2.4 fusion.79
  467.4 14.0 %all-to-all-done.3 = bf16[8,64,2112]{2,1,0:T(8,128)(2,1)} async-done(((bf16[8,64,2112]{2,1,0:T(8,128)(2,1)}), bf16[8,64,2112]{2,1,0:T(8,128)(2,1)}, u32[]{:S(2)}, u32[]{:S(2)}) %all-to-all-start.3) | async-done | bytes 2162720 | tf_op jit(solution)/shard_map/all_to_all | solution.py:340
  481.3 2.6 fusion.34
  486.6 7.1 %convolution_convert_fusion.3 = bf16[1024,2048]{1,0:T(8,128)(2,1)} fusion(bf16[2048,256]{1,0:T(8,128)(2,1)} %collective-permute-done.4, bf16[2048,512]{1,0:T(8,128)(2,1)} %constant_dynamic-update-slice_fusion.15, bf16[1024,256]{1,0:T(8,128)(2,1)S(1)} %copy-done.32, bf16[1024,512]{1,0:T(8,128)(2,1)S(1)} %pad_maximum_fusion.10), kind=kOutput, calls=%fused_computation.23 | convolution fusion | flops 3232759808 | bytes 8912896 | tf_op jit(solution)/shard_map/dot_general | solution.py:53
  494.7 3.6 convolution_convert_fusion.6
  502.5 2.6 fusion.63
  510.4 2.6 collective-permute-done.32
  515.1 2.6 collective-permute-done.25
  522.0 4.2 collective-permute-done.24
  526.2 2.6 collective-permute-done.26
  530.5 4.4 all-to-all-start.4
  534.8 2.0 convert_element_type.353
  542.9 9.1 %all-to-all-done.4 = bf16[8,64,512]{2,1,0:T(8,128)(2,1)} async-done(((bf16[8,64,512]{2,1,0:T(8,128)(2,1)}), bf16[8,64,512]{2,1,0:T(8,128)(2,1)}, u32[]{:S(2)}, u32[]{:S(2)}) %all-to-all-start.4) | async-done | bytes 524320 | tf_op jit(solution)/shard_map/all_to_all | solution.py:340
  552.0 1.9 fusion.85
  555.4 2.9 copy.114
  558.3 2.4 reshape.172
  560.8 3.5 broadcast_multiply_fusion
  568.6 2.7 fusion.21
  (311 shorter events, 137.6 us)
Async XLA Ops:
  7.2 8.1 %copy-start.37 = (bf16[64,256]{1,0:T(8,128)(2,1)S(1)}, bf16[64,256]{1,0:T(8,128)(2,1)}, u32[]{:S(2)}) copy-start(bf16[64,256]{1,0:T(8,128)(2,1)} %param.19) | copy-start | bytes 98308
  7.2 8.1 %copy-start.35 = (bf16[64,256]{1,0:T(8,128)(2,1)S(1)}, bf16[64,256]{1,0:T(8,128)(2,1)}, u32[]{:S(2)}) copy-start(bf16[64,256]{1,0:T(8,128)(2,1)} %param.18) | copy-start | bytes 98308
  7.2 88.8 %all-gather.12.cloned.1.call-start = ((), (), s32[]{:S(2)}) async-start(), calls=%async_computation.16 | async-start | bytes 4718592 | tf_op jit(solution)/shard_map/all_gather | solution.py:332
  7.9 22.1 %collective-permute-start.6 = (bf16[64,2048]{1,0:T(8,128)(2,1)}, bf16[64,2048]{1,0:T(8,128)(2,1)}, u32[]{:S(2)}, u32[]{:S(2)}) collective-permute-start(bf16[64,2048]{1,0:T(8,128)(2,1)} %param.20), channel_id=1, source_target_pairs={{0,16},{16,0},{8,24},{24,8},{1,17},{17,1},{9,25},{25,9},{2,18},{18... | collective-permute-start | bytes 786440 | tf_op jit(solution)/shard_map/ppermute | solution.py:344
  11.0 21.1 %collective-permute-start.5 = (bf16[64,2048]{1,0:T(8,128)(2,1)}, bf16[64,2048]{1,0:T(8,128)(2,1)}, u32[]{:S(2)}, u32[]{:S(2)}) collective-permute-start(bf16[64,2048]{1,0:T(8,128)(2,1)} %param.20), channel_id=1, source_target_pairs={{0,8},{8,0},{16,24},{24,16},{1,9},{9,1},{17,25},{25,17},{2,10},{10... | collective-permute-start | bytes 786440 | tf_op jit(solution)/shard_map/ppermute | solution.py:344
  15.3 6.0 %slice-start = ((bf16[64,5632]{1,0:T(8,128)(2,1)}), bf16[64,512]{1,0:T(8,128)(2,1)S(1)}, s32[]{:S(2)}) async-start(bf16[64,5632]{1,0:T(8,128)(2,1)} %param.24), calls=%async_computation.17 | async-start | bytes 131072 | tf_op jit(solution)/shard_map/slice | solution.py:447
  15.4 6.8 %slice-start.1 = ((bf16[64,5632]{1,0:T(8,128)(2,1)}), bf16[64,5120]{1,0:T(8,128)(2,1)S(1)}, s32[]{:S(2)}) async-start(bf16[64,5632]{1,0:T(8,128)(2,1)} %param.24), calls=%async_computation.18 | async-start | bytes 1310720 | tf_op jit(solution)/shard_map/slice | solution.py:446
  16.3 8.5 %copy-start.18 = (bf16[64,5632]{1,0:T(8,128)(2,1)S(1)}, bf16[64,5632]{1,0:T(8,128)(2,1)}, u32[]{:S(2)}) copy-start(bf16[64,5632]{1,0:T(8,128)(2,1)} %param.23) | copy-start | bytes 2162692
  16.3 8.5 %copy-start.19 = (bf16[64,5632]{1,0:T(8,128)(2,1)S(1)}, bf16[64,5632]{1,0:T(8,128)(2,1)}, u32[]{:S(2)}) copy-start(bf16[64,5632]{1,0:T(8,128)(2,1)} %param.22) | copy-start | bytes 2162692
  16.3 35.0 %all-to-all-start = ((bf16[8,64,512]{2,1,0:T(8,128)(2,1)}), bf16[8,64,512]{2,1,0:T(8,128)(2,1)}, u32[]{:S(2)}, u32[]{:S(2)}) async-start(bf16[8,64,512]{2,1,0:T(8,128)(2,1)} %pad_maximum_fusion.12), calls=%async_computation | async-start | bytes 1048576 | tf_op jit(solution)/shard_map/all_to_all | solution.py:340
  31.6 27.2 %collective-permute-start.8 = (bf16[32,2048]{1,0:T(8,128)(2,1)}, bf16[32,2048]{1,0:T(8,128)(2,1)S(1)}, u32[]{:S(2)}, u32[]{:S(2)}) collective-permute-start(bf16[32,2048]{1,0:T(8,128)(2,1)} %slice.233), channel_id=1, source_target_pairs={{0,8},{8,0},{16,24},{24,16},{1,9},{9,1},{17,25},{25,17},{2,10},{10... | collective-permute-start | bytes 393224 | tf_op jit(solution)/shard_map/ppermute | solution.py:352
  33.7 24.2 %collective-permute-start.7 = (bf16[32,2048]{1,0:T(8,128)(2,1)}, bf16[32,2048]{1,0:T(8,128)(2,1)}, u32[]{:S(2)}, u32[]{:S(2)}) collective-permute-start(bf16[32,2048]{1,0:T(8,128)(2,1)} %slice.232), channel_id=1, source_target_pairs={{0,16},{16,0},{8,24},{24,8},{1,17},{17,1},{9,25},{25,9},{2,18},{18... | collective-permute-start | bytes 393224 | tf_op jit(solution)/shard_map/ppermute | solution.py:351
  52.5 35.8 %all-to-all-start.1 = ((bf16[8,64,704]{2,1,0:T(8,128)(2,1)}), bf16[8,64,704]{2,1,0:T(8,128)(2,1)S(1)}, u32[]{:S(2)}, u32[]{:S(2)}) async-start(bf16[8,64,704]{2,1,0:T(8,128)(2,1)} %pad_maximum_fusion.11), calls=%async_computation.1 | async-start | bytes 1572864 | tf_op jit(solution)/shard_map/all_to_all | solution.py:340
  56.1 14.4 %collective-permute-start = (bf16[512,512]{1,0:T(8,128)(2,1)}, bf16[512,512]{1,0:T(8,128)(2,1)S(1)}, u32[]{:S(2)}, u32[]{:S(2)}) collective-permute-start(bf16[512,512]{1,0:T(8,128)(2,1)} %bitcast.8), channel_id=1, source_target_pairs={{0,8},{8,0},{16,24},{24,16},{1,9},{9,1},{17,25},{25,17},{2,10},{10... | collective-permute-start | bytes 1572872 | tf_op jit(solution)/shard_map/ppermute | solution.py:344
  57.3 19.4 %collective-permute-start.1 = (bf16[512,512]{1,0:T(8,128)(2,1)}, bf16[512,512]{1,0:T(8,128)(2,1)}, u32[]{:S(2)}, u32[]{:S(2)}) collective-permute-start(bf16[512,512]{1,0:T(8,128)(2,1)} %bitcast.8), channel_id=1, source_target_pairs={{0,16},{16,0},{8,24},{24,8},{1,17},{17,1},{9,25},{25,9},{2,18},{18... | collective-permute-start | bytes 1572872 | tf_op jit(solution)/shard_map/ppermute | solution.py:344
  58.8 14.0 %copy-start.15 = (bf16[256,2048]{1,0:T(8,128)(2,1)}, bf16[256,2048]{1,0:T(8,128)(2,1)S(1)}, u32[]{:S(2)}) copy-start(bf16[256,2048]{1,0:T(8,128)(2,1)S(1)} %constant_dynamic-update-slice_fusion.10) | copy-start | bytes 3145732
  71.3 9.7 %collective-permute-start.2 = (bf16[256,512]{1,0:T(8,128)(2,1)}, bf16[256,512]{1,0:T(8,128)(2,1)}, u32[]{:S(2)}, u32[]{:S(2)}) collective-permute-start(bf16[256,512]{1,0:T(8,128)(2,1)} %slice.225), channel_id=1, source_target_pairs={{0,16},{16,0},{8,24},{24,8},{1,17},{17,1},{9,25},{25,9},{2,18},{18... | collective-permute-start | bytes 786440 | tf_op jit(solution)/shard_map/ppermute | solution.py:351
  77.6 7.7 %collective-permute-start.3 = (bf16[256,512]{1,0:T(8,128)(2,1)S(1)}, bf16[256,512]{1,0:T(8,128)(2,1)S(1)}, u32[]{:S(2)}, u32[]{:S(2)}) collective-permute-start(bf16[256,512]{1,0:T(8,128)(2,1)S(1)} %slice.226), channel_id=1, source_target_pairs={{0,8},{8,0},{16,24},{24,16},{1,9},{9,1},{17,25},{25,17},{2,10},{10... | collective-permute-start | bytes 786440 | tf_op jit(solution)/shard_map/ppermute | solution.py:352
  88.4 16.4 %collective-permute-start.4 = (bf16[2048,256]{1,0:T(8,128)(2,1)}, bf16[2048,256]{1,0:T(8,128)(2,1)}, u32[]{:S(2)}, u32[]{:S(2)}) collective-permute-start(bf16[2048,256]{1,0:T(8,128)(2,1)} %slice.227), channel_id=1, source_target_pairs={{0,1},{1,0},{2,3},{3,2},{4,5},{5,4},{6,7},{7,6},{8,9},{9,8},{10,11... | collective-permute-start | bytes 3145736 | tf_op jit(solution)/shard_map/ppermute | solution.py:434
  91.0 40.9 %all-to-all-start.2 = ((bf16[8,64,1408]{2,1,0:T(8,128)(2,1)}), bf16[8,64,1408]{2,1,0:T(8,128)(2,1)}, u32[]{:S(2)}, u32[]{:S(2)}) async-start(bf16[8,64,1408]{2,1,0:T(8,128)(2,1)} %copy.80), calls=%async_computation.2 | async-start | bytes 2883584 | tf_op jit(solution)/shard_map/all_to_all | solution.py:340
  95.6 91.6 %reduce-scatter.5.cloned.1.call-start = ((), (), s32[]{:S(2)}) async-start(), calls=%async_computation.9 | async-start | bytes 4718592 | tf_op jit(solution)/shard_map/reduce_scatter | solution.py:336
  109.4 22.5 %collective-permute-start.10 = (bf16[512,704]{0,1:T(8,128)(2,1)}, bf16[512,704]{0,1:T(8,128)(2,1)}, u32[]{:S(2)}, u32[]{:S(2)}) collective-permute-start(bf16[512,704]{0,1:T(8,128)(2,1)} %copy.81), channel_id=1, source_target_pairs={{0,16},{16,0},{8,24},{24,8},{1,17},{17,1},{9,25},{25,9},{2,18},{18... | collective-permute-start | bytes 2162696 | tf_op jit(solution)/shard_map/ppermute | solution.py:344
  111.1 20.8 %collective-permute-start.9 = (bf16[512,704]{0,1:T(8,128)(2,1)}, bf16[512,704]{0,1:T(8,128)(2,1)}, u32[]{:S(2)}, u32[]{:S(2)}) collective-permute-start(bf16[512,704]{0,1:T(8,128)(2,1)} %copy.81), channel_id=1, source_target_pairs={{0,8},{8,0},{16,24},{24,16},{1,9},{9,1},{17,25},{25,17},{2,10},{10... | collective-permute-start | bytes 2162696 | tf_op jit(solution)/shard_map/ppermute | solution.py:344
  136.6 99.9 %all-gather.6.cloned.1.call-start = ((), (), s32[]{:S(2)}) async-start(), calls=%async_computation.10 | async-start | bytes 4718592 | tf_op jit(solution)/shard_map/all_gather | solution.py:332
  136.6 45.7 %collective-permute-start.14 = (bf16[512,1408]{1,0:T(8,128)(2,1)}, bf16[512,1408]{1,0:T(8,128)(2,1)}, u32[]{:S(2)}, u32[]{:S(2)}) collective-permute-start(bf16[512,1408]{1,0:T(8,128)(2,1)} %bitcast.19), channel_id=1, source_target_pairs={{0,16},{16,0},{8,24},{24,8},{1,17},{17,1},{9,25},{25,9},{2,18},{18... | collective-permute-start | bytes 4325384 | tf_op jit(solution)/shard_map/ppermute | solution.py:344
  137.2 45.1 %collective-permute-start.13 = (bf16[512,1408]{1,0:T(8,128)(2,1)}, bf16[512,1408]{1,0:T(8,128)(2,1)}, u32[]{:S(2)}, u32[]{:S(2)}) collective-permute-start(bf16[512,1408]{1,0:T(8,128)(2,1)} %bitcast.19), channel_id=1, source_target_pairs={{0,8},{8,0},{16,24},{24,16},{1,9},{9,1},{17,25},{25,17},{2,10},{10... | collective-permute-start | bytes 4325384 | tf_op jit(solution)/shard_map/ppermute | solution.py:344
  141.3 37.1 %collective-permute-start.12 = (bf16[256,704]{0,1:T(8,128)(2,1)}, bf16[256,704]{0,1:T(8,128)(2,1)}, u32[]{:S(2)}, u32[]{:S(2)}) collective-permute-start(bf16[256,704]{0,1:T(8,128)(2,1)} %slice.190), channel_id=1, source_target_pairs={{0,8},{8,0},{16,24},{24,16},{1,9},{9,1},{17,25},{25,17},{2,10},{10... | collective-permute-start | bytes 1081352 | tf_op jit(solution)/shard_map/ppermute | solution.py:352
  142.0 37.6 %collective-permute-start.11 = (bf16[256,704]{0,1:T(8,128)(2,1)S(1)}, bf16[256,704]{0,1:T(8,128)(2,1)}, u32[]{:S(2)}, u32[]{:S(2)}) collective-permute-start(bf16[256,704]{0,1:T(8,128)(2,1)S(1)} %slice.189), channel_id=1, source_target_pairs={{0,16},{16,0},{8,24},{24,8},{1,17},{17,1},{9,25},{25,9},{2,18},{18... | collective-permute-start | bytes 1081352 | tf_op jit(solution)/shard_map/ppermute | solution.py:351
  151.0 36.2 %copy-start.3 = (bf16[1,128,2048]{2,1,0:T(8,128)(2,1)S(1)}, bf16[1,128,2048]{2,1,0:T(8,128)(2,1)}, u32[]{:S(2)}) copy-start(bf16[1,128,2048]{2,1,0:T(8,128)(2,1)} %param.13) | copy-start | bytes 1572868
  191.0 92.6 %all-gather.8.cloned.1.call-start = ((), (), s32[]{:S(2)}) async-start(), calls=%async_computation.11 | async-start | bytes 4718592 | tf_op jit(solution)/shard_map/all_gather | solution.py:332
  191.5 143.0 %reduce-scatter.7.cloned.1.call-start = ((), (), s32[]{:S(2)}) async-start(), calls=%async_computation.12 | async-start | bytes 4718592 | tf_op jit(solution)/shard_map/reduce_scatter | solution.py:336
  192.8 16.1 %collective-permute-start.15 = (bf16[256,1408]{1,0:T(8,128)(2,1)S(1)}, bf16[256,1408]{1,0:T(8,128)(2,1)S(1)}, u32[]{:S(2)}, u32[]{:S(2)}) collective-permute-start(bf16[256,1408]{1,0:T(8,128)(2,1)S(1)} %slice.191), channel_id=1, source_target_pairs={{0,16},{16,0},{8,24},{24,8},{1,17},{17,1},{9,25},{25,9},{2,18},{18... | collective-permute-start | bytes 2162696 | tf_op jit(solution)/shard_map/ppermute | solution.py:351
  201.1 15.6 %collective-permute-start.16 = (bf16[256,1408]{1,0:T(8,128)(2,1)S(1)}, bf16[256,1408]{1,0:T(8,128)(2,1)S(1)}, u32[]{:S(2)}, u32[]{:S(2)}) collective-permute-start(bf16[256,1408]{1,0:T(8,128)(2,1)S(1)} %slice.192), channel_id=1, source_target_pairs={{0,8},{8,0},{16,24},{24,16},{1,9},{9,1},{17,25},{25,17},{2,10},{10... | collective-permute-start | bytes 2162696 | tf_op jit(solution)/shard_map/ppermute | solution.py:352
  283.6 101.4 %reduce-scatter.9.cloned.1.call-start = ((), (), s32[]{:S(2)}) async-start(), calls=%async_computation.13 | async-start | bytes 4718592 | tf_op jit(solution)/shard_map/reduce_scatter | solution.py:336
  311.3 123.3 %all-gather.10.cloned.1.call-start = ((), (), s32[]{:S(2)}) async-start(), calls=%async_computation.14 | async-start | bytes 4718592 | tf_op jit(solution)/shard_map/all_gather | solution.py:332
  311.6 7.4 %copy-start.44 = (bf16[1024,2048]{1,0:T(8,128)(2,1)S(1)}, bf16[1024,2048]{1,0:T(8,128)(2,1)}, u32[]{:S(2)}) copy-start(bf16[1024,2048]{1,0:T(8,128)(2,1)} %all-gather.6.cloned.1.call-done) | copy-start | bytes 12582916
  330.8 54.3 %copy-start.7 = (f32[128,2048]{1,0:T(8,128)S(1)}, f32[128,2048]{1,0:T(8,128)}, u32[]{:S(2)}) copy-start(f32[128,2048]{1,0:T(8,128)} %get-tuple-element.95) | copy-start | bytes 3145732
  334.5 50.6 %collective-permute-start.17 = (bf16[256,2112]{0,1:T(8,128)(2,1)}, bf16[256,2112]{0,1:T(8,128)(2,1)}, u32[]{:S(2)}, u32[]{:S(2)}) collective-permute-start(bf16[256,2112]{0,1:T(8,128)(2,1)} %pad_maximum_fusion.6), channel_id=1, source_target_pairs={{0,8},{8,0},{16,24},{24,16},{1,9},{9,1},{17,25},{25,17},{2,10},{10... | collective-permute-start | bytes 3244040 | tf_op jit(solution)/shard_map/ppermute | solution.py:389
  336.0 49.1 %collective-permute-start.18 = (bf16[256,2112]{0,1:T(8,128)(2,1)}, bf16[256,2112]{0,1:T(8,128)(2,1)}, u32[]{:S(2)}, u32[]{:S(2)}) collective-permute-start(bf16[256,2112]{0,1:T(8,128)(2,1)} %pad_maximum_fusion.7), channel_id=1, source_target_pairs={{0,16},{16,0},{8,24},{24,8},{1,17},{17,1},{9,25},{25,9},{2,18},{18... | collective-permute-start | bytes 3244040 | tf_op jit(solution)/shard_map/ppermute | solution.py:389
  337.4 47.6 %collective-permute-start.19 = (bf16[256,2112]{0,1:T(8,128)(2,1)}, bf16[256,2112]{0,1:T(8,128)(2,1)}, u32[]{:S(2)}, u32[]{:S(2)}) collective-permute-start(bf16[256,2112]{0,1:T(8,128)(2,1)} %pad_maximum_fusion.8), channel_id=1, source_target_pairs={{0,8},{8,0},{16,24},{24,16},{1,9},{9,1},{17,25},{25,17},{2,10},{10... | collective-permute-start | bytes 3244040 | tf_op jit(solution)/shard_map/ppermute | solution.py:389
  338.0 47.1 %collective-permute-start.20 = (bf16[256,2112]{0,1:T(8,128)(2,1)}, bf16[256,2112]{0,1:T(8,128)(2,1)}, u32[]{:S(2)}, u32[]{:S(2)}) collective-permute-start(bf16[256,2112]{0,1:T(8,128)(2,1)} %pad_maximum_fusion.9), channel_id=1, source_target_pairs={{0,16},{16,0},{8,24},{24,8},{1,17},{17,1},{9,25},{25,9},{2,18},{18... | collective-permute-start | bytes 3244040 | tf_op jit(solution)/shard_map/ppermute | solution.py:389
  390.9 23.8 %copy-start.21 = (bf16[256,1408]{0,1:T(8,128)(2,1)S(1)}, bf16[256,1408]{0,1:T(8,128)(2,1)}, u32[]{:S(2)}) copy-start(bf16[256,1408]{0,1:T(8,128)(2,1)} %get-tuple-element.133) | copy-start | bytes 2162692
  390.9 23.8 %copy-start.28 = (bf16[256,704]{0,1:T(8,128)(2,1)S(1)}, bf16[256,704]{0,1:T(8,128)(2,1)}, u32[]{:S(2)}) copy-start(bf16[256,704]{0,1:T(8,128)(2,1)} %get-tuple-element.151) | copy-start | bytes 1081348
  390.9 23.8 %collective-permute-start.21 = (bf16[256,2112]{0,1:T(8,128)(2,1)S(1)}, bf16[256,2112]{0,1:T(8,128)(2,1)S(1)}, u32[]{:S(2)}, u32[]{:S(2)}) collective-permute-start(bf16[256,2112]{0,1:T(8,128)(2,1)S(1)} %add_convert_fusion.3), channel_id=1, source_target_pairs={{0,16},{16,0},{8,24},{24,8},{1,17},{17,1},{9,25},{25,9},{2,18},{18... | collective-permute-start | bytes 3244040 | tf_op jit(solution)/shard_map/ppermute | solution.py:413
  394.0 23.5 %collective-permute-start.22 = (bf16[256,2112]{0,1:T(8,128)(2,1)S(1)}, bf16[256,2112]{0,1:T(8,128)(2,1)S(1)}, u32[]{:S(2)}, u32[]{:S(2)}) collective-permute-start(bf16[256,2112]{0,1:T(8,128)(2,1)S(1)} %add_convert_fusion.1), channel_id=1, source_target_pairs={{0,8},{8,0},{16,24},{24,16},{1,9},{9,1},{17,25},{25,17},{2,10},{10... | collective-permute-start | bytes 3244040 | tf_op jit(solution)/shard_map/ppermute | solution.py:414
  424.9 9.7 %copy-start.16 = (bf16[256,2048]{1,0:T(8,128)(2,1)S(1)}, bf16[256,2048]{1,0:T(8,128)(2,1)}, u32[]{:S(2)}) copy-start(bf16[256,2048]{1,0:T(8,128)(2,1)} %copy-done.15) | copy-start | bytes 3145732
  424.9 56.4 %all-to-all-start.3 = ((bf16[8,64,2112]{2,1,0:T(8,128)(2,1)}), bf16[8,64,2112]{2,1,0:T(8,128)(2,1)}, u32[]{:S(2)}, u32[]{:S(2)}) async-start(bf16[8,64,2112]{2,1,0:T(8,128)(2,1)} %bitcast.118), calls=%async_computation.6 | async-start | bytes 4456448 | tf_op jit(solution)/shard_map/all_to_all | solution.py:340
  429.4 137.8 %reduce-scatter.11.cloned.1.call-start = ((), (), s32[]{:S(2)}) async-start(), calls=%async_computation.15 | async-start | bytes 4718592 | tf_op jit(solution)/shard_map/reduce_scatter | solution.py:336
  494.7 7.8 %copy-start.12 = (bf16[1,1024,2048]{2,1,0:T(8,128)(2,1)S(1)}, bf16[1,1024,2048]{2,1,0:T(8,128)(2,1)}, u32[]{:S(2)}) copy-start(bf16[1,1024,2048]{2,1,0:T(8,128)(2,1)} %all-gather.12.cloned.1.call-done) | copy-start | bytes 12582916
  498.4 11.3 %collective-permute-start.30 = (bf16[32,2048]{1,0:T(8,128)(2,1)S(1)}, bf16[32,2048]{1,0:T(8,128)(2,1)S(1)}, u32[]{:S(2)}, u32[]{:S(2)}) collective-permute-start(bf16[32,2048]{1,0:T(8,128)(2,1)S(1)} %get-tuple-element.179), channel_id=1, source_target_pairs={{0,8},{8,0},{16,24},{24,16},{1,9},{9,1},{17,25},{25,17},{2,10},{10... | collective-permute-start | bytes 393224 | tf_op jit(solution)/shard_map/ppermute | solution.py:389
  499.9 10.5 %collective-permute-start.34 = (bf16[32,2048]{1,0:T(8,128)(2,1)S(1)}, bf16[32,2048]{1,0:T(8,128)(2,1)S(1)}, u32[]{:S(2)}, u32[]{:S(2)}) collective-permute-start(bf16[32,2048]{1,0:T(8,128)(2,1)S(1)} %get-tuple-element.180), channel_id=1, source_target_pairs={{0,16},{16,0},{8,24},{24,8},{1,17},{17,1},{9,25},{25,9},{2,18},{18... | collective-permute-start | bytes 393224 | tf_op jit(solution)/shard_map/ppermute | solution.py:389
  500.9 19.1 %collective-permute-start.33 = (bf16[32,2048]{1,0:T(8,128)(2,1)S(1)}, bf16[32,2048]{1,0:T(8,128)(2,1)S(1)}, u32[]{:S(2)}, u32[]{:S(2)}) collective-permute-start(bf16[32,2048]{1,0:T(8,128)(2,1)S(1)} %get-tuple-element.181), channel_id=1, source_target_pairs={{0,16},{16,0},{8,24},{24,8},{1,17},{17,1},{9,25},{25,9},{2,18},{18... | collective-permute-start | bytes 393224 | tf_op jit(solution)/shard_map/ppermute | solution.py:389
  501.9 5.0 collective-permute-start.31
  502.5 5.5 collective-permute-start.23
  506.9 6.0 %collective-permute-start.32 = (bf16[32,2048]{1,0:T(8,128)(2,1)S(1)}, bf16[32,2048]{1,0:T(8,128)(2,1)S(1)}, u32[]{:S(2)}, u32[]{:S(2)}) collective-permute-start(bf16[32,2048]{1,0:T(8,128)(2,1)S(1)} %add_convert_fusion.12), channel_id=1, source_target_pairs={{0,16},{16,0},{8,24},{24,8},{1,17},{17,1},{9,25},{25,9},{2,18},{18... | collective-permute-start | bytes 393224 | tf_op jit(solution)/shard_map/ppermute | solution.py:413
  508.5 9.2 %collective-permute-start.25 = (bf16[256,512]{1,0:T(8,128)(2,1)S(1)}, bf16[256,512]{1,0:T(8,128)(2,1)S(1)}, u32[]{:S(2)}, u32[]{:S(2)}) collective-permute-start(bf16[256,512]{1,0:T(8,128)(2,1)S(1)} %get-tuple-element.162), channel_id=1, source_target_pairs={{0,8},{8,0},{16,24},{24,16},{1,9},{9,1},{17,25},{25,17},{2,10},{10... | collective-permute-start | bytes 786440 | tf_op jit(solution)/shard_map/ppermute | solution.py:389
  509.7 9.2 %collective-permute-start.28 = (bf16[256,512]{1,0:T(8,128)(2,1)S(1)}, bf16[256,512]{1,0:T(8,128)(2,1)S(1)}, u32[]{:S(2)}, u32[]{:S(2)}) collective-permute-start(bf16[256,512]{1,0:T(8,128)(2,1)S(1)} %get-tuple-element.164), channel_id=1, source_target_pairs={{0,16},{16,0},{8,24},{24,8},{1,17},{17,1},{9,25},{25,9},{2,18},{18... | collective-permute-start | bytes 786440 | tf_op jit(solution)/shard_map/ppermute | solution.py:389
  513.0 8.1 %collective-permute-start.35 = (bf16[32,2048]{1,0:T(8,128)(2,1)S(1)}, bf16[32,2048]{1,0:T(8,128)(2,1)S(1)}, u32[]{:S(2)}, u32[]{:S(2)}) collective-permute-start(bf16[32,2048]{1,0:T(8,128)(2,1)S(1)} %get-tuple-element.178), channel_id=1, source_target_pairs={{0,8},{8,0},{16,24},{24,16},{1,9},{9,1},{17,25},{25,17},{2,10},{10... | collective-permute-start | bytes 393224 | tf_op jit(solution)/shard_map/ppermute | solution.py:414
  514.1 12.1 %collective-permute-start.24 = (bf16[256,512]{1,0:T(8,128)(2,1)S(1)}, bf16[256,512]{1,0:T(8,128)(2,1)S(1)}, u32[]{:S(2)}, u32[]{:S(2)}) collective-permute-start(bf16[256,512]{1,0:T(8,128)(2,1)S(1)} %get-tuple-element.161), channel_id=1, source_target_pairs={{0,8},{8,0},{16,24},{24,16},{1,9},{9,1},{17,25},{25,17},{2,10},{10... | collective-permute-start | bytes 786440 | tf_op jit(solution)/shard_map/ppermute | solution.py:389
  517.8 8.4 %collective-permute-start.27 = (bf16[256,512]{1,0:T(8,128)(2,1)S(1)}, bf16[256,512]{1,0:T(8,128)(2,1)S(1)}, u32[]{:S(2)}, u32[]{:S(2)}) collective-permute-start(bf16[256,512]{1,0:T(8,128)(2,1)S(1)} %get-tuple-element.163), channel_id=1, source_target_pairs={{0,16},{16,0},{8,24},{24,8},{1,17},{17,1},{9,25},{25,9},{2,18},{18... | collective-permute-start | bytes 786440 | tf_op jit(solution)/shard_map/ppermute | solution.py:389
  519.0 9.8 %collective-permute-start.26 = (bf16[256,512]{1,0:T(8,128)(2,1)S(1)}, bf16[256,512]{1,0:T(8,128)(2,1)S(1)}, u32[]{:S(2)}, u32[]{:S(2)}) collective-permute-start(bf16[256,512]{1,0:T(8,128)(2,1)S(1)} %get-tuple-element.165), channel_id=1, source_target_pairs={{0,16},{16,0},{8,24},{24,8},{1,17},{17,1},{9,25},{25,9},{2,18},{18... | collective-permute-start | bytes 786440 | tf_op jit(solution)/shard_map/ppermute | solution.py:413
  520.0 9.4 %collective-permute-start.29 = (bf16[256,512]{1,0:T(8,128)(2,1)S(1)}, bf16[256,512]{1,0:T(8,128)(2,1)S(1)}, u32[]{:S(2)}, u32[]{:S(2)}) collective-permute-start(bf16[256,512]{1,0:T(8,128)(2,1)S(1)} %get-tuple-element.166), channel_id=1, source_target_pairs={{0,8},{8,0},{16,24},{24,16},{1,9},{9,1},{17,25},{25,17},{2,10},{10... | collective-permute-start | bytes 786440 | tf_op jit(solution)/shard_map/ppermute | solution.py:414
  530.5 21.6 %all-to-all-start.4 = ((bf16[8,64,512]{2,1,0:T(8,128)(2,1)}), bf16[8,64,512]{2,1,0:T(8,128)(2,1)}, u32[]{:S(2)}, u32[]{:S(2)}) async-start(bf16[8,64,512]{2,1,0:T(8,128)(2,1)} %bitcast.24), calls=%async_computation.8 | async-start | bytes 1048576 | tf_op jit(solution)/shard_map/all_to_all | solution.py:340
  560.7 6.5 %copy-start.4 = (bf16[1,128,2048]{2,1,0:T(8,128)(2,1)S(1)}, bf16[1,128,2048]{2,1,0:T(8,128)(2,1)}, u32[]{:S(2)}) copy-start(bf16[1,128,2048]{2,1,0:T(8,128)(2,1)} %param.13) | copy-start | bytes 1572868
  (33 other events, 109.5 us)
Sparse Core Ops, SparseCore 0:
  9.6 75.2 all-gather.11
  136.7 50.4 reduce-scatter.4
  191.1 45.3 all-gather.5
  237.9 45.6 all-gather.7
  285.7 48.7 reduce-scatter.6
  336.6 48.3 reduce-scatter.8
  389.1 45.4 all-gather.9
  493.8 48.9 reduce-scatter.10

commit v6 on v5

--- a/solution.py
+++ b/solution.py
@@ -759,7 +759,6 @@
     key_low = turn(key_back, cosine, -sine_table).astype(bf16)
     value_low = value_back.astype(bf16)
     other_back = jnp.where(core == 0, value_low, key_low)
-    other_back, mlp_grad = tie(other_back, mlp_grad)
     other_part = contract_rows(shaped_all, other_back).astype(bf16)
     heads_back = jnp.concatenate(
         [
@@ -774,7 +773,7 @@
         jnp.concatenate([heads_back, other_back], axis=1),
         jnp.concatenate([attn_cols, other_cols], axis=1),
     ).astype(bf16)
-    weighted_part, low_all = tie(weighted_part, low_all)
+    weighted_part, low_all, mlp_grad = tie(weighted_part, low_all, mlp_grad)
     weighted_one = reduce_ctx(weighted_part).astype(f32)
     attn_part = contract_rows(shaped_all, heads_back)
     own_part = attn_part[:, head_width:] + other_part.astype(f32)
@@ -786,17 +785,17 @@
     mlp_grad = mlp_grad.astype(f32)
     attn_grad = exchange_ctx(attn_grad_own.reshape(8, rows, -1))
 
+    gate_rows = ff_rows(mlp_grad[:, :, :main], mlp_grad[:, :, 2 * main : 2 * main + tail])
+    up_rows = ff_rows(mlp_grad[:, :, main : 2 * main], mlp_grad[:, :, 2 * main + tail : both])
+    down_grad = ff_rows(mlp_grad[:, :, both : both + main], mlp_grad[:, :, both + main :])
     scale_one = rms_scale(inputs)
     shaped_one = inputs * scale_one
     input_grad = residual_back + scale_one * (
         weighted_one - shaped_one * jnp.mean(weighted_one * shaped_one, axis=-1, keepdims=True)
     )
     block_output = (residual + out_own.astype(f32)).astype(bf16)
-    gate_rows = ff_rows(mlp_grad[:, :, :main], mlp_grad[:, :, 2 * main : 2 * main + tail])
-    up_rows = ff_rows(mlp_grad[:, :, main : 2 * main], mlp_grad[:, :, 2 * main + tail : both])
-    down_grad = ff_rows(mlp_grad[:, :, both : both + main], mlp_grad[:, :, both + main :])
-    attn_grad, out_grad, gate_rows, up_rows, down_grad = tie(
-        attn_grad, out_grad, gate_rows, up_rows, down_grad
+    attn_grad, out_grad, gate_rows, up_rows, down_grad, input_grad, block_output = tie(
+        attn_grad, out_grad, gate_rows, up_rows, down_grad, input_grad, block_output
     )
     attn_grad = attn_grad.astype(f32)
     query_rows = from_head_slices(attn_grad[:, :, :head_width])

time: 586 us -> 571 us (0.974)
  waiting for transfers between devices: 224 us -> 212 us
    all_to_all x5, waiting for transfers between devices: 39.2 us -> 25.9 us  [exchange_ctx(): return lax.all_to_all(pieces, 'ctx', 0, 0, tiled=True)]
where the time goes in v6:
time: 571 us; the launch traced here: 564 us
  waiting for transfers between devices  212 us (37%)
  local copies, waits for them, and re-layouts  104 us (18%)
  matrix products  83 us (15%)
  starting transfers between devices  58.7 us (10%)
  other arithmetic  56.4 us (10%)
  Pallas kernels  33.5 us (6%)
  between operations  16.1 us (3%)
    reduce_scatter x4, waiting for transfers between devices, reduce_ctx(): return lax.psum_scatter(partial, 'ctx', scatter_dimension=0, tiled=True)  53.9 us
    all_gather x4, waiting for transfers between devices, gather_ctx(): return lax.all_gather(block, 'ctx', axis=0, tiled=True)  48.3 us
    ppermute x4, waiting for transfers between devices, gather_seq_far(): far_low = lax.ppermute(from_y[half:], 'seq', SEQ_X)  35.1 us
    dot_general x4, matrix products, contract_cols(): lax.dot_general(left, right, (((1,), (1,)), ((), ())), preferred_element_...  29.4 us
    all_to_all x5, waiting for transfers between devices, exchange_ctx(): return lax.all_to_all(pieces, 'ctx', 0, 0, tiled=True)  25.9 us
    dynamic_update_slice x20, local copies, waits for them, and re-layouts, gather_seq_far(): whole = lax.dynamic_update_slice_in_dim(whole, piece, start, 0)  25.4 us
    ppermute x3, waiting for transfers between devices, reduce_seq_far(): top_last = lax.ppermute(top_send, 'seq', SEQ_Y)  24.7 us
    all_to_all x5, starting transfers between devices, exchange_ctx(): return lax.all_to_all(pieces, 'ctx', 0, 0, tiled=True)  22.1 us
  transfers between devices with their start and end apart: 49, of which 23 were waited for; matrix products, arithmetic and copies ran while one was open for 36% of the time, Pallas kernels for 6%

profile of v6, /device:TPU:0, one launch (start us, length us, event | category | flops | bytes accessed | tf_op | source)
XLA Modules:
  0.0 563.6 jit_solution(5630939768900798677)
XLA Ops:
  7.9 3.1 collective-permute-start.6
  16.3 5.0 all-to-all-start
  27.7 2.2 concatenate.109
  35.2 16.1 %all-to-all-done = bf16[8,64,512]{2,1,0:T(8,128)(2,1)} async-done(((bf16[8,64,512]{2,1,0:T(8,128)(2,1)}), bf16[8,64,512]{2,1,0:T(8,128)(2,1)}, u32[]{:S(2)}, u32[]{:S(2)}) %all-to-all-start) | async-done | bytes 524320 | tf_op jit(solution)/shard_map/all_to_all | solution.py:340
  52.5 3.5 all-to-all-start.1
  58.8 11.7 %collective-permute-done = bf16[512,512]{1,0:T(8,128)(2,1)S(1)} collective-permute-done((bf16[512,512]{1,0:T(8,128)(2,1)}, bf16[512,512]{1,0:T(8,128)(2,1)S(1)}, u32[]{:S(2)}, u32[]{:S(2)}) %collective-permute-start) | collective-permute-done | bytes 524320 | tf_op jit(solution)/shard_map/ppermute | solution.py:344
  79.0 1.9 constant_dynamic-update-slice_fusion.17
  82.6 2.7 collective-permute-done.3
  86.0 2.3 slice.227
  88.3 2.6 copy.80
  90.9 4.6 all-to-all-start.2
  96.0 3.2 fusion
  99.4 5.3 fusion.66
  104.7 3.5 fusion.64
  118.2 13.6 %attend.1 = bf16[1024,256]{1,0:T(8,128)(2,1)} custom-call(s32[1]{0:T(128)} %bitcast.2.refs_0_, bf16[1024,256]{1,0:T(8,128)(2,1)} %get-tuple-element.170.refs_1_, bf16[1024,256]{1,0:T(8,128)(2,1)} %fusion.29.refs_2_, bf16[1024,256]{1,0:T(8,128)(2,1)} %get-tuple-element.169.refs_3_), custom_call_target="tpu_custom_call" | custom-call | flops 4294967296 | bytes 2097152 | tf_op jit(solution)/shard_map/attend/pallas_call | solution.py:581
  131.8 4.7 convolution_convert_fusion.2
  143.4 1.9 broadcast_in_dim.33
  147.7 2.3 copy.84
  150.9 2.2 constant_dynamic-update-slice_fusion.7
  153.1 25.3 %collective-permute-done.12 = bf16[256,704]{0,1:T(8,128)(2,1)} collective-permute-done((bf16[256,704]{0,1:T(8,128)(2,1)}, bf16[256,704]{0,1:T(8,128)(2,1)}, u32[]{:S(2)}, u32[]{:S(2)}) %collective-permute-start.12) | collective-permute-done | bytes 360480 | tf_op jit(solution)/shard_map/ppermute | solution.py:352
  182.3 4.8 reduce-scatter.5.cloned.1.call-done
  188.5 2.4 fusion.71
  194.3 2.9 broadcast_in_dim.34
  197.1 2.8 constant_dynamic-update-slice_fusion.4
  202.5 2.6 constant_dynamic-update-slice_fusion.3
  205.1 2.6 constant_dynamic-update-slice_fusion.2
  209.7 7.0 %collective-permute-done.16 = bf16[256,1408]{1,0:T(8,128)(2,1)S(1)} collective-permute-done((bf16[256,1408]{1,0:T(8,128)(2,1)S(1)}, bf16[256,1408]{1,0:T(8,128)(2,1)S(1)}, u32[]{:S(2)}, u32[]{:S(2)}) %collective-permute-start.16) | collective-permute-done | bytes 720928 | tf_op jit(solution)/shard_map/ppermute | solution.py:352
  217.7 18.8 %all-gather.6.cloned.1.call-done = bf16[1024,2048]{1,0:T(8,128)(2,1)} async-done(((bf16[128,2048]{1,0:T(8,128)(2,1)}), bf16[1024,2048]{1,0:T(8,128)(2,1)}) %all-gather.6.cloned.1.call-update) | async-done | bytes 4194320 | tf_op jit(solution)/shard_map/all_gather | solution.py:332
  236.4 10.6 %fusion.84 = f32[1024,1408]{1,0:T(8,128)S(1)} fusion(bf16[1024,2048]{1,0:T(8,128)(2,1)} %all-gather.6.cloned.1.call-done, bf16[2048,1408]{1,0:T(8,128)(2,1)} %constant_dynamic-update-slice_fusion), kind=kOutput, calls=%fused_computation.237 | convolution fusion | flops 5905580032 | bytes 15728640 | tf_op jit(solution)/shard_map/dot_general | solution.py:712
  252.1 7.0 %convolution_convert_fusion.4 = bf16[1024,2048]{1,0:T(8,128)(2,1)} fusion(bf16[1024,704]{1,0:T(8,128)(2,1)S(1)} %multiply_convert_fusion.2, bf16[2048,704]{1,0:T(8,128)(2,1)} %constant_dynamic-update-slice_fusion.5), kind=kOutput, calls=%fused_computation.24 | convolution fusion | flops 2954887168 | bytes 8519680 | tf_op jit(solution)/shard_map/dot_general | solution.py:53
  259.0 24.5 %all-gather.8.cloned.1.call-done = bf16[1024,2048]{1,0:T(8,128)(2,1)} async-done(((bf16[128,2048]{1,0:T(8,128)(2,1)}), bf16[1024,2048]{1,0:T(8,128)(2,1)}) %all-gather.8.cloned.1.call-update) | async-done | bytes 4194320 | tf_op jit(solution)/shard_map/all_gather | solution.py:332
  283.6 8.8 %multiply_convert_fusion = (bf16[1024,704]{1,0:T(8,128)(2,1)S(1)}, bf16[1024,704]{1,0:T(8,128)(2,1)S(1)}) fusion(f32[1024,64]{1,0:T(8,128)S(1)} %get-tuple-element.145, f32[1024,640]{1,0:T(8,128)} %copy-done.5, f32[1024,64]{1,0:T(8,128)S(1)} %get-tuple-element.146, f32[1024,640]{1,0:T(8,128)} %copy-done.6, ...), kind=kOutput, calls=%fused_computation.31 | convolution fusion | flops 2963603456 | bytes 15728640 | tf_op jit(solution)/shard_map/dot_general | solution.py:729
  295.2 5.1 concatenate.118
  300.3 11.0 %convolution_convert_fusion.1 = bf16[1024,2048]{1,0:T(8,128)(2,1)} fusion(bf16[1024,1408]{1,0:T(8,128)(2,1)} %concatenate.118, bf16[2048,1408]{1,0:T(8,128)(2,1)} %constant_dynamic-update-slice_fusion), kind=kOutput, calls=%fused_computation.21 | convolution fusion | flops 5907677184 | bytes 12845056 | tf_op jit(solution)/shard_map/dot_general | solution.py:53
  311.6 6.1 %convolution_convert_fusion.5 = bf16[2048,704]{0,1:T(8,128)(2,1)S(1)} fusion(bf16[1024,2048]{1,0:T(8,128)(2,1)} %all-gather.8.cloned.1.call-done, bf16[1024,704]{1,0:T(8,128)(2,1)} %copy-done.21), kind=kOutput, calls=%fused_computation.25 | convolution fusion | flops 2954231808 | bytes 8519680 | tf_op jit(solution)/shard_map/dot_general | solution.py:47
  320.0 6.6 %convolution_convert_fusion = bf16[2048,1408]{0,1:T(8,128)(2,1)S(1)} fusion(bf16[1024,2048]{1,0:T(8,128)(2,1)S(1)} %copy-done.34, bf16[1024,1408]{1,0:T(8,128)(2,1)S(1)} %copy-done.15), kind=kOutput, calls=%fused_computation.4 | convolution fusion | flops 5908463616 | bytes 12845056 | tf_op jit(solution)/shard_map/dot_general | solution.py:47
  326.6 2.2 constant_dynamic-slice_fusion.11
  338.5 46.5 %reduce-scatter.7.cloned.1.call-done = bf16[128,2048]{1,0:T(8,128)(2,1)} async-done(((bf16[1024,2048]{1,0:T(8,128)(2,1)}), bf16[128,2048]{1,0:T(8,128)(2,1)}) %reduce-scatter.7.cloned.1.call-update) | async-done | bytes 524304 | tf_op jit(solution)/shard_map/reduce_scatter | solution.py:336
  386.3 2.7 fusion.69
  389.0 1.9 add_convert_fusion.3
  395.5 19.2 %collective-permute-done.28 = bf16[256,2112]{0,1:T(8,128)(2,1)S(1)} collective-permute-done((bf16[256,2112]{0,1:T(8,128)(2,1)S(1)}, bf16[256,2112]{0,1:T(8,128)(2,1)S(1)}, u32[]{:S(2)}, u32[]{:S(2)}) %collective-permute-start.28) | collective-permute-done | bytes 1081376 | tf_op jit(solution)/shard_map/ppermute | solution.py:413
  414.7 1.9 add_convert_fusion.2
  420.9 4.1 copy.94
  425.0 4.5 all-to-all-start.3
  429.6 4.9 all-gather.10.cloned.1.call-done
  434.5 4.3 convolution_convert_fusion.8.refs_4_
  438.8 19.9 %attend_back.1 = (f32[1024,256]{1,0:T(8,128)}, f32[1024,256]{1,0:T(8,128)}, f32[1024,256]{1,0:T(8,128)}) custom-call(s32[1]{0:T(128)} %bitcast.2.refs_0_, bf16[1024,256]{1,0:T(8,128)(2,1)} %get-tuple-element.170.refs_1_, bf16[1024,256]{1,0:T(8,128)(2,1)} %fusion.29.refs_2_, bf16[1024,256]{1,0:T(8,128)(2,1)} %get-tuple-element.169.refs_3_, ...), custom_call_target="tpu_custom_call" | custom-call | flops 10737418240 | bytes 3670016 | tf_op jit(solution)/shard_map/attend_back/pallas_call | solution.py:602
  466.3 1.9 convolution_convert_fusion.7
  468.1 7.1 %convolution_convert_fusion.3 = bf16[1024,2048]{1,0:T(8,128)(2,1)} fusion(bf16[2048,256]{1,0:T(8,128)(2,1)} %collective-permute-done.4, bf16[2048,512]{1,0:T(8,128)(2,1)} %constant_dynamic-update-slice_fusion.15, bf16[1024,256]{1,0:T(8,128)(2,1)S(1)} %get-tuple-element.127, bf16[1024,512]{1,0:T(8,128)(2,1)S(1)} %pad_maximum_fusion.10), kind=kOutput, calls=%fused_computation.23 | convolution fusion | flops 3232759808 | bytes 8912896 | tf_op jit(solution)/shard_map/dot_general | solution.py:53
  475.2 6.2 %all-to-all-done.3 = bf16[8,64,2112]{2,1,0:T(8,128)(2,1)} async-done(((bf16[8,64,2112]{2,1,0:T(8,128)(2,1)}), bf16[8,64,2112]{2,1,0:T(8,128)(2,1)}, u32[]{:S(2)}, u32[]{:S(2)}) %all-to-all-start.3) | async-done | bytes 2162720 | tf_op jit(solution)/shard_map/all_to_all | solution.py:340
  481.5 3.6 convolution_convert_fusion.6
  489.3 2.6 fusion.61
  497.1 2.7 collective-permute-done.32
  502.0 2.4 collective-permute-done.23
  508.6 4.3 collective-permute-done.22
  512.8 2.7 collective-permute-done.24
  517.1 4.4 all-to-all-start.4
  521.5 2.0 convert_element_type.350
  532.7 3.3 add_convert_fusion.4
  536.1 3.6 all-to-all-done.4
  539.6 1.9 fusion.83
  545.7 2.8 copy.114
  550.1 1.9 broadcast_multiply_fusion.2
  552.0 3.4 broadcast_multiply_fusion
  (291 shorter events, 137.3 us)
Async XLA Ops:
  7.2 8.1 %copy-start.28 = (bf16[64,256]{1,0:T(8,128)(2,1)S(1)}, bf16[64,256]{1,0:T(8,128)(2,1)}, u32[]{:S(2)}) copy-start(bf16[64,256]{1,0:T(8,128)(2,1)} %param.19) | copy-start | bytes 98308
  7.2 8.1 %copy-start.27 = (bf16[64,256]{1,0:T(8,128)(2,1)S(1)}, bf16[64,256]{1,0:T(8,128)(2,1)}, u32[]{:S(2)}) copy-start(bf16[64,256]{1,0:T(8,128)(2,1)} %param.18) | copy-start | bytes 98308
  7.2 88.8 %all-gather.12.cloned.1.call-start = ((), (), s32[]{:S(2)}) async-start(), calls=%async_computation.16 | async-start | bytes 4718592 | tf_op jit(solution)/shard_map/all_gather | solution.py:332
  7.9 22.1 %collective-permute-start.6 = (bf16[64,2048]{1,0:T(8,128)(2,1)}, bf16[64,2048]{1,0:T(8,128)(2,1)}, u32[]{:S(2)}, u32[]{:S(2)}) collective-permute-start(bf16[64,2048]{1,0:T(8,128)(2,1)} %param.20), channel_id=1, source_target_pairs={{0,16},{16,0},{8,24},{24,8},{1,17},{17,1},{9,25},{25,9},{2,18},{18... | collective-permute-start | bytes 786440 | tf_op jit(solution)/shard_map/ppermute | solution.py:344
  11.0 21.1 %collective-permute-start.5 = (bf16[64,2048]{1,0:T(8,128)(2,1)}, bf16[64,2048]{1,0:T(8,128)(2,1)}, u32[]{:S(2)}, u32[]{:S(2)}) collective-permute-start(bf16[64,2048]{1,0:T(8,128)(2,1)} %param.20), channel_id=1, source_target_pairs={{0,8},{8,0},{16,24},{24,16},{1,9},{9,1},{17,25},{25,17},{2,10},{10... | collective-permute-start | bytes 786440 | tf_op jit(solution)/shard_map/ppermute | solution.py:344
  15.4 6.8 %slice-start.1 = ((bf16[64,5632]{1,0:T(8,128)(2,1)}), bf16[64,5120]{1,0:T(8,128)(2,1)S(1)}, s32[]{:S(2)}) async-start(bf16[64,5632]{1,0:T(8,128)(2,1)} %param.24), calls=%async_computation.18 | async-start | bytes 1310720 | tf_op jit(solution)/shard_map/slice | solution.py:446
  16.3 8.5 %copy-start.16 = (bf16[64,5632]{1,0:T(8,128)(2,1)S(1)}, bf16[64,5632]{1,0:T(8,128)(2,1)}, u32[]{:S(2)}) copy-start(bf16[64,5632]{1,0:T(8,128)(2,1)} %param.23) | copy-start | bytes 2162692
  16.3 8.5 %copy-start.17 = (bf16[64,5632]{1,0:T(8,128)(2,1)S(1)}, bf16[64,5632]{1,0:T(8,128)(2,1)}, u32[]{:S(2)}) copy-start(bf16[64,5632]{1,0:T(8,128)(2,1)} %param.22) | copy-start | bytes 2162692
  16.3 35.0 %all-to-all-start = ((bf16[8,64,512]{2,1,0:T(8,128)(2,1)}), bf16[8,64,512]{2,1,0:T(8,128)(2,1)}, u32[]{:S(2)}, u32[]{:S(2)}) async-start(bf16[8,64,512]{2,1,0:T(8,128)(2,1)} %pad_maximum_fusion.12), calls=%async_computation | async-start | bytes 1048576 | tf_op jit(solution)/shard_map/all_to_all | solution.py:340
  31.6 27.2 %collective-permute-start.8 = (bf16[32,2048]{1,0:T(8,128)(2,1)}, bf16[32,2048]{1,0:T(8,128)(2,1)S(1)}, u32[]{:S(2)}, u32[]{:S(2)}) collective-permute-start(bf16[32,2048]{1,0:T(8,128)(2,1)} %slice.233), channel_id=1, source_target_pairs={{0,8},{8,0},{16,24},{24,16},{1,9},{9,1},{17,25},{25,17},{2,10},{10... | collective-permute-start | bytes 393224 | tf_op jit(solution)/shard_map/ppermute | solution.py:352
  33.7 24.2 %collective-permute-start.7 = (bf16[32,2048]{1,0:T(8,128)(2,1)}, bf16[32,2048]{1,0:T(8,128)(2,1)}, u32[]{:S(2)}, u32[]{:S(2)}) collective-permute-start(bf16[32,2048]{1,0:T(8,128)(2,1)} %slice.232), channel_id=1, source_target_pairs={{0,16},{16,0},{8,24},{24,8},{1,17},{17,1},{9,25},{25,9},{2,18},{18... | collective-permute-start | bytes 393224 | tf_op jit(solution)/shard_map/ppermute | solution.py:351
  52.5 35.8 %all-to-all-start.1 = ((bf16[8,64,704]{2,1,0:T(8,128)(2,1)}), bf16[8,64,704]{2,1,0:T(8,128)(2,1)S(1)}, u32[]{:S(2)}, u32[]{:S(2)}) async-start(bf16[8,64,704]{2,1,0:T(8,128)(2,1)} %pad_maximum_fusion.11), calls=%async_computation.1 | async-start | bytes 1572864 | tf_op jit(solution)/shard_map/all_to_all | solution.py:340
  56.1 14.4 %collective-permute-start = (bf16[512,512]{1,0:T(8,128)(2,1)}, bf16[512,512]{1,0:T(8,128)(2,1)S(1)}, u32[]{:S(2)}, u32[]{:S(2)}) collective-permute-start(bf16[512,512]{1,0:T(8,128)(2,1)} %bitcast.7), channel_id=1, source_target_pairs={{0,8},{8,0},{16,24},{24,16},{1,9},{9,1},{17,25},{25,17},{2,10},{10... | collective-permute-start | bytes 1572872 | tf_op jit(solution)/shard_map/ppermute | solution.py:344
  57.3 19.3 %collective-permute-start.1 = (bf16[512,512]{1,0:T(8,128)(2,1)}, bf16[512,512]{1,0:T(8,128)(2,1)}, u32[]{:S(2)}, u32[]{:S(2)}) collective-permute-start(bf16[512,512]{1,0:T(8,128)(2,1)} %bitcast.7), channel_id=1, source_target_pairs={{0,16},{16,0},{8,24},{24,8},{1,17},{17,1},{9,25},{25,9},{2,18},{18... | collective-permute-start | bytes 1572872 | tf_op jit(solution)/shard_map/ppermute | solution.py:344
  58.8 14.0 %copy-start.13 = (bf16[256,2048]{1,0:T(8,128)(2,1)}, bf16[256,2048]{1,0:T(8,128)(2,1)S(1)}, u32[]{:S(2)}) copy-start(bf16[256,2048]{1,0:T(8,128)(2,1)S(1)} %constant_dynamic-update-slice_fusion.10) | copy-start | bytes 3145732
  71.3 9.6 %collective-permute-start.2 = (bf16[256,512]{1,0:T(8,128)(2,1)}, bf16[256,512]{1,0:T(8,128)(2,1)}, u32[]{:S(2)}, u32[]{:S(2)}) collective-permute-start(bf16[256,512]{1,0:T(8,128)(2,1)} %slice.225), channel_id=1, source_target_pairs={{0,16},{16,0},{8,24},{24,8},{1,17},{17,1},{9,25},{25,9},{2,18},{18... | collective-permute-start | bytes 786440 | tf_op jit(solution)/shard_map/ppermute | solution.py:351
  77.6 7.7 %collective-permute-start.3 = (bf16[256,512]{1,0:T(8,128)(2,1)S(1)}, bf16[256,512]{1,0:T(8,128)(2,1)S(1)}, u32[]{:S(2)}, u32[]{:S(2)}) collective-permute-start(bf16[256,512]{1,0:T(8,128)(2,1)S(1)} %slice.226), channel_id=1, source_target_pairs={{0,8},{8,0},{16,24},{24,16},{1,9},{9,1},{17,25},{25,17},{2,10},{10... | collective-permute-start | bytes 786440 | tf_op jit(solution)/shard_map/ppermute | solution.py:352
  88.3 16.4 %collective-permute-start.4 = (bf16[2048,256]{1,0:T(8,128)(2,1)}, bf16[2048,256]{1,0:T(8,128)(2,1)}, u32[]{:S(2)}, u32[]{:S(2)}) collective-permute-start(bf16[2048,256]{1,0:T(8,128)(2,1)} %slice.227), channel_id=1, source_target_pairs={{0,1},{1,0},{2,3},{3,2},{4,5},{5,4},{6,7},{7,6},{8,9},{9,8},{10,11... | collective-permute-start | bytes 3145736 | tf_op jit(solution)/shard_map/ppermute | solution.py:434
  90.9 40.8 %all-to-all-start.2 = ((bf16[8,64,1408]{2,1,0:T(8,128)(2,1)}), bf16[8,64,1408]{2,1,0:T(8,128)(2,1)}, u32[]{:S(2)}, u32[]{:S(2)}) async-start(bf16[8,64,1408]{2,1,0:T(8,128)(2,1)} %copy.80), calls=%async_computation.2 | async-start | bytes 2883584 | tf_op jit(solution)/shard_map/all_to_all | solution.py:340
  95.6 91.6 %reduce-scatter.5.cloned.1.call-start = ((), (), s32[]{:S(2)}) async-start(), calls=%async_computation.9 | async-start | bytes 4718592 | tf_op jit(solution)/shard_map/reduce_scatter | solution.py:336
  109.3 22.5 %collective-permute-start.10 = (bf16[512,704]{0,1:T(8,128)(2,1)}, bf16[512,704]{0,1:T(8,128)(2,1)}, u32[]{:S(2)}, u32[]{:S(2)}) collective-permute-start(bf16[512,704]{0,1:T(8,128)(2,1)} %copy.81), channel_id=1, source_target_pairs={{0,16},{16,0},{8,24},{24,8},{1,17},{17,1},{9,25},{25,9},{2,18},{18... | collective-permute-start | bytes 2162696 | tf_op jit(solution)/shard_map/ppermute | solution.py:344
  111.1 20.7 %collective-permute-start.9 = (bf16[512,704]{0,1:T(8,128)(2,1)}, bf16[512,704]{0,1:T(8,128)(2,1)}, u32[]{:S(2)}, u32[]{:S(2)}) collective-permute-start(bf16[512,704]{0,1:T(8,128)(2,1)} %copy.81), channel_id=1, source_target_pairs={{0,8},{8,0},{16,24},{24,16},{1,9},{9,1},{17,25},{25,17},{2,10},{10... | collective-permute-start | bytes 2162696 | tf_op jit(solution)/shard_map/ppermute | solution.py:344
  136.5 99.9 %all-gather.6.cloned.1.call-start = ((), (), s32[]{:S(2)}) async-start(), calls=%async_computation.10 | async-start | bytes 4718592 | tf_op jit(solution)/shard_map/all_gather | solution.py:332
  136.6 45.8 %collective-permute-start.14 = (bf16[512,1408]{1,0:T(8,128)(2,1)}, bf16[512,1408]{1,0:T(8,128)(2,1)}, u32[]{:S(2)}, u32[]{:S(2)}) collective-permute-start(bf16[512,1408]{1,0:T(8,128)(2,1)} %bitcast.19), channel_id=1, source_target_pairs={{0,16},{16,0},{8,24},{24,8},{1,17},{17,1},{9,25},{25,9},{2,18},{18... | collective-permute-start | bytes 4325384 | tf_op jit(solution)/shard_map/ppermute | solution.py:344
  137.2 45.1 %collective-permute-start.13 = (bf16[512,1408]{1,0:T(8,128)(2,1)}, bf16[512,1408]{1,0:T(8,128)(2,1)}, u32[]{:S(2)}, u32[]{:S(2)}) collective-permute-start(bf16[512,1408]{1,0:T(8,128)(2,1)} %bitcast.19), channel_id=1, source_target_pairs={{0,8},{8,0},{16,24},{24,16},{1,9},{9,1},{17,25},{25,17},{2,10},{10... | collective-permute-start | bytes 4325384 | tf_op jit(solution)/shard_map/ppermute | solution.py:344
  141.2 37.2 %collective-permute-start.12 = (bf16[256,704]{0,1:T(8,128)(2,1)}, bf16[256,704]{0,1:T(8,128)(2,1)}, u32[]{:S(2)}, u32[]{:S(2)}) collective-permute-start(bf16[256,704]{0,1:T(8,128)(2,1)} %slice.190), channel_id=1, source_target_pairs={{0,8},{8,0},{16,24},{24,16},{1,9},{9,1},{17,25},{25,17},{2,10},{10... | collective-permute-start | bytes 1081352 | tf_op jit(solution)/shard_map/ppermute | solution.py:352
  142.0 37.6 %collective-permute-start.11 = (bf16[256,704]{0,1:T(8,128)(2,1)S(1)}, bf16[256,704]{0,1:T(8,128)(2,1)}, u32[]{:S(2)}, u32[]{:S(2)}) collective-permute-start(bf16[256,704]{0,1:T(8,128)(2,1)S(1)} %slice.189), channel_id=1, source_target_pairs={{0,16},{16,0},{8,24},{24,8},{1,17},{17,1},{9,25},{25,9},{2,18},{18... | collective-permute-start | bytes 1081352 | tf_op jit(solution)/shard_map/ppermute | solution.py:351
  150.9 36.2 %copy-start.3 = (bf16[1,128,2048]{2,1,0:T(8,128)(2,1)S(1)}, bf16[1,128,2048]{2,1,0:T(8,128)(2,1)}, u32[]{:S(2)}) copy-start(bf16[1,128,2048]{2,1,0:T(8,128)(2,1)} %param.13) | copy-start | bytes 1572868
  190.9 92.6 %all-gather.8.cloned.1.call-start = ((), (), s32[]{:S(2)}) async-start(), calls=%async_computation.11 | async-start | bytes 4718592 | tf_op jit(solution)/shard_map/all_gather | solution.py:332
  191.5 143.0 %reduce-scatter.9.cloned.1.call-start = ((), (), s32[]{:S(2)}) async-start(), calls=%async_computation.13 | async-start | bytes 4718592 | tf_op jit(solution)/shard_map/reduce_scatter | solution.py:336
  192.7 16.1 %collective-permute-start.15 = (bf16[256,1408]{1,0:T(8,128)(2,1)S(1)}, bf16[256,1408]{1,0:T(8,128)(2,1)S(1)}, u32[]{:S(2)}, u32[]{:S(2)}) collective-permute-start(bf16[256,1408]{1,0:T(8,128)(2,1)S(1)} %slice.191), channel_id=1, source_target_pairs={{0,16},{16,0},{8,24},{24,8},{1,17},{17,1},{9,25},{25,9},{2,18},{18... | collective-permute-start | bytes 2162696 | tf_op jit(solution)/shard_map/ppermute | solution.py:351
  201.1 15.6 %collective-permute-start.16 = (bf16[256,1408]{1,0:T(8,128)(2,1)S(1)}, bf16[256,1408]{1,0:T(8,128)(2,1)S(1)}, u32[]{:S(2)}, u32[]{:S(2)}) collective-permute-start(bf16[256,1408]{1,0:T(8,128)(2,1)S(1)} %slice.192), channel_id=1, source_target_pairs={{0,8},{8,0},{16,24},{24,16},{1,9},{9,1},{17,25},{25,17},{2,10},{10... | collective-permute-start | bytes 2162696 | tf_op jit(solution)/shard_map/ppermute | solution.py:352
  283.6 101.4 %reduce-scatter.7.cloned.1.call-start = ((), (), s32[]{:S(2)}) async-start(), calls=%async_computation.12 | async-start | bytes 4718592 | tf_op jit(solution)/shard_map/reduce_scatter | solution.py:336
  311.4 123.2 %all-gather.10.cloned.1.call-start = ((), (), s32[]{:S(2)}) async-start(), calls=%async_computation.14 | async-start | bytes 4718592 | tf_op jit(solution)/shard_map/all_gather | solution.py:332
  311.6 7.4 %copy-start.34 = (bf16[1024,2048]{1,0:T(8,128)(2,1)S(1)}, bf16[1024,2048]{1,0:T(8,128)(2,1)}, u32[]{:S(2)}) copy-start(bf16[1024,2048]{1,0:T(8,128)(2,1)} %all-gather.6.cloned.1.call-done) | copy-start | bytes 12582916
  330.8 54.2 %copy-start.7 = (f32[128,2048]{1,0:T(8,128)S(1)}, f32[128,2048]{1,0:T(8,128)}, u32[]{:S(2)}) copy-start(f32[128,2048]{1,0:T(8,128)} %get-tuple-element.95) | copy-start | bytes 3145732
  334.5 50.5 %collective-permute-start.17 = (bf16[256,2112]{0,1:T(8,128)(2,1)}, bf16[256,2112]{0,1:T(8,128)(2,1)}, u32[]{:S(2)}, u32[]{:S(2)}) collective-permute-start(bf16[256,2112]{0,1:T(8,128)(2,1)} %pad_maximum_fusion.6), channel_id=1, source_target_pairs={{0,8},{8,0},{16,24},{24,16},{1,9},{9,1},{17,25},{25,17},{2,10},{10... | collective-permute-start | bytes 3244040 | tf_op jit(solution)/shard_map/ppermute | solution.py:389
  335.9 49.1 %collective-permute-start.18 = (bf16[256,2112]{0,1:T(8,128)(2,1)}, bf16[256,2112]{0,1:T(8,128)(2,1)}, u32[]{:S(2)}, u32[]{:S(2)}) collective-permute-start(bf16[256,2112]{0,1:T(8,128)(2,1)} %pad_maximum_fusion.7), channel_id=1, source_target_pairs={{0,16},{16,0},{8,24},{24,8},{1,17},{17,1},{9,25},{25,9},{2,18},{18... | collective-permute-start | bytes 3244040 | tf_op jit(solution)/shard_map/ppermute | solution.py:389
  337.4 47.6 %collective-permute-start.19 = (bf16[256,2112]{0,1:T(8,128)(2,1)}, bf16[256,2112]{0,1:T(8,128)(2,1)}, u32[]{:S(2)}, u32[]{:S(2)}) collective-permute-start(bf16[256,2112]{0,1:T(8,128)(2,1)} %pad_maximum_fusion.8), channel_id=1, source_target_pairs={{0,8},{8,0},{16,24},{24,16},{1,9},{9,1},{17,25},{25,17},{2,10},{10... | collective-permute-start | bytes 3244040 | tf_op jit(solution)/shard_map/ppermute | solution.py:389
  338.0 47.1 %collective-permute-start.20 = (bf16[256,2112]{0,1:T(8,128)(2,1)}, bf16[256,2112]{0,1:T(8,128)(2,1)}, u32[]{:S(2)}, u32[]{:S(2)}) collective-permute-start(bf16[256,2112]{0,1:T(8,128)(2,1)} %pad_maximum_fusion.9), channel_id=1, source_target_pairs={{0,16},{16,0},{8,24},{24,8},{1,17},{17,1},{9,25},{25,9},{2,18},{18... | collective-permute-start | bytes 3244040 | tf_op jit(solution)/shard_map/ppermute | solution.py:389
  390.9 23.8 %copy-start.19 = (bf16[256,1408]{0,1:T(8,128)(2,1)S(1)}, bf16[256,1408]{0,1:T(8,128)(2,1)}, u32[]{:S(2)}) copy-start(bf16[256,1408]{0,1:T(8,128)(2,1)} %get-tuple-element.135) | copy-start | bytes 2162692
  390.9 23.8 %copy-start.23 = (bf16[256,704]{0,1:T(8,128)(2,1)S(1)}, bf16[256,704]{0,1:T(8,128)(2,1)}, u32[]{:S(2)}) copy-start(bf16[256,704]{0,1:T(8,128)(2,1)} %get-tuple-element.153) | copy-start | bytes 1081348
  390.9 23.8 %collective-permute-start.28 = (bf16[256,2112]{0,1:T(8,128)(2,1)S(1)}, bf16[256,2112]{0,1:T(8,128)(2,1)S(1)}, u32[]{:S(2)}, u32[]{:S(2)}) collective-permute-start(bf16[256,2112]{0,1:T(8,128)(2,1)S(1)} %add_convert_fusion.3), channel_id=1, source_target_pairs={{0,16},{16,0},{8,24},{24,8},{1,17},{17,1},{9,25},{25,9},{2,18},{18... | collective-permute-start | bytes 3244040 | tf_op jit(solution)/shard_map/ppermute | solution.py:413
  393.9 23.5 %collective-permute-start.29 = (bf16[256,2112]{0,1:T(8,128)(2,1)S(1)}, bf16[256,2112]{0,1:T(8,128)(2,1)S(1)}, u32[]{:S(2)}, u32[]{:S(2)}) collective-permute-start(bf16[256,2112]{0,1:T(8,128)(2,1)S(1)} %add_convert_fusion.1), channel_id=1, source_target_pairs={{0,8},{8,0},{16,24},{24,16},{1,9},{9,1},{17,25},{25,17},{2,10},{10... | collective-permute-start | bytes 3244040 | tf_op jit(solution)/shard_map/ppermute | solution.py:414
  425.0 9.5 %copy-start.14 = (bf16[256,2048]{1,0:T(8,128)(2,1)S(1)}, bf16[256,2048]{1,0:T(8,128)(2,1)}, u32[]{:S(2)}) copy-start(bf16[256,2048]{1,0:T(8,128)(2,1)} %copy-done.13) | copy-start | bytes 3145732
  425.0 56.4 %all-to-all-start.3 = ((bf16[8,64,2112]{2,1,0:T(8,128)(2,1)}), bf16[8,64,2112]{2,1,0:T(8,128)(2,1)}, u32[]{:S(2)}, u32[]{:S(2)}) async-start(bf16[8,64,2112]{2,1,0:T(8,128)(2,1)} %bitcast.116), calls=%async_computation.6 | async-start | bytes 4456448 | tf_op jit(solution)/shard_map/all_to_all | solution.py:340
  429.5 101.8 %reduce-scatter.11.cloned.1.call-start = ((), (), s32[]{:S(2)}) async-start(), calls=%async_computation.15 | async-start | bytes 4718592 | tf_op jit(solution)/shard_map/reduce_scatter | solution.py:336
  481.5 7.8 %copy-start.11 = (bf16[1,1024,2048]{2,1,0:T(8,128)(2,1)S(1)}, bf16[1,1024,2048]{2,1,0:T(8,128)(2,1)}, u32[]{:S(2)}) copy-start(bf16[1,1024,2048]{2,1,0:T(8,128)(2,1)} %all-gather.12.cloned.1.call-done) | copy-start | bytes 12582916
  485.2 11.1 %collective-permute-start.30 = (bf16[32,2048]{1,0:T(8,128)(2,1)S(1)}, bf16[32,2048]{1,0:T(8,128)(2,1)S(1)}, u32[]{:S(2)}, u32[]{:S(2)}) collective-permute-start(bf16[32,2048]{1,0:T(8,128)(2,1)S(1)} %get-tuple-element.181), channel_id=1, source_target_pairs={{0,8},{8,0},{16,24},{24,16},{1,9},{9,1},{17,25},{25,17},{2,10},{10... | collective-permute-start | bytes 393224 | tf_op jit(solution)/shard_map/ppermute | solution.py:389
  486.7 10.5 %collective-permute-start.34 = (bf16[32,2048]{1,0:T(8,128)(2,1)S(1)}, bf16[32,2048]{1,0:T(8,128)(2,1)S(1)}, u32[]{:S(2)}, u32[]{:S(2)}) collective-permute-start(bf16[32,2048]{1,0:T(8,128)(2,1)S(1)} %get-tuple-element.182), channel_id=1, source_target_pairs={{0,16},{16,0},{8,24},{24,8},{1,17},{17,1},{9,25},{25,9},{2,18},{18... | collective-permute-start | bytes 393224 | tf_op jit(solution)/shard_map/ppermute | solution.py:389
  487.6 19.1 %collective-permute-start.33 = (bf16[32,2048]{1,0:T(8,128)(2,1)S(1)}, bf16[32,2048]{1,0:T(8,128)(2,1)S(1)}, u32[]{:S(2)}, u32[]{:S(2)}) collective-permute-start(bf16[32,2048]{1,0:T(8,128)(2,1)S(1)} %get-tuple-element.183), channel_id=1, source_target_pairs={{0,16},{16,0},{8,24},{24,8},{1,17},{17,1},{9,25},{25,9},{2,18},{18... | collective-permute-start | bytes 393224 | tf_op jit(solution)/shard_map/ppermute | solution.py:389
  488.7 5.0 collective-permute-start.31
  489.3 5.4 collective-permute-start.21
  493.7 6.2 %collective-permute-start.32 = (bf16[32,2048]{1,0:T(8,128)(2,1)S(1)}, bf16[32,2048]{1,0:T(8,128)(2,1)S(1)}, u32[]{:S(2)}, u32[]{:S(2)}) collective-permute-start(bf16[32,2048]{1,0:T(8,128)(2,1)S(1)} %add_convert_fusion.12), channel_id=1, source_target_pairs={{0,16},{16,0},{8,24},{24,8},{1,17},{17,1},{9,25},{25,9},{2,18},{18... | collective-permute-start | bytes 393224 | tf_op jit(solution)/shard_map/ppermute | solution.py:413
  495.2 9.2 %collective-permute-start.23 = (bf16[256,512]{1,0:T(8,128)(2,1)S(1)}, bf16[256,512]{1,0:T(8,128)(2,1)S(1)}, u32[]{:S(2)}, u32[]{:S(2)}) collective-permute-start(bf16[256,512]{1,0:T(8,128)(2,1)S(1)} %get-tuple-element.164), channel_id=1, source_target_pairs={{0,8},{8,0},{16,24},{24,16},{1,9},{9,1},{17,25},{25,17},{2,10},{10... | collective-permute-start | bytes 786440 | tf_op jit(solution)/shard_map/ppermute | solution.py:389
  496.3 9.3 %collective-permute-start.26 = (bf16[256,512]{1,0:T(8,128)(2,1)S(1)}, bf16[256,512]{1,0:T(8,128)(2,1)S(1)}, u32[]{:S(2)}, u32[]{:S(2)}) collective-permute-start(bf16[256,512]{1,0:T(8,128)(2,1)S(1)} %get-tuple-element.166), channel_id=1, source_target_pairs={{0,16},{16,0},{8,24},{24,8},{1,17},{17,1},{9,25},{25,9},{2,18},{18... | collective-permute-start | bytes 786440 | tf_op jit(solution)/shard_map/ppermute | solution.py:389
  499.9 7.7 %collective-permute-start.35 = (bf16[32,2048]{1,0:T(8,128)(2,1)S(1)}, bf16[32,2048]{1,0:T(8,128)(2,1)S(1)}, u32[]{:S(2)}, u32[]{:S(2)}) collective-permute-start(bf16[32,2048]{1,0:T(8,128)(2,1)S(1)} %get-tuple-element.180), channel_id=1, source_target_pairs={{0,8},{8,0},{16,24},{24,16},{1,9},{9,1},{17,25},{25,17},{2,10},{10... | collective-permute-start | bytes 393224 | tf_op jit(solution)/shard_map/ppermute | solution.py:414
  501.0 11.8 %collective-permute-start.22 = (bf16[256,512]{1,0:T(8,128)(2,1)S(1)}, bf16[256,512]{1,0:T(8,128)(2,1)S(1)}, u32[]{:S(2)}, u32[]{:S(2)}) collective-permute-start(bf16[256,512]{1,0:T(8,128)(2,1)S(1)} %get-tuple-element.163), channel_id=1, source_target_pairs={{0,8},{8,0},{16,24},{24,16},{1,9},{9,1},{17,25},{25,17},{2,10},{10... | collective-permute-start | bytes 786440 | tf_op jit(solution)/shard_map/ppermute | solution.py:389
  504.4 8.4 %collective-permute-start.25 = (bf16[256,512]{1,0:T(8,128)(2,1)S(1)}, bf16[256,512]{1,0:T(8,128)(2,1)S(1)}, u32[]{:S(2)}, u32[]{:S(2)}) collective-permute-start(bf16[256,512]{1,0:T(8,128)(2,1)S(1)} %get-tuple-element.165), channel_id=1, source_target_pairs={{0,16},{16,0},{8,24},{24,8},{1,17},{17,1},{9,25},{25,9},{2,18},{18... | collective-permute-start | bytes 786440 | tf_op jit(solution)/shard_map/ppermute | solution.py:389
  505.7 9.9 %collective-permute-start.24 = (bf16[256,512]{1,0:T(8,128)(2,1)S(1)}, bf16[256,512]{1,0:T(8,128)(2,1)S(1)}, u32[]{:S(2)}, u32[]{:S(2)}) collective-permute-start(bf16[256,512]{1,0:T(8,128)(2,1)S(1)} %get-tuple-element.167), channel_id=1, source_target_pairs={{0,16},{16,0},{8,24},{24,8},{1,17},{17,1},{9,25},{25,9},{2,18},{18... | collective-permute-start | bytes 786440 | tf_op jit(solution)/shard_map/ppermute | solution.py:413
  506.6 9.4 %collective-permute-start.27 = (bf16[256,512]{1,0:T(8,128)(2,1)S(1)}, bf16[256,512]{1,0:T(8,128)(2,1)S(1)}, u32[]{:S(2)}, u32[]{:S(2)}) collective-permute-start(bf16[256,512]{1,0:T(8,128)(2,1)S(1)} %get-tuple-element.168), channel_id=1, source_target_pairs={{0,8},{8,0},{16,24},{24,16},{1,9},{9,1},{17,25},{25,17},{2,10},{10... | collective-permute-start | bytes 786440 | tf_op jit(solution)/shard_map/ppermute | solution.py:414
  517.1 22.5 %all-to-all-start.4 = ((bf16[8,64,512]{2,1,0:T(8,128)(2,1)}), bf16[8,64,512]{2,1,0:T(8,128)(2,1)}, u32[]{:S(2)}, u32[]{:S(2)}) async-start(bf16[8,64,512]{2,1,0:T(8,128)(2,1)} %bitcast.21), calls=%async_computation.7 | async-start | bytes 1048576 | tf_op jit(solution)/shard_map/all_to_all | solution.py:340
  536.1 6.6 %copy-start.30 = (f32[64]{0:T(128)S(1)}, f32[64]{0:T(128)}, u32[]{:S(2)}) copy-start(f32[64]{0:T(128)} %copy-done.29) | copy-start | bytes 772
  545.7 6.3 %copy-start.33 = (f32[64]{0:T(128)S(1)}, f32[64]{0:T(128)}, u32[]{:S(2)}) copy-start(f32[64]{0:T(128)} %copy-done.32) | copy-start | bytes 772
  (23 other events, 66.9 us)
Sparse Core Ops, SparseCore 0:
  9.6 75.2 all-gather.11
  136.6 50.4 reduce-scatter.4
  191.0 45.3 all-gather.5
  237.9 45.6 all-gather.7
  285.7 48.7 reduce-scatter.8
  336.6 48.3 reduce-scatter.6
  389.1 45.3 all-gather.9
  481.6 49.7 reduce-scatter.10

commit v7 on v6

--- a/solution.py
+++ b/solution.py
@@ -773,13 +773,17 @@
         jnp.concatenate([heads_back, other_back], axis=1),
         jnp.concatenate([attn_cols, other_cols], axis=1),
     ).astype(bf16)
-    weighted_part, low_all, mlp_grad = tie(weighted_part, low_all, mlp_grad)
-    weighted_one = reduce_ctx(weighted_part).astype(f32)
+    weighted_part, mlp_grad, other_part = tie(weighted_part, mlp_grad, other_part)
+    weighted_one = reduce_ctx(weighted_part)
     attn_part = contract_rows(shaped_all, heads_back)
     own_part = attn_part[:, head_width:] + other_part.astype(f32)
-    attn_grad_own = reduce_seq(
-        [jnp.concatenate([attn_part[:, :head_width].astype(bf16), own_part.astype(bf16)], axis=1)]
-    )
+    attn_parts = [
+        jnp.concatenate([attn_part[:, :head_width].astype(bf16), own_part.astype(bf16)], axis=1)
+    ]
+    attn_near = reduce_seq_near(attn_parts)
+    low_all, *attn_near = tie(low_all, *attn_near)
+    attn_sums = far_sums(attn_parts, *attn_near[:2])
+    attn_grad_own = reduce_seq_far(attn_parts, attn_sums, *attn_near[2:])
     out_grad = reduce_seq([contract_rows(attn_low, low_all).astype(bf16)]).astype(f32)
     attn_grad_own, mlp_grad = tie(attn_grad_own, mlp_grad)
     mlp_grad = mlp_grad.astype(f32)
@@ -788,29 +792,31 @@
     gate_rows = ff_rows(mlp_grad[:, :, :main], mlp_grad[:, :, 2 * main : 2 * main + tail])
     up_rows = ff_rows(mlp_grad[:, :, main : 2 * main], mlp_grad[:, :, 2 * main + tail : both])
     down_grad = ff_rows(mlp_grad[:, :, both : both + main], mlp_grad[:, :, both + main :])
+    block_output = (residual + out_own.astype(f32)).astype(bf16)
+    attn_grad, out_grad, gate_rows, up_rows, down_grad, block_output = tie(
+        attn_grad, out_grad, gate_rows, up_rows, down_grad, block_output
+    )
+    attn_grad = attn_grad.astype(f32)
+    query_rows = from_head_slices(attn_grad[:, :, :head_width])
+    pair_rows = jnp.sum(attn_grad[:, :, head_width:].reshape(4, 2, rows, head_width), axis=0)
+    key_rows, value_rows = pair_rows[0], pair_rows[1]
+
+    def row_sum(weight, grad):
+        return jnp.sum(weight.astype(f32) * grad, axis=1)
+
+    attn_gain_grad = (
+        row_sum(query_weight, query_rows)
+        + row_sum(key_weight, key_rows)
+        + row_sum(value_weight, value_rows)
+    )
+    mlp_gain_grad = row_sum(gate_weight, gate_rows) + row_sum(up_weight, up_rows)
+    weighted_one, attn_gain_grad = tie(weighted_one, attn_gain_grad)
+    weighted_one = weighted_one.astype(f32)
     scale_one = rms_scale(inputs)
     shaped_one = inputs * scale_one
     input_grad = residual_back + scale_one * (
         weighted_one - shaped_one * jnp.mean(weighted_one * shaped_one, axis=-1, keepdims=True)
     )
-    block_output = (residual + out_own.astype(f32)).astype(bf16)
-    attn_grad, out_grad, gate_rows, up_rows, down_grad, input_grad, block_output = tie(
-        attn_grad, out_grad, gate_rows, up_rows, down_grad, input_grad, block_output
-    )
-    attn_grad = attn_grad.astype(f32)
-    query_rows = from_head_slices(attn_grad[:, :, :head_width])
-    pair_rows = jnp.sum(attn_grad[:, :, head_width:].reshape(4, 2, rows, head_width), axis=0)
-    key_rows, value_rows = pair_rows[0], pair_rows[1]
-
-    def row_sum(weight, grad):
-        return jnp.sum(weight.astype(f32) * grad, axis=1)
-
-    attn_gain_grad = (
-        row_sum(query_weight, query_rows)
-        + row_sum(key_weight, key_rows)
-        + row_sum(value_weight, value_rows)
-    )
-    mlp_gain_grad = row_sum(gate_weight, gate_rows) + row_sum(up_weight, up_rows)
     return (
         block_output[None],
         input_grad[None],

time: 571 us -> 585 us (1.025)
  local copies, waits for them, and re-layouts: 104 us -> 114 us
  waiting for transfers between devices: 212 us -> 206 us
    all_to_all x5, waiting for transfers between devices: 25.9 us -> 18.1 us  [exchange_ctx(): return lax.all_to_all(pieces, 'ctx', 0, 0, tiled=True)]
    ppermute x12, waiting for transfers between devices: 8.25 us -> 14.5 us  [send_parts(): lax.ppermute(part, 'seq', axis)]
    unnamed x75 -> x97, local copies, waits for them, and re-layouts: 11.4 us -> 14.5 us
  transfers between devices with their start and end apart: 49 -> 49, of which waited for: 23 -> 22; matrix products, arithmetic and copies ran while one was open for 36% -> 40% of each run, Pallas kernels for 6% -> 6%
where the time goes in v7:
time: 585 us; the launch traced here: 577 us
  waiting for transfers between devices  206 us (35%)
  local copies, waits for them, and re-layouts  114 us (19%)
  matrix products  84.3 us (14%)
  starting transfers between devices  63 us (11%)
  other arithmetic  60.8 us (10%)
  Pallas kernels  32.9 us (6%)
  between operations  16.2 us (3%)
    reduce_scatter x4, waiting for transfers between devices, reduce_ctx(): return lax.psum_scatter(partial, 'ctx', scatter_dimension=0, tiled=True)  52.8 us
    all_gather x4, waiting for transfers between devices, gather_ctx(): return lax.all_gather(block, 'ctx', axis=0, tiled=True)  48.2 us
    ppermute x4, waiting for transfers between devices, gather_seq_far(): far_low = lax.ppermute(from_y[half:], 'seq', SEQ_X)  34.3 us
    dot_general x4, matrix products, contract_cols(): lax.dot_general(left, right, (((1,), (1,)), ((), ())), preferred_element_...  29.6 us
    all_to_all x5, starting transfers between devices, exchange_ctx(): return lax.all_to_all(pieces, 'ctx', 0, 0, tiled=True)  25.9 us
    dynamic_update_slice x20, local copies, waits for them, and re-layouts, gather_seq_far(): whole = lax.dynamic_update_slice_in_dim(whole, piece, start, 0)  25.5 us
    ppermute x3, waiting for transfers between devices, reduce_seq_far(): top_last = lax.ppermute(top_send, 'seq', SEQ_Y)  22.9 us
    dot_general x5, matrix products, contract_rows(): lax.dot_general(left, right, (((0,), (0,)), ((), ())), preferred_element_...  21.6 us
  transfers between devices with their start and end apart: 49, of which 22 were waited for; matrix products, arithmetic and copies ran while one was open for 40% of the time, Pallas kernels for 6%

profile of v7, /device:TPU:0, one launch (start us, length us, event | category | flops | bytes accessed | tf_op | source)
XLA Modules:
  0.0 577.2 jit_solution(8542204273410947733)
XLA Ops:
  7.9 3.1 collective-permute-start.6
  16.3 5.0 all-to-all-start
  27.0 2.2 concatenate.109
  34.6 16.8 %all-to-all-done = bf16[8,64,512]{2,1,0:T(8,128)(2,1)} async-done(((bf16[8,64,512]{2,1,0:T(8,128)(2,1)}), bf16[8,64,512]{2,1,0:T(8,128)(2,1)}, u32[]{:S(2)}, u32[]{:S(2)}) %all-to-all-start) | async-done | bytes 524320 | tf_op jit(solution)/shard_map/all_to_all | solution.py:340
  52.5 3.5 all-to-all-start.1
  58.8 11.7 %collective-permute-done = bf16[512,512]{1,0:T(8,128)(2,1)S(1)} collective-permute-done((bf16[512,512]{1,0:T(8,128)(2,1)}, bf16[512,512]{1,0:T(8,128)(2,1)S(1)}, u32[]{:S(2)}, u32[]{:S(2)}) %collective-permute-start) | collective-permute-done | bytes 524320 | tf_op jit(solution)/shard_map/ppermute | solution.py:344
  72.8 1.9 constant_dynamic-update-slice_fusion.19
  82.6 2.7 collective-permute-done.3
  86.1 2.3 slice.227
  88.4 2.6 copy.80
  91.0 4.6 all-to-all-start.2
  96.2 3.2 fusion
  99.7 5.3 fusion.67
  104.9 3.5 fusion.65
  118.4 13.2 %attend.1 = bf16[1024,256]{1,0:T(8,128)(2,1)} custom-call(s32[1]{0:T(128)} %bitcast.2.refs_0_, bf16[1024,256]{1,0:T(8,128)(2,1)} %get-tuple-element.182.refs_1_, bf16[1024,256]{1,0:T(8,128)(2,1)} %fusion.30.refs_2_, bf16[1024,256]{1,0:T(8,128)(2,1)} %get-tuple-element.181.refs_3_), custom_call_target="tpu_custom_call" | custom-call | flops 4294967296 | bytes 2097152 | tf_op jit(solution)/shard_map/attend/pallas_call | solution.py:581
  131.7 4.6 convolution_convert_fusion.2
  144.0 1.9 broadcast_in_dim.33
  148.2 2.3 copy.84
  151.5 2.2 constant_dynamic-update-slice_fusion.7
  153.7 24.5 %collective-permute-done.12 = bf16[256,704]{0,1:T(8,128)(2,1)} collective-permute-done((bf16[256,704]{0,1:T(8,128)(2,1)}, bf16[256,704]{0,1:T(8,128)(2,1)}, u32[]{:S(2)}, u32[]{:S(2)}) %collective-permute-start.12) | collective-permute-done | bytes 360480 | tf_op jit(solution)/shard_map/ppermute | solution.py:352
  182.1 4.8 reduce-scatter.5.cloned.1.call-done
  188.3 2.4 fusion.72
  194.1 2.9 broadcast_in_dim.34
  196.9 2.8 constant_dynamic-update-slice_fusion.4
  202.3 2.6 constant_dynamic-update-slice_fusion.3
  204.9 2.6 constant_dynamic-update-slice_fusion.2
  209.5 7.0 %collective-permute-done.16 = bf16[256,1408]{1,0:T(8,128)(2,1)S(1)} collective-permute-done((bf16[256,1408]{1,0:T(8,128)(2,1)S(1)}, bf16[256,1408]{1,0:T(8,128)(2,1)S(1)}, u32[]{:S(2)}, u32[]{:S(2)}) %collective-permute-start.16) | collective-permute-done | bytes 720928 | tf_op jit(solution)/shard_map/ppermute | solution.py:352
  217.4 18.8 %all-gather.6.cloned.1.call-done = bf16[1024,2048]{1,0:T(8,128)(2,1)} async-done(((bf16[128,2048]{1,0:T(8,128)(2,1)}), bf16[1024,2048]{1,0:T(8,128)(2,1)}) %all-gather.6.cloned.1.call-update) | async-done | bytes 4194320 | tf_op jit(solution)/shard_map/all_gather | solution.py:332
  236.2 10.7 %fusion.85 = f32[1024,1408]{1,0:T(8,128)S(1)} fusion(bf16[1024,2048]{1,0:T(8,128)(2,1)} %all-gather.6.cloned.1.call-done, bf16[2048,1408]{1,0:T(8,128)(2,1)} %constant_dynamic-update-slice_fusion), kind=kOutput, calls=%fused_computation.238 | convolution fusion | flops 5905580032 | bytes 15728640 | tf_op jit(solution)/shard_map/dot_general | solution.py:712
  251.9 7.0 %convolution_convert_fusion.4 = bf16[1024,2048]{1,0:T(8,128)(2,1)} fusion(bf16[1024,704]{1,0:T(8,128)(2,1)S(1)} %multiply_convert_fusion.2, bf16[2048,704]{1,0:T(8,128)(2,1)} %constant_dynamic-update-slice_fusion.5), kind=kOutput, calls=%fused_computation.24 | convolution fusion | flops 2954887168 | bytes 8519680 | tf_op jit(solution)/shard_map/dot_general | solution.py:53
  258.9 24.5 %all-gather.8.cloned.1.call-done = bf16[1024,2048]{1,0:T(8,128)(2,1)} async-done(((bf16[128,2048]{1,0:T(8,128)(2,1)}), bf16[1024,2048]{1,0:T(8,128)(2,1)}) %all-gather.8.cloned.1.call-update) | async-done | bytes 4194320 | tf_op jit(solution)/shard_map/all_gather | solution.py:332
  283.4 9.0 %multiply_convert_fusion = (bf16[1024,704]{1,0:T(8,128)(2,1)S(1)}, bf16[1024,704]{1,0:T(8,128)(2,1)S(1)}) fusion(f32[1024,64]{1,0:T(8,128)S(1)} %get-tuple-element.157, f32[1024,640]{1,0:T(8,128)} %copy-done.4, f32[1024,64]{1,0:T(8,128)} %copy-done.22, f32[1024,640]{1,0:T(8,128)} %copy-done.5, bf16[1024,2048]{1,0:T(8,128)(2,1)} %all-gather.8.cloned.1.call-done, ...), kind=kOutput, calls=%fused_computation.31 | convolution fusion | flops 2963603456 | bytes 15728640 | tf_op jit(solution)/shard_map/dot_general | solution.py:729
  294.8 5.4 concatenate.118
  300.2 11.0 %convolution_convert_fusion.1 = bf16[1024,2048]{1,0:T(8,128)(2,1)} fusion(bf16[1024,1408]{1,0:T(8,128)(2,1)} %concatenate.118, bf16[2048,1408]{1,0:T(8,128)(2,1)} %constant_dynamic-update-slice_fusion), kind=kOutput, calls=%fused_computation.21 | convolution fusion | flops 5907677184 | bytes 12845056 | tf_op jit(solution)/shard_map/dot_general | solution.py:53
  311.7 6.1 %convolution_convert_fusion.5 = bf16[2048,704]{0,1:T(8,128)(2,1)S(1)} fusion(bf16[1024,2048]{1,0:T(8,128)(2,1)} %all-gather.8.cloned.1.call-done, bf16[1024,704]{1,0:T(8,128)(2,1)} %copy-done.23), kind=kOutput, calls=%fused_computation.25 | convolution fusion | flops 2954231808 | bytes 8519680 | tf_op jit(solution)/shard_map/dot_general | solution.py:47
  320.2 6.6 %convolution_convert_fusion = bf16[2048,1408]{0,1:T(8,128)(2,1)S(1)} fusion(bf16[1024,2048]{1,0:T(8,128)(2,1)S(1)} %copy-done.45, bf16[1024,1408]{1,0:T(8,128)(2,1)S(1)} %copy-done.14), kind=kOutput, calls=%fused_computation.4 | convolution fusion | flops 5908463616 | bytes 12845056 | tf_op jit(solution)/shard_map/dot_general | solution.py:47
  338.3 46.5 %reduce-scatter.7.cloned.1.call-done = bf16[128,2048]{1,0:T(8,128)(2,1)} async-done(((bf16[1024,2048]{1,0:T(8,128)(2,1)}), bf16[128,2048]{1,0:T(8,128)(2,1)}) %reduce-scatter.7.cloned.1.call-update) | async-done | bytes 524304 | tf_op jit(solution)/shard_map/reduce_scatter | solution.py:336
  386.5 2.7 fusion.70
  389.2 1.9 add_convert_fusion.3
  395.8 19.2 %collective-permute-done.21 = bf16[256,2112]{0,1:T(8,128)(2,1)S(1)} collective-permute-done((bf16[256,2112]{0,1:T(8,128)(2,1)S(1)}, bf16[256,2112]{0,1:T(8,128)(2,1)S(1)}, u32[]{:S(2)}, u32[]{:S(2)}) %collective-permute-start.21) | collective-permute-done | bytes 1081376 | tf_op jit(solution)/shard_map/ppermute | solution.py:413
  421.2 4.1 copy.94
  425.3 4.4 all-to-all-start.3
  429.9 4.9 all-gather.10.cloned.1.call-done
  434.8 4.6 convolution_convert_fusion.8.refs_4_
  439.3 19.7 %attend_back.1 = (f32[1024,256]{1,0:T(8,128)}, f32[1024,256]{1,0:T(8,128)}, f32[1024,256]{1,0:T(8,128)}) custom-call(s32[1]{0:T(128)} %bitcast.2.refs_0_, bf16[1024,256]{1,0:T(8,128)(2,1)} %get-tuple-element.182.refs_1_, bf16[1024,256]{1,0:T(8,128)(2,1)} %fusion.30.refs_2_, bf16[1024,256]{1,0:T(8,128)(2,1)} %get-tuple-element.181.refs_3_, ...), custom_call_target="tpu_custom_call" | custom-call | flops 10737418240 | bytes 3670016 | tf_op jit(solution)/shard_map/attend_back/pallas_call | solution.py:602
  466.6 2.8 convolution_convert_fusion.7
  469.7 2.6 fusion.62
  472.3 2.1 copy-done.20
  474.5 7.1 %convolution_convert_fusion.3 = bf16[1024,2048]{1,0:T(8,128)(2,1)} fusion(bf16[2048,256]{1,0:T(8,128)(2,1)} %collective-permute-done.4, bf16[2048,512]{1,0:T(8,128)(2,1)} %constant_dynamic-update-slice_fusion.15, bf16[1024,256]{1,0:T(8,128)(2,1)S(1)} %get-tuple-element.139, bf16[1024,512]{1,0:T(8,128)(2,1)S(1)} %pad_maximum_fusion.10), kind=kOutput, calls=%fused_computation.23 | convolution fusion | flops 3232759808 | bytes 8912896 | tf_op jit(solution)/shard_map/dot_general | solution.py:53
  482.6 2.1 fusion.6
  489.7 5.4 collective-permute-done.27
  496.9 3.3 collective-permute-done.25
  501.6 3.5 convolution_convert_fusion.6
  509.3 2.6 collective-permute-done.31
  513.1 2.1 collective-permute-start.28
  520.7 2.6 collective-permute-done.28
  525.4 8.3 %all-to-all-start.4 = ((bf16[8,64,512]{2,1,0:T(8,128)(2,1)}), bf16[8,64,512]{2,1,0:T(8,128)(2,1)}, u32[]{:S(2)}, u32[]{:S(2)}) async-start(bf16[8,64,512]{2,1,0:T(8,128)(2,1)} %bitcast.21), calls=%async_computation.7 | async-start | bytes 1048576 | tf_op jit(solution)/shard_map/all_to_all | solution.py:340
  533.6 2.0 convert_element_type.350
  549.0 2.1 fusion.84
  551.1 2.4 reshape.171
  553.6 2.8 copy.114
  556.4 2.4 reshape.172
  559.9 3.5 broadcast_multiply_fusion
  567.7 2.4 fusion.21
  (314 shorter events, 149.8 us)
Async XLA Ops:
  7.2 8.1 %copy-start.38 = (bf16[64,256]{1,0:T(8,128)(2,1)S(1)}, bf16[64,256]{1,0:T(8,128)(2,1)}, u32[]{:S(2)}) copy-start(bf16[64,256]{1,0:T(8,128)(2,1)} %param.19) | copy-start | bytes 98308
  7.2 8.1 %copy-start.36 = (bf16[64,256]{1,0:T(8,128)(2,1)S(1)}, bf16[64,256]{1,0:T(8,128)(2,1)}, u32[]{:S(2)}) copy-start(bf16[64,256]{1,0:T(8,128)(2,1)} %param.18) | copy-start | bytes 98308
  7.2 89.0 %all-gather.12.cloned.1.call-start = ((), (), s32[]{:S(2)}) async-start(), calls=%async_computation.16 | async-start | bytes 4718592 | tf_op jit(solution)/shard_map/all_gather | solution.py:332
  7.9 21.4 %collective-permute-start.6 = (bf16[64,2048]{1,0:T(8,128)(2,1)}, bf16[64,2048]{1,0:T(8,128)(2,1)}, u32[]{:S(2)}, u32[]{:S(2)}) collective-permute-start(bf16[64,2048]{1,0:T(8,128)(2,1)} %param.20), channel_id=1, source_target_pairs={{0,16},{16,0},{8,24},{24,8},{1,17},{17,1},{9,25},{25,9},{2,18},{18... | collective-permute-start | bytes 786440 | tf_op jit(solution)/shard_map/ppermute | solution.py:344
  11.0 20.5 %collective-permute-start.5 = (bf16[64,2048]{1,0:T(8,128)(2,1)}, bf16[64,2048]{1,0:T(8,128)(2,1)}, u32[]{:S(2)}, u32[]{:S(2)}) collective-permute-start(bf16[64,2048]{1,0:T(8,128)(2,1)} %param.20), channel_id=1, source_target_pairs={{0,8},{8,0},{16,24},{24,16},{1,9},{9,1},{17,25},{25,17},{2,10},{10... | collective-permute-start | bytes 786440 | tf_op jit(solution)/shard_map/ppermute | solution.py:344
  16.3 6.1 %copy-start.42 = (s32[1,1024]{1,0:T(1,128)S(1)}, s32[1,1024]{1,0:T(1,128)}, u32[]{:S(2)}) copy-start(s32[1,1024]{1,0:T(1,128)} %param.14) | copy-start | bytes 12292
  16.3 8.7 %copy-start.15 = (bf16[64,5632]{1,0:T(8,128)(2,1)S(1)}, bf16[64,5632]{1,0:T(8,128)(2,1)}, u32[]{:S(2)}) copy-start(bf16[64,5632]{1,0:T(8,128)(2,1)} %param.23) | copy-start | bytes 2162692
  16.3 8.7 %copy-start.16 = (bf16[64,5632]{1,0:T(8,128)(2,1)S(1)}, bf16[64,5632]{1,0:T(8,128)(2,1)}, u32[]{:S(2)}) copy-start(bf16[64,5632]{1,0:T(8,128)(2,1)} %param.22) | copy-start | bytes 2162692
  16.3 35.0 %all-to-all-start = ((bf16[8,64,512]{2,1,0:T(8,128)(2,1)}), bf16[8,64,512]{2,1,0:T(8,128)(2,1)}, u32[]{:S(2)}, u32[]{:S(2)}) async-start(bf16[8,64,512]{2,1,0:T(8,128)(2,1)} %pad_maximum_fusion.12), calls=%async_computation | async-start | bytes 1048576 | tf_op jit(solution)/shard_map/all_to_all | solution.py:340
  31.0 27.8 %collective-permute-start.8 = (bf16[32,2048]{1,0:T(8,128)(2,1)}, bf16[32,2048]{1,0:T(8,128)(2,1)S(1)}, u32[]{:S(2)}, u32[]{:S(2)}) collective-permute-start(bf16[32,2048]{1,0:T(8,128)(2,1)} %slice.233), channel_id=1, source_target_pairs={{0,8},{8,0},{16,24},{24,16},{1,9},{9,1},{17,25},{25,17},{2,10},{10... | collective-permute-start | bytes 393224 | tf_op jit(solution)/shard_map/ppermute | solution.py:352
  33.1 24.8 %collective-permute-start.7 = (bf16[32,2048]{1,0:T(8,128)(2,1)}, bf16[32,2048]{1,0:T(8,128)(2,1)}, u32[]{:S(2)}, u32[]{:S(2)}) collective-permute-start(bf16[32,2048]{1,0:T(8,128)(2,1)} %slice.232), channel_id=1, source_target_pairs={{0,16},{16,0},{8,24},{24,8},{1,17},{17,1},{9,25},{25,9},{2,18},{18... | collective-permute-start | bytes 393224 | tf_op jit(solution)/shard_map/ppermute | solution.py:351
  52.5 35.8 %all-to-all-start.1 = ((bf16[8,64,704]{2,1,0:T(8,128)(2,1)}), bf16[8,64,704]{2,1,0:T(8,128)(2,1)S(1)}, u32[]{:S(2)}, u32[]{:S(2)}) async-start(bf16[8,64,704]{2,1,0:T(8,128)(2,1)} %pad_maximum_fusion.11), calls=%async_computation.1 | async-start | bytes 1572864 | tf_op jit(solution)/shard_map/all_to_all | solution.py:340
  56.1 14.4 %collective-permute-start = (bf16[512,512]{1,0:T(8,128)(2,1)}, bf16[512,512]{1,0:T(8,128)(2,1)S(1)}, u32[]{:S(2)}, u32[]{:S(2)}) collective-permute-start(bf16[512,512]{1,0:T(8,128)(2,1)} %bitcast.7), channel_id=1, source_target_pairs={{0,8},{8,0},{16,24},{24,16},{1,9},{9,1},{17,25},{25,17},{2,10},{10... | collective-permute-start | bytes 1572872 | tf_op jit(solution)/shard_map/ppermute | solution.py:344
  57.3 19.4 %collective-permute-start.1 = (bf16[512,512]{1,0:T(8,128)(2,1)}, bf16[512,512]{1,0:T(8,128)(2,1)}, u32[]{:S(2)}, u32[]{:S(2)}) collective-permute-start(bf16[512,512]{1,0:T(8,128)(2,1)} %bitcast.7), channel_id=1, source_target_pairs={{0,16},{16,0},{8,24},{24,8},{1,17},{17,1},{9,25},{25,9},{2,18},{18... | collective-permute-start | bytes 1572872 | tf_op jit(solution)/shard_map/ppermute | solution.py:344
  58.8 14.0 %copy-start.13 = (bf16[256,2048]{1,0:T(8,128)(2,1)}, bf16[256,2048]{1,0:T(8,128)(2,1)S(1)}, u32[]{:S(2)}) copy-start(bf16[256,2048]{1,0:T(8,128)(2,1)S(1)} %constant_dynamic-update-slice_fusion.10) | copy-start | bytes 3145732
  71.3 9.7 %collective-permute-start.2 = (bf16[256,512]{1,0:T(8,128)(2,1)}, bf16[256,512]{1,0:T(8,128)(2,1)}, u32[]{:S(2)}, u32[]{:S(2)}) collective-permute-start(bf16[256,512]{1,0:T(8,128)(2,1)} %slice.225), channel_id=1, source_target_pairs={{0,16},{16,0},{8,24},{24,8},{1,17},{17,1},{9,25},{25,9},{2,18},{18... | collective-permute-start | bytes 786440 | tf_op jit(solution)/shard_map/ppermute | solution.py:351
  77.6 7.7 %collective-permute-start.3 = (bf16[256,512]{1,0:T(8,128)(2,1)S(1)}, bf16[256,512]{1,0:T(8,128)(2,1)S(1)}, u32[]{:S(2)}, u32[]{:S(2)}) collective-permute-start(bf16[256,512]{1,0:T(8,128)(2,1)S(1)} %slice.226), channel_id=1, source_target_pairs={{0,8},{8,0},{16,24},{24,16},{1,9},{9,1},{17,25},{25,17},{2,10},{10... | collective-permute-start | bytes 786440 | tf_op jit(solution)/shard_map/ppermute | solution.py:352
  88.4 16.6 %collective-permute-start.4 = (bf16[2048,256]{1,0:T(8,128)(2,1)}, bf16[2048,256]{1,0:T(8,128)(2,1)}, u32[]{:S(2)}, u32[]{:S(2)}) collective-permute-start(bf16[2048,256]{1,0:T(8,128)(2,1)} %slice.227), channel_id=1, source_target_pairs={{0,1},{1,0},{2,3},{3,2},{4,5},{5,4},{6,7},{7,6},{8,9},{9,8},{10,11... | collective-permute-start | bytes 3145736 | tf_op jit(solution)/shard_map/ppermute | solution.py:434
  91.0 40.7 %all-to-all-start.2 = ((bf16[8,64,1408]{2,1,0:T(8,128)(2,1)}), bf16[8,64,1408]{2,1,0:T(8,128)(2,1)}, u32[]{:S(2)}, u32[]{:S(2)}) async-start(bf16[8,64,1408]{2,1,0:T(8,128)(2,1)} %copy.80), calls=%async_computation.2 | async-start | bytes 2883584 | tf_op jit(solution)/shard_map/all_to_all | solution.py:340
  95.6 91.3 %reduce-scatter.5.cloned.1.call-start = ((), (), s32[]{:S(2)}) async-start(), calls=%async_computation.9 | async-start | bytes 4718592 | tf_op jit(solution)/shard_map/reduce_scatter | solution.py:336
  109.6 22.1 %collective-permute-start.10 = (bf16[512,704]{0,1:T(8,128)(2,1)}, bf16[512,704]{0,1:T(8,128)(2,1)}, u32[]{:S(2)}, u32[]{:S(2)}) collective-permute-start(bf16[512,704]{0,1:T(8,128)(2,1)} %copy.81), channel_id=1, source_target_pairs={{0,16},{16,0},{8,24},{24,8},{1,17},{17,1},{9,25},{25,9},{2,18},{18... | collective-permute-start | bytes 2162696 | tf_op jit(solution)/shard_map/ppermute | solution.py:344
  111.3 20.4 %collective-permute-start.9 = (bf16[512,704]{0,1:T(8,128)(2,1)}, bf16[512,704]{0,1:T(8,128)(2,1)}, u32[]{:S(2)}, u32[]{:S(2)}) collective-permute-start(bf16[512,704]{0,1:T(8,128)(2,1)} %copy.81), channel_id=1, source_target_pairs={{0,8},{8,0},{16,24},{24,16},{1,9},{9,1},{17,25},{25,17},{2,10},{10... | collective-permute-start | bytes 2162696 | tf_op jit(solution)/shard_map/ppermute | solution.py:344
  136.3 99.9 %all-gather.6.cloned.1.call-start = ((), (), s32[]{:S(2)}) async-start(), calls=%async_computation.10 | async-start | bytes 4718592 | tf_op jit(solution)/shard_map/all_gather | solution.py:332
  136.4 45.7 %collective-permute-start.14 = (bf16[512,1408]{1,0:T(8,128)(2,1)}, bf16[512,1408]{1,0:T(8,128)(2,1)}, u32[]{:S(2)}, u32[]{:S(2)}) collective-permute-start(bf16[512,1408]{1,0:T(8,128)(2,1)} %bitcast.19), channel_id=1, source_target_pairs={{0,16},{16,0},{8,24},{24,8},{1,17},{17,1},{9,25},{25,9},{2,18},{18... | collective-permute-start | bytes 4325384 | tf_op jit(solution)/shard_map/ppermute | solution.py:344
  137.2 44.9 %collective-permute-start.13 = (bf16[512,1408]{1,0:T(8,128)(2,1)}, bf16[512,1408]{1,0:T(8,128)(2,1)}, u32[]{:S(2)}, u32[]{:S(2)}) collective-permute-start(bf16[512,1408]{1,0:T(8,128)(2,1)} %bitcast.19), channel_id=1, source_target_pairs={{0,8},{8,0},{16,24},{24,16},{1,9},{9,1},{17,25},{25,17},{2,10},{10... | collective-permute-start | bytes 4325384 | tf_op jit(solution)/shard_map/ppermute | solution.py:344
  141.8 36.4 %collective-permute-start.12 = (bf16[256,704]{0,1:T(8,128)(2,1)}, bf16[256,704]{0,1:T(8,128)(2,1)}, u32[]{:S(2)}, u32[]{:S(2)}) collective-permute-start(bf16[256,704]{0,1:T(8,128)(2,1)} %slice.190), channel_id=1, source_target_pairs={{0,8},{8,0},{16,24},{24,16},{1,9},{9,1},{17,25},{25,17},{2,10},{10... | collective-permute-start | bytes 1081352 | tf_op jit(solution)/shard_map/ppermute | solution.py:352
  142.7 36.6 %collective-permute-start.11 = (bf16[256,704]{0,1:T(8,128)(2,1)}, bf16[256,704]{0,1:T(8,128)(2,1)}, u32[]{:S(2)}, u32[]{:S(2)}) collective-permute-start(bf16[256,704]{0,1:T(8,128)(2,1)} %slice.189), channel_id=1, source_target_pairs={{0,16},{16,0},{8,24},{24,8},{1,17},{17,1},{9,25},{25,9},{2,18},{18... | collective-permute-start | bytes 1081352 | tf_op jit(solution)/shard_map/ppermute | solution.py:351
  151.5 35.5 %copy-start = (bf16[1,128,2048]{2,1,0:T(8,128)(2,1)S(1)}, bf16[1,128,2048]{2,1,0:T(8,128)(2,1)}, u32[]{:S(2)}) copy-start(bf16[1,128,2048]{2,1,0:T(8,128)(2,1)} %param.13) | copy-start | bytes 1572868
  190.7 92.6 %all-gather.8.cloned.1.call-start = ((), (), s32[]{:S(2)}) async-start(), calls=%async_computation.11 | async-start | bytes 4718592 | tf_op jit(solution)/shard_map/all_gather | solution.py:332
  191.3 143.0 %reduce-scatter.9.cloned.1.call-start = ((), (), s32[]{:S(2)}) async-start(), calls=%async_computation.13 | async-start | bytes 4718592 | tf_op jit(solution)/shard_map/reduce_scatter | solution.py:336
  192.5 16.1 %collective-permute-start.15 = (bf16[256,1408]{1,0:T(8,128)(2,1)S(1)}, bf16[256,1408]{1,0:T(8,128)(2,1)S(1)}, u32[]{:S(2)}, u32[]{:S(2)}) collective-permute-start(bf16[256,1408]{1,0:T(8,128)(2,1)S(1)} %slice.191), channel_id=1, source_target_pairs={{0,16},{16,0},{8,24},{24,8},{1,17},{17,1},{9,25},{25,9},{2,18},{18... | collective-permute-start | bytes 2162696 | tf_op jit(solution)/shard_map/ppermute | solution.py:351
  200.9 15.6 %collective-permute-start.16 = (bf16[256,1408]{1,0:T(8,128)(2,1)S(1)}, bf16[256,1408]{1,0:T(8,128)(2,1)S(1)}, u32[]{:S(2)}, u32[]{:S(2)}) collective-permute-start(bf16[256,1408]{1,0:T(8,128)(2,1)S(1)} %slice.192), channel_id=1, source_target_pairs={{0,8},{8,0},{16,24},{24,16},{1,9},{9,1},{17,25},{25,17},{2,10},{10... | collective-permute-start | bytes 2162696 | tf_op jit(solution)/shard_map/ppermute | solution.py:352
  283.4 101.4 %reduce-scatter.7.cloned.1.call-start = ((), (), s32[]{:S(2)}) async-start(), calls=%async_computation.12 | async-start | bytes 4718592 | tf_op jit(solution)/shard_map/reduce_scatter | solution.py:336
  311.3 123.5 %all-gather.10.cloned.1.call-start = ((), (), s32[]{:S(2)}) async-start(), calls=%async_computation.14 | async-start | bytes 4718592 | tf_op jit(solution)/shard_map/all_gather | solution.py:332
  311.7 7.5 %copy-start.45 = (bf16[1024,2048]{1,0:T(8,128)(2,1)S(1)}, bf16[1024,2048]{1,0:T(8,128)(2,1)}, u32[]{:S(2)}) copy-start(bf16[1024,2048]{1,0:T(8,128)(2,1)} %all-gather.6.cloned.1.call-done) | copy-start | bytes 12582916
  334.3 50.6 %collective-permute-start.17 = (bf16[256,2112]{0,1:T(8,128)(2,1)}, bf16[256,2112]{0,1:T(8,128)(2,1)}, u32[]{:S(2)}, u32[]{:S(2)}) collective-permute-start(bf16[256,2112]{0,1:T(8,128)(2,1)} %pad_maximum_fusion.6), channel_id=1, source_target_pairs={{0,8},{8,0},{16,24},{24,16},{1,9},{9,1},{17,25},{25,17},{2,10},{10... | collective-permute-start | bytes 3244040 | tf_op jit(solution)/shard_map/ppermute | solution.py:389
  335.7 49.1 %collective-permute-start.18 = (bf16[256,2112]{0,1:T(8,128)(2,1)}, bf16[256,2112]{0,1:T(8,128)(2,1)}, u32[]{:S(2)}, u32[]{:S(2)}) collective-permute-start(bf16[256,2112]{0,1:T(8,128)(2,1)} %pad_maximum_fusion.7), channel_id=1, source_target_pairs={{0,16},{16,0},{8,24},{24,8},{1,17},{17,1},{9,25},{25,9},{2,18},{18... | collective-permute-start | bytes 3244040 | tf_op jit(solution)/shard_map/ppermute | solution.py:389
  337.2 47.6 %collective-permute-start.19 = (bf16[256,2112]{0,1:T(8,128)(2,1)}, bf16[256,2112]{0,1:T(8,128)(2,1)}, u32[]{:S(2)}, u32[]{:S(2)}) collective-permute-start(bf16[256,2112]{0,1:T(8,128)(2,1)} %pad_maximum_fusion.8), channel_id=1, source_target_pairs={{0,8},{8,0},{16,24},{24,16},{1,9},{9,1},{17,25},{25,17},{2,10},{10... | collective-permute-start | bytes 3244040 | tf_op jit(solution)/shard_map/ppermute | solution.py:389
  337.8 47.1 %collective-permute-start.20 = (bf16[256,2112]{0,1:T(8,128)(2,1)}, bf16[256,2112]{0,1:T(8,128)(2,1)}, u32[]{:S(2)}, u32[]{:S(2)}) collective-permute-start(bf16[256,2112]{0,1:T(8,128)(2,1)} %pad_maximum_fusion.9), channel_id=1, source_target_pairs={{0,16},{16,0},{8,24},{24,8},{1,17},{17,1},{9,25},{25,9},{2,18},{18... | collective-permute-start | bytes 3244040 | tf_op jit(solution)/shard_map/ppermute | solution.py:389
  391.1 23.8 %copy-start.17 = (bf16[256,1408]{0,1:T(8,128)(2,1)S(1)}, bf16[256,1408]{0,1:T(8,128)(2,1)}, u32[]{:S(2)}) copy-start(bf16[256,1408]{0,1:T(8,128)(2,1)} %get-tuple-element.147) | copy-start | bytes 2162692
  391.2 23.8 %copy-start.26 = (bf16[256,704]{0,1:T(8,128)(2,1)S(1)}, bf16[256,704]{0,1:T(8,128)(2,1)}, u32[]{:S(2)}) copy-start(bf16[256,704]{0,1:T(8,128)(2,1)} %get-tuple-element.165) | copy-start | bytes 1081348
  391.2 23.8 %collective-permute-start.21 = (bf16[256,2112]{0,1:T(8,128)(2,1)S(1)}, bf16[256,2112]{0,1:T(8,128)(2,1)S(1)}, u32[]{:S(2)}, u32[]{:S(2)}) collective-permute-start(bf16[256,2112]{0,1:T(8,128)(2,1)S(1)} %add_convert_fusion.3), channel_id=1, source_target_pairs={{0,16},{16,0},{8,24},{24,8},{1,17},{17,1},{9,25},{25,9},{2,18},{18... | collective-permute-start | bytes 3244040 | tf_op jit(solution)/shard_map/ppermute | solution.py:413
  394.3 23.5 %collective-permute-start.22 = (bf16[256,2112]{0,1:T(8,128)(2,1)S(1)}, bf16[256,2112]{0,1:T(8,128)(2,1)S(1)}, u32[]{:S(2)}, u32[]{:S(2)}) collective-permute-start(bf16[256,2112]{0,1:T(8,128)(2,1)S(1)} %add_convert_fusion.1), channel_id=1, source_target_pairs={{0,8},{8,0},{16,24},{24,16},{1,9},{9,1},{17,25},{25,17},{2,10},{10... | collective-permute-start | bytes 3244040 | tf_op jit(solution)/shard_map/ppermute | solution.py:414
  425.3 56.3 %all-to-all-start.3 = ((bf16[8,64,2112]{2,1,0:T(8,128)(2,1)}), bf16[8,64,2112]{2,1,0:T(8,128)(2,1)}, u32[]{:S(2)}, u32[]{:S(2)}) async-start(bf16[8,64,2112]{2,1,0:T(8,128)(2,1)} %bitcast.117), calls=%async_computation.6 | async-start | bytes 4456448 | tf_op jit(solution)/shard_map/all_to_all | solution.py:340
  429.6 136.7 %reduce-scatter.11.cloned.1.call-start = ((), (), s32[]{:S(2)}) async-start(), calls=%async_computation.15 | async-start | bytes 4718592 | tf_op jit(solution)/shard_map/reduce_scatter | solution.py:336
  469.4 12.1 %collective-permute-start.23 = (bf16[2048,256]{1,0:T(8,128)(2,1)}, bf16[2048,256]{1,0:T(8,128)(2,1)S(1)}, u32[]{:S(2)}, u32[]{:S(2)}) collective-permute-start(bf16[2048,256]{1,0:T(8,128)(2,1)} %convolution_convert_fusion.7), channel_id=1, source_target_pairs={{0,1},{1,0},{2,3},{3,2},{4,5},{5,4},{6,7},{7,6},{8,9},{9,8},{10,11... | collective-permute-start | bytes 3145736 | tf_op jit(solution)/shard_map/ppermute | solution.py:434
  484.7 17.0 %copy-start.27 = (bf16[1024,256]{1,0:T(8,128)(2,1)S(1)}, bf16[1024,256]{1,0:T(8,128)(2,1)}, u32[]{:S(2)}) copy-start(bf16[1024,256]{1,0:T(8,128)(2,1)} %attend.1) | copy-start | bytes 1572868
  485.7 9.5 %collective-permute-start.27 = (bf16[256,512]{1,0:T(8,128)(2,1)}, bf16[256,512]{1,0:T(8,128)(2,1)}, u32[]{:S(2)}, u32[]{:S(2)}) collective-permute-start(bf16[256,512]{1,0:T(8,128)(2,1)} %get-tuple-element.177), channel_id=1, source_target_pairs={{0,16},{16,0},{8,24},{24,8},{1,17},{17,1},{9,25},{25,9},{2,18},{18... | collective-permute-start | bytes 786440 | tf_op jit(solution)/shard_map/ppermute | solution.py:389
  487.5 9.4 %collective-permute-start.24 = (bf16[256,512]{1,0:T(8,128)(2,1)}, bf16[256,512]{1,0:T(8,128)(2,1)S(1)}, u32[]{:S(2)}, u32[]{:S(2)}) collective-permute-start(bf16[256,512]{1,0:T(8,128)(2,1)} %get-tuple-element.178), channel_id=1, source_target_pairs={{0,8},{8,0},{16,24},{24,16},{1,9},{9,1},{17,25},{25,17},{2,10},{10... | collective-permute-start | bytes 786440 | tf_op jit(solution)/shard_map/ppermute | solution.py:389
  489.0 11.2 %collective-permute-start.25 = (bf16[256,512]{1,0:T(8,128)(2,1)}, bf16[256,512]{1,0:T(8,128)(2,1)}, u32[]{:S(2)}, u32[]{:S(2)}) collective-permute-start(bf16[256,512]{1,0:T(8,128)(2,1)} %get-tuple-element.179), channel_id=1, source_target_pairs={{0,16},{16,0},{8,24},{24,8},{1,17},{17,1},{9,25},{25,9},{2,18},{18... | collective-permute-start | bytes 786440 | tf_op jit(solution)/shard_map/ppermute | solution.py:389
  489.1 12.5 %collective-permute-start.26 = (bf16[256,512]{1,0:T(8,128)(2,1)}, bf16[256,512]{1,0:T(8,128)(2,1)}, u32[]{:S(2)}, u32[]{:S(2)}) collective-permute-start(bf16[256,512]{1,0:T(8,128)(2,1)} %get-tuple-element.180), channel_id=1, source_target_pairs={{0,8},{8,0},{16,24},{24,16},{1,9},{9,1},{17,25},{25,17},{2,10},{10... | collective-permute-start | bytes 786440 | tf_op jit(solution)/shard_map/ppermute | solution.py:389
  489.7 17.8 %copy-start.7 = (bf16[128,2048]{1,0:T(8,128)(2,1)S(1)}, bf16[128,2048]{1,0:T(8,128)(2,1)}, u32[]{:S(2)}) copy-start(bf16[128,2048]{1,0:T(8,128)(2,1)} %reduce-scatter.5.cloned.1.call-done) | copy-start | bytes 1572868
  489.7 17.8 %copy-start.33 = (bf16[128,2048]{1,0:T(8,128)(2,1)S(1)}, bf16[128,2048]{1,0:T(8,128)(2,1)}, u32[]{:S(2)}) copy-start(bf16[128,2048]{1,0:T(8,128)(2,1)} %reduce-scatter.9.cloned.1.call-done) | copy-start | bytes 1572868
  505.2 13.3 %copy-start.28 = (bf16[256,2048]{1,0:T(8,128)(2,1)}, bf16[256,2048]{1,0:T(8,128)(2,1)S(1)}, u32[]{:S(2)}) copy-start(bf16[256,2048]{1,0:T(8,128)(2,1)S(1)} %convolution_convert_fusion.6) | copy-start | bytes 3145732
  506.0 6.0 %collective-permute-start.31 = (bf16[32,2048]{1,0:T(8,128)(2,1)S(1)}, bf16[32,2048]{1,0:T(8,128)(2,1)S(1)}, u32[]{:S(2)}, u32[]{:S(2)}) collective-permute-start(bf16[32,2048]{1,0:T(8,128)(2,1)S(1)} %get-tuple-element.196), channel_id=1, source_target_pairs={{0,8},{8,0},{16,24},{24,16},{1,9},{9,1},{17,25},{25,17},{2,10},{10... | collective-permute-start | bytes 393224 | tf_op jit(solution)/shard_map/ppermute | solution.py:389
  508.5 8.2 %collective-permute-start.30 = (bf16[32,2048]{1,0:T(8,128)(2,1)S(1)}, bf16[32,2048]{1,0:T(8,128)(2,1)S(1)}, u32[]{:S(2)}, u32[]{:S(2)}) collective-permute-start(bf16[32,2048]{1,0:T(8,128)(2,1)S(1)} %get-tuple-element.193), channel_id=1, source_target_pairs={{0,8},{8,0},{16,24},{24,16},{1,9},{9,1},{17,25},{25,17},{2,10},{10... | collective-permute-start | bytes 393224 | tf_op jit(solution)/shard_map/ppermute | solution.py:389
  509.0 8.2 %collective-permute-start.34 = (bf16[32,2048]{1,0:T(8,128)(2,1)S(1)}, bf16[32,2048]{1,0:T(8,128)(2,1)S(1)}, u32[]{:S(2)}, u32[]{:S(2)}) collective-permute-start(bf16[32,2048]{1,0:T(8,128)(2,1)S(1)} %get-tuple-element.194), channel_id=1, source_target_pairs={{0,16},{16,0},{8,24},{24,8},{1,17},{17,1},{9,25},{25,9},{2,18},{18... | collective-permute-start | bytes 393224 | tf_op jit(solution)/shard_map/ppermute | solution.py:389
  512.0 6.4 %collective-permute-start.32 = (bf16[32,2048]{1,0:T(8,128)(2,1)S(1)}, bf16[32,2048]{1,0:T(8,128)(2,1)S(1)}, u32[]{:S(2)}, u32[]{:S(2)}) collective-permute-start(bf16[32,2048]{1,0:T(8,128)(2,1)S(1)} %add_convert_fusion.12), channel_id=1, source_target_pairs={{0,16},{16,0},{8,24},{24,8},{1,17},{17,1},{9,25},{25,9},{2,18},{18... | collective-permute-start | bytes 393224 | tf_op jit(solution)/shard_map/ppermute | solution.py:413
  513.1 10.1 %collective-permute-start.28 = (bf16[256,512]{1,0:T(8,128)(2,1)S(1)}, bf16[256,512]{1,0:T(8,128)(2,1)S(1)}, u32[]{:S(2)}, u32[]{:S(2)}) collective-permute-start(bf16[256,512]{1,0:T(8,128)(2,1)S(1)} %get-tuple-element.175), channel_id=1, source_target_pairs={{0,16},{16,0},{8,24},{24,8},{1,17},{17,1},{9,25},{25,9},{2,18},{18... | collective-permute-start | bytes 786440 | tf_op jit(solution)/shard_map/ppermute | solution.py:413
  515.2 8.1 %collective-permute-start.29 = (bf16[256,512]{1,0:T(8,128)(2,1)S(1)}, bf16[256,512]{1,0:T(8,128)(2,1)S(1)}, u32[]{:S(2)}, u32[]{:S(2)}) collective-permute-start(bf16[256,512]{1,0:T(8,128)(2,1)S(1)} %get-tuple-element.176), channel_id=1, source_target_pairs={{0,8},{8,0},{16,24},{24,16},{1,9},{9,1},{17,25},{25,17},{2,10},{10... | collective-permute-start | bytes 786440 | tf_op jit(solution)/shard_map/ppermute | solution.py:414
  516.7 29.1 %collective-permute-start.33 = (bf16[32,2048]{1,0:T(8,128)(2,1)}, bf16[32,2048]{1,0:T(8,128)(2,1)}, u32[]{:S(2)}, u32[]{:S(2)}) collective-permute-start(bf16[32,2048]{1,0:T(8,128)(2,1)} %get-tuple-element.195), channel_id=1, source_target_pairs={{0,16},{16,0},{8,24},{24,8},{1,17},{17,1},{9,25},{25,9},{2,18},{18... | collective-permute-start | bytes 393224 | tf_op jit(solution)/shard_map/ppermute | solution.py:389
  519.2 26.6 %collective-permute-start.35 = (bf16[32,2048]{1,0:T(8,128)(2,1)}, bf16[32,2048]{1,0:T(8,128)(2,1)}, u32[]{:S(2)}, u32[]{:S(2)}) collective-permute-start(bf16[32,2048]{1,0:T(8,128)(2,1)} %get-tuple-element.192), channel_id=1, source_target_pairs={{0,8},{8,0},{16,24},{24,16},{1,9},{9,1},{17,25},{25,17},{2,10},{10... | collective-permute-start | bytes 393224 | tf_op jit(solution)/shard_map/ppermute | solution.py:414
  525.4 23.7 %all-to-all-start.4 = ((bf16[8,64,512]{2,1,0:T(8,128)(2,1)}), bf16[8,64,512]{2,1,0:T(8,128)(2,1)}, u32[]{:S(2)}, u32[]{:S(2)}) async-start(bf16[8,64,512]{2,1,0:T(8,128)(2,1)} %bitcast.21), calls=%async_computation.7 | async-start | bytes 1048576 | tf_op jit(solution)/shard_map/all_to_all | solution.py:340
  553.6 6.3 %copy-start.44 = (f32[64]{0:T(128)S(1)}, f32[64]{0:T(128)}, u32[]{:S(2)}) copy-start(f32[64]{0:T(128)} %copy-done.43) | copy-start | bytes 772
  (34 other events, 96.3 us)
Sparse Core Ops, SparseCore 0:
  9.6 75.2 all-gather.11
  136.5 50.4 reduce-scatter.4
  190.9 45.3 all-gather.5
  237.7 45.6 all-gather.7
  285.5 48.7 reduce-scatter.8
  336.4 48.3 reduce-scatter.6
  389.3 45.3 all-gather.9
  482.7 53.6 reduce-scatter.10

commit v8 on v7

--- a/solution.py
+++ b/solution.py
@@ -773,17 +773,15 @@
         jnp.concatenate([heads_back, other_back], axis=1),
         jnp.concatenate([attn_cols, other_cols], axis=1),
     ).astype(bf16)
-    weighted_part, mlp_grad, other_part = tie(weighted_part, mlp_grad, other_part)
+    weighted_part, mlp_grad, other_part, low_all = tie(
+        weighted_part, mlp_grad, other_part, low_all
+    )
     weighted_one = reduce_ctx(weighted_part)
     attn_part = contract_rows(shaped_all, heads_back)
     own_part = attn_part[:, head_width:] + other_part.astype(f32)
-    attn_parts = [
-        jnp.concatenate([attn_part[:, :head_width].astype(bf16), own_part.astype(bf16)], axis=1)
-    ]
-    attn_near = reduce_seq_near(attn_parts)
-    low_all, *attn_near = tie(low_all, *attn_near)
-    attn_sums = far_sums(attn_parts, *attn_near[:2])
-    attn_grad_own = reduce_seq_far(attn_parts, attn_sums, *attn_near[2:])
+    attn_grad_own = reduce_seq(
+        [jnp.concatenate([attn_part[:, :head_width].astype(bf16), own_part.astype(bf16)], axis=1)]
+    )
     out_grad = reduce_seq([contract_rows(attn_low, low_all).astype(bf16)]).astype(f32)
     attn_grad_own, mlp_grad = tie(attn_grad_own, mlp_grad)
     mlp_grad = mlp_grad.astype(f32)

time: 585 us -> 580 us (level)
    all_to_all x5, waiting for transfers between devices: 18.1 us -> 24.2 us  [exchange_ctx(): return lax.all_to_all(pieces, 'ctx', 0, 0, tiled=True)]
    ppermute x12, waiting for transfers between devices: 14.5 us -> 8.57 us  [send_parts(): lax.ppermute(part, 'seq', axis)]
    unnamed x97 -> x93, local copies, waits for them, and re-layouts: 14.5 us -> 12.5 us
  transfers between devices with their start and end apart: 49 -> 49, of which waited for: 22 -> 22; matrix products, arithmetic and copies ran while one was open for 40% -> 39% of each run, Pallas kernels for 6% -> 6%
where the time goes in v8:
time: 580 us; the launch traced here: 571 us
  waiting for transfers between devices  210 us (36%)
  local copies, waits for them, and re-layouts  111 us (19%)
  matrix products  85.1 us (15%)
  starting transfers between devices  60.9 us (10%)
  other arithmetic  55.5 us (10%)
  Pallas kernels  32.9 us (6%)
  between operations  16.2 us (3%)
    reduce_scatter x4, waiting for transfers between devices, reduce_ctx(): return lax.psum_scatter(partial, 'ctx', scatter_dimension=0, tiled=True)  52.7 us
    all_gather x4, waiting for transfers between devices, gather_ctx(): return lax.all_gather(block, 'ctx', axis=0, tiled=True)  48.2 us
    ppermute x4, waiting for transfers between devices, gather_seq_far(): far_low = lax.ppermute(from_y[half:], 'seq', SEQ_X)  34.2 us
    dot_general x4, matrix products, contract_cols(): lax.dot_general(left, right, (((1,), (1,)), ((), ())), preferred_element_...  30.1 us
    dynamic_update_slice x20, local copies, waits for them, and re-layouts, gather_seq_far(): whole = lax.dynamic_update_slice_in_dim(whole, piece, start, 0)  25.6 us
    ppermute x3, waiting for transfers between devices, reduce_seq_far(): top_last = lax.ppermute(top_send, 'seq', SEQ_Y)  25.2 us
    all_to_all x5, waiting for transfers between devices, exchange_ctx(): return lax.all_to_all(pieces, 'ctx', 0, 0, tiled=True)  24.2 us
    dot_general x5, matrix products, contract_rows(): lax.dot_general(left, right, (((0,), (0,)), ((), ())), preferred_element_...  21.9 us
  transfers between devices with their start and end apart: 49, of which 22 were waited for; matrix products, arithmetic and copies ran while one was open for 39% of the time, Pallas kernels for 6%

profile of v8, /device:TPU:0, one launch (start us, length us, event | category | flops | bytes accessed | tf_op | source)
XLA Modules:
  0.0 570.9 jit_solution(9593142224788806859)
XLA Ops:
  7.9 3.1 collective-permute-start.6
  16.3 5.0 all-to-all-start
  27.0 2.2 concatenate.109
  34.6 16.8 %all-to-all-done = bf16[8,64,512]{2,1,0:T(8,128)(2,1)} async-done(((bf16[8,64,512]{2,1,0:T(8,128)(2,1)}), bf16[8,64,512]{2,1,0:T(8,128)(2,1)}, u32[]{:S(2)}, u32[]{:S(2)}) %all-to-all-start) | async-done | bytes 524320 | tf_op jit(solution)/shard_map/all_to_all | solution.py:340
  52.5 3.5 all-to-all-start.1
  58.8 11.7 %collective-permute-done = bf16[512,512]{1,0:T(8,128)(2,1)S(1)} collective-permute-done((bf16[512,512]{1,0:T(8,128)(2,1)}, bf16[512,512]{1,0:T(8,128)(2,1)S(1)}, u32[]{:S(2)}, u32[]{:S(2)}) %collective-permute-start) | collective-permute-done | bytes 524320 | tf_op jit(solution)/shard_map/ppermute | solution.py:344
  72.8 1.9 constant_dynamic-update-slice_fusion.19
  79.1 1.9 constant_dynamic-update-slice_fusion.17
  82.6 2.7 collective-permute-done.3
  86.1 2.3 slice.227
  88.3 2.6 copy.80
  91.0 4.6 all-to-all-start.2
  96.2 3.2 fusion
  99.6 5.3 fusion.67
  104.9 3.5 fusion.65
  118.4 13.2 %attend.1 = bf16[1024,256]{1,0:T(8,128)(2,1)} custom-call(s32[1]{0:T(128)} %bitcast.2.refs_0_, bf16[1024,256]{1,0:T(8,128)(2,1)} %get-tuple-element.174.refs_1_, bf16[1024,256]{1,0:T(8,128)(2,1)} %fusion.30.refs_2_, bf16[1024,256]{1,0:T(8,128)(2,1)} %get-tuple-element.173.refs_3_), custom_call_target="tpu_custom_call" | custom-call | flops 4294967296 | bytes 2097152 | tf_op jit(solution)/shard_map/attend/pallas_call | solution.py:581
  131.7 4.7 convolution_convert_fusion.2
  144.0 1.9 broadcast_in_dim.33
  148.2 2.3 copy.84
  151.5 2.2 constant_dynamic-update-slice_fusion.7
  153.7 24.6 %collective-permute-done.12 = bf16[256,704]{0,1:T(8,128)(2,1)} collective-permute-done((bf16[256,704]{0,1:T(8,128)(2,1)}, bf16[256,704]{0,1:T(8,128)(2,1)}, u32[]{:S(2)}, u32[]{:S(2)}) %collective-permute-start.12) | collective-permute-done | bytes 360480 | tf_op jit(solution)/shard_map/ppermute | solution.py:352
  182.2 4.8 reduce-scatter.5.cloned.1.call-done
  188.4 2.4 fusion.72
  194.1 2.9 broadcast_in_dim.34
  197.0 2.8 constant_dynamic-update-slice_fusion.4
  202.3 2.6 constant_dynamic-update-slice_fusion.3
  204.9 2.6 constant_dynamic-update-slice_fusion.2
  209.6 7.0 %collective-permute-done.16 = bf16[256,1408]{1,0:T(8,128)(2,1)S(1)} collective-permute-done((bf16[256,1408]{1,0:T(8,128)(2,1)S(1)}, bf16[256,1408]{1,0:T(8,128)(2,1)S(1)}, u32[]{:S(2)}, u32[]{:S(2)}) %collective-permute-start.16) | collective-permute-done | bytes 720928 | tf_op jit(solution)/shard_map/ppermute | solution.py:352
  217.5 18.8 %all-gather.6.cloned.1.call-done = bf16[1024,2048]{1,0:T(8,128)(2,1)} async-done(((bf16[128,2048]{1,0:T(8,128)(2,1)}), bf16[1024,2048]{1,0:T(8,128)(2,1)}) %all-gather.6.cloned.1.call-update) | async-done | bytes 4194320 | tf_op jit(solution)/shard_map/all_gather | solution.py:332
  236.3 10.7 %fusion.85 = f32[1024,1408]{1,0:T(8,128)S(1)} fusion(bf16[1024,2048]{1,0:T(8,128)(2,1)} %all-gather.6.cloned.1.call-done, bf16[2048,1408]{1,0:T(8,128)(2,1)} %constant_dynamic-update-slice_fusion), kind=kOutput, calls=%fused_computation.238 | convolution fusion | flops 5905580032 | bytes 15728640 | tf_op jit(solution)/shard_map/dot_general | solution.py:712
  251.9 6.9 %convolution_convert_fusion.4 = bf16[1024,2048]{1,0:T(8,128)(2,1)} fusion(bf16[1024,704]{1,0:T(8,128)(2,1)S(1)} %multiply_convert_fusion.2, bf16[2048,704]{1,0:T(8,128)(2,1)} %constant_dynamic-update-slice_fusion.5), kind=kOutput, calls=%fused_computation.24 | convolution fusion | flops 2954887168 | bytes 8519680 | tf_op jit(solution)/shard_map/dot_general | solution.py:53
  258.9 24.6 %all-gather.8.cloned.1.call-done = bf16[1024,2048]{1,0:T(8,128)(2,1)} async-done(((bf16[128,2048]{1,0:T(8,128)(2,1)}), bf16[1024,2048]{1,0:T(8,128)(2,1)}) %all-gather.8.cloned.1.call-update) | async-done | bytes 4194320 | tf_op jit(solution)/shard_map/all_gather | solution.py:332
  283.5 9.0 %multiply_convert_fusion = (bf16[1024,704]{1,0:T(8,128)(2,1)S(1)}, bf16[1024,704]{1,0:T(8,128)(2,1)S(1)}) fusion(f32[1024,64]{1,0:T(8,128)S(1)} %get-tuple-element.149, f32[1024,640]{1,0:T(8,128)} %copy-done.4, f32[1024,64]{1,0:T(8,128)} %copy-done.21, f32[1024,640]{1,0:T(8,128)} %copy-done.5, bf16[1024,2048]{1,0:T(8,128)(2,1)} %all-gather.8.cloned.1.call-done, ...), kind=kOutput, calls=%fused_computation.31 | convolution fusion | flops 2963603456 | bytes 15728640 | tf_op jit(solution)/shard_map/dot_general | solution.py:729
  294.9 5.4 concatenate.118
  300.2 11.0 %convolution_convert_fusion.1 = bf16[1024,2048]{1,0:T(8,128)(2,1)} fusion(bf16[1024,1408]{1,0:T(8,128)(2,1)} %concatenate.118, bf16[2048,1408]{1,0:T(8,128)(2,1)} %constant_dynamic-update-slice_fusion), kind=kOutput, calls=%fused_computation.21 | convolution fusion | flops 5907677184 | bytes 12845056 | tf_op jit(solution)/shard_map/dot_general | solution.py:53
  311.8 6.1 %convolution_convert_fusion.5 = bf16[2048,704]{0,1:T(8,128)(2,1)S(1)} fusion(bf16[1024,2048]{1,0:T(8,128)(2,1)} %all-gather.8.cloned.1.call-done, bf16[1024,704]{1,0:T(8,128)(2,1)} %copy-done.22), kind=kOutput, calls=%fused_computation.25 | convolution fusion | flops 2954231808 | bytes 8519680 | tf_op jit(solution)/shard_map/dot_general | solution.py:47
  320.2 6.6 %convolution_convert_fusion = bf16[2048,1408]{0,1:T(8,128)(2,1)S(1)} fusion(bf16[1024,2048]{1,0:T(8,128)(2,1)S(1)} %copy-done.43, bf16[1024,1408]{1,0:T(8,128)(2,1)S(1)} %copy-done.14), kind=kOutput, calls=%fused_computation.4 | convolution fusion | flops 5908463616 | bytes 12845056 | tf_op jit(solution)/shard_map/dot_general | solution.py:47
  338.4 46.5 %reduce-scatter.7.cloned.1.call-done = bf16[128,2048]{1,0:T(8,128)(2,1)} async-done(((bf16[1024,2048]{1,0:T(8,128)(2,1)}), bf16[128,2048]{1,0:T(8,128)(2,1)}) %reduce-scatter.7.cloned.1.call-update) | async-done | bytes 524304 | tf_op jit(solution)/shard_map/reduce_scatter | solution.py:336
  386.6 2.7 fusion.70
  389.3 1.9 add_convert_fusion.3
  395.9 19.2 %collective-permute-done.21 = bf16[256,2112]{0,1:T(8,128)(2,1)S(1)} collective-permute-done((bf16[256,2112]{0,1:T(8,128)(2,1)S(1)}, bf16[256,2112]{0,1:T(8,128)(2,1)S(1)}, u32[]{:S(2)}, u32[]{:S(2)}) %collective-permute-start.21) | collective-permute-done | bytes 1081376 | tf_op jit(solution)/shard_map/ppermute | solution.py:413
  421.3 4.1 copy.94
  425.3 4.4 all-to-all-start.3
  429.9 4.9 all-gather.10.cloned.1.call-done
  434.8 4.6 convolution_convert_fusion.8.refs_4_
  439.4 19.7 %attend_back.1 = (f32[1024,256]{1,0:T(8,128)}, f32[1024,256]{1,0:T(8,128)}, f32[1024,256]{1,0:T(8,128)}) custom-call(s32[1]{0:T(128)} %bitcast.2.refs_0_, bf16[1024,256]{1,0:T(8,128)(2,1)} %get-tuple-element.174.refs_1_, bf16[1024,256]{1,0:T(8,128)(2,1)} %fusion.30.refs_2_, bf16[1024,256]{1,0:T(8,128)(2,1)} %get-tuple-element.173.refs_3_, ...), custom_call_target="tpu_custom_call" | custom-call | flops 10737418240 | bytes 3670016 | tf_op jit(solution)/shard_map/attend_back/pallas_call | solution.py:602
  466.8 2.8 convolution_convert_fusion.7
  469.9 7.6 %convolution_convert_fusion.3 = bf16[1024,2048]{1,0:T(8,128)(2,1)} fusion(bf16[2048,256]{1,0:T(8,128)(2,1)} %collective-permute-done.4, bf16[2048,512]{1,0:T(8,128)(2,1)} %constant_dynamic-update-slice_fusion.15, bf16[1024,256]{1,0:T(8,128)(2,1)} %copy-done.29, bf16[1024,512]{1,0:T(8,128)(2,1)S(1)} %pad_maximum_fusion.10), kind=kOutput, calls=%fused_computation.23 | convolution fusion | flops 3232759808 | bytes 8912896 | tf_op jit(solution)/shard_map/dot_general | solution.py:53
  477.5 4.1 all-to-all-done.3
  481.7 2.1 add_convert_fusion.4
  483.7 5.1 fusion.62
  501.5 3.4 collective-permute-done.32
  505.7 4.0 collective-permute-done.25
  511.2 2.7 collective-permute-done.28
  518.1 2.7 collective-permute-done.26
  523.2 4.2 all-to-all-start.4
  527.4 2.0 convert_element_type.350
  539.4 3.3 all-to-all-done.4
  542.7 2.1 fusion.84
  544.8 2.4 reshape.171
  547.3 2.8 copy.114
  550.1 2.4 reshape.172
  553.6 3.5 broadcast_multiply_fusion
  561.4 2.4 fusion.21
  (310 shorter events, 144.2 us)
Async XLA Ops:
  7.2 8.1 %copy-start.35 = (bf16[64,256]{1,0:T(8,128)(2,1)S(1)}, bf16[64,256]{1,0:T(8,128)(2,1)}, u32[]{:S(2)}) copy-start(bf16[64,256]{1,0:T(8,128)(2,1)} %param.19) | copy-start | bytes 98308
  7.2 8.1 %copy-start.33 = (bf16[64,256]{1,0:T(8,128)(2,1)S(1)}, bf16[64,256]{1,0:T(8,128)(2,1)}, u32[]{:S(2)}) copy-start(bf16[64,256]{1,0:T(8,128)(2,1)} %param.18) | copy-start | bytes 98308
  7.2 89.0 %all-gather.12.cloned.1.call-start = ((), (), s32[]{:S(2)}) async-start(), calls=%async_computation.16 | async-start | bytes 4718592 | tf_op jit(solution)/shard_map/all_gather | solution.py:332
  7.9 21.4 %collective-permute-start.6 = (bf16[64,2048]{1,0:T(8,128)(2,1)}, bf16[64,2048]{1,0:T(8,128)(2,1)}, u32[]{:S(2)}, u32[]{:S(2)}) collective-permute-start(bf16[64,2048]{1,0:T(8,128)(2,1)} %param.20), channel_id=1, source_target_pairs={{0,16},{16,0},{8,24},{24,8},{1,17},{17,1},{9,25},{25,9},{2,18},{18... | collective-permute-start | bytes 786440 | tf_op jit(solution)/shard_map/ppermute | solution.py:344
  11.0 20.5 %collective-permute-start.5 = (bf16[64,2048]{1,0:T(8,128)(2,1)}, bf16[64,2048]{1,0:T(8,128)(2,1)}, u32[]{:S(2)}, u32[]{:S(2)}) collective-permute-start(bf16[64,2048]{1,0:T(8,128)(2,1)} %param.20), channel_id=1, source_target_pairs={{0,8},{8,0},{16,24},{24,16},{1,9},{9,1},{17,25},{25,17},{2,10},{10... | collective-permute-start | bytes 786440 | tf_op jit(solution)/shard_map/ppermute | solution.py:344
  15.3 6.0 %copy-start.44 = (bf16[64]{0:T(256)(128)(2,1)S(1)}, bf16[64]{0:T(256)(128)(2,1)}, u32[]{:S(2)}) copy-start(bf16[64]{0:T(256)(128)(2,1)} %param.21) | copy-start | bytes 388
  15.3 6.0 %slice-start = ((bf16[64,5632]{1,0:T(8,128)(2,1)}), bf16[64,512]{1,0:T(8,128)(2,1)S(1)}, s32[]{:S(2)}) async-start(bf16[64,5632]{1,0:T(8,128)(2,1)} %param.24), calls=%async_computation.17 | async-start | bytes 131072 | tf_op jit(solution)/shard_map/slice | solution.py:447
  15.4 6.1 %slice-start.1 = ((bf16[64,5632]{1,0:T(8,128)(2,1)}), bf16[64,5120]{1,0:T(8,128)(2,1)S(1)}, s32[]{:S(2)}) async-start(bf16[64,5632]{1,0:T(8,128)(2,1)} %param.24), calls=%async_computation.18 | async-start | bytes 1310720 | tf_op jit(solution)/shard_map/slice | solution.py:446
  16.3 6.1 %copy-start.39 = (s32[1,1024]{1,0:T(1,128)S(1)}, s32[1,1024]{1,0:T(1,128)}, u32[]{:S(2)}) copy-start(s32[1,1024]{1,0:T(1,128)} %param.14) | copy-start | bytes 12292
  16.3 8.7 %copy-start.15 = (bf16[64,5632]{1,0:T(8,128)(2,1)S(1)}, bf16[64,5632]{1,0:T(8,128)(2,1)}, u32[]{:S(2)}) copy-start(bf16[64,5632]{1,0:T(8,128)(2,1)} %param.23) | copy-start | bytes 2162692
  16.3 8.7 %copy-start.16 = (bf16[64,5632]{1,0:T(8,128)(2,1)S(1)}, bf16[64,5632]{1,0:T(8,128)(2,1)}, u32[]{:S(2)}) copy-start(bf16[64,5632]{1,0:T(8,128)(2,1)} %param.22) | copy-start | bytes 2162692
  16.3 35.0 %all-to-all-start = ((bf16[8,64,512]{2,1,0:T(8,128)(2,1)}), bf16[8,64,512]{2,1,0:T(8,128)(2,1)}, u32[]{:S(2)}, u32[]{:S(2)}) async-start(bf16[8,64,512]{2,1,0:T(8,128)(2,1)} %pad_maximum_fusion.12), calls=%async_computation | async-start | bytes 1048576 | tf_op jit(solution)/shard_map/all_to_all | solution.py:340
  31.0 27.8 %collective-permute-start.8 = (bf16[32,2048]{1,0:T(8,128)(2,1)}, bf16[32,2048]{1,0:T(8,128)(2,1)S(1)}, u32[]{:S(2)}, u32[]{:S(2)}) collective-permute-start(bf16[32,2048]{1,0:T(8,128)(2,1)} %slice.233), channel_id=1, source_target_pairs={{0,8},{8,0},{16,24},{24,16},{1,9},{9,1},{17,25},{25,17},{2,10},{10... | collective-permute-start | bytes 393224 | tf_op jit(solution)/shard_map/ppermute | solution.py:352
  33.1 24.8 %collective-permute-start.7 = (bf16[32,2048]{1,0:T(8,128)(2,1)}, bf16[32,2048]{1,0:T(8,128)(2,1)}, u32[]{:S(2)}, u32[]{:S(2)}) collective-permute-start(bf16[32,2048]{1,0:T(8,128)(2,1)} %slice.232), channel_id=1, source_target_pairs={{0,16},{16,0},{8,24},{24,8},{1,17},{17,1},{9,25},{25,9},{2,18},{18... | collective-permute-start | bytes 393224 | tf_op jit(solution)/shard_map/ppermute | solution.py:351
  52.5 35.8 %all-to-all-start.1 = ((bf16[8,64,704]{2,1,0:T(8,128)(2,1)}), bf16[8,64,704]{2,1,0:T(8,128)(2,1)S(1)}, u32[]{:S(2)}, u32[]{:S(2)}) async-start(bf16[8,64,704]{2,1,0:T(8,128)(2,1)} %pad_maximum_fusion.11), calls=%async_computation.1 | async-start | bytes 1572864 | tf_op jit(solution)/shard_map/all_to_all | solution.py:340
  56.1 14.4 %collective-permute-start = (bf16[512,512]{1,0:T(8,128)(2,1)}, bf16[512,512]{1,0:T(8,128)(2,1)S(1)}, u32[]{:S(2)}, u32[]{:S(2)}) collective-permute-start(bf16[512,512]{1,0:T(8,128)(2,1)} %bitcast.7), channel_id=1, source_target_pairs={{0,8},{8,0},{16,24},{24,16},{1,9},{9,1},{17,25},{25,17},{2,10},{10... | collective-permute-start | bytes 1572872 | tf_op jit(solution)/shard_map/ppermute | solution.py:344
  57.3 19.4 %collective-permute-start.1 = (bf16[512,512]{1,0:T(8,128)(2,1)}, bf16[512,512]{1,0:T(8,128)(2,1)}, u32[]{:S(2)}, u32[]{:S(2)}) collective-permute-start(bf16[512,512]{1,0:T(8,128)(2,1)} %bitcast.7), channel_id=1, source_target_pairs={{0,16},{16,0},{8,24},{24,8},{1,17},{17,1},{9,25},{25,9},{2,18},{18... | collective-permute-start | bytes 1572872 | tf_op jit(solution)/shard_map/ppermute | solution.py:344
  58.8 14.0 %copy-start.13 = (bf16[256,2048]{1,0:T(8,128)(2,1)}, bf16[256,2048]{1,0:T(8,128)(2,1)S(1)}, u32[]{:S(2)}) copy-start(bf16[256,2048]{1,0:T(8,128)(2,1)S(1)} %constant_dynamic-update-slice_fusion.10) | copy-start | bytes 3145732
  71.3 9.7 %collective-permute-start.2 = (bf16[256,512]{1,0:T(8,128)(2,1)}, bf16[256,512]{1,0:T(8,128)(2,1)}, u32[]{:S(2)}, u32[]{:S(2)}) collective-permute-start(bf16[256,512]{1,0:T(8,128)(2,1)} %slice.225), channel_id=1, source_target_pairs={{0,16},{16,0},{8,24},{24,8},{1,17},{17,1},{9,25},{25,9},{2,18},{18... | collective-permute-start | bytes 786440 | tf_op jit(solution)/shard_map/ppermute | solution.py:351
  77.6 7.7 %collective-permute-start.3 = (bf16[256,512]{1,0:T(8,128)(2,1)S(1)}, bf16[256,512]{1,0:T(8,128)(2,1)S(1)}, u32[]{:S(2)}, u32[]{:S(2)}) collective-permute-start(bf16[256,512]{1,0:T(8,128)(2,1)S(1)} %slice.226), channel_id=1, source_target_pairs={{0,8},{8,0},{16,24},{24,16},{1,9},{9,1},{17,25},{25,17},{2,10},{10... | collective-permute-start | bytes 786440 | tf_op jit(solution)/shard_map/ppermute | solution.py:352
  88.3 16.6 %collective-permute-start.4 = (bf16[2048,256]{1,0:T(8,128)(2,1)}, bf16[2048,256]{1,0:T(8,128)(2,1)}, u32[]{:S(2)}, u32[]{:S(2)}) collective-permute-start(bf16[2048,256]{1,0:T(8,128)(2,1)} %slice.227), channel_id=1, source_target_pairs={{0,1},{1,0},{2,3},{3,2},{4,5},{5,4},{6,7},{7,6},{8,9},{9,8},{10,11... | collective-permute-start | bytes 3145736 | tf_op jit(solution)/shard_map/ppermute | solution.py:434
  91.0 40.7 %all-to-all-start.2 = ((bf16[8,64,1408]{2,1,0:T(8,128)(2,1)}), bf16[8,64,1408]{2,1,0:T(8,128)(2,1)}, u32[]{:S(2)}, u32[]{:S(2)}) async-start(bf16[8,64,1408]{2,1,0:T(8,128)(2,1)} %copy.80), calls=%async_computation.2 | async-start | bytes 2883584 | tf_op jit(solution)/shard_map/all_to_all | solution.py:340
  95.6 91.4 %reduce-scatter.5.cloned.1.call-start = ((), (), s32[]{:S(2)}) async-start(), calls=%async_computation.9 | async-start | bytes 4718592 | tf_op jit(solution)/shard_map/reduce_scatter | solution.py:336
  109.6 22.1 %collective-permute-start.10 = (bf16[512,704]{0,1:T(8,128)(2,1)}, bf16[512,704]{0,1:T(8,128)(2,1)}, u32[]{:S(2)}, u32[]{:S(2)}) collective-permute-start(bf16[512,704]{0,1:T(8,128)(2,1)} %copy.81), channel_id=1, source_target_pairs={{0,16},{16,0},{8,24},{24,8},{1,17},{17,1},{9,25},{25,9},{2,18},{18... | collective-permute-start | bytes 2162696 | tf_op jit(solution)/shard_map/ppermute | solution.py:344
  111.3 20.3 %collective-permute-start.9 = (bf16[512,704]{0,1:T(8,128)(2,1)}, bf16[512,704]{0,1:T(8,128)(2,1)}, u32[]{:S(2)}, u32[]{:S(2)}) collective-permute-start(bf16[512,704]{0,1:T(8,128)(2,1)} %copy.81), channel_id=1, source_target_pairs={{0,8},{8,0},{16,24},{24,16},{1,9},{9,1},{17,25},{25,17},{2,10},{10... | collective-permute-start | bytes 2162696 | tf_op jit(solution)/shard_map/ppermute | solution.py:344
  136.3 99.9 %all-gather.6.cloned.1.call-start = ((), (), s32[]{:S(2)}) async-start(), calls=%async_computation.10 | async-start | bytes 4718592 | tf_op jit(solution)/shard_map/all_gather | solution.py:332
  136.4 45.8 %collective-permute-start.14 = (bf16[512,1408]{1,0:T(8,128)(2,1)}, bf16[512,1408]{1,0:T(8,128)(2,1)}, u32[]{:S(2)}, u32[]{:S(2)}) collective-permute-start(bf16[512,1408]{1,0:T(8,128)(2,1)} %bitcast.19), channel_id=1, source_target_pairs={{0,16},{16,0},{8,24},{24,8},{1,17},{17,1},{9,25},{25,9},{2,18},{18... | collective-permute-start | bytes 4325384 | tf_op jit(solution)/shard_map/ppermute | solution.py:344
  137.3 44.9 %collective-permute-start.13 = (bf16[512,1408]{1,0:T(8,128)(2,1)}, bf16[512,1408]{1,0:T(8,128)(2,1)}, u32[]{:S(2)}, u32[]{:S(2)}) collective-permute-start(bf16[512,1408]{1,0:T(8,128)(2,1)} %bitcast.19), channel_id=1, source_target_pairs={{0,8},{8,0},{16,24},{24,16},{1,9},{9,1},{17,25},{25,17},{2,10},{10... | collective-permute-start | bytes 4325384 | tf_op jit(solution)/shard_map/ppermute | solution.py:344
  141.8 36.5 %collective-permute-start.12 = (bf16[256,704]{0,1:T(8,128)(2,1)}, bf16[256,704]{0,1:T(8,128)(2,1)}, u32[]{:S(2)}, u32[]{:S(2)}) collective-permute-start(bf16[256,704]{0,1:T(8,128)(2,1)} %slice.190), channel_id=1, source_target_pairs={{0,8},{8,0},{16,24},{24,16},{1,9},{9,1},{17,25},{25,17},{2,10},{10... | collective-permute-start | bytes 1081352 | tf_op jit(solution)/shard_map/ppermute | solution.py:352
  142.8 36.7 %collective-permute-start.11 = (bf16[256,704]{0,1:T(8,128)(2,1)}, bf16[256,704]{0,1:T(8,128)(2,1)}, u32[]{:S(2)}, u32[]{:S(2)}) collective-permute-start(bf16[256,704]{0,1:T(8,128)(2,1)} %slice.189), channel_id=1, source_target_pairs={{0,16},{16,0},{8,24},{24,8},{1,17},{17,1},{9,25},{25,9},{2,18},{18... | collective-permute-start | bytes 1081352 | tf_op jit(solution)/shard_map/ppermute | solution.py:351
  151.5 35.5 %copy-start = (bf16[1,128,2048]{2,1,0:T(8,128)(2,1)S(1)}, bf16[1,128,2048]{2,1,0:T(8,128)(2,1)}, u32[]{:S(2)}) copy-start(bf16[1,128,2048]{2,1,0:T(8,128)(2,1)} %param.13) | copy-start | bytes 1572868
  190.8 92.6 %all-gather.8.cloned.1.call-start = ((), (), s32[]{:S(2)}) async-start(), calls=%async_computation.11 | async-start | bytes 4718592 | tf_op jit(solution)/shard_map/all_gather | solution.py:332
  191.4 142.9 %reduce-scatter.9.cloned.1.call-start = ((), (), s32[]{:S(2)}) async-start(), calls=%async_computation.13 | async-start | bytes 4718592 | tf_op jit(solution)/shard_map/reduce_scatter | solution.py:336
  192.6 16.1 %collective-permute-start.15 = (bf16[256,1408]{1,0:T(8,128)(2,1)S(1)}, bf16[256,1408]{1,0:T(8,128)(2,1)S(1)}, u32[]{:S(2)}, u32[]{:S(2)}) collective-permute-start(bf16[256,1408]{1,0:T(8,128)(2,1)S(1)} %slice.191), channel_id=1, source_target_pairs={{0,16},{16,0},{8,24},{24,8},{1,17},{17,1},{9,25},{25,9},{2,18},{18... | collective-permute-start | bytes 2162696 | tf_op jit(solution)/shard_map/ppermute | solution.py:351
  201.0 15.6 %collective-permute-start.16 = (bf16[256,1408]{1,0:T(8,128)(2,1)S(1)}, bf16[256,1408]{1,0:T(8,128)(2,1)S(1)}, u32[]{:S(2)}, u32[]{:S(2)}) collective-permute-start(bf16[256,1408]{1,0:T(8,128)(2,1)S(1)} %slice.192), channel_id=1, source_target_pairs={{0,8},{8,0},{16,24},{24,16},{1,9},{9,1},{17,25},{25,17},{2,10},{10... | collective-permute-start | bytes 2162696 | tf_op jit(solution)/shard_map/ppermute | solution.py:352
  283.4 101.4 %reduce-scatter.7.cloned.1.call-start = ((), (), s32[]{:S(2)}) async-start(), calls=%async_computation.12 | async-start | bytes 4718592 | tf_op jit(solution)/shard_map/reduce_scatter | solution.py:336
  311.3 123.5 %all-gather.10.cloned.1.call-start = ((), (), s32[]{:S(2)}) async-start(), calls=%async_computation.14 | async-start | bytes 4718592 | tf_op jit(solution)/shard_map/all_gather | solution.py:332
  311.8 7.5 %copy-start.43 = (bf16[1024,2048]{1,0:T(8,128)(2,1)S(1)}, bf16[1024,2048]{1,0:T(8,128)(2,1)}, u32[]{:S(2)}) copy-start(bf16[1024,2048]{1,0:T(8,128)(2,1)} %all-gather.6.cloned.1.call-done) | copy-start | bytes 12582916
  334.3 50.6 %collective-permute-start.17 = (bf16[256,2112]{0,1:T(8,128)(2,1)}, bf16[256,2112]{0,1:T(8,128)(2,1)}, u32[]{:S(2)}, u32[]{:S(2)}) collective-permute-start(bf16[256,2112]{0,1:T(8,128)(2,1)} %pad_maximum_fusion.6), channel_id=1, source_target_pairs={{0,8},{8,0},{16,24},{24,16},{1,9},{9,1},{17,25},{25,17},{2,10},{10... | collective-permute-start | bytes 3244040 | tf_op jit(solution)/shard_map/ppermute | solution.py:389
  335.8 49.1 %collective-permute-start.18 = (bf16[256,2112]{0,1:T(8,128)(2,1)}, bf16[256,2112]{0,1:T(8,128)(2,1)}, u32[]{:S(2)}, u32[]{:S(2)}) collective-permute-start(bf16[256,2112]{0,1:T(8,128)(2,1)} %pad_maximum_fusion.7), channel_id=1, source_target_pairs={{0,16},{16,0},{8,24},{24,8},{1,17},{17,1},{9,25},{25,9},{2,18},{18... | collective-permute-start | bytes 3244040 | tf_op jit(solution)/shard_map/ppermute | solution.py:389
  337.3 47.6 %collective-permute-start.19 = (bf16[256,2112]{0,1:T(8,128)(2,1)}, bf16[256,2112]{0,1:T(8,128)(2,1)}, u32[]{:S(2)}, u32[]{:S(2)}) collective-permute-start(bf16[256,2112]{0,1:T(8,128)(2,1)} %pad_maximum_fusion.8), channel_id=1, source_target_pairs={{0,8},{8,0},{16,24},{24,16},{1,9},{9,1},{17,25},{25,17},{2,10},{10... | collective-permute-start | bytes 3244040 | tf_op jit(solution)/shard_map/ppermute | solution.py:389
  337.8 47.1 %collective-permute-start.20 = (bf16[256,2112]{0,1:T(8,128)(2,1)}, bf16[256,2112]{0,1:T(8,128)(2,1)}, u32[]{:S(2)}, u32[]{:S(2)}) collective-permute-start(bf16[256,2112]{0,1:T(8,128)(2,1)} %pad_maximum_fusion.9), channel_id=1, source_target_pairs={{0,16},{16,0},{8,24},{24,8},{1,17},{17,1},{9,25},{25,9},{2,18},{18... | collective-permute-start | bytes 3244040 | tf_op jit(solution)/shard_map/ppermute | solution.py:389
  391.2 23.8 %copy-start.17 = (bf16[256,1408]{0,1:T(8,128)(2,1)S(1)}, bf16[256,1408]{0,1:T(8,128)(2,1)}, u32[]{:S(2)}) copy-start(bf16[256,1408]{0,1:T(8,128)(2,1)} %get-tuple-element.139) | copy-start | bytes 2162692
  391.2 23.8 %copy-start.25 = (bf16[256,704]{0,1:T(8,128)(2,1)S(1)}, bf16[256,704]{0,1:T(8,128)(2,1)}, u32[]{:S(2)}) copy-start(bf16[256,704]{0,1:T(8,128)(2,1)} %get-tuple-element.157) | copy-start | bytes 1081348
  391.2 23.8 %collective-permute-start.21 = (bf16[256,2112]{0,1:T(8,128)(2,1)S(1)}, bf16[256,2112]{0,1:T(8,128)(2,1)S(1)}, u32[]{:S(2)}, u32[]{:S(2)}) collective-permute-start(bf16[256,2112]{0,1:T(8,128)(2,1)S(1)} %add_convert_fusion.3), channel_id=1, source_target_pairs={{0,16},{16,0},{8,24},{24,8},{1,17},{17,1},{9,25},{25,9},{2,18},{18... | collective-permute-start | bytes 3244040 | tf_op jit(solution)/shard_map/ppermute | solution.py:413
  394.3 23.5 %collective-permute-start.22 = (bf16[256,2112]{0,1:T(8,128)(2,1)S(1)}, bf16[256,2112]{0,1:T(8,128)(2,1)S(1)}, u32[]{:S(2)}, u32[]{:S(2)}) collective-permute-start(bf16[256,2112]{0,1:T(8,128)(2,1)S(1)} %add_convert_fusion.1), channel_id=1, source_target_pairs={{0,8},{8,0},{16,24},{24,16},{1,9},{9,1},{17,25},{25,17},{2,10},{10... | collective-permute-start | bytes 3244040 | tf_op jit(solution)/shard_map/ppermute | solution.py:414
  425.3 56.3 %all-to-all-start.3 = ((bf16[8,64,2112]{2,1,0:T(8,128)(2,1)}), bf16[8,64,2112]{2,1,0:T(8,128)(2,1)}, u32[]{:S(2)}, u32[]{:S(2)}) async-start(bf16[8,64,2112]{2,1,0:T(8,128)(2,1)} %bitcast.117), calls=%async_computation.6 | async-start | bytes 4456448 | tf_op jit(solution)/shard_map/all_to_all | solution.py:340
  429.7 130.3 %reduce-scatter.11.cloned.1.call-start = ((), (), s32[]{:S(2)}) async-start(), calls=%async_computation.15 | async-start | bytes 4718592 | tf_op jit(solution)/shard_map/reduce_scatter | solution.py:336
  469.7 12.0 %collective-permute-start.23 = (bf16[2048,256]{1,0:T(8,128)(2,1)}, bf16[2048,256]{1,0:T(8,128)(2,1)S(1)}, u32[]{:S(2)}, u32[]{:S(2)}) collective-permute-start(bf16[2048,256]{1,0:T(8,128)(2,1)} %convolution_convert_fusion.7), channel_id=1, source_target_pairs={{0,1},{1,0},{2,3},{3,2},{4,5},{5,4},{6,7},{7,6},{8,9},{9,8},{10,11... | collective-permute-start | bytes 3145736 | tf_op jit(solution)/shard_map/ppermute | solution.py:434
  483.7 5.3 copy-start.42
  490.3 6.4 %collective-permute-start.31 = (bf16[32,2048]{1,0:T(8,128)(2,1)S(1)}, bf16[32,2048]{1,0:T(8,128)(2,1)S(1)}, u32[]{:S(2)}, u32[]{:S(2)}) collective-permute-start(bf16[32,2048]{1,0:T(8,128)(2,1)S(1)} %get-tuple-element.188), channel_id=1, source_target_pairs={{0,8},{8,0},{16,24},{24,16},{1,9},{9,1},{17,25},{25,17},{2,10},{10... | collective-permute-start | bytes 393224 | tf_op jit(solution)/shard_map/ppermute | solution.py:389
  492.0 7.2 %collective-permute-start.30 = (bf16[32,2048]{1,0:T(8,128)(2,1)S(1)}, bf16[32,2048]{1,0:T(8,128)(2,1)S(1)}, u32[]{:S(2)}, u32[]{:S(2)}) collective-permute-start(bf16[32,2048]{1,0:T(8,128)(2,1)S(1)} %get-tuple-element.185), channel_id=1, source_target_pairs={{0,8},{8,0},{16,24},{24,16},{1,9},{9,1},{17,25},{25,17},{2,10},{10... | collective-permute-start | bytes 393224 | tf_op jit(solution)/shard_map/ppermute | solution.py:389
  492.9 6.9 %collective-permute-start.34 = (bf16[32,2048]{1,0:T(8,128)(2,1)S(1)}, bf16[32,2048]{1,0:T(8,128)(2,1)S(1)}, u32[]{:S(2)}, u32[]{:S(2)}) collective-permute-start(bf16[32,2048]{1,0:T(8,128)(2,1)S(1)} %get-tuple-element.186), channel_id=1, source_target_pairs={{0,16},{16,0},{8,24},{24,8},{1,17},{17,1},{9,25},{25,9},{2,18},{18... | collective-permute-start | bytes 393224 | tf_op jit(solution)/shard_map/ppermute | solution.py:389
  493.7 22.0 %collective-permute-start.33 = (bf16[32,2048]{1,0:T(8,128)(2,1)S(1)}, bf16[32,2048]{1,0:T(8,128)(2,1)S(1)}, u32[]{:S(2)}, u32[]{:S(2)}) collective-permute-start(bf16[32,2048]{1,0:T(8,128)(2,1)S(1)} %get-tuple-element.187), channel_id=1, source_target_pairs={{0,16},{16,0},{8,24},{24,8},{1,17},{17,1},{9,25},{25,9},{2,18},{18... | collective-permute-start | bytes 393224 | tf_op jit(solution)/shard_map/ppermute | solution.py:389
  496.8 8.0 %collective-permute-start.32 = (bf16[32,2048]{1,0:T(8,128)(2,1)S(1)}, bf16[32,2048]{1,0:T(8,128)(2,1)S(1)}, u32[]{:S(2)}, u32[]{:S(2)}) collective-permute-start(bf16[32,2048]{1,0:T(8,128)(2,1)S(1)} %add_convert_fusion.12), channel_id=1, source_target_pairs={{0,16},{16,0},{8,24},{24,8},{1,17},{17,1},{9,25},{25,9},{2,18},{18... | collective-permute-start | bytes 393224 | tf_op jit(solution)/shard_map/ppermute | solution.py:413
  497.7 20.4 %collective-permute-start.24 = (bf16[256,512]{1,0:T(8,128)(2,1)S(1)}, bf16[256,512]{1,0:T(8,128)(2,1)S(1)}, u32[]{:S(2)}, u32[]{:S(2)}) collective-permute-start(bf16[256,512]{1,0:T(8,128)(2,1)S(1)} %get-tuple-element.167), channel_id=1, source_target_pairs={{0,8},{8,0},{16,24},{24,16},{1,9},{9,1},{17,25},{25,17},{2,10},{10... | collective-permute-start | bytes 786440 | tf_op jit(solution)/shard_map/ppermute | solution.py:389
  499.2 10.5 %collective-permute-start.25 = (bf16[256,512]{1,0:T(8,128)(2,1)S(1)}, bf16[256,512]{1,0:T(8,128)(2,1)S(1)}, u32[]{:S(2)}, u32[]{:S(2)}) collective-permute-start(bf16[256,512]{1,0:T(8,128)(2,1)S(1)} %get-tuple-element.168), channel_id=1, source_target_pairs={{0,8},{8,0},{16,24},{24,16},{1,9},{9,1},{17,25},{25,17},{2,10},{10... | collective-permute-start | bytes 786440 | tf_op jit(solution)/shard_map/ppermute | solution.py:389
  499.8 18.3 %collective-permute-start.27 = (bf16[256,512]{1,0:T(8,128)(2,1)S(1)}, bf16[256,512]{1,0:T(8,128)(2,1)S(1)}, u32[]{:S(2)}, u32[]{:S(2)}) collective-permute-start(bf16[256,512]{1,0:T(8,128)(2,1)S(1)} %get-tuple-element.169), channel_id=1, source_target_pairs={{0,16},{16,0},{8,24},{24,8},{1,17},{17,1},{9,25},{25,9},{2,18},{18... | collective-permute-start | bytes 786440 | tf_op jit(solution)/shard_map/ppermute | solution.py:389
  504.9 9.1 %collective-permute-start.28 = (bf16[256,512]{1,0:T(8,128)(2,1)S(1)}, bf16[256,512]{1,0:T(8,128)(2,1)S(1)}, u32[]{:S(2)}, u32[]{:S(2)}) collective-permute-start(bf16[256,512]{1,0:T(8,128)(2,1)S(1)} %get-tuple-element.170), channel_id=1, source_target_pairs={{0,16},{16,0},{8,24},{24,8},{1,17},{17,1},{9,25},{25,9},{2,18},{18... | collective-permute-start | bytes 786440 | tf_op jit(solution)/shard_map/ppermute | solution.py:389
  509.8 7.4 %collective-permute-start.35 = (bf16[32,2048]{1,0:T(8,128)(2,1)S(1)}, bf16[32,2048]{1,0:T(8,128)(2,1)S(1)}, u32[]{:S(2)}, u32[]{:S(2)}) collective-permute-start(bf16[32,2048]{1,0:T(8,128)(2,1)S(1)} %get-tuple-element.184), channel_id=1, source_target_pairs={{0,8},{8,0},{16,24},{24,16},{1,9},{9,1},{17,25},{25,17},{2,10},{10... | collective-permute-start | bytes 393224 | tf_op jit(solution)/shard_map/ppermute | solution.py:414
  514.1 6.7 %collective-permute-start.26 = (bf16[256,512]{1,0:T(8,128)(2,1)S(1)}, bf16[256,512]{1,0:T(8,128)(2,1)S(1)}, u32[]{:S(2)}, u32[]{:S(2)}) collective-permute-start(bf16[256,512]{1,0:T(8,128)(2,1)S(1)} %get-tuple-element.171), channel_id=1, source_target_pairs={{0,16},{16,0},{8,24},{24,8},{1,17},{17,1},{9,25},{25,9},{2,18},{18... | collective-permute-start | bytes 786440 | tf_op jit(solution)/shard_map/ppermute | solution.py:413
  515.7 6.5 %collective-permute-start.29 = (bf16[256,512]{1,0:T(8,128)(2,1)S(1)}, bf16[256,512]{1,0:T(8,128)(2,1)S(1)}, u32[]{:S(2)}, u32[]{:S(2)}) collective-permute-start(bf16[256,512]{1,0:T(8,128)(2,1)S(1)} %get-tuple-element.172), channel_id=1, source_target_pairs={{0,8},{8,0},{16,24},{24,16},{1,9},{9,1},{17,25},{25,17},{2,10},{10... | collective-permute-start | bytes 786440 | tf_op jit(solution)/shard_map/ppermute | solution.py:414
  523.2 19.5 %all-to-all-start.4 = ((bf16[8,64,512]{2,1,0:T(8,128)(2,1)}), bf16[8,64,512]{2,1,0:T(8,128)(2,1)}, u32[]{:S(2)}, u32[]{:S(2)}) async-start(bf16[8,64,512]{2,1,0:T(8,128)(2,1)} %bitcast.21), calls=%async_computation.7 | async-start | bytes 1048576 | tf_op jit(solution)/shard_map/all_to_all | solution.py:340
  547.3 6.3 %copy-start.41 = (f32[64]{0:T(128)S(1)}, f32[64]{0:T(128)}, u32[]{:S(2)}) copy-start(f32[64]{0:T(128)} %copy-done.40) | copy-start | bytes 772
  (32 other events, 87.6 us)
Sparse Core Ops, SparseCore 0:
  9.6 75.2 all-gather.11
  136.5 50.5 reduce-scatter.4
  190.9 45.2 all-gather.5
  237.7 45.6 all-gather.7
  285.6 48.7 reduce-scatter.8
  336.5 48.3 reduce-scatter.6
  389.4 45.3 all-gather.9
  481.8 48.0 reduce-scatter.10

commit v9 on v6

--- a/solution.py
+++ b/solution.py
@@ -782,12 +782,13 @@
     )
     out_grad = reduce_seq([contract_rows(attn_low, low_all).astype(bf16)]).astype(f32)
     attn_grad_own, mlp_grad = tie(attn_grad_own, mlp_grad)
-    mlp_grad = mlp_grad.astype(f32)
     attn_grad = exchange_ctx(attn_grad_own.reshape(8, rows, -1))
 
-    gate_rows = ff_rows(mlp_grad[:, :, :main], mlp_grad[:, :, 2 * main : 2 * main + tail])
+    gate_rows = ff_rows(mlp_grad[:, :, :main], mlp_grad[:, :, 2 * main : 2 * main + tail]).astype(f32)
     up_rows = ff_rows(mlp_grad[:, :, main : 2 * main], mlp_grad[:, :, 2 * main + tail : both])
+    up_rows = up_rows.astype(f32)
     down_grad = ff_rows(mlp_grad[:, :, both : both + main], mlp_grad[:, :, both + main :])
+    down_grad = down_grad.astype(f32)
     scale_one = rms_scale(inputs)
     shaped_one = inputs * scale_one
     input_grad = residual_back + scale_one * (
@@ -797,9 +798,8 @@
     attn_grad, out_grad, gate_rows, up_rows, down_grad, input_grad, block_output = tie(
         attn_grad, out_grad, gate_rows, up_rows, down_grad, input_grad, block_output
     )
-    attn_grad = attn_grad.astype(f32)
-    query_rows = from_head_slices(attn_grad[:, :, :head_width])
-    pair_rows = jnp.sum(attn_grad[:, :, head_width:].reshape(4, 2, rows, head_width), axis=0)
+    query_rows = from_head_slices(attn_grad[:, :, :head_width]).astype(f32)
+    pair_rows = jnp.sum(attn_grad[:, :, head_width:].astype(f32).reshape(4, 2, rows, head_width), axis=0)
     key_rows, value_rows = pair_rows[0], pair_rows[1]
 
     def row_sum(weight, grad):

time: 571 us -> 571 us (level)
    convert_element_type x0 -> x3, local copies, waits for them, and re-layouts: none -> 5.82 us  [local_columns(): query_rows = from_head_slices(attn_grad[:, :, :head_width]).astype(f32)]
    reshape x3 -> x0, local copies, waits for them, and re-layouts: 5.82 us -> none  [the longest x2 4.24 us: from_head_slices(): split = pieces.reshape(8, rows, KV_HEADS, HEAD)]
    unnamed x75 -> x79, local copies, waits for them, and re-layouts: 11.4 us -> 11.8 us
  transfers between devices with their start and end apart: 49 -> 49, of which waited for: 23 -> 24; matrix products, arithmetic and copies ran while one was open for 36% -> 36% of each run, Pallas kernels for 6% -> 6%
where the time goes in v9:
time: 571 us; the launch traced here: 562 us
  waiting for transfers between devices  214 us (37%)
  local copies, waits for them, and re-layouts  103 us (18%)
  matrix products  83.8 us (15%)
  starting transfers between devices  58.4 us (10%)
  other arithmetic  53.3 us (9%)
  Pallas kernels  33 us (6%)
  between operations  16.4 us (3%)
    reduce_scatter x4, waiting for transfers between devices, reduce_ctx(): return lax.psum_scatter(partial, 'ctx', scatter_dimension=0, tiled=True)  57.2 us
    all_gather x4, waiting for transfers between devices, gather_ctx(): return lax.all_gather(block, 'ctx', axis=0, tiled=True)  48.1 us
    ppermute x4, waiting for transfers between devices, gather_seq_far(): far_low = lax.ppermute(from_y[half:], 'seq', SEQ_X)  34.4 us
    dot_general x4, matrix products, contract_cols(): lax.dot_general(left, right, (((1,), (1,)), ((), ())), preferred_element_...  29.7 us
    all_to_all x5, waiting for transfers between devices, exchange_ctx(): return lax.all_to_all(pieces, 'ctx', 0, 0, tiled=True)  25.6 us
    dynamic_update_slice x20, local copies, waits for them, and re-layouts, gather_seq_far(): whole = lax.dynamic_update_slice_in_dim(whole, piece, start, 0)  25.5 us
    ppermute x3, waiting for transfers between devices, reduce_seq_far(): top_last = lax.ppermute(top_send, 'seq', SEQ_Y)  24.4 us
    all_to_all x5, starting transfers between devices, exchange_ctx(): return lax.all_to_all(pieces, 'ctx', 0, 0, tiled=True)  22 us
  transfers between devices with their start and end apart: 49, of which 24 were waited for; matrix products, arithmetic and copies ran while one was open for 36% of the time, Pallas kernels for 6%

profile of v9, /device:TPU:0, one launch (start us, length us, event | category | flops | bytes accessed | tf_op | source)
XLA Modules:
  0.0 561.9 jit_solution(11617027299247503896)
XLA Ops:
  7.9 3.1 collective-permute-start.6
  16.3 5.0 all-to-all-start
  27.0 2.2 concatenate.109
  34.6 16.8 %all-to-all-done = bf16[8,64,512]{2,1,0:T(8,128)(2,1)} async-done(((bf16[8,64,512]{2,1,0:T(8,128)(2,1)}), bf16[8,64,512]{2,1,0:T(8,128)(2,1)}, u32[]{:S(2)}, u32[]{:S(2)}) %all-to-all-start) | async-done | bytes 524320 | tf_op jit(solution)/shard_map/all_to_all | solution.py:340
  52.5 3.5 all-to-all-start.1
  58.8 11.7 %collective-permute-done = bf16[512,512]{1,0:T(8,128)(2,1)S(1)} collective-permute-done((bf16[512,512]{1,0:T(8,128)(2,1)}, bf16[512,512]{1,0:T(8,128)(2,1)S(1)}, u32[]{:S(2)}, u32[]{:S(2)}) %collective-permute-start) | collective-permute-done | bytes 524320 | tf_op jit(solution)/shard_map/ppermute | solution.py:344
  72.8 1.9 constant_dynamic-update-slice_fusion.19
  79.0 1.9 constant_dynamic-update-slice_fusion.17
  82.6 2.7 collective-permute-done.3
  86.0 2.3 slice.227
  88.3 2.6 copy.80
  90.9 4.6 all-to-all-start.2
  95.9 3.2 fusion
  99.3 5.3 fusion.66
  104.6 3.5 fusion.64
  118.0 13.3 %attend.1 = bf16[1024,256]{1,0:T(8,128)(2,1)} custom-call(s32[1]{0:T(128)} %bitcast.2.refs_0_, bf16[1024,256]{1,0:T(8,128)(2,1)} %get-tuple-element.170.refs_1_, bf16[1024,256]{1,0:T(8,128)(2,1)} %fusion.29.refs_2_, bf16[1024,256]{1,0:T(8,128)(2,1)} %get-tuple-element.169.refs_3_), custom_call_target="tpu_custom_call" | custom-call | flops 4294967296 | bytes 2097152 | tf_op jit(solution)/shard_map/attend/pallas_call | solution.py:581
  131.3 4.7 convolution_convert_fusion.2
  143.7 1.9 broadcast_in_dim.33
  147.9 2.3 copy.84
  151.2 2.2 constant_dynamic-update-slice_fusion.7
  153.4 24.6 %collective-permute-done.12 = bf16[256,704]{0,1:T(8,128)(2,1)} collective-permute-done((bf16[256,704]{0,1:T(8,128)(2,1)}, bf16[256,704]{0,1:T(8,128)(2,1)}, u32[]{:S(2)}, u32[]{:S(2)}) %collective-permute-start.12) | collective-permute-done | bytes 360480 | tf_op jit(solution)/shard_map/ppermute | solution.py:352
  182.0 4.7 reduce-scatter.5.cloned.1.call-done
  188.1 2.4 fusion.71
  193.8 2.9 broadcast_in_dim.34
  196.7 2.8 constant_dynamic-update-slice_fusion.4
  202.1 2.6 constant_dynamic-update-slice_fusion.3
  204.7 2.6 constant_dynamic-update-slice_fusion.2
  209.3 7.0 %collective-permute-done.16 = bf16[256,1408]{1,0:T(8,128)(2,1)S(1)} collective-permute-done((bf16[256,1408]{1,0:T(8,128)(2,1)S(1)}, bf16[256,1408]{1,0:T(8,128)(2,1)S(1)}, u32[]{:S(2)}, u32[]{:S(2)}) %collective-permute-start.16) | collective-permute-done | bytes 720928 | tf_op jit(solution)/shard_map/ppermute | solution.py:352
  217.2 18.8 %all-gather.6.cloned.1.call-done = bf16[1024,2048]{1,0:T(8,128)(2,1)} async-done(((bf16[128,2048]{1,0:T(8,128)(2,1)}), bf16[1024,2048]{1,0:T(8,128)(2,1)}) %all-gather.6.cloned.1.call-update) | async-done | bytes 4194320 | tf_op jit(solution)/shard_map/all_gather | solution.py:332
  236.0 10.9 %fusion.83 = f32[1024,1408]{1,0:T(8,128)S(1)} fusion(bf16[1024,2048]{1,0:T(8,128)(2,1)} %all-gather.6.cloned.1.call-done, bf16[2048,1408]{1,0:T(8,128)(2,1)} %constant_dynamic-update-slice_fusion), kind=kOutput, calls=%fused_computation.238 | convolution fusion | flops 5905580032 | bytes 15728640 | tf_op jit(solution)/shard_map/dot_general | solution.py:712
  251.9 7.0 %convolution_convert_fusion.4 = bf16[1024,2048]{1,0:T(8,128)(2,1)} fusion(bf16[1024,704]{1,0:T(8,128)(2,1)S(1)} %multiply_convert_fusion.2, bf16[2048,704]{1,0:T(8,128)(2,1)} %constant_dynamic-update-slice_fusion.5), kind=kOutput, calls=%fused_computation.24 | convolution fusion | flops 2954887168 | bytes 8519680 | tf_op jit(solution)/shard_map/dot_general | solution.py:53
  258.9 24.3 %all-gather.8.cloned.1.call-done = bf16[1024,2048]{1,0:T(8,128)(2,1)} async-done(((bf16[128,2048]{1,0:T(8,128)(2,1)}), bf16[1024,2048]{1,0:T(8,128)(2,1)}) %all-gather.8.cloned.1.call-update) | async-done | bytes 4194320 | tf_op jit(solution)/shard_map/all_gather | solution.py:332
  283.2 9.0 %multiply_convert_fusion = (bf16[1024,704]{1,0:T(8,128)(2,1)S(1)}, bf16[1024,704]{1,0:T(8,128)(2,1)S(1)}) fusion(f32[1024,64]{1,0:T(8,128)S(1)} %get-tuple-element.145, f32[1024,640]{1,0:T(8,128)} %copy-done.4, f32[1024,64]{1,0:T(8,128)} %copy-done.20, f32[1024,640]{1,0:T(8,128)} %copy-done.5, bf16[1024,2048]{1,0:T(8,128)(2,1)} %all-gather.8.cloned.1.call-done, ...), kind=kOutput, calls=%fused_computation.31 | convolution fusion | flops 2963603456 | bytes 15728640 | tf_op jit(solution)/shard_map/dot_general | solution.py:729
  294.6 5.4 concatenate.118
  300.0 11.0 %convolution_convert_fusion.1 = bf16[1024,2048]{1,0:T(8,128)(2,1)} fusion(bf16[1024,1408]{1,0:T(8,128)(2,1)} %concatenate.118, bf16[2048,1408]{1,0:T(8,128)(2,1)} %constant_dynamic-update-slice_fusion), kind=kOutput, calls=%fused_computation.21 | convolution fusion | flops 5907677184 | bytes 12845056 | tf_op jit(solution)/shard_map/dot_general | solution.py:53
  311.3 6.1 %convolution_convert_fusion.5 = bf16[2048,704]{0,1:T(8,128)(2,1)S(1)} fusion(bf16[1024,2048]{1,0:T(8,128)(2,1)} %all-gather.8.cloned.1.call-done, bf16[1024,704]{1,0:T(8,128)(2,1)} %copy-done.21), kind=kOutput, calls=%fused_computation.25 | convolution fusion | flops 2954231808 | bytes 8519680 | tf_op jit(solution)/shard_map/dot_general | solution.py:47
  319.7 6.6 %convolution_convert_fusion = bf16[2048,1408]{0,1:T(8,128)(2,1)S(1)} fusion(bf16[1024,2048]{1,0:T(8,128)(2,1)S(1)} %copy-done.36, bf16[1024,1408]{1,0:T(8,128)(2,1)S(1)} %copy-done.13), kind=kOutput, calls=%fused_computation.4 | convolution fusion | flops 5908463616 | bytes 12845056 | tf_op jit(solution)/shard_map/dot_general | solution.py:47
  326.3 1.9 constant_dynamic-slice_fusion.11
  338.1 46.5 %reduce-scatter.7.cloned.1.call-done = bf16[128,2048]{1,0:T(8,128)(2,1)} async-done(((bf16[1024,2048]{1,0:T(8,128)(2,1)}), bf16[128,2048]{1,0:T(8,128)(2,1)}) %reduce-scatter.7.cloned.1.call-update) | async-done | bytes 524304 | tf_op jit(solution)/shard_map/reduce_scatter | solution.py:336
  386.3 2.7 fusion.69
  389.0 1.9 add_convert_fusion.3
  395.5 19.2 %collective-permute-done.28 = bf16[256,2112]{0,1:T(8,128)(2,1)S(1)} collective-permute-done((bf16[256,2112]{0,1:T(8,128)(2,1)S(1)}, bf16[256,2112]{0,1:T(8,128)(2,1)S(1)}, u32[]{:S(2)}, u32[]{:S(2)}) %collective-permute-start.28) | collective-permute-done | bytes 1081376 | tf_op jit(solution)/shard_map/ppermute | solution.py:413
  414.7 1.9 add_convert_fusion.2
  420.9 4.1 copy.94
  425.0 4.4 all-to-all-start.3
  429.4 5.1 all-gather.10.cloned.1.call-done
  434.5 4.6 convolution_convert_fusion.8.refs_4_
  439.1 19.7 %attend_back.1 = (f32[1024,256]{1,0:T(8,128)}, f32[1024,256]{1,0:T(8,128)}, f32[1024,256]{1,0:T(8,128)}) custom-call(s32[1]{0:T(128)} %bitcast.2.refs_0_, bf16[1024,256]{1,0:T(8,128)(2,1)} %get-tuple-element.170.refs_1_, bf16[1024,256]{1,0:T(8,128)(2,1)} %fusion.29.refs_2_, bf16[1024,256]{1,0:T(8,128)(2,1)} %get-tuple-element.169.refs_3_, ...), custom_call_target="tpu_custom_call" | custom-call | flops 10737418240 | bytes 3670016 | tf_op jit(solution)/shard_map/attend_back/pallas_call | solution.py:602
  466.3 1.9 convolution_convert_fusion.7
  468.2 7.2 %convolution_convert_fusion.3 = bf16[1024,2048]{1,0:T(8,128)(2,1)} fusion(bf16[2048,256]{1,0:T(8,128)(2,1)} %collective-permute-done.4, bf16[2048,512]{1,0:T(8,128)(2,1)} %constant_dynamic-update-slice_fusion.15, bf16[1024,256]{1,0:T(8,128)(2,1)S(1)} %get-tuple-element.127, bf16[1024,512]{1,0:T(8,128)(2,1)S(1)} %pad_maximum_fusion.7), kind=kOutput, calls=%fused_computation.23 | convolution fusion | flops 3232759808 | bytes 8912896 | tf_op jit(solution)/shard_map/dot_general | solution.py:53
  475.4 5.9 %all-to-all-done.3 = bf16[8,64,2112]{2,1,0:T(8,128)(2,1)} async-done(((bf16[8,64,2112]{2,1,0:T(8,128)(2,1)}), bf16[8,64,2112]{2,1,0:T(8,128)(2,1)}, u32[]{:S(2)}, u32[]{:S(2)}) %all-to-all-start.3) | async-done | bytes 2162720 | tf_op jit(solution)/shard_map/all_to_all | solution.py:340
  481.4 3.6 convolution_convert_fusion.6
  489.2 2.6 fusion.61
  497.0 2.6 collective-permute-done.32
  501.7 2.6 collective-permute-done.23
  508.7 4.1 collective-permute-done.22
  512.8 2.6 collective-permute-done.24
  517.1 4.4 all-to-all-start.4
  528.4 4.4 reduce-scatter.11.cloned.1.call-done
  534.2 3.3 add_convert_fusion.4
  537.5 2.9 all-to-all-done.4
  543.8 2.8 copy.114
  548.2 1.9 broadcast_multiply_fusion.2
  550.2 3.4 broadcast_multiply_fusion
  (294 shorter events, 134.2 us)
Async XLA Ops:
  7.2 8.1 %copy-start.29 = (bf16[64,256]{1,0:T(8,128)(2,1)S(1)}, bf16[64,256]{1,0:T(8,128)(2,1)}, u32[]{:S(2)}) copy-start(bf16[64,256]{1,0:T(8,128)(2,1)} %param.19) | copy-start | bytes 98308
  7.2 8.1 %copy-start.27 = (bf16[64,256]{1,0:T(8,128)(2,1)S(1)}, bf16[64,256]{1,0:T(8,128)(2,1)}, u32[]{:S(2)}) copy-start(bf16[64,256]{1,0:T(8,128)(2,1)} %param.18) | copy-start | bytes 98308
  7.2 88.6 %all-gather.12.cloned.1.call-start = ((), (), s32[]{:S(2)}) async-start(), calls=%async_computation.16 | async-start | bytes 4718592 | tf_op jit(solution)/shard_map/all_gather | solution.py:332
  7.9 21.4 %collective-permute-start.6 = (bf16[64,2048]{1,0:T(8,128)(2,1)}, bf16[64,2048]{1,0:T(8,128)(2,1)}, u32[]{:S(2)}, u32[]{:S(2)}) collective-permute-start(bf16[64,2048]{1,0:T(8,128)(2,1)} %param.20), channel_id=1, source_target_pairs={{0,16},{16,0},{8,24},{24,8},{1,17},{17,1},{9,25},{25,9},{2,18},{18... | collective-permute-start | bytes 786440 | tf_op jit(solution)/shard_map/ppermute | solution.py:344
  11.0 20.5 %collective-permute-start.5 = (bf16[64,2048]{1,0:T(8,128)(2,1)}, bf16[64,2048]{1,0:T(8,128)(2,1)}, u32[]{:S(2)}, u32[]{:S(2)}) collective-permute-start(bf16[64,2048]{1,0:T(8,128)(2,1)} %param.20), channel_id=1, source_target_pairs={{0,8},{8,0},{16,24},{24,16},{1,9},{9,1},{17,25},{25,17},{2,10},{10... | collective-permute-start | bytes 786440 | tf_op jit(solution)/shard_map/ppermute | solution.py:344
  16.3 6.1 %copy-start.33 = (s32[1,1024]{1,0:T(1,128)S(1)}, s32[1,1024]{1,0:T(1,128)}, u32[]{:S(2)}) copy-start(s32[1,1024]{1,0:T(1,128)} %param.14) | copy-start | bytes 12292
  16.3 8.7 %copy-start.14 = (bf16[64,5632]{1,0:T(8,128)(2,1)S(1)}, bf16[64,5632]{1,0:T(8,128)(2,1)}, u32[]{:S(2)}) copy-start(bf16[64,5632]{1,0:T(8,128)(2,1)} %param.23) | copy-start | bytes 2162692
  16.3 8.7 %copy-start.15 = (bf16[64,5632]{1,0:T(8,128)(2,1)S(1)}, bf16[64,5632]{1,0:T(8,128)(2,1)}, u32[]{:S(2)}) copy-start(bf16[64,5632]{1,0:T(8,128)(2,1)} %param.22) | copy-start | bytes 2162692
  16.3 35.0 %all-to-all-start = ((bf16[8,64,512]{2,1,0:T(8,128)(2,1)}), bf16[8,64,512]{2,1,0:T(8,128)(2,1)}, u32[]{:S(2)}, u32[]{:S(2)}) async-start(bf16[8,64,512]{2,1,0:T(8,128)(2,1)} %pad_maximum_fusion.9), calls=%async_computation | async-start | bytes 1048576 | tf_op jit(solution)/shard_map/all_to_all | solution.py:340
  31.0 27.8 %collective-permute-start.8 = (bf16[32,2048]{1,0:T(8,128)(2,1)}, bf16[32,2048]{1,0:T(8,128)(2,1)S(1)}, u32[]{:S(2)}, u32[]{:S(2)}) collective-permute-start(bf16[32,2048]{1,0:T(8,128)(2,1)} %slice.233), channel_id=1, source_target_pairs={{0,8},{8,0},{16,24},{24,16},{1,9},{9,1},{17,25},{25,17},{2,10},{10... | collective-permute-start | bytes 393224 | tf_op jit(solution)/shard_map/ppermute | solution.py:352
  33.1 24.8 %collective-permute-start.7 = (bf16[32,2048]{1,0:T(8,128)(2,1)}, bf16[32,2048]{1,0:T(8,128)(2,1)}, u32[]{:S(2)}, u32[]{:S(2)}) collective-permute-start(bf16[32,2048]{1,0:T(8,128)(2,1)} %slice.232), channel_id=1, source_target_pairs={{0,16},{16,0},{8,24},{24,8},{1,17},{17,1},{9,25},{25,9},{2,18},{18... | collective-permute-start | bytes 393224 | tf_op jit(solution)/shard_map/ppermute | solution.py:351
  52.5 35.8 %all-to-all-start.1 = ((bf16[8,64,704]{2,1,0:T(8,128)(2,1)}), bf16[8,64,704]{2,1,0:T(8,128)(2,1)S(1)}, u32[]{:S(2)}, u32[]{:S(2)}) async-start(bf16[8,64,704]{2,1,0:T(8,128)(2,1)} %pad_maximum_fusion.8), calls=%async_computation.1 | async-start | bytes 1572864 | tf_op jit(solution)/shard_map/all_to_all | solution.py:340
  56.1 14.4 %collective-permute-start = (bf16[512,512]{1,0:T(8,128)(2,1)}, bf16[512,512]{1,0:T(8,128)(2,1)S(1)}, u32[]{:S(2)}, u32[]{:S(2)}) collective-permute-start(bf16[512,512]{1,0:T(8,128)(2,1)} %bitcast.7), channel_id=1, source_target_pairs={{0,8},{8,0},{16,24},{24,16},{1,9},{9,1},{17,25},{25,17},{2,10},{10... | collective-permute-start | bytes 1572872 | tf_op jit(solution)/shard_map/ppermute | solution.py:344
  57.3 19.3 %collective-permute-start.1 = (bf16[512,512]{1,0:T(8,128)(2,1)}, bf16[512,512]{1,0:T(8,128)(2,1)}, u32[]{:S(2)}, u32[]{:S(2)}) collective-permute-start(bf16[512,512]{1,0:T(8,128)(2,1)} %bitcast.7), channel_id=1, source_target_pairs={{0,16},{16,0},{8,24},{24,8},{1,17},{17,1},{9,25},{25,9},{2,18},{18... | collective-permute-start | bytes 1572872 | tf_op jit(solution)/shard_map/ppermute | solution.py:344
  58.8 14.0 %copy-start.12 = (bf16[256,2048]{1,0:T(8,128)(2,1)}, bf16[256,2048]{1,0:T(8,128)(2,1)S(1)}, u32[]{:S(2)}) copy-start(bf16[256,2048]{1,0:T(8,128)(2,1)S(1)} %constant_dynamic-update-slice_fusion.10) | copy-start | bytes 3145732
  71.3 9.7 %collective-permute-start.2 = (bf16[256,512]{1,0:T(8,128)(2,1)}, bf16[256,512]{1,0:T(8,128)(2,1)}, u32[]{:S(2)}, u32[]{:S(2)}) collective-permute-start(bf16[256,512]{1,0:T(8,128)(2,1)} %slice.225), channel_id=1, source_target_pairs={{0,16},{16,0},{8,24},{24,8},{1,17},{17,1},{9,25},{25,9},{2,18},{18... | collective-permute-start | bytes 786440 | tf_op jit(solution)/shard_map/ppermute | solution.py:351
  77.6 7.7 %collective-permute-start.3 = (bf16[256,512]{1,0:T(8,128)(2,1)S(1)}, bf16[256,512]{1,0:T(8,128)(2,1)S(1)}, u32[]{:S(2)}, u32[]{:S(2)}) collective-permute-start(bf16[256,512]{1,0:T(8,128)(2,1)S(1)} %slice.226), channel_id=1, source_target_pairs={{0,8},{8,0},{16,24},{24,16},{1,9},{9,1},{17,25},{25,17},{2,10},{10... | collective-permute-start | bytes 786440 | tf_op jit(solution)/shard_map/ppermute | solution.py:352
  88.3 16.3 %collective-permute-start.4 = (bf16[2048,256]{1,0:T(8,128)(2,1)}, bf16[2048,256]{1,0:T(8,128)(2,1)}, u32[]{:S(2)}, u32[]{:S(2)}) collective-permute-start(bf16[2048,256]{1,0:T(8,128)(2,1)} %slice.227), channel_id=1, source_target_pairs={{0,1},{1,0},{2,3},{3,2},{4,5},{5,4},{6,7},{7,6},{8,9},{9,8},{10,11... | collective-permute-start | bytes 3145736 | tf_op jit(solution)/shard_map/ppermute | solution.py:434
  90.9 40.4 %all-to-all-start.2 = ((bf16[8,64,1408]{2,1,0:T(8,128)(2,1)}), bf16[8,64,1408]{2,1,0:T(8,128)(2,1)}, u32[]{:S(2)}, u32[]{:S(2)}) async-start(bf16[8,64,1408]{2,1,0:T(8,128)(2,1)} %copy.80), calls=%async_computation.2 | async-start | bytes 2883584 | tf_op jit(solution)/shard_map/all_to_all | solution.py:340
  95.6 91.1 %reduce-scatter.5.cloned.1.call-start = ((), (), s32[]{:S(2)}) async-start(), calls=%async_computation.9 | async-start | bytes 4718592 | tf_op jit(solution)/shard_map/reduce_scatter | solution.py:336
  109.2 22.1 %collective-permute-start.10 = (bf16[512,704]{0,1:T(8,128)(2,1)}, bf16[512,704]{0,1:T(8,128)(2,1)}, u32[]{:S(2)}, u32[]{:S(2)}) collective-permute-start(bf16[512,704]{0,1:T(8,128)(2,1)} %copy.81), channel_id=1, source_target_pairs={{0,16},{16,0},{8,24},{24,8},{1,17},{17,1},{9,25},{25,9},{2,18},{18... | collective-permute-start | bytes 2162696 | tf_op jit(solution)/shard_map/ppermute | solution.py:344
  111.0 20.4 %collective-permute-start.9 = (bf16[512,704]{0,1:T(8,128)(2,1)}, bf16[512,704]{0,1:T(8,128)(2,1)}, u32[]{:S(2)}, u32[]{:S(2)}) collective-permute-start(bf16[512,704]{0,1:T(8,128)(2,1)} %copy.81), channel_id=1, source_target_pairs={{0,8},{8,0},{16,24},{24,16},{1,9},{9,1},{17,25},{25,17},{2,10},{10... | collective-permute-start | bytes 2162696 | tf_op jit(solution)/shard_map/ppermute | solution.py:344
  136.0 99.9 %all-gather.6.cloned.1.call-start = ((), (), s32[]{:S(2)}) async-start(), calls=%async_computation.10 | async-start | bytes 4718592 | tf_op jit(solution)/shard_map/all_gather | solution.py:332
  136.1 45.9 %collective-permute-start.14 = (bf16[512,1408]{1,0:T(8,128)(2,1)}, bf16[512,1408]{1,0:T(8,128)(2,1)}, u32[]{:S(2)}, u32[]{:S(2)}) collective-permute-start(bf16[512,1408]{1,0:T(8,128)(2,1)} %bitcast.19), channel_id=1, source_target_pairs={{0,16},{16,0},{8,24},{24,8},{1,17},{17,1},{9,25},{25,9},{2,18},{18... | collective-permute-start | bytes 4325384 | tf_op jit(solution)/shard_map/ppermute | solution.py:344
  137.3 44.7 %collective-permute-start.13 = (bf16[512,1408]{1,0:T(8,128)(2,1)}, bf16[512,1408]{1,0:T(8,128)(2,1)}, u32[]{:S(2)}, u32[]{:S(2)}) collective-permute-start(bf16[512,1408]{1,0:T(8,128)(2,1)} %bitcast.19), channel_id=1, source_target_pairs={{0,8},{8,0},{16,24},{24,16},{1,9},{9,1},{17,25},{25,17},{2,10},{10... | collective-permute-start | bytes 4325384 | tf_op jit(solution)/shard_map/ppermute | solution.py:344
  141.5 36.5 %collective-permute-start.12 = (bf16[256,704]{0,1:T(8,128)(2,1)}, bf16[256,704]{0,1:T(8,128)(2,1)}, u32[]{:S(2)}, u32[]{:S(2)}) collective-permute-start(bf16[256,704]{0,1:T(8,128)(2,1)} %slice.190), channel_id=1, source_target_pairs={{0,8},{8,0},{16,24},{24,16},{1,9},{9,1},{17,25},{25,17},{2,10},{10... | collective-permute-start | bytes 1081352 | tf_op jit(solution)/shard_map/ppermute | solution.py:352
  142.8 36.4 %collective-permute-start.11 = (bf16[256,704]{0,1:T(8,128)(2,1)}, bf16[256,704]{0,1:T(8,128)(2,1)}, u32[]{:S(2)}, u32[]{:S(2)}) collective-permute-start(bf16[256,704]{0,1:T(8,128)(2,1)} %slice.189), channel_id=1, source_target_pairs={{0,16},{16,0},{8,24},{24,8},{1,17},{17,1},{9,25},{25,9},{2,18},{18... | collective-permute-start | bytes 1081352 | tf_op jit(solution)/shard_map/ppermute | solution.py:351
  151.2 35.5 %copy-start.3 = (bf16[1,128,2048]{2,1,0:T(8,128)(2,1)S(1)}, bf16[1,128,2048]{2,1,0:T(8,128)(2,1)}, u32[]{:S(2)}) copy-start(bf16[1,128,2048]{2,1,0:T(8,128)(2,1)} %param.13) | copy-start | bytes 1572868
  190.5 92.6 %all-gather.8.cloned.1.call-start = ((), (), s32[]{:S(2)}) async-start(), calls=%async_computation.11 | async-start | bytes 4718592 | tf_op jit(solution)/shard_map/all_gather | solution.py:332
  191.1 143.0 %reduce-scatter.9.cloned.1.call-start = ((), (), s32[]{:S(2)}) async-start(), calls=%async_computation.13 | async-start | bytes 4718592 | tf_op jit(solution)/shard_map/reduce_scatter | solution.py:336
  192.3 16.1 %collective-permute-start.15 = (bf16[256,1408]{1,0:T(8,128)(2,1)S(1)}, bf16[256,1408]{1,0:T(8,128)(2,1)S(1)}, u32[]{:S(2)}, u32[]{:S(2)}) collective-permute-start(bf16[256,1408]{1,0:T(8,128)(2,1)S(1)} %slice.191), channel_id=1, source_target_pairs={{0,16},{16,0},{8,24},{24,8},{1,17},{17,1},{9,25},{25,9},{2,18},{18... | collective-permute-start | bytes 2162696 | tf_op jit(solution)/shard_map/ppermute | solution.py:351
  200.7 15.6 %collective-permute-start.16 = (bf16[256,1408]{1,0:T(8,128)(2,1)S(1)}, bf16[256,1408]{1,0:T(8,128)(2,1)S(1)}, u32[]{:S(2)}, u32[]{:S(2)}) collective-permute-start(bf16[256,1408]{1,0:T(8,128)(2,1)S(1)} %slice.192), channel_id=1, source_target_pairs={{0,8},{8,0},{16,24},{24,16},{1,9},{9,1},{17,25},{25,17},{2,10},{10... | collective-permute-start | bytes 2162696 | tf_op jit(solution)/shard_map/ppermute | solution.py:352
  283.1 101.5 %reduce-scatter.7.cloned.1.call-start = ((), (), s32[]{:S(2)}) async-start(), calls=%async_computation.12 | async-start | bytes 4718592 | tf_op jit(solution)/shard_map/reduce_scatter | solution.py:336
  311.0 123.5 %all-gather.10.cloned.1.call-start = ((), (), s32[]{:S(2)}) async-start(), calls=%async_computation.14 | async-start | bytes 4718592 | tf_op jit(solution)/shard_map/all_gather | solution.py:332
  311.3 7.5 %copy-start.36 = (bf16[1024,2048]{1,0:T(8,128)(2,1)S(1)}, bf16[1024,2048]{1,0:T(8,128)(2,1)}, u32[]{:S(2)}) copy-start(bf16[1024,2048]{1,0:T(8,128)(2,1)} %all-gather.6.cloned.1.call-done) | copy-start | bytes 12582916
  334.0 50.6 %collective-permute-start.17 = (bf16[256,2112]{0,1:T(8,128)(2,1)}, bf16[256,2112]{0,1:T(8,128)(2,1)}, u32[]{:S(2)}, u32[]{:S(2)}) collective-permute-start(bf16[256,2112]{0,1:T(8,128)(2,1)} %pad_maximum_fusion.3), channel_id=1, source_target_pairs={{0,8},{8,0},{16,24},{24,16},{1,9},{9,1},{17,25},{25,17},{2,10},{10... | collective-permute-start | bytes 3244040 | tf_op jit(solution)/shard_map/ppermute | solution.py:389
  335.5 49.1 %collective-permute-start.18 = (bf16[256,2112]{0,1:T(8,128)(2,1)}, bf16[256,2112]{0,1:T(8,128)(2,1)}, u32[]{:S(2)}, u32[]{:S(2)}) collective-permute-start(bf16[256,2112]{0,1:T(8,128)(2,1)} %pad_maximum_fusion.4), channel_id=1, source_target_pairs={{0,16},{16,0},{8,24},{24,8},{1,17},{17,1},{9,25},{25,9},{2,18},{18... | collective-permute-start | bytes 3244040 | tf_op jit(solution)/shard_map/ppermute | solution.py:389
  337.0 47.6 %collective-permute-start.19 = (bf16[256,2112]{0,1:T(8,128)(2,1)}, bf16[256,2112]{0,1:T(8,128)(2,1)}, u32[]{:S(2)}, u32[]{:S(2)}) collective-permute-start(bf16[256,2112]{0,1:T(8,128)(2,1)} %pad_maximum_fusion.5), channel_id=1, source_target_pairs={{0,8},{8,0},{16,24},{24,16},{1,9},{9,1},{17,25},{25,17},{2,10},{10... | collective-permute-start | bytes 3244040 | tf_op jit(solution)/shard_map/ppermute | solution.py:389
  337.5 47.1 %collective-permute-start.20 = (bf16[256,2112]{0,1:T(8,128)(2,1)}, bf16[256,2112]{0,1:T(8,128)(2,1)}, u32[]{:S(2)}, u32[]{:S(2)}) collective-permute-start(bf16[256,2112]{0,1:T(8,128)(2,1)} %pad_maximum_fusion.6), channel_id=1, source_target_pairs={{0,16},{16,0},{8,24},{24,8},{1,17},{17,1},{9,25},{25,9},{2,18},{18... | collective-permute-start | bytes 3244040 | tf_op jit(solution)/shard_map/ppermute | solution.py:389
  390.9 23.8 %copy-start.16 = (bf16[256,1408]{0,1:T(8,128)(2,1)S(1)}, bf16[256,1408]{0,1:T(8,128)(2,1)}, u32[]{:S(2)}) copy-start(bf16[256,1408]{0,1:T(8,128)(2,1)} %get-tuple-element.135) | copy-start | bytes 2162692
  390.9 23.8 %copy-start.24 = (bf16[256,704]{0,1:T(8,128)(2,1)S(1)}, bf16[256,704]{0,1:T(8,128)(2,1)}, u32[]{:S(2)}) copy-start(bf16[256,704]{0,1:T(8,128)(2,1)} %get-tuple-element.147) | copy-start | bytes 1081348
  390.9 23.8 %collective-permute-start.28 = (bf16[256,2112]{0,1:T(8,128)(2,1)S(1)}, bf16[256,2112]{0,1:T(8,128)(2,1)S(1)}, u32[]{:S(2)}, u32[]{:S(2)}) collective-permute-start(bf16[256,2112]{0,1:T(8,128)(2,1)S(1)} %add_convert_fusion.3), channel_id=1, source_target_pairs={{0,16},{16,0},{8,24},{24,8},{1,17},{17,1},{9,25},{25,9},{2,18},{18... | collective-permute-start | bytes 3244040 | tf_op jit(solution)/shard_map/ppermute | solution.py:413
  394.0 23.5 %collective-permute-start.29 = (bf16[256,2112]{0,1:T(8,128)(2,1)S(1)}, bf16[256,2112]{0,1:T(8,128)(2,1)S(1)}, u32[]{:S(2)}, u32[]{:S(2)}) collective-permute-start(bf16[256,2112]{0,1:T(8,128)(2,1)S(1)} %add_convert_fusion.1), channel_id=1, source_target_pairs={{0,8},{8,0},{16,24},{24,16},{1,9},{9,1},{17,25},{25,17},{2,10},{10... | collective-permute-start | bytes 3244040 | tf_op jit(solution)/shard_map/ppermute | solution.py:414
  425.0 56.3 %all-to-all-start.3 = ((bf16[8,64,2112]{2,1,0:T(8,128)(2,1)}), bf16[8,64,2112]{2,1,0:T(8,128)(2,1)}, u32[]{:S(2)}, u32[]{:S(2)}) async-start(bf16[8,64,2112]{2,1,0:T(8,128)(2,1)} %bitcast.117), calls=%async_computation.6 | async-start | bytes 4456448 | tf_op jit(solution)/shard_map/all_to_all | solution.py:340
  429.4 103.4 %reduce-scatter.11.cloned.1.call-start = ((), (), s32[]{:S(2)}) async-start(), calls=%async_computation.15 | async-start | bytes 4718592 | tf_op jit(solution)/shard_map/reduce_scatter | solution.py:336
  481.4 7.8 %copy-start.10 = (bf16[1,1024,2048]{2,1,0:T(8,128)(2,1)S(1)}, bf16[1,1024,2048]{2,1,0:T(8,128)(2,1)}, u32[]{:S(2)}) copy-start(bf16[1,1024,2048]{2,1,0:T(8,128)(2,1)} %all-gather.12.cloned.1.call-done) | copy-start | bytes 12582916
  485.0 11.3 %collective-permute-start.30 = (bf16[32,2048]{1,0:T(8,128)(2,1)S(1)}, bf16[32,2048]{1,0:T(8,128)(2,1)S(1)}, u32[]{:S(2)}, u32[]{:S(2)}) collective-permute-start(bf16[32,2048]{1,0:T(8,128)(2,1)S(1)} %get-tuple-element.181), channel_id=1, source_target_pairs={{0,8},{8,0},{16,24},{24,16},{1,9},{9,1},{17,25},{25,17},{2,10},{10... | collective-permute-start | bytes 393224 | tf_op jit(solution)/shard_map/ppermute | solution.py:389
  486.5 10.5 %collective-permute-start.34 = (bf16[32,2048]{1,0:T(8,128)(2,1)S(1)}, bf16[32,2048]{1,0:T(8,128)(2,1)S(1)}, u32[]{:S(2)}, u32[]{:S(2)}) collective-permute-start(bf16[32,2048]{1,0:T(8,128)(2,1)S(1)} %get-tuple-element.182), channel_id=1, source_target_pairs={{0,16},{16,0},{8,24},{24,8},{1,17},{17,1},{9,25},{25,9},{2,18},{18... | collective-permute-start | bytes 393224 | tf_op jit(solution)/shard_map/ppermute | solution.py:389
  487.5 19.1 %collective-permute-start.33 = (bf16[32,2048]{1,0:T(8,128)(2,1)S(1)}, bf16[32,2048]{1,0:T(8,128)(2,1)S(1)}, u32[]{:S(2)}, u32[]{:S(2)}) collective-permute-start(bf16[32,2048]{1,0:T(8,128)(2,1)S(1)} %get-tuple-element.183), channel_id=1, source_target_pairs={{0,16},{16,0},{8,24},{24,8},{1,17},{17,1},{9,25},{25,9},{2,18},{18... | collective-permute-start | bytes 393224 | tf_op jit(solution)/shard_map/ppermute | solution.py:389
  488.5 5.0 collective-permute-start.31
  489.2 5.5 collective-permute-start.21
  493.5 6.0 %collective-permute-start.32 = (bf16[32,2048]{1,0:T(8,128)(2,1)S(1)}, bf16[32,2048]{1,0:T(8,128)(2,1)S(1)}, u32[]{:S(2)}, u32[]{:S(2)}) collective-permute-start(bf16[32,2048]{1,0:T(8,128)(2,1)S(1)} %add_convert_fusion.12), channel_id=1, source_target_pairs={{0,16},{16,0},{8,24},{24,8},{1,17},{17,1},{9,25},{25,9},{2,18},{18... | collective-permute-start | bytes 393224 | tf_op jit(solution)/shard_map/ppermute | solution.py:413
  495.1 9.2 %collective-permute-start.23 = (bf16[256,512]{1,0:T(8,128)(2,1)S(1)}, bf16[256,512]{1,0:T(8,128)(2,1)S(1)}, u32[]{:S(2)}, u32[]{:S(2)}) collective-permute-start(bf16[256,512]{1,0:T(8,128)(2,1)S(1)} %get-tuple-element.164), channel_id=1, source_target_pairs={{0,8},{8,0},{16,24},{24,16},{1,9},{9,1},{17,25},{25,17},{2,10},{10... | collective-permute-start | bytes 786440 | tf_op jit(solution)/shard_map/ppermute | solution.py:389
  496.3 9.2 %collective-permute-start.26 = (bf16[256,512]{1,0:T(8,128)(2,1)S(1)}, bf16[256,512]{1,0:T(8,128)(2,1)S(1)}, u32[]{:S(2)}, u32[]{:S(2)}) collective-permute-start(bf16[256,512]{1,0:T(8,128)(2,1)S(1)} %get-tuple-element.166), channel_id=1, source_target_pairs={{0,16},{16,0},{8,24},{24,8},{1,17},{17,1},{9,25},{25,9},{2,18},{18... | collective-permute-start | bytes 786440 | tf_op jit(solution)/shard_map/ppermute | solution.py:389
  499.7 8.1 %collective-permute-start.35 = (bf16[32,2048]{1,0:T(8,128)(2,1)S(1)}, bf16[32,2048]{1,0:T(8,128)(2,1)S(1)}, u32[]{:S(2)}, u32[]{:S(2)}) collective-permute-start(bf16[32,2048]{1,0:T(8,128)(2,1)S(1)} %get-tuple-element.180), channel_id=1, source_target_pairs={{0,8},{8,0},{16,24},{24,16},{1,9},{9,1},{17,25},{25,17},{2,10},{10... | collective-permute-start | bytes 393224 | tf_op jit(solution)/shard_map/ppermute | solution.py:414
  500.7 12.1 %collective-permute-start.22 = (bf16[256,512]{1,0:T(8,128)(2,1)S(1)}, bf16[256,512]{1,0:T(8,128)(2,1)S(1)}, u32[]{:S(2)}, u32[]{:S(2)}) collective-permute-start(bf16[256,512]{1,0:T(8,128)(2,1)S(1)} %get-tuple-element.163), channel_id=1, source_target_pairs={{0,8},{8,0},{16,24},{24,16},{1,9},{9,1},{17,25},{25,17},{2,10},{10... | collective-permute-start | bytes 786440 | tf_op jit(solution)/shard_map/ppermute | solution.py:389
  504.4 8.4 %collective-permute-start.25 = (bf16[256,512]{1,0:T(8,128)(2,1)S(1)}, bf16[256,512]{1,0:T(8,128)(2,1)S(1)}, u32[]{:S(2)}, u32[]{:S(2)}) collective-permute-start(bf16[256,512]{1,0:T(8,128)(2,1)S(1)} %get-tuple-element.165), channel_id=1, source_target_pairs={{0,16},{16,0},{8,24},{24,8},{1,17},{17,1},{9,25},{25,9},{2,18},{18... | collective-permute-start | bytes 786440 | tf_op jit(solution)/shard_map/ppermute | solution.py:389
  505.7 9.8 %collective-permute-start.24 = (bf16[256,512]{1,0:T(8,128)(2,1)S(1)}, bf16[256,512]{1,0:T(8,128)(2,1)S(1)}, u32[]{:S(2)}, u32[]{:S(2)}) collective-permute-start(bf16[256,512]{1,0:T(8,128)(2,1)S(1)} %get-tuple-element.167), channel_id=1, source_target_pairs={{0,16},{16,0},{8,24},{24,8},{1,17},{17,1},{9,25},{25,9},{2,18},{18... | collective-permute-start | bytes 786440 | tf_op jit(solution)/shard_map/ppermute | solution.py:413
  506.6 9.4 %collective-permute-start.27 = (bf16[256,512]{1,0:T(8,128)(2,1)S(1)}, bf16[256,512]{1,0:T(8,128)(2,1)S(1)}, u32[]{:S(2)}, u32[]{:S(2)}) collective-permute-start(bf16[256,512]{1,0:T(8,128)(2,1)S(1)} %get-tuple-element.168), channel_id=1, source_target_pairs={{0,8},{8,0},{16,24},{24,16},{1,9},{9,1},{17,25},{25,17},{2,10},{10... | collective-permute-start | bytes 786440 | tf_op jit(solution)/shard_map/ppermute | solution.py:414
  517.1 23.3 %all-to-all-start.4 = ((bf16[8,64,512]{2,1,0:T(8,128)(2,1)}), bf16[8,64,512]{2,1,0:T(8,128)(2,1)}, u32[]{:S(2)}, u32[]{:S(2)}) async-start(bf16[8,64,512]{2,1,0:T(8,128)(2,1)} %bitcast.21), calls=%async_computation.7 | async-start | bytes 1048576 | tf_op jit(solution)/shard_map/all_to_all | solution.py:340
  534.1 7.4 %copy-start.28 = (bf16[64,256]{1,0:T(8,128)(2,1)S(1)}, bf16[64,256]{1,0:T(8,128)(2,1)}, u32[]{:S(2)}) copy-start(bf16[64,256]{1,0:T(8,128)(2,1)} %param.18) | copy-start | bytes 98308
  534.1 7.4 %copy-start.30 = (bf16[64,256]{1,0:T(8,128)(2,1)S(1)}, bf16[64,256]{1,0:T(8,128)(2,1)}, u32[]{:S(2)}) copy-start(bf16[64,256]{1,0:T(8,128)(2,1)} %param.19) | copy-start | bytes 98308
  534.1 7.4 %copy-start.32 = (f32[64]{0:T(128)S(1)}, f32[64]{0:T(128)}, u32[]{:S(2)}) copy-start(f32[64]{0:T(128)} %copy-done.31) | copy-start | bytes 772
  543.8 6.3 %copy-start.35 = (f32[64]{0:T(128)S(1)}, f32[64]{0:T(128)}, u32[]{:S(2)}) copy-start(f32[64]{0:T(128)} %copy-done.34) | copy-start | bytes 772
  (25 other events, 69.8 us)
Sparse Core Ops, SparseCore 0:
  9.6 75.2 all-gather.11
  136.2 50.5 reduce-scatter.4
  190.6 45.3 all-gather.5
  237.4 45.6 all-gather.7
  285.3 48.7 reduce-scatter.8
  336.2 48.3 reduce-scatter.6
  389.1 45.3 all-gather.9
  481.4 51.2 reduce-scatter.10

commit v10 on v9

--- a/solution.py
+++ b/solution.py
@@ -795,22 +795,24 @@
         weighted_one - shaped_one * jnp.mean(weighted_one * shaped_one, axis=-1, keepdims=True)
     )
     block_output = (residual + out_own.astype(f32)).astype(bf16)
-    attn_grad, out_grad, gate_rows, up_rows, down_grad, input_grad, block_output = tie(
-        attn_grad, out_grad, gate_rows, up_rows, down_grad, input_grad, block_output
+    def row_sum(weight, grad):
+        return jnp.sum(weight.astype(f32) * grad, axis=1)
+
+    mlp_gain_grad = row_sum(gate_weight, gate_rows) + row_sum(up_weight, up_rows)
+    gate_grad = gate_rows * gain_two
+    up_grad = up_rows * gain_two
+    attn_grad, out_grad, gate_grad, up_grad, down_grad, input_grad, block_output, mlp_gain_grad = tie(
+        attn_grad, out_grad, gate_grad, up_grad, down_grad, input_grad, block_output, mlp_gain_grad
     )
     query_rows = from_head_slices(attn_grad[:, :, :head_width]).astype(f32)
     pair_rows = jnp.sum(attn_grad[:, :, head_width:].astype(f32).reshape(4, 2, rows, head_width), axis=0)
     key_rows, value_rows = pair_rows[0], pair_rows[1]
-
-    def row_sum(weight, grad):
-        return jnp.sum(weight.astype(f32) * grad, axis=1)
 
     attn_gain_grad = (
         row_sum(query_weight, query_rows)
         + row_sum(key_weight, key_rows)
         + row_sum(value_weight, value_rows)
     )
-    mlp_gain_grad = row_sum(gate_weight, gate_rows) + row_sum(up_weight, up_rows)
     return (
         block_output[None],
         input_grad[None],
@@ -820,8 +822,8 @@
         value_rows * gain_one,
         out_grad,
         mlp_gain_grad,
-        gate_rows * gain_two,
-        up_rows * gain_two,
+        gate_grad,
+        up_grad,
         down_grad,
     )
 

time: 571 us -> 561 us (0.982)
    unnamed x79 -> x93, local copies, waits for them, and re-layouts: 11.8 us -> 11.8 us
  transfers between devices with their start and end apart: 49 -> 49, of which waited for: 24 -> 23; matrix products, arithmetic and copies ran while one was open for 36% -> 38% of each run, Pallas kernels for 6% -> 6%
where the time goes in v10:
time: 561 us; the launch traced here: 553 us
  waiting for transfers between devices  209 us (37%)
  local copies, waits for them, and re-layouts  102 us (18%)
  matrix products  83.8 us (15%)
  starting transfers between devices  58.4 us (10%)
  other arithmetic  50.3 us (9%)
  Pallas kernels  33 us (6%)
  between operations  16.5 us (3%)
    reduce_scatter x4, waiting for transfers between devices, reduce_ctx(): return lax.psum_scatter(partial, 'ctx', scatter_dimension=0, tiled=True)  52.9 us
    all_gather x4, waiting for transfers between devices, gather_ctx(): return lax.all_gather(block, 'ctx', axis=0, tiled=True)  48.1 us
    ppermute x4, waiting for transfers between devices, gather_seq_far(): far_low = lax.ppermute(from_y[half:], 'seq', SEQ_X)  34.3 us
    dot_general x4, matrix products, contract_cols(): lax.dot_general(left, right, (((1,), (1,)), ((), ())), preferred_element_...  29.7 us
    dynamic_update_slice x20, local copies, waits for them, and re-layouts, gather_seq_far(): whole = lax.dynamic_update_slice_in_dim(whole, piece, start, 0)  25.5 us
    all_to_all x5, waiting for transfers between devices, exchange_ctx(): return lax.all_to_all(pieces, 'ctx', 0, 0, tiled=True)  24.9 us
    ppermute x3, waiting for transfers between devices, reduce_seq_far(): top_last = lax.ppermute(top_send, 'seq', SEQ_Y)  24.4 us
    all_to_all x5, starting transfers between devices, exchange_ctx(): return lax.all_to_all(pieces, 'ctx', 0, 0, tiled=True)  21.9 us
  transfers between devices with their start and end apart: 49, of which 23 were waited for; matrix products, arithmetic and copies ran while one was open for 38% of the time, Pallas kernels for 6%

profile of v10, /device:TPU:0, one launch (start us, length us, event | category | flops | bytes accessed | tf_op | source)
XLA Modules:
  0.0 552.5 jit_solution(7871800422637356937)
XLA Ops:
  7.9 3.1 collective-permute-start.6
  16.3 5.0 all-to-all-start
  27.1 2.2 concatenate.109
  34.6 16.7 %all-to-all-done = bf16[8,64,512]{2,1,0:T(8,128)(2,1)} async-done(((bf16[8,64,512]{2,1,0:T(8,128)(2,1)}), bf16[8,64,512]{2,1,0:T(8,128)(2,1)}, u32[]{:S(2)}, u32[]{:S(2)}) %all-to-all-start) | async-done | bytes 524320 | tf_op jit(solution)/shard_map/all_to_all | solution.py:340
  52.5 3.5 all-to-all-start.1
  58.8 11.7 %collective-permute-done = bf16[512,512]{1,0:T(8,128)(2,1)S(1)} collective-permute-done((bf16[512,512]{1,0:T(8,128)(2,1)}, bf16[512,512]{1,0:T(8,128)(2,1)S(1)}, u32[]{:S(2)}, u32[]{:S(2)}) %collective-permute-start) | collective-permute-done | bytes 524320 | tf_op jit(solution)/shard_map/ppermute | solution.py:344
  72.8 1.9 constant_dynamic-update-slice_fusion.19
  79.0 1.9 constant_dynamic-update-slice_fusion.17
  82.6 2.7 collective-permute-done.3
  86.0 2.3 slice.227
  88.3 2.6 copy.80
  90.9 4.6 all-to-all-start.2
  95.8 3.2 fusion
  99.3 5.3 fusion.66
  104.6 3.5 fusion.64
  114.6 1.8 select_convert_fusion
  118.1 13.3 %attend.1 = bf16[1024,256]{1,0:T(8,128)(2,1)} custom-call(s32[1]{0:T(128)} %bitcast.2.refs_0_, bf16[1024,256]{1,0:T(8,128)(2,1)} %get-tuple-element.172.refs_1_, bf16[1024,256]{1,0:T(8,128)(2,1)} %fusion.29.refs_2_, bf16[1024,256]{1,0:T(8,128)(2,1)} %get-tuple-element.171.refs_3_), custom_call_target="tpu_custom_call" | custom-call | flops 4294967296 | bytes 2097152 | tf_op jit(solution)/shard_map/attend/pallas_call | solution.py:581
  131.4 4.6 convolution_convert_fusion.2
  143.7 1.9 broadcast_in_dim.33
  147.9 2.3 copy.84
  151.2 2.2 constant_dynamic-update-slice_fusion.7
  153.4 24.6 %collective-permute-done.12 = bf16[256,704]{0,1:T(8,128)(2,1)} collective-permute-done((bf16[256,704]{0,1:T(8,128)(2,1)}, bf16[256,704]{0,1:T(8,128)(2,1)}, u32[]{:S(2)}, u32[]{:S(2)}) %collective-permute-start.12) | collective-permute-done | bytes 360480 | tf_op jit(solution)/shard_map/ppermute | solution.py:352
  181.9 4.8 reduce-scatter.5.cloned.1.call-done
  188.1 2.4 fusion.71
  193.8 2.9 broadcast_in_dim.34
  196.7 2.8 constant_dynamic-update-slice_fusion.4
  202.0 2.6 constant_dynamic-update-slice_fusion.3
  204.6 2.6 constant_dynamic-update-slice_fusion.2
  209.2 7.0 %collective-permute-done.16 = bf16[256,1408]{1,0:T(8,128)(2,1)S(1)} collective-permute-done((bf16[256,1408]{1,0:T(8,128)(2,1)S(1)}, bf16[256,1408]{1,0:T(8,128)(2,1)S(1)}, u32[]{:S(2)}, u32[]{:S(2)}) %collective-permute-start.16) | collective-permute-done | bytes 720928 | tf_op jit(solution)/shard_map/ppermute | solution.py:352
  217.1 18.8 %all-gather.6.cloned.1.call-done = bf16[1024,2048]{1,0:T(8,128)(2,1)} async-done(((bf16[128,2048]{1,0:T(8,128)(2,1)}), bf16[1024,2048]{1,0:T(8,128)(2,1)}) %all-gather.6.cloned.1.call-update) | async-done | bytes 4194320 | tf_op jit(solution)/shard_map/all_gather | solution.py:332
  235.9 10.9 %fusion.83 = f32[1024,1408]{1,0:T(8,128)S(1)} fusion(bf16[1024,2048]{1,0:T(8,128)(2,1)} %all-gather.6.cloned.1.call-done, bf16[2048,1408]{1,0:T(8,128)(2,1)} %constant_dynamic-update-slice_fusion), kind=kOutput, calls=%fused_computation.238 | convolution fusion | flops 5905580032 | bytes 15728640 | tf_op jit(solution)/shard_map/dot_general | solution.py:712
  251.9 6.9 %convolution_convert_fusion.4 = bf16[1024,2048]{1,0:T(8,128)(2,1)} fusion(bf16[1024,704]{1,0:T(8,128)(2,1)S(1)} %multiply_convert_fusion.2, bf16[2048,704]{1,0:T(8,128)(2,1)} %constant_dynamic-update-slice_fusion.5), kind=kOutput, calls=%fused_computation.24 | convolution fusion | flops 2954887168 | bytes 8519680 | tf_op jit(solution)/shard_map/dot_general | solution.py:53
  258.8 24.3 %all-gather.8.cloned.1.call-done = bf16[1024,2048]{1,0:T(8,128)(2,1)} async-done(((bf16[128,2048]{1,0:T(8,128)(2,1)}), bf16[1024,2048]{1,0:T(8,128)(2,1)}) %all-gather.8.cloned.1.call-update) | async-done | bytes 4194320 | tf_op jit(solution)/shard_map/all_gather | solution.py:332
  283.2 9.0 %multiply_convert_fusion = (bf16[1024,704]{1,0:T(8,128)(2,1)S(1)}, bf16[1024,704]{1,0:T(8,128)(2,1)S(1)}) fusion(f32[1024,64]{1,0:T(8,128)S(1)} %get-tuple-element.147, f32[1024,640]{1,0:T(8,128)} %copy-done.4, f32[1024,64]{1,0:T(8,128)} %copy-done.23, f32[1024,640]{1,0:T(8,128)} %copy-done.5, bf16[1024,2048]{1,0:T(8,128)(2,1)} %all-gather.8.cloned.1.call-done, ...), kind=kOutput, calls=%fused_computation.31 | convolution fusion | flops 2963603456 | bytes 15728640 | tf_op jit(solution)/shard_map/dot_general | solution.py:729
  294.6 5.4 concatenate.118
  299.9 11.1 %convolution_convert_fusion.1 = bf16[1024,2048]{1,0:T(8,128)(2,1)} fusion(bf16[1024,1408]{1,0:T(8,128)(2,1)} %concatenate.118, bf16[2048,1408]{1,0:T(8,128)(2,1)} %constant_dynamic-update-slice_fusion), kind=kOutput, calls=%fused_computation.21 | convolution fusion | flops 5907677184 | bytes 12845056 | tf_op jit(solution)/shard_map/dot_general | solution.py:53
  311.3 6.1 %convolution_convert_fusion.5 = bf16[2048,704]{0,1:T(8,128)(2,1)S(1)} fusion(bf16[1024,2048]{1,0:T(8,128)(2,1)} %all-gather.8.cloned.1.call-done, bf16[1024,704]{1,0:T(8,128)(2,1)} %copy-done.24), kind=kOutput, calls=%fused_computation.25 | convolution fusion | flops 2954231808 | bytes 8519680 | tf_op jit(solution)/shard_map/dot_general | solution.py:47
  319.7 6.6 %convolution_convert_fusion = bf16[2048,1408]{0,1:T(8,128)(2,1)S(1)} fusion(bf16[1024,2048]{1,0:T(8,128)(2,1)S(1)} %copy-done.43, bf16[1024,1408]{1,0:T(8,128)(2,1)S(1)} %copy-done.19), kind=kOutput, calls=%fused_computation.4 | convolution fusion | flops 5908463616 | bytes 12845056 | tf_op jit(solution)/shard_map/dot_general | solution.py:47
  326.3 1.9 constant_dynamic-slice_fusion.11
  338.1 46.5 %reduce-scatter.7.cloned.1.call-done = bf16[128,2048]{1,0:T(8,128)(2,1)} async-done(((bf16[1024,2048]{1,0:T(8,128)(2,1)}), bf16[128,2048]{1,0:T(8,128)(2,1)}) %reduce-scatter.7.cloned.1.call-update) | async-done | bytes 524304 | tf_op jit(solution)/shard_map/reduce_scatter | solution.py:336
  386.3 2.7 fusion.69
  389.0 1.9 add_convert_fusion.3
  395.5 19.1 %collective-permute-done.28 = bf16[256,2112]{0,1:T(8,128)(2,1)S(1)} collective-permute-done((bf16[256,2112]{0,1:T(8,128)(2,1)S(1)}, bf16[256,2112]{0,1:T(8,128)(2,1)S(1)}, u32[]{:S(2)}, u32[]{:S(2)}) %collective-permute-start.28) | collective-permute-done | bytes 1081376 | tf_op jit(solution)/shard_map/ppermute | solution.py:413
  414.7 1.9 add_convert_fusion.2
  420.9 4.1 copy.94
  425.0 4.4 all-to-all-start.3
  429.4 5.1 all-gather.10.cloned.1.call-done
  434.5 4.6 convolution_convert_fusion.8.refs_4_
  439.0 19.7 %attend_back.1 = (f32[1024,256]{1,0:T(8,128)}, f32[1024,256]{1,0:T(8,128)}, f32[1024,256]{1,0:T(8,128)}) custom-call(s32[1]{0:T(128)} %bitcast.2.refs_0_, bf16[1024,256]{1,0:T(8,128)(2,1)} %get-tuple-element.172.refs_1_, bf16[1024,256]{1,0:T(8,128)(2,1)} %fusion.29.refs_2_, bf16[1024,256]{1,0:T(8,128)(2,1)} %get-tuple-element.171.refs_3_, ...), custom_call_target="tpu_custom_call" | custom-call | flops 10737418240 | bytes 3670016 | tf_op jit(solution)/shard_map/attend_back/pallas_call | solution.py:602
  466.3 1.9 convolution_convert_fusion.7
  468.2 7.2 %convolution_convert_fusion.3 = bf16[1024,2048]{1,0:T(8,128)(2,1)} fusion(bf16[2048,256]{1,0:T(8,128)(2,1)} %collective-permute-done.4, bf16[2048,512]{1,0:T(8,128)(2,1)} %constant_dynamic-update-slice_fusion.15, bf16[1024,256]{1,0:T(8,128)(2,1)S(1)} %get-tuple-element.129, bf16[1024,512]{1,0:T(8,128)(2,1)S(1)} %pad_maximum_fusion.7), kind=kOutput, calls=%fused_computation.23 | convolution fusion | flops 3232759808 | bytes 8912896 | tf_op jit(solution)/shard_map/dot_general | solution.py:53
  475.3 5.9 %all-to-all-done.3 = bf16[8,64,2112]{2,1,0:T(8,128)(2,1)} async-done(((bf16[8,64,2112]{2,1,0:T(8,128)(2,1)}), bf16[8,64,2112]{2,1,0:T(8,128)(2,1)}, u32[]{:S(2)}, u32[]{:S(2)}) %all-to-all-start.3) | async-done | bytes 2162720 | tf_op jit(solution)/shard_map/all_to_all | solution.py:340
  481.4 3.6 convolution_convert_fusion.6
  489.2 2.6 fusion.61
  497.0 2.6 collective-permute-done.32
  501.8 2.5 collective-permute-done.23
  508.6 4.2 collective-permute-done.22
  512.8 2.7 collective-permute-done.24
  517.1 4.4 all-to-all-start.4
  521.4 2.5 slice_bitcast_fusion
  524.0 1.8 slice_bitcast_fusion.3
  530.0 2.2 fusion.12
  535.4 2.7 add_convert_fusion.4
  538.1 2.2 all-to-all-done.4
  (308 shorter events, 130.3 us)
Async XLA Ops:
  7.2 8.1 %copy-start.36 = (bf16[64,256]{1,0:T(8,128)(2,1)S(1)}, bf16[64,256]{1,0:T(8,128)(2,1)}, u32[]{:S(2)}) copy-start(bf16[64,256]{1,0:T(8,128)(2,1)} %param.19) | copy-start | bytes 98308
  7.2 8.1 %copy-start.34 = (bf16[64,256]{1,0:T(8,128)(2,1)S(1)}, bf16[64,256]{1,0:T(8,128)(2,1)}, u32[]{:S(2)}) copy-start(bf16[64,256]{1,0:T(8,128)(2,1)} %param.18) | copy-start | bytes 98308
  7.2 88.6 %all-gather.12.cloned.1.call-start = ((), (), s32[]{:S(2)}) async-start(), calls=%async_computation.16 | async-start | bytes 4718592 | tf_op jit(solution)/shard_map/all_gather | solution.py:332
  7.9 21.5 %collective-permute-start.6 = (bf16[64,2048]{1,0:T(8,128)(2,1)}, bf16[64,2048]{1,0:T(8,128)(2,1)}, u32[]{:S(2)}, u32[]{:S(2)}) collective-permute-start(bf16[64,2048]{1,0:T(8,128)(2,1)} %param.20), channel_id=1, source_target_pairs={{0,16},{16,0},{8,24},{24,8},{1,17},{17,1},{9,25},{25,9},{2,18},{18... | collective-permute-start | bytes 786440 | tf_op jit(solution)/shard_map/ppermute | solution.py:344
  11.0 20.5 %collective-permute-start.5 = (bf16[64,2048]{1,0:T(8,128)(2,1)}, bf16[64,2048]{1,0:T(8,128)(2,1)}, u32[]{:S(2)}, u32[]{:S(2)}) collective-permute-start(bf16[64,2048]{1,0:T(8,128)(2,1)} %param.20), channel_id=1, source_target_pairs={{0,8},{8,0},{16,24},{24,16},{1,9},{9,1},{17,25},{25,17},{2,10},{10... | collective-permute-start | bytes 786440 | tf_op jit(solution)/shard_map/ppermute | solution.py:344
  15.3 6.0 %copy-start.44 = (bf16[64]{0:T(256)(128)(2,1)S(1)}, bf16[64]{0:T(256)(128)(2,1)}, u32[]{:S(2)}) copy-start(bf16[64]{0:T(256)(128)(2,1)} %param.21) | copy-start | bytes 388
  15.3 6.0 %slice-start = ((bf16[64,5632]{1,0:T(8,128)(2,1)}), bf16[64,512]{1,0:T(8,128)(2,1)S(1)}, s32[]{:S(2)}) async-start(bf16[64,5632]{1,0:T(8,128)(2,1)} %param.24), calls=%async_computation.17 | async-start | bytes 131072 | tf_op jit(solution)/shard_map/slice | solution.py:447
  15.4 6.1 %slice-start.1 = ((bf16[64,5632]{1,0:T(8,128)(2,1)}), bf16[64,5120]{1,0:T(8,128)(2,1)S(1)}, s32[]{:S(2)}) async-start(bf16[64,5632]{1,0:T(8,128)(2,1)} %param.24), calls=%async_computation.18 | async-start | bytes 1310720 | tf_op jit(solution)/shard_map/slice | solution.py:446
  16.3 6.1 %copy-start.40 = (s32[1,1024]{1,0:T(1,128)S(1)}, s32[1,1024]{1,0:T(1,128)}, u32[]{:S(2)}) copy-start(s32[1,1024]{1,0:T(1,128)} %param.14) | copy-start | bytes 12292
  16.3 35.0 %all-to-all-start = ((bf16[8,64,512]{2,1,0:T(8,128)(2,1)}), bf16[8,64,512]{2,1,0:T(8,128)(2,1)}, u32[]{:S(2)}, u32[]{:S(2)}) async-start(bf16[8,64,512]{2,1,0:T(8,128)(2,1)} %pad_maximum_fusion.11), calls=%async_computation | async-start | bytes 1048576 | tf_op jit(solution)/shard_map/all_to_all | solution.py:340
  31.0 27.8 %collective-permute-start.8 = (bf16[32,2048]{1,0:T(8,128)(2,1)}, bf16[32,2048]{1,0:T(8,128)(2,1)S(1)}, u32[]{:S(2)}, u32[]{:S(2)}) collective-permute-start(bf16[32,2048]{1,0:T(8,128)(2,1)} %slice.233), channel_id=1, source_target_pairs={{0,8},{8,0},{16,24},{24,16},{1,9},{9,1},{17,25},{25,17},{2,10},{10... | collective-permute-start | bytes 393224 | tf_op jit(solution)/shard_map/ppermute | solution.py:352
  33.1 24.8 %collective-permute-start.7 = (bf16[32,2048]{1,0:T(8,128)(2,1)}, bf16[32,2048]{1,0:T(8,128)(2,1)}, u32[]{:S(2)}, u32[]{:S(2)}) collective-permute-start(bf16[32,2048]{1,0:T(8,128)(2,1)} %slice.232), channel_id=1, source_target_pairs={{0,16},{16,0},{8,24},{24,8},{1,17},{17,1},{9,25},{25,9},{2,18},{18... | collective-permute-start | bytes 393224 | tf_op jit(solution)/shard_map/ppermute | solution.py:351
  52.5 35.8 %all-to-all-start.1 = ((bf16[8,64,704]{2,1,0:T(8,128)(2,1)}), bf16[8,64,704]{2,1,0:T(8,128)(2,1)S(1)}, u32[]{:S(2)}, u32[]{:S(2)}) async-start(bf16[8,64,704]{2,1,0:T(8,128)(2,1)} %pad_maximum_fusion.8), calls=%async_computation.1 | async-start | bytes 1572864 | tf_op jit(solution)/shard_map/all_to_all | solution.py:340
  56.1 14.4 %collective-permute-start = (bf16[512,512]{1,0:T(8,128)(2,1)}, bf16[512,512]{1,0:T(8,128)(2,1)S(1)}, u32[]{:S(2)}, u32[]{:S(2)}) collective-permute-start(bf16[512,512]{1,0:T(8,128)(2,1)} %bitcast.7), channel_id=1, source_target_pairs={{0,8},{8,0},{16,24},{24,16},{1,9},{9,1},{17,25},{25,17},{2,10},{10... | collective-permute-start | bytes 1572872 | tf_op jit(solution)/shard_map/ppermute | solution.py:344
  57.3 19.3 %collective-permute-start.1 = (bf16[512,512]{1,0:T(8,128)(2,1)}, bf16[512,512]{1,0:T(8,128)(2,1)}, u32[]{:S(2)}, u32[]{:S(2)}) collective-permute-start(bf16[512,512]{1,0:T(8,128)(2,1)} %bitcast.7), channel_id=1, source_target_pairs={{0,16},{16,0},{8,24},{24,8},{1,17},{17,1},{9,25},{25,9},{2,18},{18... | collective-permute-start | bytes 1572872 | tf_op jit(solution)/shard_map/ppermute | solution.py:344
  58.8 14.0 %copy-start.14 = (bf16[256,2048]{1,0:T(8,128)(2,1)}, bf16[256,2048]{1,0:T(8,128)(2,1)S(1)}, u32[]{:S(2)}) copy-start(bf16[256,2048]{1,0:T(8,128)(2,1)S(1)} %constant_dynamic-update-slice_fusion.10) | copy-start | bytes 3145732
  71.2 9.7 %collective-permute-start.2 = (bf16[256,512]{1,0:T(8,128)(2,1)}, bf16[256,512]{1,0:T(8,128)(2,1)}, u32[]{:S(2)}, u32[]{:S(2)}) collective-permute-start(bf16[256,512]{1,0:T(8,128)(2,1)} %slice.225), channel_id=1, source_target_pairs={{0,16},{16,0},{8,24},{24,8},{1,17},{17,1},{9,25},{25,9},{2,18},{18... | collective-permute-start | bytes 786440 | tf_op jit(solution)/shard_map/ppermute | solution.py:351
  77.6 7.7 %collective-permute-start.3 = (bf16[256,512]{1,0:T(8,128)(2,1)S(1)}, bf16[256,512]{1,0:T(8,128)(2,1)S(1)}, u32[]{:S(2)}, u32[]{:S(2)}) collective-permute-start(bf16[256,512]{1,0:T(8,128)(2,1)S(1)} %slice.226), channel_id=1, source_target_pairs={{0,8},{8,0},{16,24},{24,16},{1,9},{9,1},{17,25},{25,17},{2,10},{10... | collective-permute-start | bytes 786440 | tf_op jit(solution)/shard_map/ppermute | solution.py:352
  88.3 16.3 %collective-permute-start.4 = (bf16[2048,256]{1,0:T(8,128)(2,1)}, bf16[2048,256]{1,0:T(8,128)(2,1)}, u32[]{:S(2)}, u32[]{:S(2)}) collective-permute-start(bf16[2048,256]{1,0:T(8,128)(2,1)} %slice.227), channel_id=1, source_target_pairs={{0,1},{1,0},{2,3},{3,2},{4,5},{5,4},{6,7},{7,6},{8,9},{9,8},{10,11... | collective-permute-start | bytes 3145736 | tf_op jit(solution)/shard_map/ppermute | solution.py:434
  90.9 40.4 %all-to-all-start.2 = ((bf16[8,64,1408]{2,1,0:T(8,128)(2,1)}), bf16[8,64,1408]{2,1,0:T(8,128)(2,1)}, u32[]{:S(2)}, u32[]{:S(2)}) async-start(bf16[8,64,1408]{2,1,0:T(8,128)(2,1)} %copy.80), calls=%async_computation.2 | async-start | bytes 2883584 | tf_op jit(solution)/shard_map/all_to_all | solution.py:340
  95.6 91.1 %reduce-scatter.5.cloned.1.call-start = ((), (), s32[]{:S(2)}) async-start(), calls=%async_computation.9 | async-start | bytes 4718592 | tf_op jit(solution)/shard_map/reduce_scatter | solution.py:336
  109.2 22.2 %collective-permute-start.10 = (bf16[512,704]{0,1:T(8,128)(2,1)}, bf16[512,704]{0,1:T(8,128)(2,1)}, u32[]{:S(2)}, u32[]{:S(2)}) collective-permute-start(bf16[512,704]{0,1:T(8,128)(2,1)} %copy.81), channel_id=1, source_target_pairs={{0,16},{16,0},{8,24},{24,8},{1,17},{17,1},{9,25},{25,9},{2,18},{18... | collective-permute-start | bytes 2162696 | tf_op jit(solution)/shard_map/ppermute | solution.py:344
  110.9 20.4 %collective-permute-start.9 = (bf16[512,704]{0,1:T(8,128)(2,1)}, bf16[512,704]{0,1:T(8,128)(2,1)}, u32[]{:S(2)}, u32[]{:S(2)}) collective-permute-start(bf16[512,704]{0,1:T(8,128)(2,1)} %copy.81), channel_id=1, source_target_pairs={{0,8},{8,0},{16,24},{24,16},{1,9},{9,1},{17,25},{25,17},{2,10},{10... | collective-permute-start | bytes 2162696 | tf_op jit(solution)/shard_map/ppermute | solution.py:344
  136.0 99.9 %all-gather.6.cloned.1.call-start = ((), (), s32[]{:S(2)}) async-start(), calls=%async_computation.10 | async-start | bytes 4718592 | tf_op jit(solution)/shard_map/all_gather | solution.py:332
  136.1 45.8 %collective-permute-start.14 = (bf16[512,1408]{1,0:T(8,128)(2,1)}, bf16[512,1408]{1,0:T(8,128)(2,1)}, u32[]{:S(2)}, u32[]{:S(2)}) collective-permute-start(bf16[512,1408]{1,0:T(8,128)(2,1)} %bitcast.19), channel_id=1, source_target_pairs={{0,16},{16,0},{8,24},{24,8},{1,17},{17,1},{9,25},{25,9},{2,18},{18... | collective-permute-start | bytes 4325384 | tf_op jit(solution)/shard_map/ppermute | solution.py:344
  137.2 44.7 %collective-permute-start.13 = (bf16[512,1408]{1,0:T(8,128)(2,1)}, bf16[512,1408]{1,0:T(8,128)(2,1)}, u32[]{:S(2)}, u32[]{:S(2)}) collective-permute-start(bf16[512,1408]{1,0:T(8,128)(2,1)} %bitcast.19), channel_id=1, source_target_pairs={{0,8},{8,0},{16,24},{24,16},{1,9},{9,1},{17,25},{25,17},{2,10},{10... | collective-permute-start | bytes 4325384 | tf_op jit(solution)/shard_map/ppermute | solution.py:344
  141.5 36.5 %collective-permute-start.12 = (bf16[256,704]{0,1:T(8,128)(2,1)}, bf16[256,704]{0,1:T(8,128)(2,1)}, u32[]{:S(2)}, u32[]{:S(2)}) collective-permute-start(bf16[256,704]{0,1:T(8,128)(2,1)} %slice.190), channel_id=1, source_target_pairs={{0,8},{8,0},{16,24},{24,16},{1,9},{9,1},{17,25},{25,17},{2,10},{10... | collective-permute-start | bytes 1081352 | tf_op jit(solution)/shard_map/ppermute | solution.py:352
  142.7 36.4 %collective-permute-start.11 = (bf16[256,704]{0,1:T(8,128)(2,1)}, bf16[256,704]{0,1:T(8,128)(2,1)}, u32[]{:S(2)}, u32[]{:S(2)}) collective-permute-start(bf16[256,704]{0,1:T(8,128)(2,1)} %slice.189), channel_id=1, source_target_pairs={{0,16},{16,0},{8,24},{24,8},{1,17},{17,1},{9,25},{25,9},{2,18},{18... | collective-permute-start | bytes 1081352 | tf_op jit(solution)/shard_map/ppermute | solution.py:351
  151.2 35.5 %copy-start.3 = (bf16[1,128,2048]{2,1,0:T(8,128)(2,1)S(1)}, bf16[1,128,2048]{2,1,0:T(8,128)(2,1)}, u32[]{:S(2)}) copy-start(bf16[1,128,2048]{2,1,0:T(8,128)(2,1)} %param.13) | copy-start | bytes 1572868
  190.5 92.6 %all-gather.8.cloned.1.call-start = ((), (), s32[]{:S(2)}) async-start(), calls=%async_computation.11 | async-start | bytes 4718592 | tf_op jit(solution)/shard_map/all_gather | solution.py:332
  191.0 142.9 %reduce-scatter.9.cloned.1.call-start = ((), (), s32[]{:S(2)}) async-start(), calls=%async_computation.13 | async-start | bytes 4718592 | tf_op jit(solution)/shard_map/reduce_scatter | solution.py:336
  192.3 16.0 %collective-permute-start.15 = (bf16[256,1408]{1,0:T(8,128)(2,1)S(1)}, bf16[256,1408]{1,0:T(8,128)(2,1)S(1)}, u32[]{:S(2)}, u32[]{:S(2)}) collective-permute-start(bf16[256,1408]{1,0:T(8,128)(2,1)S(1)} %slice.191), channel_id=1, source_target_pairs={{0,16},{16,0},{8,24},{24,8},{1,17},{17,1},{9,25},{25,9},{2,18},{18... | collective-permute-start | bytes 2162696 | tf_op jit(solution)/shard_map/ppermute | solution.py:351
  200.6 15.6 %collective-permute-start.16 = (bf16[256,1408]{1,0:T(8,128)(2,1)S(1)}, bf16[256,1408]{1,0:T(8,128)(2,1)S(1)}, u32[]{:S(2)}, u32[]{:S(2)}) collective-permute-start(bf16[256,1408]{1,0:T(8,128)(2,1)S(1)} %slice.192), channel_id=1, source_target_pairs={{0,8},{8,0},{16,24},{24,16},{1,9},{9,1},{17,25},{25,17},{2,10},{10... | collective-permute-start | bytes 2162696 | tf_op jit(solution)/shard_map/ppermute | solution.py:352
  283.1 101.5 %reduce-scatter.7.cloned.1.call-start = ((), (), s32[]{:S(2)}) async-start(), calls=%async_computation.12 | async-start | bytes 4718592 | tf_op jit(solution)/shard_map/reduce_scatter | solution.py:336
  311.0 123.5 %all-gather.10.cloned.1.call-start = ((), (), s32[]{:S(2)}) async-start(), calls=%async_computation.14 | async-start | bytes 4718592 | tf_op jit(solution)/shard_map/all_gather | solution.py:332
  311.2 7.5 %copy-start.43 = (bf16[1024,2048]{1,0:T(8,128)(2,1)S(1)}, bf16[1024,2048]{1,0:T(8,128)(2,1)}, u32[]{:S(2)}) copy-start(bf16[1024,2048]{1,0:T(8,128)(2,1)} %all-gather.6.cloned.1.call-done) | copy-start | bytes 12582916
  334.0 50.6 %collective-permute-start.17 = (bf16[256,2112]{0,1:T(8,128)(2,1)}, bf16[256,2112]{0,1:T(8,128)(2,1)}, u32[]{:S(2)}, u32[]{:S(2)}) collective-permute-start(bf16[256,2112]{0,1:T(8,128)(2,1)} %pad_maximum_fusion.3), channel_id=1, source_target_pairs={{0,8},{8,0},{16,24},{24,16},{1,9},{9,1},{17,25},{25,17},{2,10},{10... | collective-permute-start | bytes 3244040 | tf_op jit(solution)/shard_map/ppermute | solution.py:389
  335.5 49.1 %collective-permute-start.18 = (bf16[256,2112]{0,1:T(8,128)(2,1)}, bf16[256,2112]{0,1:T(8,128)(2,1)}, u32[]{:S(2)}, u32[]{:S(2)}) collective-permute-start(bf16[256,2112]{0,1:T(8,128)(2,1)} %pad_maximum_fusion.4), channel_id=1, source_target_pairs={{0,16},{16,0},{8,24},{24,8},{1,17},{17,1},{9,25},{25,9},{2,18},{18... | collective-permute-start | bytes 3244040 | tf_op jit(solution)/shard_map/ppermute | solution.py:389
  336.9 47.6 %collective-permute-start.19 = (bf16[256,2112]{0,1:T(8,128)(2,1)}, bf16[256,2112]{0,1:T(8,128)(2,1)}, u32[]{:S(2)}, u32[]{:S(2)}) collective-permute-start(bf16[256,2112]{0,1:T(8,128)(2,1)} %pad_maximum_fusion.5), channel_id=1, source_target_pairs={{0,8},{8,0},{16,24},{24,16},{1,9},{9,1},{17,25},{25,17},{2,10},{10... | collective-permute-start | bytes 3244040 | tf_op jit(solution)/shard_map/ppermute | solution.py:389
  337.5 47.1 %collective-permute-start.20 = (bf16[256,2112]{0,1:T(8,128)(2,1)}, bf16[256,2112]{0,1:T(8,128)(2,1)}, u32[]{:S(2)}, u32[]{:S(2)}) collective-permute-start(bf16[256,2112]{0,1:T(8,128)(2,1)} %pad_maximum_fusion.6), channel_id=1, source_target_pairs={{0,16},{16,0},{8,24},{24,8},{1,17},{17,1},{9,25},{25,9},{2,18},{18... | collective-permute-start | bytes 3244040 | tf_op jit(solution)/shard_map/ppermute | solution.py:389
  390.9 23.8 %copy-start.20 = (bf16[256,1408]{0,1:T(8,128)(2,1)S(1)}, bf16[256,1408]{0,1:T(8,128)(2,1)}, u32[]{:S(2)}) copy-start(bf16[256,1408]{0,1:T(8,128)(2,1)} %get-tuple-element.137) | copy-start | bytes 2162692
  390.9 23.8 %copy-start.27 = (bf16[256,704]{0,1:T(8,128)(2,1)S(1)}, bf16[256,704]{0,1:T(8,128)(2,1)}, u32[]{:S(2)}) copy-start(bf16[256,704]{0,1:T(8,128)(2,1)} %get-tuple-element.149) | copy-start | bytes 1081348
  390.9 23.8 %collective-permute-start.28 = (bf16[256,2112]{0,1:T(8,128)(2,1)S(1)}, bf16[256,2112]{0,1:T(8,128)(2,1)S(1)}, u32[]{:S(2)}, u32[]{:S(2)}) collective-permute-start(bf16[256,2112]{0,1:T(8,128)(2,1)S(1)} %add_convert_fusion.3), channel_id=1, source_target_pairs={{0,16},{16,0},{8,24},{24,8},{1,17},{17,1},{9,25},{25,9},{2,18},{18... | collective-permute-start | bytes 3244040 | tf_op jit(solution)/shard_map/ppermute | solution.py:413
  394.0 23.5 %collective-permute-start.29 = (bf16[256,2112]{0,1:T(8,128)(2,1)S(1)}, bf16[256,2112]{0,1:T(8,128)(2,1)S(1)}, u32[]{:S(2)}, u32[]{:S(2)}) collective-permute-start(bf16[256,2112]{0,1:T(8,128)(2,1)S(1)} %add_convert_fusion.1), channel_id=1, source_target_pairs={{0,8},{8,0},{16,24},{24,16},{1,9},{9,1},{17,25},{25,17},{2,10},{10... | collective-permute-start | bytes 3244040 | tf_op jit(solution)/shard_map/ppermute | solution.py:414
  425.0 56.3 %all-to-all-start.3 = ((bf16[8,64,2112]{2,1,0:T(8,128)(2,1)}), bf16[8,64,2112]{2,1,0:T(8,128)(2,1)}, u32[]{:S(2)}, u32[]{:S(2)}) async-start(bf16[8,64,2112]{2,1,0:T(8,128)(2,1)} %bitcast.117), calls=%async_computation.6 | async-start | bytes 4456448 | tf_op jit(solution)/shard_map/all_to_all | solution.py:340
  429.4 104.5 %reduce-scatter.11.cloned.1.call-start = ((), (), s32[]{:S(2)}) async-start(), calls=%async_computation.15 | async-start | bytes 4718592 | tf_op jit(solution)/shard_map/reduce_scatter | solution.py:336
  481.3 7.8 %copy-start.11 = (bf16[1,1024,2048]{2,1,0:T(8,128)(2,1)S(1)}, bf16[1,1024,2048]{2,1,0:T(8,128)(2,1)}, u32[]{:S(2)}) copy-start(bf16[1,1024,2048]{2,1,0:T(8,128)(2,1)} %all-gather.12.cloned.1.call-done) | copy-start | bytes 12582916
  485.0 11.3 %collective-permute-start.30 = (bf16[32,2048]{1,0:T(8,128)(2,1)S(1)}, bf16[32,2048]{1,0:T(8,128)(2,1)S(1)}, u32[]{:S(2)}, u32[]{:S(2)}) collective-permute-start(bf16[32,2048]{1,0:T(8,128)(2,1)S(1)} %get-tuple-element.179), channel_id=1, source_target_pairs={{0,8},{8,0},{16,24},{24,16},{1,9},{9,1},{17,25},{25,17},{2,10},{10... | collective-permute-start | bytes 393224 | tf_op jit(solution)/shard_map/ppermute | solution.py:389
  486.5 10.5 %collective-permute-start.34 = (bf16[32,2048]{1,0:T(8,128)(2,1)S(1)}, bf16[32,2048]{1,0:T(8,128)(2,1)S(1)}, u32[]{:S(2)}, u32[]{:S(2)}) collective-permute-start(bf16[32,2048]{1,0:T(8,128)(2,1)S(1)} %get-tuple-element.180), channel_id=1, source_target_pairs={{0,16},{16,0},{8,24},{24,8},{1,17},{17,1},{9,25},{25,9},{2,18},{18... | collective-permute-start | bytes 393224 | tf_op jit(solution)/shard_map/ppermute | solution.py:389
  487.5 19.1 %collective-permute-start.33 = (bf16[32,2048]{1,0:T(8,128)(2,1)S(1)}, bf16[32,2048]{1,0:T(8,128)(2,1)S(1)}, u32[]{:S(2)}, u32[]{:S(2)}) collective-permute-start(bf16[32,2048]{1,0:T(8,128)(2,1)S(1)} %get-tuple-element.181), channel_id=1, source_target_pairs={{0,16},{16,0},{8,24},{24,8},{1,17},{17,1},{9,25},{25,9},{2,18},{18... | collective-permute-start | bytes 393224 | tf_op jit(solution)/shard_map/ppermute | solution.py:389
  488.5 5.0 collective-permute-start.31
  489.1 5.5 collective-permute-start.21
  493.5 6.1 %collective-permute-start.32 = (bf16[32,2048]{1,0:T(8,128)(2,1)S(1)}, bf16[32,2048]{1,0:T(8,128)(2,1)S(1)}, u32[]{:S(2)}, u32[]{:S(2)}) collective-permute-start(bf16[32,2048]{1,0:T(8,128)(2,1)S(1)} %add_convert_fusion.12), channel_id=1, source_target_pairs={{0,16},{16,0},{8,24},{24,8},{1,17},{17,1},{9,25},{25,9},{2,18},{18... | collective-permute-start | bytes 393224 | tf_op jit(solution)/shard_map/ppermute | solution.py:413
  495.1 9.2 %collective-permute-start.23 = (bf16[256,512]{1,0:T(8,128)(2,1)S(1)}, bf16[256,512]{1,0:T(8,128)(2,1)S(1)}, u32[]{:S(2)}, u32[]{:S(2)}) collective-permute-start(bf16[256,512]{1,0:T(8,128)(2,1)S(1)} %get-tuple-element.166), channel_id=1, source_target_pairs={{0,8},{8,0},{16,24},{24,16},{1,9},{9,1},{17,25},{25,17},{2,10},{10... | collective-permute-start | bytes 786440 | tf_op jit(solution)/shard_map/ppermute | solution.py:389
  496.3 9.2 %collective-permute-start.26 = (bf16[256,512]{1,0:T(8,128)(2,1)S(1)}, bf16[256,512]{1,0:T(8,128)(2,1)S(1)}, u32[]{:S(2)}, u32[]{:S(2)}) collective-permute-start(bf16[256,512]{1,0:T(8,128)(2,1)S(1)} %get-tuple-element.168), channel_id=1, source_target_pairs={{0,16},{16,0},{8,24},{24,8},{1,17},{17,1},{9,25},{25,9},{2,18},{18... | collective-permute-start | bytes 786440 | tf_op jit(solution)/shard_map/ppermute | solution.py:389
  499.7 8.0 %collective-permute-start.35 = (bf16[32,2048]{1,0:T(8,128)(2,1)S(1)}, bf16[32,2048]{1,0:T(8,128)(2,1)S(1)}, u32[]{:S(2)}, u32[]{:S(2)}) collective-permute-start(bf16[32,2048]{1,0:T(8,128)(2,1)S(1)} %get-tuple-element.178), channel_id=1, source_target_pairs={{0,8},{8,0},{16,24},{24,16},{1,9},{9,1},{17,25},{25,17},{2,10},{10... | collective-permute-start | bytes 393224 | tf_op jit(solution)/shard_map/ppermute | solution.py:414
  500.8 12.0 %collective-permute-start.22 = (bf16[256,512]{1,0:T(8,128)(2,1)S(1)}, bf16[256,512]{1,0:T(8,128)(2,1)S(1)}, u32[]{:S(2)}, u32[]{:S(2)}) collective-permute-start(bf16[256,512]{1,0:T(8,128)(2,1)S(1)} %get-tuple-element.165), channel_id=1, source_target_pairs={{0,8},{8,0},{16,24},{24,16},{1,9},{9,1},{17,25},{25,17},{2,10},{10... | collective-permute-start | bytes 786440 | tf_op jit(solution)/shard_map/ppermute | solution.py:389
  504.4 8.4 %collective-permute-start.25 = (bf16[256,512]{1,0:T(8,128)(2,1)S(1)}, bf16[256,512]{1,0:T(8,128)(2,1)S(1)}, u32[]{:S(2)}, u32[]{:S(2)}) collective-permute-start(bf16[256,512]{1,0:T(8,128)(2,1)S(1)} %get-tuple-element.167), channel_id=1, source_target_pairs={{0,16},{16,0},{8,24},{24,8},{1,17},{17,1},{9,25},{25,9},{2,18},{18... | collective-permute-start | bytes 786440 | tf_op jit(solution)/shard_map/ppermute | solution.py:389
  505.6 9.8 %collective-permute-start.24 = (bf16[256,512]{1,0:T(8,128)(2,1)S(1)}, bf16[256,512]{1,0:T(8,128)(2,1)S(1)}, u32[]{:S(2)}, u32[]{:S(2)}) collective-permute-start(bf16[256,512]{1,0:T(8,128)(2,1)S(1)} %get-tuple-element.169), channel_id=1, source_target_pairs={{0,16},{16,0},{8,24},{24,8},{1,17},{17,1},{9,25},{25,9},{2,18},{18... | collective-permute-start | bytes 786440 | tf_op jit(solution)/shard_map/ppermute | solution.py:413
  506.6 9.4 %collective-permute-start.27 = (bf16[256,512]{1,0:T(8,128)(2,1)S(1)}, bf16[256,512]{1,0:T(8,128)(2,1)S(1)}, u32[]{:S(2)}, u32[]{:S(2)}) collective-permute-start(bf16[256,512]{1,0:T(8,128)(2,1)S(1)} %get-tuple-element.170), channel_id=1, source_target_pairs={{0,8},{8,0},{16,24},{24,16},{1,9},{9,1},{17,25},{25,17},{2,10},{10... | collective-permute-start | bytes 786440 | tf_op jit(solution)/shard_map/ppermute | solution.py:414
  517.1 23.2 %all-to-all-start.4 = ((bf16[8,64,512]{2,1,0:T(8,128)(2,1)}), bf16[8,64,512]{2,1,0:T(8,128)(2,1)}, u32[]{:S(2)}, u32[]{:S(2)}) async-start(bf16[8,64,512]{2,1,0:T(8,128)(2,1)} %bitcast.21), calls=%async_computation.7 | async-start | bytes 1048576 | tf_op jit(solution)/shard_map/all_to_all | solution.py:340
  535.3 6.1 %copy-start.35 = (bf16[64,256]{1,0:T(8,128)(2,1)S(1)}, bf16[64,256]{1,0:T(8,128)(2,1)}, u32[]{:S(2)}) copy-start(bf16[64,256]{1,0:T(8,128)(2,1)} %param.18) | copy-start | bytes 98308
  535.3 6.1 %copy-start.37 = (bf16[64,256]{1,0:T(8,128)(2,1)S(1)}, bf16[64,256]{1,0:T(8,128)(2,1)}, u32[]{:S(2)}) copy-start(bf16[64,256]{1,0:T(8,128)(2,1)} %param.19) | copy-start | bytes 98308
  535.3 6.1 %copy-start.39 = (f32[64]{0:T(128)S(1)}, f32[64]{0:T(128)}, u32[]{:S(2)}) copy-start(f32[64]{0:T(128)} %copy-done.38) | copy-start | bytes 772
  (32 other events, 85.9 us)
Sparse Core Ops, SparseCore 0:
  9.6 75.3 all-gather.11
  136.2 50.4 reduce-scatter.4
  190.6 45.2 all-gather.5
  237.4 45.6 all-gather.7
  285.2 48.7 reduce-scatter.8
  336.1 48.3 reduce-scatter.6
  389.1 45.3 all-gather.9
  481.4 51.0 reduce-scatter.10
